TPU v7x, 32 devices: a whole 2x2x4 slice. The times are simulated.
32 devices in a mesh: expert: 4 (over y, x), shard: 8 (over z, core).
Axes of the slice: x: 2, y: 2, z: 4, core: 2. Of those that a mesh axis runs over, the one named last changes fastest.
Arguments:
- inputs: bfloat16 [8, 1024, 2048], P('shard', 'expert'), may hold values from -6 to 6
- cotangent: bfloat16 [8, 1024, 2048], P('shard', 'expert'), may hold values from -6 to 6
- blocks: int32 [8, 1024], P('shard', 'expert'), may hold values from 0 to 3, never falling along the last dimension, each value on 1 to 512 neighbouring positions
- attn_routes: int32 [8, 1024, 2], P('shard', 'expert'), may hold values from 0 to 3, all different within a row; in each aligned block of 256 rows (0 to 255, 256 to 511, ..., all dimensions but the last counted through in order) at most 160 rows name the same one
- ffn_routes: int32 [8, 1024, 2], P('shard', 'expert'), may hold values from 0 to 3, all different within a row; in each aligned block of 256 rows (0 to 255, 256 to 511, ..., all dimensions but the last counted through in order) at most 160 rows name the same one
- w_key: bfloat16 [2048, 2048], P(('expert', 'shard')), may hold values from -0.125 to 0.125
- w_value: bfloat16 [2048, 2048], P(('expert', 'shard')), may hold values from -0.125 to 0.125
- attn_router: bfloat16 [2048, 4], P(('expert', 'shard')), may hold values from -0.09375 to 0.09375
- ffn_router: bfloat16 [2048, 4], P(('expert', 'shard')), may hold values from -0.09375 to 0.09375
- attn_gain: bfloat16 [2048], P(('expert', 'shard')), may hold values from 0.5 to 1.5
- ffn_gain: bfloat16 [2048], P(('expert', 'shard')), may hold values from 0.5 to 1.5
- attn_bias: bfloat16 [2048], P(('expert', 'shard')), may hold values from -0.59765625 to 0.59765625
- ffn_bias: bfloat16 [2048], P(('expert', 'shard')), may hold values from -0.59765625 to 0.59765625
- w_query: bfloat16 [4, 2048, 2048], P('expert', 'shard'), may hold values from -0.125 to 0.125
- w_out: bfloat16 [4, 2048, 2048], P('expert', 'shard'), may hold values from -1.5 to 1.5
- w_gate: bfloat16 [4, 2048, 5632], P('expert', 'shard'), may hold values from -0.125 to 0.125
- w_up: bfloat16 [4, 2048, 5632], P('expert', 'shard'), may hold values from -0.125 to 0.125
- w_down: bfloat16 [4, 5632, 2048], P('expert', 'shard'), may hold values from -0.078125 to 0.078125
Outputs:
- outputs: bfloat16 [8, 1024, 2048], P('shard', 'expert')
- input_grad: bfloat16 [8, 1024, 2048], P('shard', 'expert')
- grad_w_key: float32 [2048, 2048], P(('expert', 'shard'))
- grad_w_value: float32 [2048, 2048], P(('expert', 'shard'))
- grad_attn_router: float32 [2048, 4], P(('expert', 'shard'))
- grad_ffn_router: float32 [2048, 4], P(('expert', 'shard'))
- grad_attn_gain: float32 [2048], P(('expert', 'shard'))
- grad_ffn_gain: float32 [2048], P(('expert', 'shard'))
- grad_attn_bias: float32 [2048], P(('expert', 'shard'))
- grad_ffn_bias: float32 [2048], P(('expert', 'shard'))
- grad_w_query: float32 [4, 2048, 2048], P('expert', 'shard')
- grad_w_out: float32 [4, 2048, 2048], P('expert', 'shard')
- grad_w_gate: float32 [4, 2048, 5632], P('expert', 'shard')
- grad_w_up: float32 [4, 2048, 5632], P('expert', 'shard')
- grad_w_down: float32 [4, 5632, 2048], P('expert', 'shard')
Inputs may be any that keep to these rules, and one draw needn't show every extreme that they name: `attn_routes`: each token names 2 different experts. Among the 256 tokens of one device (aligned blocks of rows), no expert is named by more than 160 tokens, and in some blocks one expert is named by exactly 160. `ffn_routes`: each token names 2 different experts. Among the 256 tokens of one device (aligned blocks of rows), no expert is named by more than 160 tokens, and in some blocks one expert is named by exactly 160. `blocks`: in every sequence the block ids start at 0, never fall and rise by one at a time; a block holds 1 to 512 positions, and one holds exactly 512.
All inputs are finite; a program needn't handle non-finite values.
Results may differ from a plain program's by a relative error of at most 0.02.
Values may be sent and summed in bfloat16 or wider, within the bound.
A program may use at most 512 MiB of HBM per device.

v0:
```python
import math

import jax
import jax.numpy as jnp
from jax import lax
from jax.sharding import PartitionSpec as P

HD = 128


EPSILON = 1e-06
NEGATIVE = -1e30
ROPE_BASE = 10000.0
PRECISE = lax.Precision.HIGHEST


def rms_norm(values, scaling):
    return values * lax.rsqrt(jnp.mean(values * values, axis=-1, keepdims=True) + EPSILON) * scaling


def rotate_pairs(tensor, position, direction):
    half_width = tensor.shape[-1] // 2
    frequency = jnp.exp(
        -math.log(ROPE_BASE) * jnp.arange(half_width, dtype=jnp.float32) / half_width
    )
    angles = position[..., None, None] * frequency
    cosine = jnp.cos(angles)
    sine_part = jnp.sin(angles) * direction
    first_half = tensor[..., :half_width]
    second_half = tensor[..., half_width:]
    return jnp.concatenate(
        [
            first_half * cosine - second_half * sine_part,
            second_half * cosine + first_half * sine_part,
        ],
        axis=-1,
    )


def rotary(tensor, position):
    return rotate_pairs(tensor, position, 1.0)


def unrotary(tensor, position):
    return rotate_pairs(tensor, position, -1.0)


def gate_weights(logits, routes):
    picked = jnp.take_along_axis(logits, routes, axis=-1)
    return jax.nn.softmax(picked, axis=-1)


def product(left_side, right_side):
    return jnp.dot(left_side, right_side, preferred_element_type=jnp.float32)


def contract_first(left_side, right_side, precision=None):
    return lax.dot_general(
        left_side,
        right_side,
        (((0,), (0,)), ((), ())),
        precision=precision,
        preferred_element_type=jnp.float32,
    )


def contract_last(left_side, right_side):
    return lax.dot_general(
        left_side, right_side, (((1,), (1,)), ((), ())), preferred_element_type=jnp.float32
    )


def flatten_rows(tensor):
    return tensor.reshape(-1, tensor.shape[-1])


def dispatch(routes, experts, capacity):
    token_count = routes.shape[0]
    top_count = routes.shape[1]
    spread = routes.reshape(-1)
    onehot = (spread[:, None] == jnp.arange(experts, dtype=jnp.int32)[None, :]).astype(jnp.int32)
    ranking = jnp.sum(onehot * (jnp.cumsum(onehot, axis=0) - 1), axis=1)
    slot_index = spread * capacity + ranking
    route_ids = jnp.arange(token_count * top_count, dtype=jnp.int32)
    route_of_slot = jnp.zeros((experts * capacity,), jnp.int32).at[slot_index].set(route_ids)
    filled = jnp.zeros((experts * capacity,), jnp.int32).at[slot_index].set(1) > 0
    return (slot_index.reshape(token_count, top_count), route_of_slot, filled)


def combine(returned, slot_index, gates):
    picked = returned[slot_index].astype(jnp.float32)
    return jnp.sum(gates[..., None] * picked, axis=1)


def split_heads(tensor, head_count):
    return tensor.reshape(tensor.shape[0], head_count, -1).transpose(1, 0, 2)


def attend_forward(query_rows, query_meta, query_w, out_w, key_heads, value_heads, key_blocks):
    row_count = query_rows.shape[0]
    head_count = key_heads.shape[0]
    head_width = key_heads.shape[2]
    score_scale = head_width ** (-0.5)
    query_raw = product(query_rows, query_w)
    queries = rotary(
        query_raw.reshape(row_count, head_count, head_width), query_meta[:, 0].astype(jnp.float32)
    ).astype(jnp.bfloat16)
    allowed = key_blocks[None, :] <= query_meta[:, 1:2]

    def one_head(operands):
        query_head, key_head, value_head = operands
        scores = jnp.where(allowed, contract_last(query_head, key_head) * score_scale, NEGATIVE)
        row_peak = jnp.max(scores, axis=-1, keepdims=True)
        exponent = jnp.exp(scores - row_peak)
        row_total = jnp.sum(exponent, axis=-1, keepdims=True)
        weights = (exponent / row_total).astype(jnp.bfloat16)
        return (
            product(weights, value_head).astype(jnp.bfloat16),
            (row_peak + jnp.log(row_total))[:, 0],
        )

    mixed_heads, log_total = lax.map(one_head, (queries.transpose(1, 0, 2), key_heads, value_heads))
    mixed_rows = mixed_heads.transpose(1, 0, 2).reshape(row_count, -1)
    out_rows = product(mixed_rows, out_w).astype(jnp.bfloat16)
    return (out_rows, queries.reshape(row_count, -1), mixed_rows, log_total.T)


def attend_backward(
    grad_out,
    query_rows,
    query_meta,
    queries,
    mixed_rows,
    log_total,
    query_w,
    out_w,
    key_heads,
    value_heads,
    key_blocks,
):
    row_count = query_rows.shape[0]
    head_count = key_heads.shape[0]
    head_width = key_heads.shape[2]
    length = key_heads.shape[1]
    score_scale = head_width ** (-0.5)
    grad_out_w = contract_first(mixed_rows, grad_out)
    grad_mixed = contract_last(grad_out, out_w).astype(jnp.bfloat16)
    allowed = key_blocks[None, :] <= query_meta[:, 1:2]

    def one_head(operands):
        query_head, key_head, value_head, grad_head, total_head = operands
        scores = jnp.where(allowed, contract_last(query_head, key_head) * score_scale, NEGATIVE)
        probs_full = jnp.exp(scores - total_head[:, None])
        grad_value = contract_first(probs_full.astype(jnp.bfloat16), grad_head)
        grad_probs = contract_last(grad_head, value_head)
        center = jnp.sum(probs_full * grad_probs, axis=-1, keepdims=True)
        grad_scores = (probs_full * (grad_probs - center)).astype(jnp.bfloat16)
        grad_query = product(grad_scores, key_head) * score_scale
        grad_key = contract_first(grad_scores, query_head) * score_scale
        return (grad_query, grad_key, grad_value)

    grad_q_heads, grad_k_heads, grad_v_heads = lax.map(
        one_head,
        (
            split_heads(queries, head_count),
            key_heads,
            value_heads,
            split_heads(grad_mixed, head_count),
            log_total.T,
        ),
    )
    grad_query_raw = (
        unrotary(grad_q_heads.transpose(1, 0, 2), query_meta[:, 0].astype(jnp.float32))
        .reshape(row_count, -1)
        .astype(jnp.bfloat16)
    )
    grad_query_w = contract_first(query_rows, grad_query_raw)
    grad_rows = contract_last(grad_query_raw, query_w).astype(jnp.bfloat16)
    grad_keys = grad_k_heads.transpose(1, 0, 2).reshape(length, -1)
    grad_values = grad_v_heads.transpose(1, 0, 2).reshape(length, -1)
    return (grad_rows, grad_query_w, grad_out_w, grad_keys, grad_values)


def ffn_forward(ffn_rows, gate_w, up_w, down_w):
    gate_pre = product(ffn_rows, gate_w)
    up_pre = product(ffn_rows, up_w)
    hidden = (jax.nn.silu(gate_pre) * up_pre).astype(jnp.bfloat16)
    return (product(hidden, down_w).astype(jnp.bfloat16), gate_pre, up_pre)


def ffn_backward(grad_out, ffn_rows, gate_pre, up_pre, gate_w, up_w, down_w):
    hidden, pull_back = jax.vjp(
        lambda gate_in, up_in: jax.nn.silu(gate_in) * up_in, gate_pre, up_pre
    )
    grad_down_w = contract_first(hidden.astype(jnp.bfloat16), grad_out)
    grad_gate, grad_up = pull_back(contract_last(grad_out, down_w))
    grad_gate = grad_gate.astype(jnp.bfloat16)
    grad_up = grad_up.astype(jnp.bfloat16)
    grad_gate_w = contract_first(ffn_rows, grad_gate)
    grad_up_w = contract_first(ffn_rows, grad_up)
    grad_rows = (contract_last(grad_gate, gate_w) + contract_last(grad_up, up_w)).astype(
        jnp.bfloat16
    )
    return (grad_rows, grad_gate_w, grad_up_w, grad_down_w)


def gather_experts(w_query, w_out, w_gate, w_up, w_down):
    gathered = (
        lax.all_gather(w_query, "shard", axis=1, tiled=True),
        lax.all_gather(w_out, "shard", axis=1, tiled=True),
        lax.all_gather(w_gate, "shard", axis=1, tiled=True),
        lax.all_gather(w_up, "shard", axis=1, tiled=True),
        lax.all_gather(w_down, "shard", axis=1, tiled=True),
    )
    return tuple((member[0] for member in gathered))


def local(
    inputs,
    cotangent,
    blocks,
    attn_routes,
    ffn_routes,
    w_key,
    w_value,
    attn_router,
    ffn_router,
    attn_gain,
    ffn_gain,
    attn_bias,
    ffn_bias,
    w_query,
    w_out,
    w_gate,
    w_up,
    w_down,
):
    token_count = inputs.shape[1]
    top_count = attn_routes.shape[2]
    experts = lax.axis_size("expert")
    capacity = 5 * token_count * top_count // (4 * experts)
    expert_place = lax.axis_index("expert")
    shared = (
        lax.all_gather(w_key, ("expert", "shard"), axis=0, tiled=True),
        lax.all_gather(w_value, ("expert", "shard"), axis=0, tiled=True),
        lax.all_gather(attn_router, ("expert", "shard"), axis=0, tiled=True),
        lax.all_gather(ffn_router, ("expert", "shard"), axis=0, tiled=True),
        lax.all_gather(attn_gain, ("expert", "shard"), axis=0, tiled=True),
        lax.all_gather(ffn_gain, ("expert", "shard"), axis=0, tiled=True),
        lax.all_gather(attn_bias, ("expert", "shard"), axis=0, tiled=True),
        lax.all_gather(ffn_bias, ("expert", "shard"), axis=0, tiled=True),
    )
    key_w = shared[0]
    value_w = shared[1]
    router_a = shared[2]
    router_f = shared[3]
    gain_a = shared[4].astype(jnp.float32)
    gain_f = shared[5].astype(jnp.float32)
    bias_a = shared[6].astype(jnp.float32)
    bias_f = shared[7].astype(jnp.float32)
    query_w, out_w, gate_w, up_w, down_w = gather_experts(w_query, w_out, w_gate, w_up, w_down)
    head_count = key_w.shape[1] // HD
    positions = (expert_place * token_count + jnp.arange(token_count, dtype=jnp.int32)).astype(
        jnp.float32
    )
    block_in = inputs[0].astype(jnp.float32)
    own_blocks = blocks[0]
    routes_a = attn_routes[0]
    routes_f = ffn_routes[0]
    h_attn = rms_norm(block_in, gain_a).astype(jnp.bfloat16)
    logits_a = product(h_attn, router_a)
    gates_a = gate_weights(logits_a, routes_a)
    key_rot = (
        rotary(product(h_attn, key_w).reshape(token_count, head_count, HD), positions)
        .reshape(token_count, -1)
        .astype(jnp.bfloat16)
    )
    value_own = product(h_attn, value_w).astype(jnp.bfloat16)
    key_seq, value_seq, block_seq = (
        lax.all_gather(key_rot[None], "expert", axis=1, tiled=True),
        lax.all_gather(value_own[None], "expert", axis=1, tiled=True),
        lax.all_gather(blocks, "expert", axis=1, tiled=True),
    )
    length = key_seq.shape[1]
    key_heads = key_seq[0].reshape(length, head_count, HD).transpose(1, 0, 2)
    value_heads = value_seq[0].reshape(length, head_count, HD).transpose(1, 0, 2)
    key_blocks = block_seq[0]
    slot_a, route_slot_a, filled_a = dispatch(routes_a, experts, capacity)
    token_a = route_slot_a // top_count
    send_a = jnp.where(filled_a[:, None], h_attn[token_a], jnp.zeros((), jnp.bfloat16)).reshape(
        experts, capacity, -1
    )
    meta_a = jnp.where(
        filled_a[:, None],
        jnp.stack([expert_place * token_count + token_a, own_blocks[token_a]], axis=1),
        0,
    ).reshape(experts, capacity, 2)
    piece_rows = lax.all_to_all(send_a, "expert", split_axis=0, concat_axis=0, tiled=True)
    piece_meta = lax.all_to_all(meta_a, "expert", split_axis=0, concat_axis=0, tiled=True)
    lead_shape = piece_rows.shape[:2]
    outcome = attend_forward(
        flatten_rows(piece_rows),
        flatten_rows(piece_meta),
        query_w,
        out_w,
        key_heads,
        value_heads,
        key_blocks,
    )
    out_a, queries_a, mixed_a, total_a, rows_a, kept_meta = tuple(
        (member.reshape(lead_shape + (-1,)) for member in outcome)
    ) + (piece_rows, piece_meta)
    back_a = lax.all_to_all(out_a, "expert", split_axis=0, concat_axis=0, tiled=True).reshape(
        experts * capacity, -1
    )
    middle = block_in + combine(back_a, slot_a, gates_a) + bias_a
    h_ffn = rms_norm(middle, gain_f).astype(jnp.bfloat16)
    logits_f = product(h_ffn, router_f)
    gates_f = gate_weights(logits_f, routes_f)
    slot_f, route_slot_f, filled_f = dispatch(routes_f, experts, capacity)
    token_f = route_slot_f // top_count
    send_f = jnp.where(filled_f[:, None], h_ffn[token_f], jnp.zeros((), jnp.bfloat16)).reshape(
        experts, capacity, -1
    )
    piece_rows = lax.all_to_all(send_f, "expert", split_axis=0, concat_axis=0, tiled=True)
    lead_shape = piece_rows.shape[:2]
    outcome = ffn_forward(flatten_rows(piece_rows), gate_w, up_w, down_w)
    out_f, gate_pre, up_pre, rows_f = tuple(
        (member.reshape(lead_shape + (-1,)) for member in outcome)
    ) + (piece_rows,)
    back_f = lax.all_to_all(out_f, "expert", split_axis=0, concat_axis=0, tiled=True).reshape(
        experts * capacity, -1
    )
    outputs = middle + combine(back_f, slot_f, gates_f) + bias_f
    back_query_w, back_out_w, back_gate_w, back_up_w, back_down_w = gather_experts(
        w_query, w_out, w_gate, w_up, w_down
    )

    def row_grads(grad_tokens, gates, route_slot, filled):
        weight_of_slot = gates.reshape(-1)[route_slot]
        return jnp.where(
            filled[:, None], weight_of_slot[:, None] * grad_tokens[route_slot // top_count], 0.0
        ).astype(jnp.bfloat16)

    grad_out = cotangent[0].astype(jnp.float32)
    grad_bias_f = jnp.sum(grad_out, axis=0)
    grad_gates_f = jnp.sum(grad_out[:, None, :] * back_f[slot_f].astype(jnp.float32), axis=-1)
    arrived_f = lax.all_to_all(
        row_grads(grad_out, gates_f, route_slot_f, filled_f).reshape(experts, capacity, -1),
        "expert",
        split_axis=0,
        concat_axis=0,
        tiled=True,
    )
    grad_rows_f, grad_gate_w, grad_up_w, grad_down_w = ffn_backward(
        flatten_rows(arrived_f),
        flatten_rows(rows_f),
        flatten_rows(gate_pre),
        flatten_rows(up_pre),
        back_gate_w,
        back_up_w,
        back_down_w,
    )
    ffn_sums = (grad_gate_w, grad_up_w, grad_down_w)
    returned_f = lax.all_to_all(
        grad_rows_f.reshape(experts, capacity, -1),
        "expert",
        split_axis=0,
        concat_axis=0,
        tiled=True,
    ).reshape(experts * capacity, -1)
    gate_pull_f = jax.vjp(lambda logit_in: gate_weights(logit_in, routes_f), logits_f)[1]
    grad_logits_f = gate_pull_f(grad_gates_f)[0]
    grad_router_f = contract_first(h_ffn.astype(jnp.float32), grad_logits_f, PRECISE)
    grad_h_ffn = jnp.sum(returned_f[slot_f].astype(jnp.float32), axis=1) + jnp.dot(
        grad_logits_f, router_f.astype(jnp.float32).T, precision=PRECISE
    )
    norm_pull_f = jax.vjp(rms_norm, middle, gain_f)[1]
    grad_norm_f, grad_gain_f = norm_pull_f(grad_h_ffn)
    grad_middle = grad_out + grad_norm_f
    grad_bias_a = jnp.sum(grad_middle, axis=0)
    grad_gates_a = jnp.sum(grad_middle[:, None, :] * back_a[slot_a].astype(jnp.float32), axis=-1)
    arrived_a = lax.all_to_all(
        row_grads(grad_middle, gates_a, route_slot_a, filled_a).reshape(experts, capacity, -1),
        "expert",
        split_axis=0,
        concat_axis=0,
        tiled=True,
    )
    grad_rows_a, grad_query_w, grad_out_w, grad_keys, grad_values = attend_backward(
        flatten_rows(arrived_a),
        flatten_rows(rows_a),
        flatten_rows(kept_meta),
        flatten_rows(queries_a),
        flatten_rows(mixed_a),
        flatten_rows(total_a),
        back_query_w,
        back_out_w,
        key_heads,
        value_heads,
        key_blocks,
    )
    attn_sums = (grad_query_w, grad_out_w)
    returned_a = lax.all_to_all(
        grad_rows_a.reshape(experts, capacity, -1),
        "expert",
        split_axis=0,
        concat_axis=0,
        tiled=True,
    ).reshape(experts * capacity, -1)
    grad_key_seq, grad_value_seq = (
        lax.psum_scatter(
            grad_keys[None].astype(jnp.bfloat16), "expert", scatter_dimension=1, tiled=True
        ).astype(jnp.float32),
        lax.psum_scatter(
            grad_values[None].astype(jnp.bfloat16), "expert", scatter_dimension=1, tiled=True
        ).astype(jnp.float32),
    )
    grad_key_raw = (
        unrotary(grad_key_seq[0].reshape(token_count, head_count, HD), positions)
        .reshape(token_count, -1)
        .astype(jnp.bfloat16)
    )
    grad_value_own = grad_value_seq[0].astype(jnp.bfloat16)
    grad_key_w = contract_first(h_attn, grad_key_raw)
    grad_value_w = contract_first(h_attn, grad_value_own)
    gate_pull_a = jax.vjp(lambda logit_in: gate_weights(logit_in, routes_a), logits_a)[1]
    grad_logits_a = gate_pull_a(grad_gates_a)[0]
    grad_router_a = contract_first(h_attn.astype(jnp.float32), grad_logits_a, PRECISE)
    grad_h_attn = jnp.sum(returned_a[slot_a].astype(jnp.float32), axis=1)
    grad_h_attn = (
        grad_h_attn + contract_last(grad_key_raw, key_w) + contract_last(grad_value_own, value_w)
    )
    grad_h_attn = grad_h_attn + jnp.dot(
        grad_logits_a, router_a.astype(jnp.float32).T, precision=PRECISE
    )
    norm_pull_a = jax.vjp(rms_norm, block_in, gain_a)[1]
    grad_norm_a, grad_gain_a = norm_pull_a(grad_h_attn)
    input_grad = (grad_middle + grad_norm_a).astype(jnp.bfloat16)[None]
    expert_sums = (
        lax.psum_scatter(
            attn_sums[0][None].astype(jnp.bfloat16), "shard", scatter_dimension=1, tiled=True
        ).astype(jnp.float32),
        lax.psum_scatter(
            attn_sums[1][None].astype(jnp.bfloat16), "shard", scatter_dimension=1, tiled=True
        ).astype(jnp.float32),
        lax.psum_scatter(
            ffn_sums[0][None].astype(jnp.bfloat16), "shard", scatter_dimension=1, tiled=True
        ).astype(jnp.float32),
        lax.psum_scatter(
            ffn_sums[1][None].astype(jnp.bfloat16), "shard", scatter_dimension=1, tiled=True
        ).astype(jnp.float32),
        lax.psum_scatter(
            ffn_sums[2][None].astype(jnp.bfloat16), "shard", scatter_dimension=1, tiled=True
        ).astype(jnp.float32),
    )
    shared_sums = (
        lax.psum_scatter(grad_key_w, ("expert", "shard"), scatter_dimension=0, tiled=True),
        lax.psum_scatter(grad_value_w, ("expert", "shard"), scatter_dimension=0, tiled=True),
        lax.psum_scatter(grad_router_a, ("expert", "shard"), scatter_dimension=0, tiled=True),
        lax.psum_scatter(grad_router_f, ("expert", "shard"), scatter_dimension=0, tiled=True),
        lax.psum_scatter(grad_gain_a, ("expert", "shard"), scatter_dimension=0, tiled=True),
        lax.psum_scatter(grad_gain_f, ("expert", "shard"), scatter_dimension=0, tiled=True),
        lax.psum_scatter(grad_bias_a, ("expert", "shard"), scatter_dimension=0, tiled=True),
        lax.psum_scatter(grad_bias_f, ("expert", "shard"), scatter_dimension=0, tiled=True),
    )
    return (
        outputs.astype(jnp.bfloat16)[None],
        input_grad,
        shared_sums[0],
        shared_sums[1],
        shared_sums[2],
        shared_sums[3],
        shared_sums[4],
        shared_sums[5],
        shared_sums[6],
        shared_sums[7],
        expert_sums[0],
        expert_sums[1],
        expert_sums[2],
        expert_sums[3],
        expert_sums[4],
    )


def solution(mesh):
    in_specs = (
        P("shard", "expert", None),
        P("shard", "expert", None),
        P("shard", "expert"),
        P("shard", "expert", None),
        P("shard", "expert", None),
        P(("expert", "shard"), None),
        P(("expert", "shard"), None),
        P(("expert", "shard"), None),
        P(("expert", "shard"), None),
        P(("expert", "shard")),
        P(("expert", "shard")),
        P(("expert", "shard")),
        P(("expert", "shard")),
        P("expert", "shard", None),
        P("expert", "shard", None),
        P("expert", "shard", None),
        P("expert", "shard", None),
        P("expert", "shard", None),
    )
    out_specs = (
        P("shard", "expert", None),
        P("shard", "expert", None),
        P(("expert", "shard"), None),
        P(("expert", "shard"), None),
        P(("expert", "shard"), None),
        P(("expert", "shard"), None),
        P(("expert", "shard")),
        P(("expert", "shard")),
        P(("expert", "shard")),
        P(("expert", "shard")),
        P("expert", "shard", None),
        P("expert", "shard", None),
        P("expert", "shard", None),
        P("expert", "shard", None),
        P("expert", "shard", None),
    )
    return jax.shard_map(local, mesh=mesh, in_specs=in_specs, out_specs=out_specs, check_vma=False)
```

profile of v0, /device:TPU:0, one launch (start us, length us, event | category | flops | bytes accessed | tf_op | source)
XLA Modules:
  0.0 3214.2 jit_solution(8614644973968229846)
XLA Ops:
  12.9 42.9 %all-reduce.9 = (bf16[2048]{0:T(1024)(128)(2,1)S(1)}, bf16[2048]{0:T(1024)(128)(2,1)S(1)}, bf16[2048]{0:T(1024)(128)(2,1)S(1)}, bf16[2048]{0:T(1024)(128)(2,1)}) all-reduce(bf16[2048]{0:T(1024)(128)(2,1)S(1)} %dynamic-update-slice, bf16[2048]{0:T(1024)(128)(2,1)S(1)} %dynamic-update-slice.1, ...), channel_id=1, replica_groups=mesh['expert'=4,'shard'=8] {'expert','shard'}, use_global_device_ids=true, to_apply=%add | all-reduce | flops 8192 | bytes 32768
  58.9 32.2 %all-gather.15.cloned.1.call-done = bf16[2048,2048]{1,0:T(8,128)(2,1)} async-done(((bf16[64,2048]{1,0:T(8,128)(2,1)}), bf16[2048,2048]{1,0:T(8,128)(2,1)}) %all-gather.15.cloned.1.call-update) | async-done | bytes 8388624 | tf_op jit(solution)/shard_map/all_gather | solution.py:244
  111.1 58.7 %all-gather.19.cloned.1.call-done = bf16[2048,2048]{1,0:T(8,128)(2,1)} async-done(((bf16[64,2048]{1,0:T(8,128)(2,1)}), bf16[2048,2048]{1,0:T(8,128)(2,1)}) %all-gather.19.cloned.1.call-update) | async-done | bytes 8388624 | tf_op jit(solution)/shard_map/all_gather | solution.py:245
  222.9 41.7 %all-gather.1 = bf16[32,64,4]{1,2,0:T(4,128)(2,1)S(1)} all-gather(bf16[1,64,4]{1,2,0:T(4,128)(2,1)S(1)} %bitcast.429), channel_id=1, replica_groups=mesh['expert'=4,'shard'=8] {'expert','shard'}, dimensions={0}, use_global_device_ids=true | all-gather | bytes 16896 | tf_op jit(solution)/shard_map/all_gather | solution.py:246
  319.7 40.7 %all-gather.29.cloned.1.call-done = bf16[1024,2048]{1,0:T(8,128)(2,1)} async-done(((bf16[256,2048]{1,0:T(8,128)(2,1)}), bf16[1024,2048]{1,0:T(8,128)(2,1)}) %all-gather.29.cloned.1.call-update) | async-done | bytes 4194320 | tf_op jit(solution)/shard_map/all_gather | solution.py:281
  365.7 97.6 %while.28 = (s32[]{:T(128)}, bf16[16,640,128]{1,2,0:T(8,128)(2,1)}, f32[16,640]{1,0:T(8,128)}, bf16[16,640,128]{2,1,0:T(8,128)(2,1)}, bf16[16,1024,128]{2,1,0:T(...) while((s32[]{:T(128)}, bf16[16,640,128]{1,2,0:T(8,128)(2,1)}, ...), condition=%wide.region_11.13_spmd.clone, body=%wide.region_8.12_spmd.clone.sunk | while | flops 341523840 | bytes 9411177 | solution.py:122
  483.4 48.7 %all-gather.2 = bf16[32,64,4]{1,2,0:T(4,128)(2,1)S(1)} all-gather(bf16[1,64,4]{1,2,0:T(4,128)(2,1)S(1)} %bitcast.430), channel_id=1, replica_groups=mesh['expert'=4,'shard'=8] {'expert','shard'}, dimensions={0}, use_global_device_ids=true | all-gather | bytes 16896 | tf_op jit(solution)/shard_map/all_gather | solution.py:247
  600.8 23.7 all-to-all-done.5
  647.0 23.7 fusion.46
  670.7 178.8 %all-gather.25.cloned.1.call-done = bf16[1,2048,5632]{2,1,0:T(8,128)(2,1)} async-done(((bf16[1,256,5632]{2,1,0:T(8,128)(2,1)}), bf16[1,2048,5632]{2,1,0:T(8,128)(2,1)}) %all-gather.25.cloned.1.call-update) | async-done | bytes 23068688 | tf_op jit(solution)/shard_map/all_gather | solution.py:212
  849.6 22.5 fusion.52
  872.0 180.1 %all-gather.23.cloned.1.call-done = bf16[1,2048,5632]{2,1,0:T(8,128)(2,1)} async-done(((bf16[1,256,5632]{2,1,0:T(8,128)(2,1)}), bf16[1,2048,5632]{2,1,0:T(8,128)(2,1)}) %all-gather.23.cloned.1.call-update) | async-done | bytes 23068688 | tf_op jit(solution)/shard_map/all_gather | solution.py:211
  1052.1 32.5 %fusion.60 = (bf16[640,5632]{1,0:T(8,128)(2,1)}, bf16[640,5632]{1,0:T(8,128)(2,1)}, bf16[640,5632]{1,0:T(8,128)(2,1)}) fusion(f32[640,5632]{1,0:T(8,128)} %fusion.46, f32[640,5632]{1,0:T(8,128)} %fusion.52, bf16[640,2048]{1,0:T(8,128)(2,1)S(1)} %bitcast.410, bf16[1,2048,5632]{2,1,0:T(8,128)(2,1)} %all-gather.23.cloned.1.call-done), kind=kOutput, calls=%fused_computation.92 | convolution fusion | flops 14821621760 | bytes 76152832 | tf_op jit(solution)/shard_map/dot_general | solution.py:54
  1084.6 21.2 fusion.73
  1109.4 20.4 fusion.50
  1129.9 21.4 add_convert_fusion
  1206.7 24.4 scatter_fusion
  1250.5 30.3 all-to-all-done.7
  1292.8 294.2 %while.29 = (s32[]{:T(128)}, f32[16,640,128]{1,2,0:T(8,128)}, bf16[16,1024,128]{1,2,0:T(8,128)(2,1)}, bf16[16,1024,128]{1,2,0:T(8,128)(2,1)}, bf16[16,640,128]{2...) while((s32[]{:T(128)}, f32[16,640,128]{1,2,0:T(8,128)}, ...), condition=%wide.region_31.34_spmd.clone, body=%wide.region_29.33_spmd.clone.sunk | while | flops 845757824 | bytes 35086484 | solution.py:162
  1595.4 24.4 scatter_fusion.1
  1652.1 24.8 convert_bitcast_fusion.2
  1676.9 25.0 convert_bitcast_fusion.1
  1702.0 25.8 convert_bitcast_fusion
  1769.3 63.3 %reduce-scatter.36.cloned.1.call-done = f32[64,4]{1,0:T(8,128)} async-done(((f32[2048,4]{1,0:T(8,128)}), f32[64,4]{1,0:T(8,128)}) %reduce-scatter.36.cloned.1.call-update) | async-done | bytes 1040
  1834.0 134.8 %reduce-scatter.34.cloned.1.call-done = f32[64,4]{1,0:T(8,128)} async-done(((f32[2048,4]{1,0:T(8,128)}), f32[64,4]{1,0:T(8,128)}) %reduce-scatter.34.cloned.1.call-update) | async-done | bytes 1040
  2001.6 39.0 %all-reduce.8 = (f32[2048]{0:T(1024)S(1)}, f32[2048]{0:T(1024)S(1)}, f32[2048]{0:T(1024)S(1)}, f32[2048]{0:T(1024)S(1)}) all-reduce(f32[2048]{0:T(1024)S(1)} %get-tuple-element.285, f32[2048]{0:T(1024)S(1)} %copy-done.63, f32[2048]{0:T(1024)S(1)} %copy-done.66, ...), channel_id=9, replica_groups=mesh['expert'=4,'shard'=8] {'expert','shard'}, use_global_device_ids=true, to_apply=%region_46.49.clone | all-reduce | flops 8192 | bytes 65536
  2060.5 87.4 %reduce-scatter.24.cloned.1.call-done = bf16[1,256,2048]{2,1,0:T(8,128)(2,1)} async-done(((bf16[1,2048,2048]{2,1,0:T(8,128)(2,1)}), bf16[1,256,2048]{2,1,0:T(8,128)(2,1)}) %reduce-scatter.24.cloned.1.call-update) | async-done | bytes 1048592 | tf_op jit(solution)/shard_map/reduce_scatter | solution.py:441
  2150.7 225.3 %reduce-scatter.28.cloned.1.call-done = bf16[1,256,5632]{2,1,0:T(8,128)(2,1)} async-done(((bf16[1,2048,5632]{2,1,0:T(8,128)(2,1)}), bf16[1,256,5632]{2,1,0:T(8,128)(2,1)}) %reduce-scatter.28.cloned.1.call-update) | async-done | bytes 2883600 | tf_op jit(solution)/shard_map/reduce_scatter | solution.py:447
  2380.9 223.0 %reduce-scatter.30.cloned.1.call-done = bf16[1,256,5632]{2,1,0:T(8,128)(2,1)} async-done(((bf16[1,2048,5632]{2,1,0:T(8,128)(2,1)}), bf16[1,256,5632]{2,1,0:T(8,128)(2,1)}) %reduce-scatter.30.cloned.1.call-update) | async-done | bytes 2883600 | tf_op jit(solution)/shard_map/reduce_scatter | solution.py:450
  2609.0 223.1 %reduce-scatter.32.cloned.1.call-done = bf16[1,704,2048]{2,1,0:T(8,128)(2,1)} async-done(((bf16[1,5632,2048]{2,1,0:T(8,128)(2,1)}), bf16[1,704,2048]{2,1,0:T(8,128)(2,1)}) %reduce-scatter.32.cloned.1.call-update) | async-done | bytes 2883600 | tf_op jit(solution)/shard_map/reduce_scatter | solution.py:453
  2837.2 182.8 %reduce-scatter.20.cloned.1.call-done = f32[64,2048]{1,0:T(8,128)} async-done(((f32[2048,2048]{1,0:T(8,128)}), f32[64,2048]{1,0:T(8,128)}) %reduce-scatter.20.cloned.1.call-update) | async-done | bytes 524304 | tf_op jit(solution)/shard_map/reduce_scatter | solution.py:458
  3020.0 187.1 %reduce-scatter.22.cloned.1.call-done = f32[64,2048]{1,0:T(8,128)} async-done(((f32[2048,2048]{1,0:T(8,128)}), f32[64,2048]{1,0:T(8,128)}) %reduce-scatter.22.cloned.1.call-update) | async-done | bytes 524304 | tf_op jit(solution)/shard_map/reduce_scatter | solution.py:459
  (801 shorter events, 887.6 us)
Async XLA Ops:
  7.2 83.9 %all-gather.15.cloned.1.call-start = ((), (), s32[]{:S(2)}) async-start(), calls=%async_computation.21 | async-start | bytes 8650752 | tf_op jit(solution)/shard_map/all_gather | solution.py:244
  7.9 161.9 %all-gather.19.cloned.1.call-start = ((), (), s32[]{:S(2)}) async-start(), calls=%async_computation.23 | async-start | bytes 8650752 | tf_op jit(solution)/shard_map/all_gather | solution.py:245
  8.7 278.5 %all-gather.13.cloned.1.call-start = ((), (), s32[]{:S(2)}) async-start(), calls=%async_computation.20 | async-start | bytes 9437184 | tf_op jit(solution)/shard_map/all_gather | solution.py:209
  9.4 303.8 %all-gather.17.cloned.1.call-start = ((), (), s32[]{:S(2)}) async-start(), calls=%async_computation.22 | async-start | bytes 5242880 | tf_op jit(solution)/shard_map/all_gather | solution.py:280
  110.7 249.7 %all-gather.29.cloned.1.call-start = ((), (), s32[]{:S(2)}) async-start(), calls=%async_computation.37 | async-start | bytes 5242880 | tf_op jit(solution)/shard_map/all_gather | solution.py:281
  176.6 286.8 %all-gather.21.cloned.1.call-start = ((), (), s32[]{:S(2)}) async-start(), calls=%async_computation.24 | async-start | bytes 9437184 | tf_op jit(solution)/shard_map/all_gather | solution.py:210
  177.1 469.9 %all-gather.27.cloned.1.call-start = ((), (), s32[]{:S(2)}) async-start(), calls=%async_computation.27 | async-start | bytes 25952256 | tf_op jit(solution)/shard_map/all_gather | solution.py:213
  177.9 671.7 %all-gather.25.cloned.1.call-start = ((), (), s32[]{:S(2)}) async-start(), calls=%async_computation.26 | async-start | bytes 25952256 | tf_op jit(solution)/shard_map/all_gather | solution.py:212
  178.7 873.4 %all-gather.23.cloned.1.call-start = ((), (), s32[]{:S(2)}) async-start(), calls=%async_computation.25 | async-start | bytes 25952256 | tf_op jit(solution)/shard_map/all_gather | solution.py:211
  192.6 24.4 all-to-all-start.1
  217.0 82.5 %all-to-all-start = ((bf16[4,160,2048]{2,1,0:T(8,128)(2,1)}), bf16[4,160,2048]{2,1,0:T(8,128)(2,1)}, u32[]{:S(2)}, u32[]{:S(2)}) async-start(bf16[4,160,2048]{2,1,0:T(8,128)(2,1)} %broadcast_select_fusion.1), calls=%async_computation | async-start | bytes 5242880 | tf_op jit(solution)/shard_map/all_to_all | solution.py:298
  276.4 283.2 %copy-start.51 = (f32[2048]{0:T(1024)}, f32[2048]{0:T(1024)S(1)}, u32[]{:S(2)}) copy-start(f32[2048]{0:T(1024)S(1)} %convert_element_type.289) | copy-start | bytes 24580
  473.3 65.4 %all-to-all-start.2 = ((bf16[4,160,2048]{2,1,0:T(8,128)(2,1)}), bf16[4,160,2048]{2,1,0:T(8,128)(2,1)}, u32[]{:S(2)}, u32[]{:S(2)}) async-start(bf16[4,160,2048]{2,1,0:T(8,128)(2,1)} %bitcast.415), calls=%async_computation.2 | async-start | bytes 5242880 | tf_op jit(solution)/shard_map/all_to_all | solution.py:313
  581.8 42.7 %all-to-all-start.5 = ((bf16[4,160,2048]{2,1,0:T(8,128)(2,1)}), bf16[4,160,2048]{2,1,0:T(8,128)(2,1)}, u32[]{:S(2)}, u32[]{:S(2)}) async-start(bf16[4,160,2048]{2,1,0:T(8,128)(2,1)} %select_convert_fusion.1), calls=%async_computation.5 | async-start | bytes 5242880 | tf_op jit(solution)/shard_map/all_to_all | solution.py:348
  624.5 46.2 %all-to-all-start.3 = ((bf16[4,160,2048]{2,1,0:T(8,128)(2,1)}), bf16[4,160,2048]{2,1,0:T(8,128)(2,1)S(1)}, u32[]{:S(2)}, u32[]{:S(2)}) async-start(bf16[4,160,2048]{2,1,0:T(8,128)(2,1)} %broadcast_select_fusion), calls=%async_computation.3 | async-start | bytes 5242880 | tf_op jit(solution)/shard_map/all_to_all | solution.py:325
  670.7 381.4 %copy-start.26 = (bf16[4,160,2048]{2,1,0:T(8,128)(2,1)}, bf16[4,160,2048]{2,1,0:T(8,128)(2,1)S(1)}, u32[]{:S(2)}) copy-start(bf16[4,160,2048]{2,1,0:T(8,128)(2,1)S(1)} %all-to-all-done.3) | copy-start | bytes 7864324
  1105.8 45.5 %all-to-all-start.4 = ((bf16[4,160,2048]{2,1,0:T(8,128)(2,1)}), bf16[4,160,2048]{2,1,0:T(8,128)(2,1)S(1)}, u32[]{:S(2)}, u32[]{:S(2)}) async-start(bf16[4,160,2048]{2,1,0:T(8,128)(2,1)} %bitcast.418), calls=%async_computation.4 | async-start | bytes 5242880 | tf_op jit(solution)/shard_map/all_to_all | solution.py:331
  1151.3 36.3 %all-to-all-start.6 = ((bf16[4,160,2048]{2,1,0:T(8,128)(2,1)}), bf16[4,160,2048]{2,1,0:T(8,128)(2,1)}, u32[]{:S(2)}, u32[]{:S(2)}) async-start(bf16[4,160,2048]{2,1,0:T(8,128)(2,1)} %bitcast.416), calls=%async_computation.6 | async-start | bytes 5242880 | tf_op jit(solution)/shard_map/all_to_all | solution.py:365
  1236.7 351.4 %copy-start.3 = (f32[256,2048]{1,0:T(8,128)}, f32[256,2048]{1,0:T(8,128)S(1)}, u32[]{:S(2)}) copy-start(f32[256,2048]{1,0:T(8,128)S(1)} %get-tuple-element.342) | copy-start | bytes 6291460
  1245.8 34.9 %all-to-all-start.7 = ((bf16[4,160,2048]{2,1,0:T(8,128)(2,1)}), bf16[4,160,2048]{2,1,0:T(8,128)(2,1)}, u32[]{:S(2)}, u32[]{:S(2)}) async-start(bf16[4,160,2048]{2,1,0:T(8,128)(2,1)} %select_convert_fusion), calls=%async_computation.7 | async-start | bytes 5242880 | tf_op jit(solution)/shard_map/all_to_all | solution.py:383
  1250.4 477.6 %reduce-scatter.16.cloned.1.call-start = ((), (), s32[]{:S(2)}) async-start(), calls=%async_computation.28 | async-start | bytes 5242880 | tf_op jit(solution)/shard_map/reduce_scatter | solution.py:412
  1587.0 152.6 %reduce-scatter.18.cloned.1.call-start = ((), (), s32[]{:S(2)}) async-start(), calls=%async_computation.29 | async-start | bytes 5242880 | tf_op jit(solution)/shard_map/reduce_scatter | solution.py:415
  1587.8 244.8 %reduce-scatter.36.cloned.1.call-start = ((), (), s32[]{:S(2)}) async-start(), calls=%async_computation.39 | async-start | bytes 1081344
  1595.3 373.4 %reduce-scatter.34.cloned.1.call-start = ((), (), s32[]{:S(2)}) async-start(), calls=%async_computation.38 | async-start | bytes 1081344
  1622.0 435.7 %reduce-scatter.26.cloned.1.call-start = ((), (), s32[]{:S(2)}) async-start(), calls=%async_computation.33 | async-start | bytes 9437184 | tf_op jit(solution)/shard_map/reduce_scatter | solution.py:444
  1633.4 514.4 %reduce-scatter.24.cloned.1.call-start = ((), (), s32[]{:S(2)}) async-start(), calls=%async_computation.32 | async-start | bytes 9437184 | tf_op jit(solution)/shard_map/reduce_scatter | solution.py:441
  1650.3 725.6 %reduce-scatter.28.cloned.1.call-start = ((), (), s32[]{:S(2)}) async-start(), calls=%async_computation.34 | async-start | bytes 25952256 | tf_op jit(solution)/shard_map/reduce_scatter | solution.py:447
  1676.9 927.1 %reduce-scatter.30.cloned.1.call-start = ((), (), s32[]{:S(2)}) async-start(), calls=%async_computation.35 | async-start | bytes 25952256 | tf_op jit(solution)/shard_map/reduce_scatter | solution.py:450
  1702.0 1130.1 %reduce-scatter.32.cloned.1.call-start = ((), (), s32[]{:S(2)}) async-start(), calls=%async_computation.36 | async-start | bytes 25952256 | tf_op jit(solution)/shard_map/reduce_scatter | solution.py:453
  1727.9 1292.1 %reduce-scatter.20.cloned.1.call-start = ((), (), s32[]{:S(2)}) async-start(), calls=%async_computation.30 | async-start | bytes 17301504 | tf_op jit(solution)/shard_map/reduce_scatter | solution.py:458
  1739.2 1467.9 %reduce-scatter.22.cloned.1.call-start = ((), (), s32[]{:S(2)}) async-start(), calls=%async_computation.31 | async-start | bytes 17301504 | tf_op jit(solution)/shard_map/reduce_scatter | solution.py:459
  1760.0 210.2 %all-to-all-start.8 = ((bf16[4,160,2048]{2,1,0:T(8,128)(2,1)}), bf16[4,160,2048]{2,1,0:T(8,128)(2,1)S(1)}, u32[]{:S(2)}, u32[]{:S(2)}) async-start(bf16[4,160,2048]{2,1,0:T(8,128)(2,1)} %bitcast.417), calls=%async_computation.8 | async-start | bytes 5242880 | tf_op jit(solution)/shard_map/all_to_all | solution.py:404
  (104 other events, 1806.7 us)
Sparse Core Ops, SparseCore 0:
  11.0 80.0 all-gather.14
  94.1 75.7 all-gather.18
  171.4 80.8 all-gather.12
  254.6 50.9 all-gather.16
  307.8 52.5 all-gather.28
  361.9 82.0 all-gather.20
  445.6 201.4 all-gather.26
  648.7 200.8 all-gather.24
  851.2 200.8 all-gather.22
  1587.1 49.9 reduce-scatter.15
  1640.1 52.5 reduce-scatter.17
  1695.4 137.1 reduce-scatter.35
  1835.4 133.3 reduce-scatter.33
  1970.9 86.7 reduce-scatter.25
  2059.8 88.0 reduce-scatter.23
  2150.1 225.7 reduce-scatter.27
  2378.1 225.8 reduce-scatter.29
  2606.2 225.8 reduce-scatter.31
  2834.9 185.0 reduce-scatter.19
  3022.7 184.3 reduce-scatter.21
where the time goes:
time: 3230 us; the launch traced here: 3210 us
  waiting for transfers between devices  1910 us (59%)
  matrix products  557 us (17%)
  local copies, waits for them, and re-layouts  319 us (10%)
  blocking collectives  180 us (6%)
  other arithmetic  170 us (5%)
  starting transfers between devices  59 us (2%)
    reduce_scatter x1, waiting for transfers between devices, local(): lax.psum_scatter(ffn_sums[0][None].astype(jnp.bfloat16), 'shard', scatter...  225 us
    reduce_scatter x1, waiting for transfers between devices, local(): lax.psum_scatter(ffn_sums[2][None].astype(jnp.bfloat16), 'shard', scatter...  223 us
    reduce_scatter x1, waiting for transfers between devices, local(): lax.psum_scatter(ffn_sums[1][None].astype(jnp.bfloat16), 'shard', scatter...  223 us
    unnamed x22, waiting for transfers between devices  204 us
    dot_general x39, matrix products, contract_first(): lax.dot_general(left_side, right_side, (((0,), (0,)), ((), ())), precisio...  196 us
    reduce_scatter x1, waiting for transfers between devices, local(): lax.psum_scatter(grad_value_w, ('expert', 'shard'), scatter_dimension=0,...  187 us
    reduce_scatter x1, waiting for transfers between devices, local(): lax.psum_scatter(grad_key_w, ('expert', 'shard'), scatter_dimension=0, ti...  183 us
    all_gather x1, waiting for transfers between devices, gather_experts(): lax.all_gather(w_gate, 'shard', axis=1, tiled=True)  180 us
  transfers between devices with their start and end apart: 29, of which 18 were waited for; matrix products, arithmetic and copies ran while one was open for 19% of the time, Pallas kernels for 0%

commit v1 on v0

v1 whole, which is shorter than its diff:
```python
import functools
import math

import jax
import jax.numpy as jnp
from jax import lax
from jax.experimental import pallas as pl
from jax.experimental.pallas import tpu as pltpu
from jax.sharding import PartitionSpec as P

HD = 128
TOPK = 2
EPSILON = 1e-06
NEGATIVE = -1e30
ROPE_BASE = 10000.0
PRECISE = lax.Precision.HIGHEST
BF = jnp.bfloat16
F32 = jnp.float32
LOG2E = 1.4426950408889634


def dot(a, b):
    return jnp.dot(a, b, preferred_element_type=F32)


def dot_tn(a, b, precision=None):
    return lax.dot_general(a, b, (((0,), (0,)), ((), ())), precision=precision, preferred_element_type=F32)


def dot_nt(a, b):
    return lax.dot_general(a, b, (((1,), (1,)), ((), ())), preferred_element_type=F32)


def inverse_rms(values):
    return lax.rsqrt(jnp.mean(values * values, axis=-1, keepdims=True) + EPSILON)


def norm_back(grad, values, inv, gain):
    u = grad * gain
    centre = jnp.mean(u * values, axis=-1, keepdims=True)
    return inv * (u - values * (inv * inv) * centre), jnp.sum(grad * values * inv, axis=0)


def rope_tables(position):
    half = HD // 2
    frequency = jnp.exp(-math.log(ROPE_BASE) * jnp.arange(half, dtype=F32) / half)
    angles = position[:, None] * frequency
    cosine, sine = jnp.cos(angles), jnp.sin(angles)
    return jnp.concatenate([cosine, cosine], -1), jnp.concatenate([-sine, sine], -1)


def rotate(tensor, cosine, sine):
    heads = tensor.reshape(tensor.shape[:-1] + (-1, HD))
    swapped = jnp.concatenate([heads[..., HD // 2:], heads[..., :HD // 2]], -1)
    return (heads * cosine[:, None, :] + swapped * sine[:, None, :]).reshape(tensor.shape)


def attend_kernel(scale, q_ref, k_ref, v_ref, qb_ref, kb_ref, o_ref, l_ref):
    s = dot_nt(k_ref[...], q_ref[...])
    s = jnp.where(kb_ref[...] <= qb_ref[0], s * (scale * LOG2E), NEGATIVE)
    peak = jnp.max(s, axis=0, keepdims=True)
    p = jnp.exp2(s - peak)
    total = jnp.sum(p, axis=0, keepdims=True)
    o = dot_tn(v_ref[...], p.astype(BF))
    o_ref[...] = (o / total).T.astype(BF)
    l_ref[0] = peak + jnp.log2(total)


def attend(q, k, v, q_blocks, k_blocks):
    rows, width = q.shape
    length = k.shape[0]
    heads = width // HD
    tile = 256
    return pl.pallas_call(
        functools.partial(attend_kernel, HD ** -0.5),
        grid=(heads, rows // tile),
        in_specs=[
            pl.BlockSpec((tile, HD), lambda h, i: (i, h)),
            pl.BlockSpec((length, HD), lambda h, i: (0, h)),
            pl.BlockSpec((length, HD), lambda h, i: (0, h)),
            pl.BlockSpec((1, 1, tile), lambda h, i: (0, 0, i)),
            pl.BlockSpec((length, 1), lambda h, i: (0, 0)),
        ],
        out_specs=[
            pl.BlockSpec((tile, HD), lambda h, i: (i, h)),
            pl.BlockSpec((1, 1, tile), lambda h, i: (h, 0, i)),
        ],
        out_shape=[
            jax.ShapeDtypeStruct((rows, width), BF),
            jax.ShapeDtypeStruct((heads, 1, rows), F32),
        ],
        cost_estimate=pl.CostEstimate(
            flops=4 * rows * length * width,
            transcendentals=rows * length * heads,
            bytes_accessed=4 * rows * width + 4 * length * width,
        ),
        name="attend",
    )(q, k, v, q_blocks.reshape(1, 1, rows), k_blocks.reshape(length, 1))


def attend_back_kernel(scale, q_ref, k_ref, v_ref, d_ref, o_ref, l_ref, qb_ref, kb_ref, dq_ref, dk_ref, dv_ref):
    q, k, d = q_ref[...], k_ref[...], d_ref[...]
    s = dot_nt(k, q)
    p = jnp.exp2(s * (scale * LOG2E) - l_ref[0])
    p = jnp.where(kb_ref[...] <= qb_ref[0], p, 0.0)
    centre = jnp.sum((d.astype(F32) * o_ref[...].astype(F32)).T, axis=0, keepdims=True)
    grad_p = dot_nt(v_ref[...], d)
    grad_s = (p * (grad_p - centre)).astype(BF)
    dq_ref[...] = (dot_tn(k, grad_s) * scale).T
    new_k = dot(grad_s, q) * scale
    new_v = dot(p.astype(BF), d)

    @pl.when(pl.program_id(1) == 0)
    def _():
        dk_ref[...] = new_k
        dv_ref[...] = new_v

    @pl.when(pl.program_id(1) > 0)
    def _():
        dk_ref[...] += new_k
        dv_ref[...] += new_v


def attend_back(q, k, v, d, o, total, q_blocks, k_blocks):
    rows, width = q.shape
    length = k.shape[0]
    heads = width // HD
    tile = 256
    row_spec = pl.BlockSpec((tile, HD), lambda h, i: (i, h))
    key_spec = pl.BlockSpec((length, HD), lambda h, i: (0, h))
    return pl.pallas_call(
        functools.partial(attend_back_kernel, HD ** -0.5),
        grid=(heads, rows // tile),
        in_specs=[
            row_spec, key_spec, key_spec, row_spec, row_spec,
            pl.BlockSpec((1, 1, tile), lambda h, i: (h, 0, i)),
            pl.BlockSpec((1, 1, tile), lambda h, i: (0, 0, i)),
            pl.BlockSpec((length, 1), lambda h, i: (0, 0)),
        ],
        out_specs=[row_spec, key_spec, key_spec],
        out_shape=[
            jax.ShapeDtypeStruct((rows, width), F32),
            jax.ShapeDtypeStruct((length, width), F32),
            jax.ShapeDtypeStruct((length, width), F32),
        ],
        cost_estimate=pl.CostEstimate(
            flops=10 * rows * length * width,
            transcendentals=rows * length * heads,
            bytes_accessed=10 * rows * width + 12 * length * width,
        ),
        name="attend_back",
    )(q, k, v, d, o, total, q_blocks.reshape(1, 1, rows), k_blocks.reshape(length, 1))


def pick(table, routes, ids):
    parts = jnp.split(table, len(ids), axis=1)
    return [sum(jnp.where(routes[:, j:j + 1] == e, part, 0.0) for e, part in zip(ids, parts)) for j in range(TOPK)]


def place(pieces, routes, ids):
    return jnp.concatenate(
        [sum(jnp.where(routes[:, j:j + 1] == e, pieces[j], 0.0) for j in range(TOPK)) for e in ids], axis=1
    )


def pair_softmax(logits):
    peak = jnp.maximum(logits[0], logits[1])
    powers = [jnp.exp(v - peak) for v in logits]
    total = powers[0] + powers[1]
    return [v / total for v in powers]


def local(
    inputs, cotangent, blocks, attn_routes, ffn_routes, w_key, w_value, attn_router, ffn_router, attn_gain, ffn_gain,
    attn_bias, ffn_bias, w_query, w_out, w_gate, w_up, w_down,
):
    n_e, n_s = lax.axis_size("expert"), lax.axis_size("shard")
    me = lax.axis_index("expert")
    tokens, width = inputs.shape[1:]
    ids = list(range(n_e))
    capacity = 5 * tokens * TOPK // (4 * n_e)
    group = w_key.shape[1] // n_e
    length = n_e * tokens
    small_rows = w_key.shape[0]

    def swap(value, k):
        return lax.ppermute(value, "expert", [(i, i ^ k) for i in range(n_e)])

    def spread(value):
        return jnp.concatenate([value] + [swap(value, k) for k in range(1, n_e)], axis=0)

    def collect(value):
        parts = jnp.split(value, n_e, axis=0)
        return sum([parts[0].astype(F32)] + [swap(parts[k], k).astype(F32) for k in range(1, n_e)])

    def shuffle(value, axis):
        return lax.all_to_all(value, axis, split_axis=0, concat_axis=0, tiled=True)

    def gather_shard(value):
        return lax.all_gather(value, "shard", axis=0, tiled=True)

    def scatter_shard(value):
        return lax.psum_scatter(value, "shard", scatter_dimension=0, tiled=True)

    small = jnp.concatenate(
        [attn_router, ffn_router, attn_gain[:, None], ffn_gain[:, None], attn_bias[:, None], ffn_bias[:, None]], axis=1
    )
    small_width = small.shape[1]
    small = jnp.pad(small, ((0, 0), (0, 128 - small_width)))
    packed = jnp.concatenate(
        [
            w_key.reshape(small_rows, n_e, group).transpose(1, 0, 2),
            w_value.reshape(small_rows, n_e, group).transpose(1, 0, 2),
            jnp.broadcast_to(small[None], (n_e,) + small.shape),
        ],
        axis=2,
    )
    packed = gather_shard(shuffle(packed, "expert")[None])
    packed = packed.transpose(1, 0, 2, 3).reshape(width, -1)
    key_value_w = packed[:, :2 * group]
    small = packed[:, 2 * group:2 * group + small_width].astype(F32)
    router_a, router_f = small[:, :n_e], small[:, n_e:2 * n_e]
    gain_a, gain_f, bias_a, bias_f = (small[:, 2 * n_e + i] for i in range(4))

    def to_heads(value):
        rows = value.shape[0]
        value = shuffle(value.reshape(rows, n_e, group).transpose(1, 0, 2), "expert")
        return gather_shard(value.transpose(1, 0, 2).reshape(rows, n_e * group))

    def from_heads(value):
        value = scatter_shard(value)
        rows = value.shape[0]
        value = shuffle(value.reshape(rows, n_e, group).transpose(1, 0, 2), "expert")
        return value.transpose(1, 0, 2).reshape(rows, n_e * group)

    query_w = to_heads(w_query[0])
    out_rows = w_out.shape[1]
    turned = shuffle(w_out[0].T, "shard").reshape(n_s, width // n_s, out_rows).transpose(1, 0, 2)
    out_wt = to_heads(turned.reshape(width // n_s, n_s * out_rows))

    def to_columns(value):
        rows = value.shape[0]
        return shuffle(value.reshape(rows, n_s, -1).transpose(1, 0, 2), "shard").reshape(rows * n_s, -1)

    def from_columns(value):
        rows = value.shape[0] // n_s
        value = shuffle(value, "shard").reshape(n_s, rows, -1)
        return value.transpose(1, 0, 2).reshape(rows, -1)

    gate_own, up_own, down_own = to_columns(w_gate[0]), to_columns(w_up[0]), w_down[0]
    gate_w = [gate_own] + [swap(gate_own, k) for k in range(1, n_e)]
    up_w = [up_own] + [swap(up_own, k) for k in range(1, n_e)]
    down_w = [down_own] + [swap(down_own, k) for k in range(1, n_e)]

    own = inputs[0].astype(F32)
    cot = cotangent[0]
    seq_in = spread(inputs[0]).astype(F32)
    meta = spread(jnp.concatenate([blocks, attn_routes[0].T], axis=0)[None])
    seq_blocks = meta[:, 0].reshape(-1)
    routes_a = meta[:, 1:].transpose(0, 2, 1).reshape(-1, TOPK)
    position = jnp.concatenate([(me ^ k) * tokens + jnp.arange(tokens, dtype=jnp.int32) for k in range(n_e)]).astype(F32)
    cosine, sine = rope_tables(position)
    h_attn = (seq_in * inverse_rms(seq_in) * gain_a).astype(BF)
    logits_a = dot(h_attn, router_a.astype(BF))
    gates_a = pair_softmax(pick(logits_a, routes_a, ids))
    key_value = dot(h_attn, key_value_w)
    keys = rotate(key_value[:, :group], cosine, sine).astype(BF)
    values = key_value[:, group:].astype(BF)
    queries = pick(dot(h_attn, query_w), routes_a, ids)
    queries = jnp.concatenate([rotate(v, cosine, sine).astype(BF) for v in queries], axis=0)
    row_blocks = jnp.concatenate([seq_blocks, seq_blocks])
    mixed_rows, log_total = attend(queries, keys, values, row_blocks, seq_blocks)
    mixed = [v.astype(F32) for v in jnp.split(mixed_rows, TOPK, axis=0)]
    mixed_all = place([gates_a[j] * mixed[j] for j in range(TOPK)], routes_a, ids).astype(BF)
    middle = own + collect(dot_nt(mixed_all, out_wt).astype(BF)) + bias_a

    inv_f = inverse_rms(middle)
    h_ffn = (middle * inv_f * gain_f).astype(BF)
    h_all = gather_shard(h_ffn)
    cot_all = gather_shard(cot)
    routes_f = gather_shard(ffn_routes[0].T[None])
    logits_f = dot(h_all, router_f.astype(BF))
    flat_routes = routes_f.transpose(0, 2, 1).reshape(-1, TOPK)
    gates_f = pair_softmax(pick(logits_f, flat_routes, ids))
    h_blocks = h_all.reshape(n_s, tokens, width)
    cot_blocks = cot_all.reshape(n_s, tokens, width)
    triangle = (jnp.arange(tokens)[:, None] <= jnp.arange(tokens)[None, :]).astype(BF)

    def rows_of(select, source):
        return lax.dot_general(
            select, source, (((2,), (1,)), ((0,), (0,))), preferred_element_type=F32
        ).astype(BF).reshape(n_s * capacity, width)

    selects, out_rows_f, back_rows_f = [], [], []
    grad_gate_f = [0.0] * TOPK
    weight_grads = []
    for k in range(n_e):
        expert = me ^ k
        named = [routes_f[:, j] == expert for j in range(TOPK)]
        any_named = named[0] | named[1]
        rank = dot(any_named.astype(BF), triangle).astype(jnp.int32) - 1
        hit = (rank[:, None, :] == jnp.arange(capacity, dtype=jnp.int32)[None, :, None]) & any_named[:, None, :]
        select = hit.astype(BF)
        gate_token = sum(jnp.where(named[j], gates_f[j].reshape(n_s, tokens), 0.0) for j in range(TOPK))
        gate_slot = jnp.sum(jnp.where(hit, gate_token[:, None, :], 0.0), axis=2).reshape(-1, 1)
        rows, cot_rows = rows_of(select, h_blocks), rows_of(select, cot_blocks)
        gate_pre, up_pre = dot(rows, gate_w[k]), dot(rows, up_w[k])
        grad_hidden = dot_nt(cot_rows, down_w[k])
        sigma = 1.0 / (1.0 + jnp.exp(-gate_pre))
        silu = gate_pre * sigma
        hidden = silu * up_pre
        grad_slot = jnp.sum(grad_hidden * hidden, axis=1).reshape(n_s, capacity)
        grad_hidden = grad_hidden * gate_slot
        hidden = (hidden * gate_slot).astype(BF)
        grad_gate = (grad_hidden * up_pre * sigma * (1.0 + gate_pre * (1.0 - sigma))).astype(BF)
        grad_up = (grad_hidden * silu).astype(BF)
        back = (dot_nt(grad_gate, gate_w[k]) + dot_nt(grad_up, up_w[k])).astype(BF)
        selects.append(select)
        back_rows_f.append(back.reshape(n_s, capacity, width))
        out_rows_f.append(dot(hidden, down_w[k]).astype(BF).reshape(n_s, capacity, width))
        grad_token = jnp.sum(jnp.where(hit, grad_slot[:, :, None], 0.0), axis=1)
        grad_gate_f = [grad_gate_f[j] + jnp.where(named[j], grad_token, 0.0) for j in range(TOPK)]
        weight_grads.append(
            (dot_tn(rows, grad_gate).astype(BF), dot_tn(rows, grad_up).astype(BF), dot_tn(hidden, cot_rows).astype(BF))
        )
    select = jnp.concatenate(selects, axis=1)

    def tokens_of(row_list):
        return lax.dot_general(
            select, jnp.concatenate(row_list, axis=1), (((1,), (1,)), ((0,), (0,))), preferred_element_type=F32
        ).astype(BF).reshape(n_s * tokens, width)

    back_f = scatter_shard(tokens_of(back_rows_f)).astype(F32)
    ffn_out = scatter_shard(tokens_of(out_rows_f)).astype(F32)
    outputs = (middle + ffn_out + bias_f).astype(BF)[None]
    grad_gates_f = jnp.sum(
        shuffle(jnp.stack(grad_gate_f, axis=1).reshape(n_s, TOPK * tokens), "shard"), axis=0
    ).reshape(TOPK, tokens, 1)

    def expert_sum(which):
        return weight_grads[0][which].astype(F32) + sum(
            swap(weight_grads[k][which], k).astype(F32) for k in range(1, n_e)
        )

    grad_gate_w = from_columns(expert_sum(0).astype(BF)).astype(F32)[None]
    grad_up_w = from_columns(expert_sum(1).astype(BF)).astype(F32)[None]
    grad_down_w = expert_sum(2)[None]

    grad_out = cot.astype(F32)
    own_routes_f = ffn_routes[0]
    own_gates_f = pair_softmax(pick(dot(h_ffn, router_f.astype(BF)), own_routes_f, ids))

    def logit_grads(gates, grads, routes):
        centre = sum(gates[j] * grads[j] for j in range(TOPK))
        return place([gates[j] * (grads[j] - centre) for j in range(TOPK)], routes, ids)

    grad_logits_f = logit_grads(own_gates_f, grad_gates_f, own_routes_f)
    grad_router_f = dot_tn(h_ffn.astype(F32), grad_logits_f, PRECISE)
    grad_h_ffn = back_f + jnp.dot(grad_logits_f, router_f.T, precision=PRECISE)
    grad_norm, grad_gain_f = norm_back(grad_h_ffn, middle, inv_f, gain_f)
    grad_middle = grad_out + grad_norm
    grad_bias_f = jnp.sum(grad_out, axis=0)
    grad_bias_a = jnp.sum(grad_middle, axis=0)

    seq_grad = spread(grad_middle.astype(BF))
    grad_mixed = pick(dot(seq_grad, out_wt), routes_a, ids)
    grad_gates_a = [collect(jnp.sum(grad_mixed[j] * mixed[j], axis=1, keepdims=True)) for j in range(TOPK)]
    grad_mixed = jnp.concatenate([(gates_a[j] * grad_mixed[j]).astype(BF) for j in range(TOPK)], axis=0)
    grad_out_wt = dot_tn(seq_grad, mixed_all).astype(BF)
    grad_q, grad_k, grad_v = attend_back(queries, keys, values, grad_mixed, mixed_rows, log_total, row_blocks, seq_blocks)
    grad_q = [rotate(v, cosine, -sine) for v in jnp.split(grad_q, TOPK, axis=0)]
    grad_query_all = place(grad_q, routes_a, ids).astype(BF)
    grad_key_value = jnp.concatenate([rotate(grad_k, cosine, -sine), grad_v], axis=1).astype(BF)
    back_a = collect((dot_nt(grad_query_all, query_w) + dot_nt(grad_key_value, key_value_w)).astype(BF))
    grad_query_w = from_heads(dot_tn(h_attn, grad_query_all).astype(BF)).astype(F32)[None]
    value = from_heads(grad_out_wt)
    value = value.reshape(width // n_s, n_s, out_rows).transpose(1, 0, 2)
    grad_out_w = shuffle(value, "shard").reshape(width, out_rows).T.astype(F32)[None]
    value = dot_tn(h_attn, grad_key_value).astype(BF).reshape(n_e, n_s, small_rows, 2 * group).transpose(1, 0, 2, 3)
    value = shuffle(scatter_shard(value)[0], "expert")
    grad_key_w = value[:, :, :group].transpose(1, 0, 2).reshape(small_rows, -1).astype(F32)
    grad_value_w = value[:, :, group:].transpose(1, 0, 2).reshape(small_rows, -1).astype(F32)

    h_own = h_attn[:tokens]
    own_routes_a = attn_routes[0]
    own_gates_a = [v[:tokens] for v in gates_a]
    grad_logits_a = logit_grads(own_gates_a, grad_gates_a, own_routes_a)
    grad_router_a = dot_tn(h_own.astype(F32), grad_logits_a, PRECISE)
    grad_h_attn = back_a + jnp.dot(grad_logits_a, router_a.T, precision=PRECISE)
    grad_norm, grad_gain_a = norm_back(grad_h_attn, own, inverse_rms(own), gain_a)
    input_grad = (grad_middle + grad_norm).astype(BF)[None]

    shared = jnp.concatenate(
        [grad_router_a, grad_router_f]
        + [v[:, None] for v in (grad_gain_a, grad_gain_f, grad_bias_a, grad_bias_f)],
        axis=1,
    )
    shared = shuffle(shared.reshape(n_e * n_s, -1), ("expert", "shard"))
    shared = jnp.sum(shared, axis=0).reshape(small_rows, small_width)
    return (
        outputs,
        input_grad,
        grad_key_w,
        grad_value_w,
        shared[:, :n_e],
        shared[:, n_e:2 * n_e],
        shared[:, 2 * n_e],
        shared[:, 2 * n_e + 1],
        shared[:, 2 * n_e + 2],
        shared[:, 2 * n_e + 3],
        grad_query_w,
        grad_out_w,
        grad_gate_w,
        grad_up_w,
        grad_down_w,
    )


def solution(mesh):
    rows = P("shard", "expert", None)
    shared, vector = P(("expert", "shard"), None), P(("expert", "shard"))
    weight = P("expert", "shard", None)
    in_specs = (rows, rows, P("shard", "expert"), rows, rows) + (shared,) * 4 + (vector,) * 4 + (weight,) * 5
    out_specs = (rows, rows) + (shared,) * 4 + (vector,) * 4 + (weight,) * 5
    return jax.shard_map(local, mesh=mesh, in_specs=in_specs, out_specs=out_specs, check_vma=False)
```

time: 3230 us -> 2080 us (0.64)
  waiting for transfers between devices: 1910 us -> 969 us
  local copies, waits for them, and re-layouts: 319 us -> 127 us
  matrix products: 557 us -> 470 us
  Pallas kernels: 0 us -> 69 us
  other arithmetic: 170 us -> 101 us
  blocking collectives: 180 us -> 234 us
    reduce_scatter x9 -> x4, waiting for transfers between devices: 1140 us -> 115 us  [scatter_shard(): return lax.psum_scatter(value, 'shard', scatter_dimension=0, tiled=True)]
    ppermute x0 -> x39, waiting for transfers between devices: none -> 586 us  [swap(): return lax.ppermute(value, 'expert', [(i, i ^ k) for i in range(n_e)])]
    all_gather x9 -> x5, waiting for transfers between devices: 509 us -> 0.06 us  [gather_shard(): return lax.all_gather(value, 'shard', axis=0, tiled=True)]
    all_to_all x9 -> x10, waiting for transfers between devices: 60 us -> 267 us  [shuffle(): return lax.all_to_all(value, axis, split_axis=0, concat_axis=0, tiled=True)]
    unnamed x22 -> x11, waiting for transfers between devices: 204 us -> 0.68 us
    dynamic_update_slice x112 -> x0, local copies, waits for them, and re-layouts: 121 us -> none  [the longest x64 86.2 us: attend_backward(): lax.map(one_head, (split_heads(queries, head_count), key_heads, value_hea...]
    all_to_all x0 -> x4, blocking collectives: none -> 101 us  [shuffle(): return lax.all_to_all(value, axis, split_axis=0, concat_axis=0, tiled=True)]
    dot_general x137 -> x66, matrix products: 553 us -> 470 us  [the longest x15 148 us: dot_nt(): lax.dot_general(a, b, (((1,), (1,)), ((), ())), preferred_element_type=F32)]
  transfers between devices with their start and end apart: 29 -> 59, of which waited for: 18 -> 23; matrix products, arithmetic and copies ran while one was open for 19% -> 22% of each run, Pallas kernels for 0% -> 1%
where the time goes in v1:
time: 2080 us; the launch traced here: 2070 us
  waiting for transfers between devices  969 us (47%)
  matrix products  470 us (23%)
  blocking collectives  234 us (11%)
  local copies, waits for them, and re-layouts  127 us (6%)
  other arithmetic  101 us (5%)
  starting transfers between devices  87.9 us (4%)
  Pallas kernels  69 us (3%)
    ppermute x39, waiting for transfers between devices, swap(): return lax.ppermute(value, 'expert', [(i, i ^ k) for i in range(n_e)])  586 us
    all_to_all x10, waiting for transfers between devices, shuffle(): return lax.all_to_all(value, axis, split_axis=0, concat_axis=0, tiled=True)  267 us
    dot_general x15, matrix products, dot_nt(): lax.dot_general(a, b, (((1,), (1,)), ((), ())), preferred_element_type=F32)  148 us
    all_gather x1, blocking collectives, gather_shard(): return lax.all_gather(value, 'shard', axis=0, tiled=True)  133 us
    dot_general x22, matrix products, dot(): return jnp.dot(a, b, preferred_element_type=F32)  123 us
    dot_general x17, matrix products, dot_tn(): lax.dot_general(a, b, (((0,), (0,)), ((), ())), precision=precision, pref...  122 us
    reduce_scatter x4, waiting for transfers between devices, scatter_shard(): return lax.psum_scatter(value, 'shard', scatter_dimension=0, tiled=True)  115 us
    all_to_all x4, blocking collectives, shuffle(): return lax.all_to_all(value, axis, split_axis=0, concat_axis=0, tiled=True)  101 us
  transfers between devices with their start and end apart: 59, of which 23 were waited for; matrix products, arithmetic and copies ran while one was open for 22% of the time, Pallas kernels for 1%

profile of v1, /device:TPU:0, one launch (start us, length us, event | category | flops | bytes accessed | tf_op | source)
XLA Modules:
  0.0 2073.9 jit_solution(3944246325844918090)
XLA Ops:
  11.5 14.5 all_to_all.91
  27.2 15.7 all_to_all.92
  44.8 53.1 %all_to_all.93 = bf16[8,256,256]{2,1,0:T(8,128)(2,1)S(1)} all-to-all(bf16[8,256,256]{2,1,0:T(8,128)(2,1)S(1)} %bitcast.475), channel_id=1, replica_groups=mesh['expert'=4,'shard'=8] {'shard'}, dimensions={0} | all-to-all | bytes 2097152 | tf_op jit(solution)/shard_map/all_to_all | solution.py:197
  98.4 17.8 all_to_all.94
  124.5 38.3 %collective-permute-done = s32[1,3,256]{2,1,0:T(4,128)S(1)} collective-permute-done((s32[1,3,256]{2,1,0:T(4,128)S(1)}, s32[1,3,256]{2,1,0:T(4,128)S(1)}, u32[]{:S(2)}, u32[]{:S(2)}) %collective-permute-start) | collective-permute-done | bytes 3104 | tf_op jit(solution)/shard_map/ppermute | solution.py:187
  196.2 12.8 fusion.180
  240.4 29.7 %attend.1 = (bf16[2048,512]{1,0:T(8,128)(2,1)}, f32[4,1,2048]{2,1,0:T(1,128)}) custom-call(bf16[2048,512]{1,0:T(8,128)(2,1)} %pad_maximum_fusion.4.q_ref, bf16[1024,512]{1,0:T(8,128)(2,1)} %get-tuple-element.204.k_ref, bf16[1024,512]{1,0:T(8,128)(2,1)} %slice.394.v_ref, s32[1,1,2048]{2,1,0:T(1,128)} %bitcast.510, s32[1024,1]{1,0:T(8,128)} %copy.178.kb_ref), custom_call_target="tpu_custom_call" | custom-call | flops 4294967296 | bytes 6291456 | tf_op jit(solution)/shard_map/attend/pallas_call | solution.py:74
  276.9 12.6 convolution_convert_fusion.14
  293.3 22.5 %collective-permute-done.6 = bf16[256,2048]{1,0:T(8,128)(2,1)S(1)} collective-permute-done((bf16[256,2048]{1,0:T(8,128)(2,1)S(1)}, bf16[256,2048]{1,0:T(8,128)(2,1)S(1)}, u32[]{:S(2)}, u32[]{:S(2)}) %collective-permute-start.6) | collective-permute-done | bytes 1048608 | tf_op jit(solution)/shard_map/ppermute | solution.py:187
  315.8 20.4 collective-permute-done.7
  352.1 125.4 %all-to-all-done.4 = bf16[8,256,704]{1,2,0:T(8,128)(2,1)S(1)} async-done(((bf16[8,256,704]{1,2,0:T(8,128)(2,1)}), bf16[8,256,704]{1,2,0:T(8,128)(2,1)S(1)}, u32[]{:S(2)}, u32[]{:S(2)}) %all-to-all-start.4) | async-done | bytes 2883616 | tf_op jit(solution)/shard_map/all_to_all | solution.py:197
  485.7 132.9 %all-gather.3 = s32[8,2,256]{2,1,0:T(2,128)S(1)} all-gather(s32[1,2,256]{2,1,0:T(2,128)S(1)} %bitcast.502), channel_id=3, replica_groups=mesh['expert'=4,'shard'=8] {'shard'}, dimensions={0}, use_global_device_ids=true | all-gather | bytes 18432 | tf_op jit(solution)/shard_map/all_gather | solution.py:200
  653.7 32.5 %collective-permute-done.9 = bf16[2048,704]{0,1:T(8,128)(2,1)} collective-permute-done((bf16[2048,704]{0,1:T(8,128)(2,1)}, bf16[2048,704]{0,1:T(8,128)(2,1)}, u32[]{:S(2)}, u32[]{:S(2)}) %collective-permute-start.9) | collective-permute-done | bytes 2883616 | tf_op jit(solution)/shard_map/ppermute | solution.py:187
  692.6 54.8 %collective-permute-done.10 = bf16[2048,704]{0,1:T(8,128)(2,1)} collective-permute-done((bf16[2048,704]{0,1:T(8,128)(2,1)S(1)}, bf16[2048,704]{0,1:T(8,128)(2,1)}, u32[]{:S(2)}, u32[]{:S(2)}) %collective-permute-start.10) | collective-permute-done | bytes 2883616 | tf_op jit(solution)/shard_map/ppermute | solution.py:187
  793.4 141.8 %collective-permute-done.13 = bf16[2048,704]{0,1:T(8,128)(2,1)} collective-permute-done((bf16[2048,704]{0,1:T(8,128)(2,1)S(1)}, bf16[2048,704]{0,1:T(8,128)(2,1)}, u32[]{:S(2)}, u32[]{:S(2)}) %collective-permute-start.13) | collective-permute-done | bytes 2883616 | tf_op jit(solution)/shard_map/ppermute | solution.py:187
  1110.0 12.6 fusion.19
  1154.7 12.7 fusion.22
  1180.5 29.8 %reduce-scatter.10.cloned.1.call-done = bf16[256,2048]{1,0:T(8,128)(2,1)} async-done(((bf16[2048,2048]{1,0:T(8,128)(2,1)}), bf16[256,2048]{1,0:T(8,128)(2,1)}) %reduce-scatter.10.cloned.1.call-update) | async-done | bytes 1048592 | tf_op jit(solution)/shard_map/reduce_scatter | solution.py:203
  1215.4 85.1 %reduce-scatter.8.cloned.1.call-done = bf16[256,2048]{1,0:T(8,128)(2,1)} async-done(((bf16[2048,2048]{1,0:T(8,128)(2,1)}), bf16[256,2048]{1,0:T(8,128)(2,1)}) %reduce-scatter.8.cloned.1.call-update) | async-done | bytes 1048592 | tf_op jit(solution)/shard_map/reduce_scatter | solution.py:203
  1310.0 22.5 %collective-permute-done.18 = bf16[256,2048]{1,0:T(8,128)(2,1)S(1)} collective-permute-done((bf16[256,2048]{1,0:T(8,128)(2,1)S(1)}, bf16[256,2048]{1,0:T(8,128)(2,1)S(1)}, u32[]{:S(2)}, u32[]{:S(2)}) %collective-permute-start.18) | collective-permute-done | bytes 1048608 | tf_op jit(solution)/shard_map/ppermute | solution.py:187
  1332.5 20.7 collective-permute-done.19
  1355.2 11.8 fusion.78
  1373.2 39.3 %attend_back.1 = (f32[2048,512]{1,0:T(8,128)}, f32[1024,512]{1,0:T(8,128)}, f32[1024,512]{1,0:T(8,128)}) custom-call(bf16[2048,512]{1,0:T(8,128)(2,1)} %pad_maximum_fusion.4.q_ref, bf16[1024,512]{1,0:T(8,128)(2,1)} %get-tuple-element.204.k_ref, bf16[1024,512]{1,0:T(8,128)(2,1)} %slice.394.v_ref, bf16[2048,512]{1,0:T(8,128)(2,1)} %pad_maximum_fusion.5.d_ref, ...), custom_call_target="tpu_custom_call" | custom-call | flops 10737418240 | bytes 16777216 | tf_op jit(solution)/shard_map/attend_back/pallas_call | solution.py:131
  1447.4 13.8 convolution_convert_fusion
  1516.6 19.2 collective-permute-done.33
  1535.8 66.0 %collective-permute-done.34 = bf16[2048,704]{0,1:T(8,128)(2,1)} collective-permute-done((bf16[2048,704]{0,1:T(8,128)(2,1)}, bf16[2048,704]{0,1:T(8,128)(2,1)}, u32[]{:S(2)}, u32[]{:S(2)}) %collective-permute-start.34) | collective-permute-done | bytes 2883616 | tf_op jit(solution)/shard_map/ppermute | solution.py:187
  1641.6 48.4 %collective-permute-done.30 = bf16[2048,704]{0,1:T(8,128)(2,1)S(1)} collective-permute-done((bf16[2048,704]{0,1:T(8,128)(2,1)S(1)}, bf16[2048,704]{0,1:T(8,128)(2,1)S(1)}, u32[]{:S(2)}, u32[]{:S(2)}) %collective-permute-start.30) | collective-permute-done | bytes 2883616 | tf_op jit(solution)/shard_map/ppermute | solution.py:187
  1690.0 62.3 %collective-permute-done.31 = bf16[2048,704]{0,1:T(8,128)(2,1)S(1)} collective-permute-done((bf16[2048,704]{0,1:T(8,128)(2,1)S(1)}, bf16[2048,704]{0,1:T(8,128)(2,1)S(1)}, u32[]{:S(2)}, u32[]{:S(2)}) %collective-permute-start.31) | collective-permute-done | bytes 2883616 | tf_op jit(solution)/shard_map/ppermute | solution.py:187
  1771.5 15.2 fusion.77
  1808.3 34.2 %collective-permute-done.28 = f32[256,1]{0,1:T(1,128)S(1)} collective-permute-done((f32[256,1]{0,1:T(1,128)S(1)}, f32[256,1]{0,1:T(1,128)S(1)}, u32[]{:S(2)}, u32[]{:S(2)}) %collective-permute-start.28) | collective-permute-done | bytes 1056 | tf_op jit(solution)/shard_map/ppermute | solution.py:187
  1863.1 106.5 %all-to-all-done.8 = f32[32,1,768]{2,1,0:T(1,128)S(1)} async-done(((f32[32,1,768]{2,1,0:T(1,128)}), f32[32,1,768]{2,1,0:T(1,128)S(1)}, u32[]{:S(2)}, u32[]{:S(2)}) %all-to-all-start.8) | async-done | bytes 98336 | tf_op jit(solution)/shard_map/all_to_all | solution.py:197
  2019.7 12.2 add_bitcast_fusion
  (721 shorter events, 719.7 us)
Async XLA Ops:
  7.2 164.2 %all-gather.16.cloned.1.call-start = ((), (), s32[]{:S(2)}) async-start(), calls=%async_computation.25 | async-start | bytes 5308416 | tf_op jit(solution)/shard_map/all_gather | solution.py:200
  26.1 170.1 %all-gather.10.cloned.1.call-start = ((), (), s32[]{:S(2)}) async-start(), calls=%async_computation.18 | async-start | bytes 9437184 | tf_op jit(solution)/shard_map/all_gather | solution.py:200
  44.2 232.7 %all-gather.12.cloned.1.call-start = ((), (), s32[]{:S(2)}) async-start(), calls=%async_computation.19 | async-start | bytes 9437184 | tf_op jit(solution)/shard_map/all_gather | solution.py:200
  116.2 508.7 %all-gather.14.cloned.1.call-start = ((), (), s32[]{:S(2)}) async-start(), calls=%async_computation.20 | async-start | bytes 9437184 | tf_op jit(solution)/shard_map/all_gather | solution.py:200
  340.5 291.2 %all-gather.18.cloned.1.call-start = ((), (), s32[]{:S(2)}) async-start(), calls=%async_computation.26 | async-start | bytes 9437184 | tf_op jit(solution)/shard_map/all_gather | solution.py:200
  343.8 133.7 %all-to-all-start.4 = ((bf16[8,256,704]{1,2,0:T(8,128)(2,1)}), bf16[8,256,704]{1,2,0:T(8,128)(2,1)S(1)}, u32[]{:S(2)}, u32[]{:S(2)}) async-start(bf16[8,256,704]{1,2,0:T(8,128)(2,1)} %bitcast.405), calls=%async_computation.4 | async-start | bytes 5767168 | tf_op jit(solution)/shard_map/all_to_all | solution.py:197
  477.5 143.5 %all-to-all-start.5 = ((bf16[8,256,704]{1,2,0:T(8,128)(2,1)}), bf16[8,256,704]{1,2,0:T(8,128)(2,1)}, u32[]{:S(2)}, u32[]{:S(2)}) async-start(bf16[8,256,704]{1,2,0:T(8,128)(2,1)} %bitcast.404), calls=%async_computation.5 | async-start | bytes 5767168 | tf_op jit(solution)/shard_map/all_to_all | solution.py:197
  482.1 728.1 %reduce-scatter.10.cloned.1.call-start = ((), (), s32[]{:S(2)}) async-start(), calls=%async_computation.22 | async-start | bytes 9437184 | tf_op jit(solution)/shard_map/reduce_scatter | solution.py:203
  482.1 271.8 %collective-permute-start.11 = (bf16[704,2048]{1,0:T(8,128)(2,1)}, bf16[704,2048]{1,0:T(8,128)(2,1)}, u32[]{:S(2)}, u32[]{:S(2)}) collective-permute-start(bf16[704,2048]{1,0:T(8,128)(2,1)} %bitcast.526), channel_id=1, source_target_pairs={{0,8},{8,0},{16,24},{24,16},{1,9},{9,1},{17,25},{25,17},{2,10},{10... | collective-permute-start | bytes 8650760 | tf_op jit(solution)/shard_map/ppermute | solution.py:187
  482.9 458.2 %collective-permute-start.14 = (bf16[704,2048]{1,0:T(8,128)(2,1)}, bf16[704,2048]{1,0:T(8,128)(2,1)}, u32[]{:S(2)}, u32[]{:S(2)}) collective-permute-start(bf16[704,2048]{1,0:T(8,128)(2,1)} %bitcast.527), channel_id=1, source_target_pairs={{0,16},{8,24},{16,0},{24,8},{1,17},{9,25},{17,1},{25,9},{2,18},{10... | collective-permute-start | bytes 8650760 | tf_op jit(solution)/shard_map/ppermute | solution.py:187
  484.7 504.5 %collective-permute-start.17 = (bf16[704,2048]{1,0:T(8,128)(2,1)}, bf16[704,2048]{1,0:T(8,128)(2,1)}, u32[]{:S(2)}, u32[]{:S(2)}) collective-permute-start(bf16[704,2048]{1,0:T(8,128)(2,1)} %bitcast.528), channel_id=1, source_target_pairs={{0,24},{8,16},{16,8},{24,0},{1,25},{9,17},{17,9},{25,1},{2,26},{10... | collective-permute-start | bytes 8650760 | tf_op jit(solution)/shard_map/ppermute | solution.py:187
  620.6 65.7 %collective-permute-start.9 = (bf16[2048,704]{0,1:T(8,128)(2,1)}, bf16[2048,704]{0,1:T(8,128)(2,1)}, u32[]{:S(2)}, u32[]{:S(2)}) collective-permute-start(bf16[2048,704]{0,1:T(8,128)(2,1)} %bitcast.150), channel_id=1, source_target_pairs={{0,8},{8,0},{16,24},{24,16},{1,9},{9,1},{17,25},{25,17},{2,10},{10... | collective-permute-start | bytes 8650760 | tf_op jit(solution)/shard_map/ppermute | solution.py:187
  623.3 124.2 %collective-permute-start.10 = (bf16[2048,704]{0,1:T(8,128)(2,1)S(1)}, bf16[2048,704]{0,1:T(8,128)(2,1)}, u32[]{:S(2)}, u32[]{:S(2)}) collective-permute-start(bf16[2048,704]{0,1:T(8,128)(2,1)S(1)} %bitcast.476), channel_id=1, source_target_pairs={{0,8},{8,0},{16,24},{24,16},{1,9},{9,1},{17,25},{25,17},{2,10},{10... | collective-permute-start | bytes 8650760 | tf_op jit(solution)/shard_map/ppermute | solution.py:187
  686.3 99.4 %collective-permute-start.12 = (bf16[2048,704]{0,1:T(8,128)(2,1)}, bf16[2048,704]{0,1:T(8,128)(2,1)}, u32[]{:S(2)}, u32[]{:S(2)}) collective-permute-start(bf16[2048,704]{0,1:T(8,128)(2,1)} %bitcast.150), channel_id=1, source_target_pairs={{0,16},{8,24},{16,0},{24,8},{1,17},{9,25},{17,1},{25,9},{2,18},{10... | collective-permute-start | bytes 8650760 | tf_op jit(solution)/shard_map/ppermute | solution.py:187
  747.4 187.8 %collective-permute-start.13 = (bf16[2048,704]{0,1:T(8,128)(2,1)S(1)}, bf16[2048,704]{0,1:T(8,128)(2,1)}, u32[]{:S(2)}, u32[]{:S(2)}) collective-permute-start(bf16[2048,704]{0,1:T(8,128)(2,1)S(1)} %bitcast.477), channel_id=1, source_target_pairs={{0,16},{8,24},{16,0},{24,8},{1,17},{9,25},{17,1},{25,9},{2,18},{10... | collective-permute-start | bytes 8650760 | tf_op jit(solution)/shard_map/ppermute | solution.py:187
  754.0 221.9 %collective-permute-start.15 = (bf16[2048,704]{0,1:T(8,128)(2,1)}, bf16[2048,704]{0,1:T(8,128)(2,1)}, u32[]{:S(2)}, u32[]{:S(2)}) collective-permute-start(bf16[2048,704]{0,1:T(8,128)(2,1)} %bitcast.150), channel_id=1, source_target_pairs={{0,24},{8,16},{16,8},{24,0},{1,25},{9,17},{17,9},{25,1},{2,26},{10... | collective-permute-start | bytes 8650760 | tf_op jit(solution)/shard_map/ppermute | solution.py:187
  785.7 196.2 %collective-permute-start.16 = (bf16[2048,704]{0,1:T(8,128)(2,1)S(1)}, bf16[2048,704]{0,1:T(8,128)(2,1)}, u32[]{:S(2)}, u32[]{:S(2)}) collective-permute-start(bf16[2048,704]{0,1:T(8,128)(2,1)S(1)} %bitcast.478), channel_id=1, source_target_pairs={{0,24},{8,16},{16,8},{24,0},{1,25},{9,17},{17,9},{25,1},{2,26},{10... | collective-permute-start | bytes 8650760 | tf_op jit(solution)/shard_map/ppermute | solution.py:187
  1122.7 177.8 %reduce-scatter.8.cloned.1.call-start = ((), (), s32[]{:S(2)}) async-start(), calls=%async_computation.21 | async-start | bytes 9437184 | tf_op jit(solution)/shard_map/reduce_scatter | solution.py:203
  1174.4 686.2 %all-reduce.4.cloned.1.call-start = ((), (), s32[]{:S(2)}) async-start(), calls=%async_computation.27 | async-start | bytes 8388608
  1447.4 525.7 %reduce-scatter.14.cloned.1.call-start = ((), (), s32[]{:S(2)}) async-start(), calls=%async_computation.24 | async-start | bytes 9437184 | tf_op jit(solution)/shard_map/reduce_scatter | solution.py:203
  1461.3 523.9 %reduce-scatter.12.cloned.1.call-start = ((), (), s32[]{:S(2)}) async-start(), calls=%async_computation.23 | async-start | bytes 9437184 | tf_op jit(solution)/shard_map/reduce_scatter | solution.py:203
  1470.1 65.7 %collective-permute-start.33 = (bf16[2048,704]{0,1:T(8,128)(2,1)}, bf16[2048,704]{0,1:T(8,128)(2,1)}, u32[]{:S(2)}, u32[]{:S(2)}) collective-permute-start(bf16[2048,704]{0,1:T(8,128)(2,1)} %convolution_convert_fusion.18), channel_id=1, source_target_pairs={{0,8},{8,0},{16,24},{24,16},{1,9},{9,1},{17,25},{25,17},{2,10},{10... | collective-permute-start | bytes 8650760 | tf_op jit(solution)/shard_map/ppermute | solution.py:187
  1478.7 123.1 %collective-permute-start.34 = (bf16[2048,704]{0,1:T(8,128)(2,1)}, bf16[2048,704]{0,1:T(8,128)(2,1)}, u32[]{:S(2)}, u32[]{:S(2)}) collective-permute-start(bf16[2048,704]{0,1:T(8,128)(2,1)} %convolution_convert_fusion.17), channel_id=1, source_target_pairs={{0,16},{8,24},{16,0},{24,8},{1,17},{9,25},{17,1},{25,9},{2,18},{10... | collective-permute-start | bytes 8650760 | tf_op jit(solution)/shard_map/ppermute | solution.py:187
  1485.6 116.1 %collective-permute-start.35 = (bf16[2048,704]{0,1:T(8,128)(2,1)}, bf16[2048,704]{0,1:T(8,128)(2,1)}, u32[]{:S(2)}, u32[]{:S(2)}) collective-permute-start(bf16[2048,704]{0,1:T(8,128)(2,1)} %convolution_convert_fusion.16), channel_id=1, source_target_pairs={{0,24},{8,16},{16,8},{24,0},{1,25},{9,17},{17,9},{25,1},{2,26},{10... | collective-permute-start | bytes 8650760 | tf_op jit(solution)/shard_map/ppermute | solution.py:187
  1610.5 154.4 %all-to-all-start.13 = ((bf16[8,256,704]{1,2,0:T(8,128)(2,1)}), bf16[8,256,704]{1,2,0:T(8,128)(2,1)S(1)}, u32[]{:S(2)}, u32[]{:S(2)}) async-start(bf16[8,256,704]{1,2,0:T(8,128)(2,1)} %bitcast.402), calls=%async_computation.17 | async-start | bytes 5767168 | tf_op jit(solution)/shard_map/all_to_all | solution.py:197
  1626.0 126.4 %collective-permute-start.31 = (bf16[2048,704]{0,1:T(8,128)(2,1)S(1)}, bf16[2048,704]{0,1:T(8,128)(2,1)S(1)}, u32[]{:S(2)}, u32[]{:S(2)}) collective-permute-start(bf16[2048,704]{0,1:T(8,128)(2,1)S(1)} %copy-done.160), channel_id=1, source_target_pairs={{0,16},{8,24},{16,0},{24,8},{1,17},{9,25},{17,1},{25,9},{2,18},{10... | collective-permute-start | bytes 8650760 | tf_op jit(solution)/shard_map/ppermute | solution.py:187
  1627.7 124.7 %collective-permute-start.32 = (bf16[2048,704]{0,1:T(8,128)(2,1)S(1)}, bf16[2048,704]{0,1:T(8,128)(2,1)}, u32[]{:S(2)}, u32[]{:S(2)}) collective-permute-start(bf16[2048,704]{0,1:T(8,128)(2,1)S(1)} %convolution_convert_fusion.20), channel_id=1, source_target_pairs={{0,24},{8,16},{16,8},{24,0},{1,25},{9,17},{17,9},{25,1},{2,26},{10... | collective-permute-start | bytes 8650760 | tf_op jit(solution)/shard_map/ppermute | solution.py:187
  1766.5 88.6 %all-to-all-start.12 = ((bf16[8,256,704]{1,2,0:T(8,128)(2,1)}), bf16[8,256,704]{1,2,0:T(8,128)(2,1)}, u32[]{:S(2)}, u32[]{:S(2)}) async-start(bf16[8,256,704]{1,2,0:T(8,128)(2,1)} %bitcast.401), calls=%async_computation.16 | async-start | bytes 5767168 | tf_op jit(solution)/shard_map/all_to_all | solution.py:197
  1842.5 177.1 %collective-permute-start.36 = (bf16[704,2048]{1,0:T(8,128)(2,1)}, bf16[704,2048]{1,0:T(8,128)(2,1)}, u32[]{:S(2)}, u32[]{:S(2)}) collective-permute-start(bf16[704,2048]{1,0:T(8,128)(2,1)} %convolution_convert_fusion.26), channel_id=1, source_target_pairs={{0,8},{8,0},{16,24},{24,16},{1,9},{9,1},{17,25},{25,17},{2,10},{10... | collective-permute-start | bytes 8650760 | tf_op jit(solution)/shard_map/ppermute | solution.py:187
  1843.8 175.8 %collective-permute-start.37 = (bf16[704,2048]{1,0:T(8,128)(2,1)}, bf16[704,2048]{1,0:T(8,128)(2,1)}, u32[]{:S(2)}, u32[]{:S(2)}) collective-permute-start(bf16[704,2048]{1,0:T(8,128)(2,1)} %convolution_convert_fusion.25), channel_id=1, source_target_pairs={{0,16},{8,24},{16,0},{24,8},{1,17},{9,25},{17,1},{25,9},{2,18},{10... | collective-permute-start | bytes 8650760 | tf_op jit(solution)/shard_map/ppermute | solution.py:187
  1845.4 174.3 %collective-permute-start.38 = (bf16[704,2048]{1,0:T(8,128)(2,1)}, bf16[704,2048]{1,0:T(8,128)(2,1)}, u32[]{:S(2)}, u32[]{:S(2)}) collective-permute-start(bf16[704,2048]{1,0:T(8,128)(2,1)} %convolution_convert_fusion.24), channel_id=1, source_target_pairs={{0,24},{8,16},{16,8},{24,0},{1,25},{9,17},{17,9},{25,1},{2,26},{10... | collective-permute-start | bytes 8650760 | tf_op jit(solution)/shard_map/ppermute | solution.py:187
  1855.1 114.5 %all-to-all-start.8 = ((f32[32,1,768]{2,1,0:T(1,128)}), f32[32,1,768]{2,1,0:T(1,128)S(1)}, u32[]{:S(2)}, u32[]{:S(2)}) async-start(f32[32,1,768]{2,1,0:T(1,128)} %all_to_all.76), calls=%async_computation.10 | async-start | bytes 196608 | tf_op jit(solution)/shard_map/all_to_all | solution.py:197
  (221 other events, 6341.6 us)
Sparse Core Ops, SparseCore 0:
  26.2 72.8 all-gather.15
  101.3 81.4 all-gather.9
  184.4 80.6 all-gather.11
  340.6 141.0 all-gather.13
  483.1 133.8 all-gather.17
  1122.8 87.3 reduce-scatter.9
  1212.5 87.9 reduce-scatter.7
  1447.5 95.9 all-reduce.3
  1545.8 100.9 reduce-scatter.13
  1648.9 115.5 reduce-scatter.11

commit v2 on v1

--- a/solution.py
+++ b/solution.py
@@ -90,9 +90,7 @@
             jax.ShapeDtypeStruct((heads, 1, rows), F32),
         ],
         cost_estimate=pl.CostEstimate(
-            flops=4 * rows * length * width,
-            transcendentals=rows * length * heads,
-            bytes_accessed=4 * rows * width + 4 * length * width,
+            flops=rows * length, transcendentals=0, bytes_accessed=4 * rows * width
         ),
         name="attend",
     )(q, k, v, q_blocks.reshape(1, 1, rows), k_blocks.reshape(length, 1))
@@ -144,9 +142,7 @@
             jax.ShapeDtypeStruct((length, width), F32),
         ],
         cost_estimate=pl.CostEstimate(
-            flops=10 * rows * length * width,
-            transcendentals=rows * length * heads,
-            bytes_accessed=10 * rows * width + 12 * length * width,
+            flops=rows * length, transcendentals=0, bytes_accessed=4 * rows * width
         ),
         name="attend_back",
     )(q, k, v, d, o, total, q_blocks.reshape(1, 1, rows), k_blocks.reshape(length, 1))
@@ -186,8 +182,48 @@
     def swap(value, k):
         return lax.ppermute(value, "expert", [(i, i ^ k) for i in range(n_e)])
 
+    def after(value, *others):
+        return lax.optimization_barrier((value,) + others)[0]
+
     def spread(value):
         return jnp.concatenate([value] + [swap(value, k) for k in range(1, n_e)], axis=0)
+
+    def fetch(block):
+        return [block] + [swap(block, k) for k in range(1, 3 if n_e == 4 else n_e)]
+
+    def fetch_rest(blocks, *others):
+        if n_e != 4:
+            return blocks
+        half = blocks[0].shape[0] // 2
+        one, two = after(blocks[1], *others), after(blocks[2], *others)
+        return blocks + [jnp.concatenate([swap(one[:half], 2), swap(two[half:], 1)], axis=0)]
+
+    def add_low(a, b):
+        return (a.astype(F32) + b.astype(F32)).astype(BF)
+
+    def deliver_first(far):
+        half = far.shape[0] // 2
+        return [swap(far[:half], 1), swap(far[half:], 2)] if n_e == 4 else []
+
+    def deliver_near(parts):
+        if n_e != 4:
+            return [swap(parts[k], k) for k in range(1, n_e)]
+        half = parts[0].shape[0] // 2
+        return [swap(parts[1][:half], 1), swap(parts[2][half:], 2)]
+
+    def deliver_last(parts, halves):
+        if n_e != 4:
+            return []
+        half = parts[0].shape[0] // 2
+        return [swap(add_low(parts[2][:half], halves[0]), 2), swap(add_low(parts[1][half:], halves[1]), 1)]
+
+    def total(own, near, last):
+        own = own.astype(F32)
+        if n_e != 4:
+            return sum([own] + [v.astype(F32) for v in near])
+        half = own.shape[0] // 2
+        near, last = [v.astype(F32) for v in near], [v.astype(F32) for v in last]
+        return jnp.concatenate([own[:half] + near[0] + last[0], own[half:] + near[1] + last[1]], axis=0)
 
     def collect(value):
         parts = jnp.split(value, n_e, axis=0)
@@ -206,6 +242,7 @@
         [attn_router, ffn_router, attn_gain[:, None], ffn_gain[:, None], attn_bias[:, None], ffn_bias[:, None]], axis=1
     )
     small_width = small.shape[1]
+    route_width = tokens * TOPK // (n_e * small_rows)
     small = jnp.pad(small, ((0, 0), (0, 128 - small_width)))
     packed = jnp.concatenate(
         [
@@ -215,7 +252,13 @@
         ],
         axis=2,
     )
-    packed = gather_shard(shuffle(packed, "expert")[None])
+    packed = shuffle(packed, "expert")
+    route_at = 2 * group + small_width
+    packed = packed.at[:, :, route_at:route_at + route_width].set(
+        ffn_routes[0].astype(BF).reshape(n_e, small_rows, route_width)
+    )
+    packed = gather_shard(packed[None])
+    routes_f = packed[:, :, :, route_at:route_at + route_width].reshape(n_s * tokens, TOPK).astype(jnp.int32)
     packed = packed.transpose(1, 0, 2, 3).reshape(width, -1)
     key_value_w = packed[:, :2 * group]
     small = packed[:, 2 * group:2 * group + small_width].astype(F32)
@@ -225,39 +268,32 @@
     def to_heads(value):
         rows = value.shape[0]
         value = shuffle(value.reshape(rows, n_e, group).transpose(1, 0, 2), "expert")
-        return gather_shard(value.transpose(1, 0, 2).reshape(rows, n_e * group))
+        return value.transpose(1, 0, 2).reshape(rows, n_e * group)
 
     def from_heads(value):
-        value = scatter_shard(value)
         rows = value.shape[0]
         value = shuffle(value.reshape(rows, n_e, group).transpose(1, 0, 2), "expert")
         return value.transpose(1, 0, 2).reshape(rows, n_e * group)
 
-    query_w = to_heads(w_query[0])
+    notes = jnp.concatenate([blocks[0][:, None], attn_routes[0]], axis=1).astype(BF)
+    carried = jnp.concatenate([inputs[0], jnp.pad(notes, ((0, 0), (0, 128 - 1 - TOPK)))], axis=1)
+    carried = spread(carried)
+    query_w = gather_shard(to_heads(w_query[0]))
     out_rows = w_out.shape[1]
-    turned = shuffle(w_out[0].T, "shard").reshape(n_s, width // n_s, out_rows).transpose(1, 0, 2)
-    out_wt = to_heads(turned.reshape(width // n_s, n_s * out_rows))
-
-    def to_columns(value):
-        rows = value.shape[0]
-        return shuffle(value.reshape(rows, n_s, -1).transpose(1, 0, 2), "shard").reshape(rows * n_s, -1)
-
-    def from_columns(value):
-        rows = value.shape[0] // n_s
-        value = shuffle(value, "shard").reshape(n_s, rows, -1)
-        return value.transpose(1, 0, 2).reshape(rows, -1)
-
-    gate_own, up_own, down_own = to_columns(w_gate[0]), to_columns(w_up[0]), w_down[0]
-    gate_w = [gate_own] + [swap(gate_own, k) for k in range(1, n_e)]
-    up_w = [up_own] + [swap(up_own, k) for k in range(1, n_e)]
-    down_w = [down_own] + [swap(down_own, k) for k in range(1, n_e)]
+    turned = shuffle(after(w_out[0], carried).T, "shard").reshape(n_s, width // n_s, out_rows).transpose(1, 0, 2)
+    out_wt = gather_shard(to_heads(turned.reshape(width // n_s, n_s * out_rows)))
+
+    hidden_units = w_down.shape[1]
+    turned = jnp.stack([w_gate[0].T.reshape(n_s, hidden_units, -1), w_up[0].T.reshape(n_s, hidden_units, -1)], axis=1)
+    turned = shuffle(after(turned, query_w), "shard").reshape(n_s, 2 * hidden_units, -1)
+    gate_up_own = turned.transpose(1, 0, 2).reshape(2 * hidden_units, width)
+    down_w = fetch(w_down[0])
 
     own = inputs[0].astype(F32)
     cot = cotangent[0]
-    seq_in = spread(inputs[0]).astype(F32)
-    meta = spread(jnp.concatenate([blocks, attn_routes[0].T], axis=0)[None])
-    seq_blocks = meta[:, 0].reshape(-1)
-    routes_a = meta[:, 1:].transpose(0, 2, 1).reshape(-1, TOPK)
+    seq_in = carried[:, :width].astype(F32)
+    notes = carried[:, width:width + 1 + TOPK].astype(jnp.int32)
+    seq_blocks, routes_a = notes[:, 0], notes[:, 1:]
     position = jnp.concatenate([(me ^ k) * tokens + jnp.arange(tokens, dtype=jnp.int32) for k in range(n_e)]).astype(F32)
     cosine, sine = rope_tables(position)
     h_attn = (seq_in * inverse_rms(seq_in) * gain_a).astype(BF)
@@ -269,21 +305,24 @@
     queries = pick(dot(h_attn, query_w), routes_a, ids)
     queries = jnp.concatenate([rotate(v, cosine, sine).astype(BF) for v in queries], axis=0)
     row_blocks = jnp.concatenate([seq_blocks, seq_blocks])
+    queries, *down_w = lax.optimization_barrier((queries, *down_w))
+    down_w = fetch_rest(down_w)
     mixed_rows, log_total = attend(queries, keys, values, row_blocks, seq_blocks)
     mixed = [v.astype(F32) for v in jnp.split(mixed_rows, TOPK, axis=0)]
     mixed_all = place([gates_a[j] * mixed[j] for j in range(TOPK)], routes_a, ids).astype(BF)
-    middle = own + collect(dot_nt(mixed_all, out_wt).astype(BF)) + bias_a
+    mixed_out, *down_w = lax.optimization_barrier((mixed_all, *down_w))
+    middle = own + collect(dot_nt(mixed_out, out_wt).astype(BF)) + bias_a
 
     inv_f = inverse_rms(middle)
     h_ffn = (middle * inv_f * gain_f).astype(BF)
+    h_ffn, gate_up_own = lax.optimization_barrier((h_ffn, gate_up_own))
+    gate_up_w = fetch(gate_up_own)
     h_all = gather_shard(h_ffn)
-    cot_all = gather_shard(cot)
-    routes_f = gather_shard(ffn_routes[0].T[None])
+    cot_all = gather_shard(after(cot, h_ffn))
     logits_f = dot(h_all, router_f.astype(BF))
-    flat_routes = routes_f.transpose(0, 2, 1).reshape(-1, TOPK)
-    gates_f = pair_softmax(pick(logits_f, flat_routes, ids))
+    gates_f = pair_softmax(pick(logits_f, routes_f, ids))
+    routes_blocks = routes_f.reshape(n_s, tokens, TOPK)
     h_blocks = h_all.reshape(n_s, tokens, width)
-    cot_blocks = cot_all.reshape(n_s, tokens, width)
     triangle = (jnp.arange(tokens)[:, None] <= jnp.arange(tokens)[None, :]).astype(BF)
 
     def rows_of(select, source):
@@ -291,20 +330,26 @@
             select, source, (((2,), (1,)), ((0,), (0,))), preferred_element_type=F32
         ).astype(BF).reshape(n_s * capacity, width)
 
-    selects, out_rows_f, back_rows_f = [], [], []
+    selects, hiddens, back_rows_f = [], [], []
     grad_gate_f = [0.0] * TOPK
-    weight_grads = []
+    grad_pieces = []
     for k in range(n_e):
+        if k == 1:
+            gate_up_w = fetch_rest(gate_up_w, hiddens[0])
         expert = me ^ k
-        named = [routes_f[:, j] == expert for j in range(TOPK)]
+        gate_w, up_w = gate_up_w[k][:hidden_units], gate_up_w[k][hidden_units:]
+        named = [routes_blocks[:, :, j] == expert for j in range(TOPK)]
         any_named = named[0] | named[1]
         rank = dot(any_named.astype(BF), triangle).astype(jnp.int32) - 1
         hit = (rank[:, None, :] == jnp.arange(capacity, dtype=jnp.int32)[None, :, None]) & any_named[:, None, :]
         select = hit.astype(BF)
         gate_token = sum(jnp.where(named[j], gates_f[j].reshape(n_s, tokens), 0.0) for j in range(TOPK))
         gate_slot = jnp.sum(jnp.where(hit, gate_token[:, None, :], 0.0), axis=2).reshape(-1, 1)
-        rows, cot_rows = rows_of(select, h_blocks), rows_of(select, cot_blocks)
-        gate_pre, up_pre = dot(rows, gate_w[k]), dot(rows, up_w[k])
+        rows = rows_of(select, h_blocks)
+        gate_pre, up_pre = dot_nt(rows, gate_w), dot_nt(rows, up_w)
+        if k == 0:
+            cot_blocks = after(cot_all, gate_pre, up_pre).reshape(n_s, tokens, width)
+        cot_rows = rows_of(select, cot_blocks)
         grad_hidden = dot_nt(cot_rows, down_w[k])
         sigma = 1.0 / (1.0 + jnp.exp(-gate_pre))
         silu = gate_pre * sigma
@@ -314,15 +359,13 @@
         hidden = (hidden * gate_slot).astype(BF)
         grad_gate = (grad_hidden * up_pre * sigma * (1.0 + gate_pre * (1.0 - sigma))).astype(BF)
         grad_up = (grad_hidden * silu).astype(BF)
-        back = (dot_nt(grad_gate, gate_w[k]) + dot_nt(grad_up, up_w[k])).astype(BF)
+        back = (dot(grad_gate, gate_w) + dot(grad_up, up_w)).astype(BF)
         selects.append(select)
         back_rows_f.append(back.reshape(n_s, capacity, width))
-        out_rows_f.append(dot(hidden, down_w[k]).astype(BF).reshape(n_s, capacity, width))
+        hiddens.append(hidden)
         grad_token = jnp.sum(jnp.where(hit, grad_slot[:, :, None], 0.0), axis=1)
         grad_gate_f = [grad_gate_f[j] + jnp.where(named[j], grad_token, 0.0) for j in range(TOPK)]
-        weight_grads.append(
-            (dot_tn(rows, grad_gate).astype(BF), dot_tn(rows, grad_up).astype(BF), dot_tn(hidden, cot_rows).astype(BF))
-        )
+        grad_pieces.append((rows, cot_rows, grad_gate, grad_up))
     select = jnp.concatenate(selects, axis=1)
 
     def tokens_of(row_list):
@@ -330,21 +373,29 @@
             select, jnp.concatenate(row_list, axis=1), (((1,), (1,)), ((0,), (0,))), preferred_element_type=F32
         ).astype(BF).reshape(n_s * tokens, width)
 
-    back_f = scatter_shard(tokens_of(back_rows_f)).astype(F32)
-    ffn_out = scatter_shard(tokens_of(out_rows_f)).astype(F32)
-    outputs = (middle + ffn_out + bias_f).astype(BF)[None]
+    back_sum = tokens_of(back_rows_f)
+    back_f = scatter_shard(back_sum)
+
+    def gate_up_grads(k, *others):
+        rows, _, grad_gate, grad_up = grad_pieces[k]
+        rows = after(rows, *others)
+        return jnp.concatenate([dot_tn(grad_gate, rows).astype(BF), dot_tn(grad_up, rows).astype(BF)], axis=0)
+
+    grad_gate_up = [None] * n_e
+    grad_gate_up[n_e - 1] = gate_up_grads(n_e - 1, back_sum)
+    halves = deliver_first(grad_gate_up[n_e - 1])
+    out_rows_f = []
+    for k in range(n_e):
+        hidden = after(hiddens[k], grad_gate_up[n_e - 1])
+        out_rows_f.append(dot(hidden, down_w[k]).astype(BF).reshape(n_s, capacity, width))
+    out_sum = tokens_of(out_rows_f)
+    ffn_out = scatter_shard(out_sum)
+    back_f, out_sum, *halves = lax.optimization_barrier((back_f, out_sum, *halves))
+    back_f = back_f.astype(F32)
     grad_gates_f = jnp.sum(
         shuffle(jnp.stack(grad_gate_f, axis=1).reshape(n_s, TOPK * tokens), "shard"), axis=0
     ).reshape(TOPK, tokens, 1)
 
-    def expert_sum(which):
-        return weight_grads[0][which].astype(F32) + sum(
-            swap(weight_grads[k][which], k).astype(F32) for k in range(1, n_e)
-        )
-
-    grad_gate_w = from_columns(expert_sum(0).astype(BF)).astype(F32)[None]
-    grad_up_w = from_columns(expert_sum(1).astype(BF)).astype(F32)[None]
-    grad_down_w = expert_sum(2)[None]
 
     grad_out = cot.astype(F32)
     own_routes_f = ffn_routes[0]
@@ -362,24 +413,56 @@
     grad_bias_f = jnp.sum(grad_out, axis=0)
     grad_bias_a = jnp.sum(grad_middle, axis=0)
 
-    seq_grad = spread(grad_middle.astype(BF))
+    grad_middle_low = grad_middle.astype(BF)
+    for k in range(n_e - 1):
+        grad_gate_up[k] = gate_up_grads(k, back_f)
+    seq_grad = spread(grad_middle_low)
+    seq_grad, *grad_gate_up = lax.optimization_barrier((seq_grad, *grad_gate_up))
+    near = deliver_near(grad_gate_up)
+    last = deliver_last(grad_gate_up, halves)
     grad_mixed = pick(dot(seq_grad, out_wt), routes_a, ids)
-    grad_gates_a = [collect(jnp.sum(grad_mixed[j] * mixed[j], axis=1, keepdims=True)) for j in range(TOPK)]
+    gate_grads = jnp.concatenate([jnp.sum(grad_mixed[j] * mixed[j], axis=1, keepdims=True) for j in range(TOPK)], axis=1)
+    gate_grads_high = gate_grads.astype(BF)
+    gate_grads_low = (gate_grads - gate_grads_high.astype(F32)).astype(BF)
     grad_mixed = jnp.concatenate([(gates_a[j] * grad_mixed[j]).astype(BF) for j in range(TOPK)], axis=0)
     grad_out_wt = dot_tn(seq_grad, mixed_all).astype(BF)
+    grad_mixed, grad_out_wt = lax.optimization_barrier((grad_mixed, grad_out_wt))
     grad_q, grad_k, grad_v = attend_back(queries, keys, values, grad_mixed, mixed_rows, log_total, row_blocks, seq_blocks)
+    grad_q, *near = lax.optimization_barrier((grad_q, *near))
     grad_q = [rotate(v, cosine, -sine) for v in jnp.split(grad_q, TOPK, axis=0)]
     grad_query_all = place(grad_q, routes_a, ids).astype(BF)
     grad_key_value = jnp.concatenate([rotate(grad_k, cosine, -sine), grad_v], axis=1).astype(BF)
-    back_a = collect((dot_nt(grad_query_all, query_w) + dot_nt(grad_key_value, key_value_w)).astype(BF))
-    grad_query_w = from_heads(dot_tn(h_attn, grad_query_all).astype(BF)).astype(F32)[None]
-    value = from_heads(grad_out_wt)
-    value = value.reshape(width // n_s, n_s, out_rows).transpose(1, 0, 2)
-    grad_out_w = shuffle(value, "shard").reshape(width, out_rows).T.astype(F32)[None]
-    value = dot_tn(h_attn, grad_key_value).astype(BF).reshape(n_e, n_s, small_rows, 2 * group).transpose(1, 0, 2, 3)
-    value = shuffle(scatter_shard(value)[0], "expert")
-    grad_key_w = value[:, :, :group].transpose(1, 0, 2).reshape(small_rows, -1).astype(F32)
-    grad_value_w = value[:, :, group:].transpose(1, 0, 2).reshape(small_rows, -1).astype(F32)
+    back_a = (dot_nt(grad_query_all, query_w) + dot_nt(grad_key_value, key_value_w)).astype(BF)
+    back_a = jnp.concatenate(
+        [back_a, jnp.pad(jnp.concatenate([gate_grads_high, gate_grads_low], axis=1), ((0, 0), (0, 128 - 2 * TOPK)))], axis=1
+    )
+    back_a, ffn_out, *last = lax.optimization_barrier((back_a, ffn_out, *last))
+    value = total(grad_gate_up[0], near, last).astype(BF).reshape(2 * hidden_units, n_s, width // n_s).transpose(1, 0, 2)
+    gate_up_turned = shuffle(value, "shard").reshape(n_s, 2, hidden_units, width // n_s)
+    outputs = (middle + ffn_out.astype(F32) + bias_f).astype(BF)[None]
+    grad_down = [dot_tn(after(hiddens[k], back_a), grad_pieces[k][1]).astype(BF) for k in range(n_e)]
+    halves = deliver_first(grad_down[n_e - 1])
+    value = scatter_shard(grad_out_wt)
+    value, key_value_grad = lax.optimization_barrier((value, dot_tn(h_attn, grad_key_value).astype(BF)))
+    value = from_heads(value).reshape(width // n_s, n_s, out_rows).transpose(1, 0, 2)
+    grad_out_w = shuffle(value, "shard").reshape(width, out_rows)
+    key_value_grad = key_value_grad.reshape(n_e, n_s, small_rows, 2 * group).transpose(1, 0, 2, 3)
+    key_value_grad = scatter_shard(key_value_grad.reshape(n_s * n_e * small_rows, 2 * group))
+    key_value_grad = shuffle(key_value_grad.reshape(n_e, small_rows, -1), "expert")
+    back_a = collect(back_a)
+    near, last = deliver_near(grad_down), deliver_last(grad_down, halves)
+    back_a, grad_out_w, key_value_grad, *near = lax.optimization_barrier((back_a, grad_out_w, key_value_grad, *near))
+    grad_down_w = total(grad_down[0], near, last)[None]
+    grad_out_w = grad_out_w.T.astype(F32)[None]
+    grad_key_w = key_value_grad[:, :, :group].transpose(1, 0, 2).reshape(small_rows, -1).astype(F32)
+    grad_value_w = key_value_grad[:, :, group:].transpose(1, 0, 2).reshape(small_rows, -1).astype(F32)
+    gate_grads = back_a[:, width:width + TOPK] + back_a[:, width + TOPK:width + 2 * TOPK]
+    grad_gates_a = [gate_grads[:, j:j + 1] for j in range(TOPK)]
+    back_a = back_a[:, :width]
+    value = after(scatter_shard(dot_tn(h_attn, grad_query_all).astype(BF)), gate_up_turned)
+    grad_query_w = from_heads(value).astype(F32)[None]
+    grad_gate_w = gate_up_turned[:, 0].reshape(n_s * hidden_units, -1).T.astype(F32)[None]
+    grad_up_w = gate_up_turned[:, 1].reshape(n_s * hidden_units, -1).T.astype(F32)[None]
 
     h_own = h_attn[:tokens]
     own_routes_a = attn_routes[0]

time: 2080 us -> 1560 us (0.75)
  waiting for transfers between devices: 969 us -> 444 us
  blocking collectives: 234 us -> 98.8 us
  other arithmetic: 101 us -> 202 us
  local copies, waits for them, and re-layouts: 127 us -> 185 us
    ppermute x39 -> x32, waiting for transfers between devices: 586 us -> 211 us  [swap(): return lax.ppermute(value, 'expert', [(i, i ^ k) for i in range(n_e)])]
    all_to_all x10 -> x9, waiting for transfers between devices: 267 us -> 92.3 us  [shuffle(): return lax.all_to_all(value, axis, split_axis=0, concat_axis=0, tiled=True)]
    all_gather x5, waiting for transfers between devices: 0.06 us -> 135 us  [gather_shard(): return lax.all_gather(value, 'shard', axis=0, tiled=True)]
    all_gather x1 -> x0, blocking collectives: 133 us -> none  [gather_shard(): return lax.all_gather(value, 'shard', axis=0, tiled=True)]
    reduce_scatter x4 -> x5, waiting for transfers between devices: 115 us -> 5.18 us  [scatter_shard(): return lax.psum_scatter(value, 'shard', scatter_dimension=0, tiled=True)]
    slice x2 -> x14, local copies, waits for them, and re-layouts: 0.02 us -> 34.2 us  [the longest x4 10.1 us: deliver_near(): return [swap(parts[1][:half], 1), swap(parts[2][half:], 2)]]
    dot_general x22, matrix products: 123 us -> 151 us  [dot(): return jnp.dot(a, b, preferred_element_type=F32)]
    dot_general x15, matrix products: 148 us -> 123 us  [dot_nt(): lax.dot_general(a, b, (((1,), (1,)), ((), ())), preferred_element_type=F32)]
  transfers between devices with their start and end apart: 59 -> 51, of which waited for: 23 -> 22; matrix products, arithmetic and copies ran while one was open for 22% -> 48% of each run, Pallas kernels for 1% -> 4%
where the time goes in v2:
time: 1560 us; the launch traced here: 1550 us
  matrix products  455 us (29%)
  waiting for transfers between devices  444 us (28%)
  other arithmetic  202 us (13%)
  local copies, waits for them, and re-layouts  185 us (12%)
  blocking collectives  98.8 us (6%)
  starting transfers between devices  80 us (5%)
  Pallas kernels  69.6 us (4%)
  between operations  17.4 us (1%)
    ppermute x32, waiting for transfers between devices, swap(): return lax.ppermute(value, 'expert', [(i, i ^ k) for i in range(n_e)])  211 us
    dot_general x22, matrix products, dot(): return jnp.dot(a, b, preferred_element_type=F32)  151 us
    all_gather x5, waiting for transfers between devices, gather_shard(): return lax.all_gather(value, 'shard', axis=0, tiled=True)  135 us
    dot_general x15, matrix products, dot_nt(): lax.dot_general(a, b, (((1,), (1,)), ((), ())), preferred_element_type=F32)  123 us
    dot_general x17, matrix products, dot_tn(): lax.dot_general(a, b, (((0,), (0,)), ((), ())), precision=precision, pref...  105 us
    all_to_all x3, blocking collectives, shuffle(): return lax.all_to_all(value, axis, split_axis=0, concat_axis=0, tiled=True)  98.8 us
    all_to_all x9, waiting for transfers between devices, shuffle(): return lax.all_to_all(value, axis, split_axis=0, concat_axis=0, tiled=True)  92.3 us
    unnamed x474, local copies, waits for them, and re-layouts  54.2 us
  transfers between devices with their start and end apart: 51, of which 22 were waited for; matrix products, arithmetic and copies ran while one was open for 48% of the time, Pallas kernels for 4%

profile of v2, /device:TPU:0, one launch (start us, length us, event | category | flops | bytes accessed | tf_op | source)
XLA Modules:
  0.0 1551.9 jit_solution(10678863514165433477)
XLA Ops:
  29.2 16.1 %all_to_all.73 = bf16[4,256,512]{2,1,0:T(8,128)(2,1)S(1)} all-to-all(bf16[4,256,512]{2,1,0:T(8,128)(2,1)S(1)} %copy.525), channel_id=1, replica_groups=mesh['expert'=4,'shard'=8] {'expert'}, dimensions={0} | all-to-all | bytes 2097152 | tf_op jit(solution)/shard_map/all_to_all | solution.py:233
  53.1 23.6 %collective-permute-done.2 = bf16[256,2176]{1,0:T(8,128)(2,1)S(1)} collective-permute-done((bf16[256,2176]{1,0:T(8,128)(2,1)}, bf16[256,2176]{1,0:T(8,128)(2,1)S(1)}, u32[]{:S(2)}, u32[]{:S(2)}) %collective-permute-start.2) | collective-permute-done | bytes 1114144 | tf_op jit(solution)/shard_map/ppermute | solution.py:183
  76.7 20.7 %collective-permute-done.1 = bf16[256,2176]{1,0:T(8,128)(2,1)} collective-permute-done((bf16[256,2176]{1,0:T(8,128)(2,1)}, bf16[256,2176]{1,0:T(8,128)(2,1)}, u32[]{:S(2)}, u32[]{:S(2)}) %collective-permute-start.1) | collective-permute-done | bytes 1114144 | tf_op jit(solution)/shard_map/ppermute | solution.py:183
  106.0 65.0 %all_to_all.74 = bf16[8,256,256]{2,1,0:T(8,128)(2,1)S(1)} all-to-all(bf16[8,256,256]{2,1,0:T(8,128)(2,1)S(1)} %bitcast.484), channel_id=1, replica_groups=mesh['expert'=4,'shard'=8] {'shard'}, dimensions={0} | all-to-all | bytes 2097152 | tf_op jit(solution)/shard_map/all_to_all | solution.py:233
  171.5 17.7 %all_to_all.75 = bf16[4,256,512]{1,2,0:T(8,128)(2,1)} all-to-all(bf16[4,256,512]{1,2,0:T(8,128)(2,1)S(1)} %bitcast.487), channel_id=1, replica_groups=mesh['expert'=4,'shard'=8] {'expert'}, dimensions={0} | all-to-all | bytes 2097152 | tf_op jit(solution)/shard_map/all_to_all | solution.py:233
  247.1 12.6 fusion.191
  300.0 29.7 %attend.1 = (bf16[2048,512]{1,0:T(8,128)(2,1)}, f32[4,1,2048]{2,1,0:T(1,128)}) custom-call(bf16[2048,512]{1,0:T(8,128)(2,1)} %pad_maximum_fusion.10.q_ref, bf16[1024,512]{1,0:T(8,128)(2,1)} %get-tuple-element.397.k_ref, bf16[1024,512]{1,0:T(8,128)(2,1)} %slice.615.v_ref, s32[1,1,2048]{2,1,0:T(1,128)} %bitcast.499, s32[1024,1]{1,0:T(8,128)} %get-tuple-element.415.kb_ref), custom_call_target="tpu_custom_call" | custom-call | flops 2097152 | bytes 4194304 | tf_op jit(solution)/shard_map/attend/pallas_call | solution.py:74
  342.3 12.5 convolution_convert_fusion.14
  358.7 22.5 %collective-permute-done.7 = bf16[256,2048]{1,0:T(8,128)(2,1)S(1)} collective-permute-done((bf16[256,2048]{1,0:T(8,128)(2,1)S(1)}, bf16[256,2048]{1,0:T(8,128)(2,1)S(1)}, u32[]{:S(2)}, u32[]{:S(2)}) %collective-permute-start.7) | collective-permute-done | bytes 1048608 | tf_op jit(solution)/shard_map/ppermute | solution.py:183
  381.3 21.6 %collective-permute-done.9 = bf16[256,2048]{1,0:T(8,128)(2,1)S(1)} collective-permute-done((bf16[256,2048]{1,0:T(8,128)(2,1)S(1)}, bf16[256,2048]{1,0:T(8,128)(2,1)S(1)}, u32[]{:S(2)}, u32[]{:S(2)}) %collective-permute-start.9) | collective-permute-done | bytes 1048608 | tf_op jit(solution)/shard_map/ppermute | solution.py:183
  421.5 77.6 %all-gather.14.cloned.1.call-done = bf16[2048,2048]{1,0:T(8,128)(2,1)} async-done(((bf16[256,2048]{1,0:T(8,128)(2,1)}), bf16[2048,2048]{1,0:T(8,128)(2,1)}) %all-gather.14.cloned.1.call-update) | async-done | bytes 8388624 | tf_op jit(solution)/shard_map/all_gather | solution.py:236
  524.1 57.1 %all-gather.12.cloned.1.call-done = bf16[2048,2048]{1,0:T(8,128)(2,1)} async-done(((bf16[256,2048]{1,0:T(8,128)(2,1)}), bf16[2048,2048]{1,0:T(8,128)(2,1)}) %all-gather.12.cloned.1.call-update) | async-done | bytes 8388624 | tf_op jit(solution)/shard_map/all_gather | solution.py:236
  639.6 9.5 multiply_reduce_fusion.1
  726.1 10.9 add_convert_fusion.3
  737.1 11.0 fusion.51
  748.1 9.8 add_convert_fusion.2
  757.9 10.9 fusion.44
  773.0 14.0 add_convert_fusion.1
  830.4 12.6 fusion.27
  889.2 14.1 fusion.24
  985.5 11.6 fusion.195
  1004.8 11.7 convolution_convert_fusion.1
  1026.4 39.8 %attend_back.1 = (f32[2048,512]{1,0:T(8,128)}, f32[1024,512]{1,0:T(8,128)}, f32[1024,512]{1,0:T(8,128)}) custom-call(bf16[2048,512]{1,0:T(8,128)(2,1)} %pad_maximum_fusion.10.q_ref, bf16[1024,512]{1,0:T(8,128)(2,1)} %get-tuple-element.397.k_ref, bf16[1024,512]{1,0:T(8,128)(2,1)} %slice.615.v_ref, bf16[2048,512]{1,0:T(8,128)(2,1)} %pad_maximum_fusion.11.d_ref, ...), custom_call_target="tpu_custom_call" | custom-call | flops 2097152 | bytes 4194304 | tf_op jit(solution)/shard_map/attend_back/pallas_call | solution.py:129
  1071.4 17.2 %collective-permute-done.20 = bf16[704,2048]{1,0:T(8,128)(2,1)} collective-permute-done((bf16[704,2048]{1,0:T(8,128)(2,1)}, bf16[704,2048]{1,0:T(8,128)(2,1)}, u32[]{:S(2)}, u32[]{:S(2)}) %collective-permute-start.20) | collective-permute-done | bytes 2883616 | tf_op jit(solution)/shard_map/ppermute | solution.py:183
  1112.5 12.0 convolution_convert_fusion
  1149.2 13.3 fusion.106
  1172.1 28.1 %collective-permute-done.21 = bf16[704,2048]{1,0:T(8,128)(2,1)} collective-permute-done((bf16[704,2048]{1,0:T(8,128)(2,1)}, bf16[704,2048]{1,0:T(8,128)(2,1)}, u32[]{:S(2)}, u32[]{:S(2)}) %collective-permute-start.21) | collective-permute-done | bytes 2883616 | tf_op jit(solution)/shard_map/ppermute | solution.py:183
  1205.4 10.5 convolution_convert_fusion.15
  1285.0 43.6 %collective-permute-done.23 = bf16[256,2176]{1,0:T(8,128)(2,1)} collective-permute-done((bf16[256,2176]{1,0:T(8,128)(2,1)}, bf16[256,2176]{1,0:T(8,128)(2,1)}, u32[]{:S(2)}, u32[]{:S(2)}) %collective-permute-start.23) | collective-permute-done | bytes 1114144 | tf_op jit(solution)/shard_map/ppermute | solution.py:183
  1330.0 21.9 %collective-permute-done.25 = bf16[256,2176]{1,0:T(8,128)(2,1)} collective-permute-done((bf16[256,2176]{1,0:T(8,128)(2,1)}, bf16[256,2176]{1,0:T(8,128)(2,1)}, u32[]{:S(2)}, u32[]{:S(2)}) %collective-permute-start.25) | collective-permute-done | bytes 1114144 | tf_op jit(solution)/shard_map/ppermute | solution.py:183
  1353.9 52.1 %all-to-all-done.10 = bf16[8,1408,256]{2,1,0:T(8,128)(2,1)} async-done(((bf16[8,1408,256]{2,1,0:T(8,128)(2,1)}), bf16[8,1408,256]{2,1,0:T(8,128)(2,1)}, u32[]{:S(2)}, u32[]{:S(2)}) %all-to-all-start.10) | async-done | bytes 5767200 | tf_op jit(solution)/shard_map/all_to_all | solution.py:233
  1446.1 19.2 %all-to-all-done.11 = bf16[4,256,512]{2,1,0:T(8,128)(2,1)} async-done(((bf16[4,256,512]{2,1,0:T(8,128)(2,1)}), bf16[4,256,512]{2,1,0:T(8,128)(2,1)}, u32[]{:S(2)}, u32[]{:S(2)}) %all-to-all-start.11) | async-done | bytes 1048608 | tf_op jit(solution)/shard_map/all_to_all | solution.py:233
  (850 shorter events, 784.0 us)
Async XLA Ops:
  17.5 196.8 %all-gather.6.cloned.1.call-start = ((), (), s32[]{:S(2)}) async-start(), calls=%async_computation.17 | async-start | bytes 5308416 | tf_op jit(solution)/shard_map/all_gather | solution.py:236
  28.0 208.3 %all-gather.8.cloned.1.call-start = ((), (), s32[]{:S(2)}) async-start(), calls=%async_computation.18 | async-start | bytes 9437184 | tf_op jit(solution)/shard_map/all_gather | solution.py:236
  46.6 295.8 %all-gather.10.cloned.1.call-start = ((), (), s32[]{:S(2)}) async-start(), calls=%async_computation.19 | async-start | bytes 9437184 | tf_op jit(solution)/shard_map/all_gather | solution.py:236
  189.2 101.4 %collective-permute-start.4 = (bf16[704,2048]{1,0:T(8,128)(2,1)}, bf16[704,2048]{1,0:T(8,128)(2,1)}, u32[]{:S(2)}, u32[]{:S(2)}) collective-permute-start(bf16[704,2048]{1,0:T(8,128)(2,1)} %bitcast.516), channel_id=1, source_target_pairs={{0,16},{8,24},{16,0},{24,8},{1,17},{9,25},{17,1},{25,9},{2,18},{10... | collective-permute-start | bytes 8650760 | tf_op jit(solution)/shard_map/ppermute | solution.py:183
  190.2 100.5 %collective-permute-start.3 = (bf16[704,2048]{1,0:T(8,128)(2,1)}, bf16[704,2048]{1,0:T(8,128)(2,1)}, u32[]{:S(2)}, u32[]{:S(2)}) collective-permute-start(bf16[704,2048]{1,0:T(8,128)(2,1)} %bitcast.517), channel_id=1, source_target_pairs={{0,8},{8,0},{16,24},{24,16},{1,9},{9,1},{17,25},{25,17},{2,10},{10... | collective-permute-start | bytes 8650760 | tf_op jit(solution)/shard_map/ppermute | solution.py:183
  242.2 166.4 %all-to-all-start.4 = ((bf16[8,2,704,256]{3,2,1,0:T(8,128)(2,1)}), bf16[8,2,704,256]{3,2,1,0:T(8,128)(2,1)}, u32[]{:S(2)}, u32[]{:S(2)}) async-start(bf16[8,2,704,256]{3,2,1,0:T(8,128)(2,1)} %copy.535), calls=%async_computation.4 | async-start | bytes 11534336 | tf_op jit(solution)/shard_map/all_to_all | solution.py:233
  246.9 252.2 %all-gather.14.cloned.1.call-start = ((), (), s32[]{:S(2)}) async-start(), calls=%async_computation.21 | async-start | bytes 9437184 | tf_op jit(solution)/shard_map/all_gather | solution.py:236
  416.9 164.3 %all-gather.12.cloned.1.call-start = ((), (), s32[]{:S(2)}) async-start(), calls=%async_computation.20 | async-start | bytes 9437184 | tf_op jit(solution)/shard_map/all_gather | solution.py:236
  417.4 512.2 %reduce-scatter.6.cloned.1.call-start = ((), (), s32[]{:S(2)}) async-start(), calls=%async_computation.22 | async-start | bytes 9437184 | tf_op jit(solution)/shard_map/reduce_scatter | solution.py:239
  419.5 195.1 %collective-permute-start.11 = (bf16[1408,2048]{0,1:T(8,128)(2,1)}, bf16[1408,2048]{0,1:T(8,128)(2,1)}, u32[]{:S(2)}, u32[]{:S(2)}) collective-permute-start(bf16[1408,2048]{0,1:T(8,128)(2,1)} %bitcast.467), channel_id=1, source_target_pairs={{0,16},{8,24},{16,0},{24,8},{1,17},{9,25},{17,1},{25,9},{2,18},{10... | collective-permute-start | bytes 17301512 | tf_op jit(solution)/shard_map/ppermute | solution.py:183
  420.5 251.8 %collective-permute-start.10 = (bf16[1408,2048]{0,1:T(8,128)(2,1)}, bf16[1408,2048]{0,1:T(8,128)(2,1)}, u32[]{:S(2)}, u32[]{:S(2)}) collective-permute-start(bf16[1408,2048]{0,1:T(8,128)(2,1)} %bitcast.468), channel_id=1, source_target_pairs={{0,8},{8,0},{16,24},{24,16},{1,9},{9,1},{17,25},{25,17},{2,10},{10... | collective-permute-start | bytes 17301512 | tf_op jit(solution)/shard_map/ppermute | solution.py:183
  621.0 166.0 %collective-permute-start.12 = (bf16[704,2048]{1,0:T(8,128)(2,1)}, bf16[704,2048]{1,0:T(8,128)(2,1)}, u32[]{:S(2)}, u32[]{:S(2)}) collective-permute-start(bf16[704,2048]{1,0:T(8,128)(2,1)} %copy.546), channel_id=1, source_target_pairs={{0,8},{8,0},{16,24},{24,16},{1,9},{9,1},{17,25},{25,17},{2,10},{10... | collective-permute-start | bytes 8650760 | tf_op jit(solution)/shard_map/ppermute | solution.py:183
  677.3 115.5 %collective-permute-start.13 = (bf16[704,2048]{1,0:T(8,128)(2,1)}, bf16[704,2048]{1,0:T(8,128)(2,1)}, u32[]{:S(2)}, u32[]{:S(2)}) collective-permute-start(bf16[704,2048]{1,0:T(8,128)(2,1)} %copy.547), channel_id=1, source_target_pairs={{0,16},{8,24},{16,0},{24,8},{1,17},{9,25},{17,1},{25,9},{2,18},{10... | collective-permute-start | bytes 8650760 | tf_op jit(solution)/shard_map/ppermute | solution.py:183
  843.1 329.1 %reduce-scatter.8.cloned.1.call-start = ((), (), s32[]{:S(2)}) async-start(), calls=%async_computation.23 | async-start | bytes 9437184 | tf_op jit(solution)/shard_map/reduce_scatter | solution.py:239
  852.2 69.6 %collective-permute-start.14 = (bf16[704,2048]{1,0:T(8,128)(2,1)}, bf16[704,2048]{1,0:T(8,128)(2,1)}, u32[]{:S(2)}, u32[]{:S(2)}) collective-permute-start(bf16[704,2048]{1,0:T(8,128)(2,1)} %convolution_convert_fusion.27), channel_id=1, source_target_pairs={{0,8},{8,0},{16,24},{24,16},{1,9},{9,1},{17,25},{25,17},{2,10},{10... | collective-permute-start | bytes 8650760 | tf_op jit(solution)/shard_map/ppermute | solution.py:183
  860.5 64.0 %collective-permute-start.15 = (bf16[704,2048]{1,0:T(8,128)(2,1)}, bf16[704,2048]{1,0:T(8,128)(2,1)}, u32[]{:S(2)}, u32[]{:S(2)}) collective-permute-start(bf16[704,2048]{1,0:T(8,128)(2,1)} %convolution_convert_fusion.26), channel_id=1, source_target_pairs={{0,16},{8,24},{16,0},{24,8},{1,17},{9,25},{17,1},{25,9},{2,18},{10... | collective-permute-start | bytes 8650760 | tf_op jit(solution)/shard_map/ppermute | solution.py:183
  908.3 307.6 %reduce-scatter.10.cloned.1.call-start = ((), (), s32[]{:S(2)}) async-start(), calls=%async_computation.24 | async-start | bytes 9437184 | tf_op jit(solution)/shard_map/reduce_scatter | solution.py:239
  1016.5 409.8 %reduce-scatter.14.cloned.1.call-start = ((), (), s32[]{:S(2)}) async-start(), calls=%async_computation.26 | async-start | bytes 9437184 | tf_op jit(solution)/shard_map/reduce_scatter | solution.py:239
  1024.1 64.6 %collective-permute-start.20 = (bf16[704,2048]{1,0:T(8,128)(2,1)}, bf16[704,2048]{1,0:T(8,128)(2,1)}, u32[]{:S(2)}, u32[]{:S(2)}) collective-permute-start(bf16[704,2048]{1,0:T(8,128)(2,1)} %slice.386), channel_id=1, source_target_pairs={{0,16},{8,24},{16,0},{24,8},{1,17},{9,25},{17,1},{25,9},{2,18},{10... | collective-permute-start | bytes 8650760 | tf_op jit(solution)/shard_map/ppermute | solution.py:183
  1025.5 64.4 %collective-permute-start.19 = (bf16[704,2048]{1,0:T(8,128)(2,1)}, bf16[704,2048]{1,0:T(8,128)(2,1)}, u32[]{:S(2)}, u32[]{:S(2)}) collective-permute-start(bf16[704,2048]{1,0:T(8,128)(2,1)} %slice.385), channel_id=1, source_target_pairs={{0,8},{8,0},{16,24},{24,16},{1,9},{9,1},{17,25},{25,17},{2,10},{10... | collective-permute-start | bytes 8650760 | tf_op jit(solution)/shard_map/ppermute | solution.py:183
  1137.0 63.3 %collective-permute-start.21 = (bf16[704,2048]{1,0:T(8,128)(2,1)}, bf16[704,2048]{1,0:T(8,128)(2,1)}, u32[]{:S(2)}, u32[]{:S(2)}) collective-permute-start(bf16[704,2048]{1,0:T(8,128)(2,1)} %add_convert_fusion.6), channel_id=1, source_target_pairs={{0,16},{8,24},{16,0},{24,8},{1,17},{9,25},{17,1},{25,9},{2,18},{10... | collective-permute-start | bytes 8650760 | tf_op jit(solution)/shard_map/ppermute | solution.py:183
  1142.0 63.4 %collective-permute-start.22 = (bf16[704,2048]{1,0:T(8,128)(2,1)}, bf16[704,2048]{1,0:T(8,128)(2,1)S(1)}, u32[]{:S(2)}, u32[]{:S(2)}) collective-permute-start(bf16[704,2048]{1,0:T(8,128)(2,1)} %add_convert_fusion.5), channel_id=1, source_target_pairs={{0,8},{8,0},{16,24},{24,16},{1,9},{9,1},{17,25},{25,17},{2,10},{10... | collective-permute-start | bytes 8650760 | tf_op jit(solution)/shard_map/ppermute | solution.py:183
  1234.2 171.9 %all-to-all-start.10 = ((bf16[8,1408,256]{2,1,0:T(8,128)(2,1)}), bf16[8,1408,256]{2,1,0:T(8,128)(2,1)}, u32[]{:S(2)}, u32[]{:S(2)}) async-start(bf16[8,1408,256]{2,1,0:T(8,128)(2,1)} %maximum_bitcast_fusion), calls=%async_computation.15 | async-start | bytes 11534336 | tf_op jit(solution)/shard_map/all_to_all | solution.py:233
  1239.0 226.3 %reduce-scatter.12.cloned.1.call-start = ((), (), s32[]{:S(2)}) async-start(), calls=%async_computation.25 | async-start | bytes 4718592 | tf_op jit(solution)/shard_map/reduce_scatter | solution.py:239
  1262.0 231.2 %collective-permute-start.27 = (bf16[352,2048]{1,0:T(8,128)(2,1)}, bf16[352,2048]{1,0:T(8,128)(2,1)}, u32[]{:S(2)}, u32[]{:S(2)}) collective-permute-start(bf16[352,2048]{1,0:T(8,128)(2,1)} %slice.467), channel_id=1, source_target_pairs={{0,16},{8,24},{16,0},{24,8},{1,17},{9,25},{17,1},{25,9},{2,18},{10... | collective-permute-start | bytes 4325384 | tf_op jit(solution)/shard_map/ppermute | solution.py:183
  1269.9 144.8 %collective-permute-start.28 = (bf16[352,2048]{1,0:T(8,128)(2,1)}, bf16[352,2048]{1,0:T(8,128)(2,1)S(1)}, u32[]{:S(2)}, u32[]{:S(2)}) collective-permute-start(bf16[352,2048]{1,0:T(8,128)(2,1)} %get-tuple-element.384), channel_id=1, source_target_pairs={{0,8},{8,0},{16,24},{24,16},{1,9},{9,1},{17,25},{25,17},{2,10},{10... | collective-permute-start | bytes 4325384 | tf_op jit(solution)/shard_map/ppermute | solution.py:183
  1273.8 78.1 %collective-permute-start.25 = (bf16[256,2176]{1,0:T(8,128)(2,1)}, bf16[256,2176]{1,0:T(8,128)(2,1)}, u32[]{:S(2)}, u32[]{:S(2)}) collective-permute-start(bf16[256,2176]{1,0:T(8,128)(2,1)} %get-tuple-element.374), channel_id=1, source_target_pairs={{0,24},{8,16},{16,8},{24,0},{1,25},{9,17},{17,9},{25,1},{2,26},{10... | collective-permute-start | bytes 3342344 | tf_op jit(solution)/shard_map/ppermute | solution.py:183
  1275.3 135.2 %collective-permute-start.24 = (bf16[256,2176]{1,0:T(8,128)(2,1)}, bf16[256,2176]{1,0:T(8,128)(2,1)}, u32[]{:S(2)}, u32[]{:S(2)}) collective-permute-start(bf16[256,2176]{1,0:T(8,128)(2,1)} %get-tuple-element.375), channel_id=1, source_target_pairs={{0,16},{8,24},{16,0},{24,8},{1,17},{9,25},{17,1},{25,9},{2,18},{10... | collective-permute-start | bytes 3342344 | tf_op jit(solution)/shard_map/ppermute | solution.py:183
  1328.6 164.6 %collective-permute-start.26 = (bf16[352,2048]{1,0:T(8,128)(2,1)}, bf16[352,2048]{1,0:T(8,128)(2,1)}, u32[]{:S(2)}, u32[]{:S(2)}) collective-permute-start(bf16[352,2048]{1,0:T(8,128)(2,1)} %slice.466), channel_id=1, source_target_pairs={{0,8},{8,0},{16,24},{24,16},{1,9},{9,1},{17,25},{25,17},{2,10},{10... | collective-permute-start | bytes 4325384 | tf_op jit(solution)/shard_map/ppermute | solution.py:183
  1351.9 66.5 %collective-permute-start.30 = (bf16[352,2048]{1,0:T(8,128)(2,1)}, bf16[352,2048]{1,0:T(8,128)(2,1)S(1)}, u32[]{:S(2)}, u32[]{:S(2)}) collective-permute-start(bf16[352,2048]{1,0:T(8,128)(2,1)} %get-tuple-element.385), channel_id=1, source_target_pairs={{0,16},{8,24},{16,0},{24,8},{1,17},{9,25},{17,1},{25,9},{2,18},{10... | collective-permute-start | bytes 4325384 | tf_op jit(solution)/shard_map/ppermute | solution.py:183
  1416.4 117.5 %collective-permute-start.29 = (bf16[352,2048]{1,0:T(8,128)(2,1)}, bf16[352,2048]{1,0:T(8,128)(2,1)}, u32[]{:S(2)}, u32[]{:S(2)}) collective-permute-start(bf16[352,2048]{1,0:T(8,128)(2,1)} %add_convert_fusion.8), channel_id=1, source_target_pairs={{0,16},{8,24},{16,0},{24,8},{1,17},{9,25},{17,1},{25,9},{2,18},{10... | collective-permute-start | bytes 4325384 | tf_op jit(solution)/shard_map/ppermute | solution.py:183
  1420.0 113.9 %collective-permute-start.31 = (bf16[352,2048]{1,0:T(8,128)(2,1)}, bf16[352,2048]{1,0:T(8,128)(2,1)}, u32[]{:S(2)}, u32[]{:S(2)}) collective-permute-start(bf16[352,2048]{1,0:T(8,128)(2,1)} %add_convert_fusion.7), channel_id=1, source_target_pairs={{0,8},{8,0},{16,24},{24,16},{1,9},{9,1},{17,25},{25,17},{2,10},{10... | collective-permute-start | bytes 4325384 | tf_op jit(solution)/shard_map/ppermute | solution.py:183
  (249 other events, 4162.1 us)
Sparse Core Ops, SparseCore 0:
  28.1 51.4 all-gather.5
  81.8 103.3 all-gather.7
  189.4 101.1 all-gather.9
  417.0 82.1 all-gather.13
  500.6 80.5 all-gather.11
  843.2 86.4 reduce-scatter.5
  932.0 87.9 reduce-scatter.7
  1022.3 87.9 reduce-scatter.9
  1124.7 88.7 reduce-scatter.13
  1252.3 108.0 reduce-scatter.11

commit v3 on v2

--- a/solution.py
+++ b/solution.py
@@ -202,28 +202,23 @@
         return (a.astype(F32) + b.astype(F32)).astype(BF)
 
     def deliver_first(far):
-        half = far.shape[0] // 2
-        return [swap(far[:half], 1), swap(far[half:], 2)] if n_e == 4 else []
+        return [swap(far[0], 1), swap(far[1], 2)] if n_e == 4 else []
 
     def deliver_near(parts):
         if n_e != 4:
-            return [swap(parts[k], k) for k in range(1, n_e)]
-        half = parts[0].shape[0] // 2
-        return [swap(parts[1][:half], 1), swap(parts[2][half:], 2)]
+            return [swap(parts[k][i], k) for i in range(2) for k in range(1, n_e)]
+        return [swap(parts[1][0], 1), swap(parts[2][1], 2)]
 
     def deliver_last(parts, halves):
         if n_e != 4:
             return []
-        half = parts[0].shape[0] // 2
-        return [swap(add_low(parts[2][:half], halves[0]), 2), swap(add_low(parts[1][half:], halves[1]), 1)]
+        return [swap(add_low(parts[2][0], halves[0]), 2), swap(add_low(parts[1][1], halves[1]), 1)]
 
     def total(own, near, last):
-        own = own.astype(F32)
-        if n_e != 4:
-            return sum([own] + [v.astype(F32) for v in near])
-        half = own.shape[0] // 2
-        near, last = [v.astype(F32) for v in near], [v.astype(F32) for v in last]
-        return jnp.concatenate([own[:half] + near[0] + last[0], own[half:] + near[1] + last[1]], axis=0)
+        count = len(near) // 2
+        return [
+            sum(v.astype(F32) for v in [own[i]] + near[i * count:(i + 1) * count] + last[i:i + 1]) for i in range(2)
+        ]
 
     def collect(value):
         parts = jnp.split(value, n_e, axis=0)
@@ -231,6 +226,13 @@
 
     def shuffle(value, axis):
         return lax.all_to_all(value, axis, split_axis=0, concat_axis=0, tiled=True)
+
+    def trade(value):
+        out = jnp.zeros_like(value)
+        for k in range(n_e):
+            piece = lax.dynamic_index_in_dim(value, me ^ k, 0, False)
+            out = lax.dynamic_update_index_in_dim(out, swap(piece, k) if k else piece, me ^ k, 0)
+        return out
 
     def gather_shard(value):
         return lax.all_gather(value, "shard", axis=0, tiled=True)
@@ -272,15 +274,18 @@
 
     def from_heads(value):
         rows = value.shape[0]
-        value = shuffle(value.reshape(rows, n_e, group).transpose(1, 0, 2), "expert")
+        value = trade(value.reshape(rows, n_e, group).transpose(1, 0, 2))
         return value.transpose(1, 0, 2).reshape(rows, n_e * group)
 
     notes = jnp.concatenate([blocks[0][:, None], attn_routes[0]], axis=1).astype(BF)
     carried = jnp.concatenate([inputs[0], jnp.pad(notes, ((0, 0), (0, 128 - 1 - TOPK)))], axis=1)
-    carried = spread(carried)
-    query_w = gather_shard(to_heads(w_query[0]))
-    out_rows = w_out.shape[1]
-    turned = shuffle(after(w_out[0], carried).T, "shard").reshape(n_s, width // n_s, out_rows).transpose(1, 0, 2)
+    carried = [carried] + [swap(carried, k) for k in range(1, n_e)]
+    query_w = to_heads(w_query[0])
+    out_w, query_w, carried[1] = lax.optimization_barrier((w_out[0], query_w, carried[1]))
+    carried = jnp.concatenate(carried, axis=0)
+    query_w = gather_shard(query_w)
+    out_rows = out_w.shape[0]
+    turned = shuffle(out_w.T, "shard").reshape(n_s, width // n_s, out_rows).transpose(1, 0, 2)
     out_wt = gather_shard(to_heads(turned.reshape(width // n_s, n_s * out_rows)))
 
     hidden_units = w_down.shape[1]
@@ -337,35 +342,35 @@
         if k == 1:
             gate_up_w = fetch_rest(gate_up_w, hiddens[0])
         expert = me ^ k
-        gate_w, up_w = gate_up_w[k][:hidden_units], gate_up_w[k][hidden_units:]
         named = [routes_blocks[:, :, j] == expert for j in range(TOPK)]
         any_named = named[0] | named[1]
         rank = dot(any_named.astype(BF), triangle).astype(jnp.int32) - 1
         hit = (rank[:, None, :] == jnp.arange(capacity, dtype=jnp.int32)[None, :, None]) & any_named[:, None, :]
         select = hit.astype(BF)
         gate_token = sum(jnp.where(named[j], gates_f[j].reshape(n_s, tokens), 0.0) for j in range(TOPK))
-        gate_slot = jnp.sum(jnp.where(hit, gate_token[:, None, :], 0.0), axis=2).reshape(-1, 1)
+        gate_slot = jnp.sum(jnp.where(hit, gate_token[:, None, :], 0.0), axis=2).reshape(1, -1)
         rows = rows_of(select, h_blocks)
-        gate_pre, up_pre = dot_nt(rows, gate_w), dot_nt(rows, up_w)
+        pre = dot_nt(gate_up_w[k], rows)
         if k == 0:
-            cot_blocks = after(cot_all, gate_pre, up_pre).reshape(n_s, tokens, width)
+            cot_blocks = after(cot_all, pre).reshape(n_s, tokens, width)
+        gate_pre, up_pre = pre[:hidden_units], pre[hidden_units:]
         cot_rows = rows_of(select, cot_blocks)
-        grad_hidden = dot_nt(cot_rows, down_w[k])
+        grad_hidden = dot_nt(down_w[k], cot_rows)
         sigma = 1.0 / (1.0 + jnp.exp(-gate_pre))
         silu = gate_pre * sigma
         hidden = silu * up_pre
-        grad_slot = jnp.sum(grad_hidden * hidden, axis=1).reshape(n_s, capacity)
+        grad_slot = jnp.sum(grad_hidden * hidden, axis=0).reshape(n_s, capacity)
         grad_hidden = grad_hidden * gate_slot
         hidden = (hidden * gate_slot).astype(BF)
         grad_gate = (grad_hidden * up_pre * sigma * (1.0 + gate_pre * (1.0 - sigma))).astype(BF)
-        grad_up = (grad_hidden * silu).astype(BF)
-        back = (dot(grad_gate, gate_w) + dot(grad_up, up_w)).astype(BF)
+        grad_pre = jnp.concatenate([grad_gate, (grad_hidden * silu).astype(BF)], axis=0)
+        back = dot_tn(grad_pre, gate_up_w[k]).astype(BF)
         selects.append(select)
         back_rows_f.append(back.reshape(n_s, capacity, width))
         hiddens.append(hidden)
         grad_token = jnp.sum(jnp.where(hit, grad_slot[:, :, None], 0.0), axis=1)
         grad_gate_f = [grad_gate_f[j] + jnp.where(named[j], grad_token, 0.0) for j in range(TOPK)]
-        grad_pieces.append((rows, cot_rows, grad_gate, grad_up))
+        grad_pieces.append((rows, cot_rows, grad_pre))
     select = jnp.concatenate(selects, axis=1)
 
     def tokens_of(row_list):
@@ -377,17 +382,17 @@
     back_f = scatter_shard(back_sum)
 
     def gate_up_grads(k, *others):
-        rows, _, grad_gate, grad_up = grad_pieces[k]
+        rows, _, grad_pre = grad_pieces[k]
         rows = after(rows, *others)
-        return jnp.concatenate([dot_tn(grad_gate, rows).astype(BF), dot_tn(grad_up, rows).astype(BF)], axis=0)
+        return [dot(v, rows).astype(BF) for v in jnp.split(grad_pre, 2, axis=0)]
 
     grad_gate_up = [None] * n_e
     grad_gate_up[n_e - 1] = gate_up_grads(n_e - 1, back_sum)
     halves = deliver_first(grad_gate_up[n_e - 1])
     out_rows_f = []
     for k in range(n_e):
-        hidden = after(hiddens[k], grad_gate_up[n_e - 1])
-        out_rows_f.append(dot(hidden, down_w[k]).astype(BF).reshape(n_s, capacity, width))
+        hidden = after(hiddens[k], *grad_gate_up[n_e - 1])
+        out_rows_f.append(dot_tn(hidden, down_w[k]).astype(BF).reshape(n_s, capacity, width))
     out_sum = tokens_of(out_rows_f)
     ffn_out = scatter_shard(out_sum)
     back_f, out_sum, *halves = lax.optimization_barrier((back_f, out_sum, *halves))
@@ -417,7 +422,7 @@
     for k in range(n_e - 1):
         grad_gate_up[k] = gate_up_grads(k, back_f)
     seq_grad = spread(grad_middle_low)
-    seq_grad, *grad_gate_up = lax.optimization_barrier((seq_grad, *grad_gate_up))
+    seq_grad, grad_gate_up = lax.optimization_barrier((seq_grad, grad_gate_up))
     near = deliver_near(grad_gate_up)
     last = deliver_last(grad_gate_up, halves)
     grad_mixed = pick(dot(seq_grad, out_wt), routes_a, ids)
@@ -436,33 +441,44 @@
     back_a = jnp.concatenate(
         [back_a, jnp.pad(jnp.concatenate([gate_grads_high, gate_grads_low], axis=1), ((0, 0), (0, 128 - 2 * TOPK)))], axis=1
     )
+    value = scatter_shard(grad_out_wt)
     back_a, ffn_out, *last = lax.optimization_barrier((back_a, ffn_out, *last))
-    value = total(grad_gate_up[0], near, last).astype(BF).reshape(2 * hidden_units, n_s, width // n_s).transpose(1, 0, 2)
-    gate_up_turned = shuffle(value, "shard").reshape(n_s, 2, hidden_units, width // n_s)
+    gate_up_total = [v.astype(BF) for v in total(grad_gate_up[0], near, last)]
     outputs = (middle + ffn_out.astype(F32) + bias_f).astype(BF)[None]
-    grad_down = [dot_tn(after(hiddens[k], back_a), grad_pieces[k][1]).astype(BF) for k in range(n_e)]
-    halves = deliver_first(grad_down[n_e - 1])
-    value = scatter_shard(grad_out_wt)
-    value, key_value_grad = lax.optimization_barrier((value, dot_tn(h_attn, grad_key_value).astype(BF)))
-    value = from_heads(value).reshape(width // n_s, n_s, out_rows).transpose(1, 0, 2)
-    grad_out_w = shuffle(value, "shard").reshape(width, out_rows)
+    key_value_grad = after(dot_tn(h_attn, grad_key_value).astype(BF), back_a)
     key_value_grad = key_value_grad.reshape(n_e, n_s, small_rows, 2 * group).transpose(1, 0, 2, 3)
     key_value_grad = scatter_shard(key_value_grad.reshape(n_s * n_e * small_rows, 2 * group))
-    key_value_grad = shuffle(key_value_grad.reshape(n_e, small_rows, -1), "expert")
+    query_grad = dot_tn(h_attn, grad_query_all).astype(BF)
+    query_grad, value = lax.optimization_barrier((query_grad, value))
+    query_grad = scatter_shard(query_grad)
+    value = from_heads(value).reshape(width // n_s, n_s, out_rows).transpose(1, 0, 2)
+
+    def to_rows(value):
+        value = shuffle(value.reshape(hidden_units, n_s, width // n_s).transpose(1, 0, 2), "shard")
+        return value.reshape(n_s * hidden_units, width // n_s)
+
+    gate_turned = to_rows(gate_up_total[0])
+    grad_down = []
+    for k in range(n_e):
+        hidden = after(hiddens[k], back_a)
+        grad_down.append([dot(v, grad_pieces[k][1]).astype(BF) for v in jnp.split(hidden, 2, axis=0)])
+    halves = deliver_first(grad_down[n_e - 1])
     back_a = collect(back_a)
     near, last = deliver_near(grad_down), deliver_last(grad_down, halves)
-    back_a, grad_out_w, key_value_grad, *near = lax.optimization_barrier((back_a, grad_out_w, key_value_grad, *near))
-    grad_down_w = total(grad_down[0], near, last)[None]
-    grad_out_w = grad_out_w.T.astype(F32)[None]
+    back_a, gate_turned, *near = lax.optimization_barrier((back_a, gate_turned, *near))
+    up_total, key_value_grad = lax.optimization_barrier((after(gate_up_total[1], gate_turned), key_value_grad))
+    up_turned = to_rows(up_total)
+    grad_out_w = shuffle(after(value, gate_turned), "shard").reshape(width, out_rows).T.astype(F32)[None]
+    grad_down_w = jnp.concatenate(total(grad_down[0], near, last), axis=0)[None]
+    key_value_grad = trade(key_value_grad.reshape(n_e, small_rows, -1))
     grad_key_w = key_value_grad[:, :, :group].transpose(1, 0, 2).reshape(small_rows, -1).astype(F32)
     grad_value_w = key_value_grad[:, :, group:].transpose(1, 0, 2).reshape(small_rows, -1).astype(F32)
     gate_grads = back_a[:, width:width + TOPK] + back_a[:, width + TOPK:width + 2 * TOPK]
     grad_gates_a = [gate_grads[:, j:j + 1] for j in range(TOPK)]
     back_a = back_a[:, :width]
-    value = after(scatter_shard(dot_tn(h_attn, grad_query_all).astype(BF)), gate_up_turned)
-    grad_query_w = from_heads(value).astype(F32)[None]
-    grad_gate_w = gate_up_turned[:, 0].reshape(n_s * hidden_units, -1).T.astype(F32)[None]
-    grad_up_w = gate_up_turned[:, 1].reshape(n_s * hidden_units, -1).T.astype(F32)[None]
+    grad_query_w = from_heads(query_grad).astype(F32)[None]
+    grad_gate_w = gate_turned.T.astype(F32)[None]
+    grad_up_w = up_turned.T.astype(F32)[None]
 
     h_own = h_attn[:tokens]
     own_routes_a = attn_routes[0]

time: 1560 us -> 1460 us (0.936)
  waiting for transfers between devices: 444 us -> 404 us
  matrix products: 455 us -> 419 us
  blocking collectives: 98.8 us -> 66 us
  starting transfers between devices: 80 us -> 96.1 us
    all_to_all x3 -> x2, blocking collectives: 98.8 us -> 66 us  [shuffle(): return lax.all_to_all(value, axis, split_axis=0, concat_axis=0, tiled=True)]
    dot_general x22 -> x26, matrix products: 151 us -> 120 us  [dot(): return jnp.dot(a, b, preferred_element_type=F32)]
    all_to_all x9 -> x8, waiting for transfers between devices: 92.3 us -> 62.2 us  [shuffle(): return lax.all_to_all(value, axis, split_axis=0, concat_axis=0, tiled=True)]
    slice x6 -> x0, local copies, waits for them, and re-layouts: 16.6 us -> none  [the longest x4 10.1 us: deliver_near(): return [swap(parts[1][:half], 1), swap(parts[2][half:], 2)]]
    convert_element_type x6 -> x8, other arithmetic: 23.7 us -> 37.7 us  [the longest x4 25.9 us: local(): (grad_hidden * up_pre * sigma * (1.0 + gate_pre * (1.0 - sigma))).astype(BF)]
    dot_general x15 -> x11, matrix products: 123 us -> 111 us  [dot_nt(): lax.dot_general(a, b, (((1,), (1,)), ((), ())), preferred_element_type=F32)]
    ppermute x32 -> x41, starting transfers between devices: 38.1 us -> 48.4 us  [swap(): return lax.ppermute(value, 'expert', [(i, i ^ k) for i in range(n_e)])]
    dot_general x17 -> x13, matrix products: 105 us -> 114 us  [dot_tn(): lax.dot_general(a, b, (((0,), (0,)), ((), ())), precision=precision, pref...]
  transfers between devices with their start and end apart: 51 -> 59, of which waited for: 22 -> 21; matrix products, arithmetic and copies ran while one was open for 48% -> 46% of each run, Pallas kernels for 4% -> 5%
where the time goes in v3:
time: 1460 us
  matrix products  419 us (29%)
  waiting for transfers between devices  404 us (28%)
  local copies, waits for them, and re-layouts  197 us (13%)
  other arithmetic  187 us (13%)
  starting transfers between devices  96.1 us (7%)
  Pallas kernels  69.2 us (5%)
  blocking collectives  66 us (5%)
  between operations  17.6 us (1%)
    ppermute x41, waiting for transfers between devices, swap(): return lax.ppermute(value, 'expert', [(i, i ^ k) for i in range(n_e)])  207 us
    all_gather x5, waiting for transfers between devices, gather_shard(): return lax.all_gather(value, 'shard', axis=0, tiled=True)  134 us
    dot_general x26, matrix products, dot(): return jnp.dot(a, b, preferred_element_type=F32)  120 us
    dot_general x13, matrix products, dot_tn(): lax.dot_general(a, b, (((0,), (0,)), ((), ())), precision=precision, pref...  114 us
    dot_general x11, matrix products, dot_nt(): lax.dot_general(a, b, (((1,), (1,)), ((), ())), preferred_element_type=F32)  111 us
    all_to_all x2, blocking collectives, shuffle(): return lax.all_to_all(value, axis, split_axis=0, concat_axis=0, tiled=True)  66 us
    all_to_all x8, waiting for transfers between devices, shuffle(): return lax.all_to_all(value, axis, split_axis=0, concat_axis=0, tiled=True)  62.2 us
    unnamed x429, local copies, waits for them, and re-layouts  54.6 us
  transfers between devices with their start and end apart: 59, of which 21 were waited for; matrix products, arithmetic and copies ran while one was open for 46% of the time, Pallas kernels for 5%

profile of v3, /device:TPU:0, one launch (start us, length us, event | category | flops | bytes accessed | tf_op | source)
XLA Modules:
  0.0 1455.9 jit_solution(7694469938695195803)
XLA Ops:
  40.0 26.9 %all-to-all-done = bf16[4,256,512]{2,1,0:T(8,128)(2,1)} async-done(((bf16[4,256,512]{2,1,0:T(8,128)(2,1)}), bf16[4,256,512]{2,1,0:T(8,128)(2,1)}, u32[]{:S(2)}, u32[]{:S(2)}) %all-to-all-start) | async-done | bytes 1048608 | tf_op jit(solution)/shard_map/all_to_all | solution.py:228
  69.2 48.9 %all_to_all.63 = bf16[8,256,256]{2,1,0:T(8,128)(2,1)} all-to-all(bf16[8,256,256]{2,1,0:T(8,128)(2,1)S(1)} %bitcast.487), channel_id=1, replica_groups=mesh['expert'=4,'shard'=8] {'shard'}, dimensions={0} | all-to-all | bytes 2097152 | tf_op jit(solution)/shard_map/all_to_all | solution.py:228
  119.6 17.1 %all_to_all.64 = bf16[4,256,512]{1,2,0:T(8,128)(2,1)} all-to-all(bf16[4,256,512]{1,2,0:T(8,128)(2,1)S(1)} %bitcast.489), channel_id=1, replica_groups=mesh['expert'=4,'shard'=8] {'expert'}, dimensions={0} | all-to-all | bytes 2097152 | tf_op jit(solution)/shard_map/all_to_all | solution.py:228
  159.3 28.0 %collective-permute-done.1 = bf16[256,2176]{1,0:T(8,128)(2,1)S(1)} collective-permute-done((bf16[256,2176]{1,0:T(8,128)(2,1)}, bf16[256,2176]{1,0:T(8,128)(2,1)S(1)}, u32[]{:S(2)}, u32[]{:S(2)}) %collective-permute-start.1) | collective-permute-done | bytes 1114144 | tf_op jit(solution)/shard_map/ppermute | solution.py:183
  200.2 16.7 %fusion.19 = bf16[1024,2048]{1,0:T(8,128)(2,1)S(1)} fusion(f32[2048]{0:T(1024)S(1)} %get-tuple-element.288, f32[1024]{0:T(1024)S(1)} %add_rsqrt_fusion, bf16[256,2176]{1,0:T(8,128)(2,1)} %collective-permute-done.2, bf16[256,2176]{1,0:T(8,128)(2,1)S(1)} %collective-permute-done.1, bf16[256,2176]{1,0:T(8,128)(2,1)S(1)} %collective-permute-done, ...), kind=kLoop, calls=%fused_computation.22 | loop fusion | flops 27262976 | bytes 8663040 | tf_op jit(solution)/shard_map/convert_element_type | solution.py:304
  236.5 15.6 %all-to-all-start.4 = ((bf16[8,2,704,256]{3,2,1,0:T(8,128)(2,1)}), bf16[8,2,704,256]{3,2,1,0:T(8,128)(2,1)}, u32[]{:S(2)}, u32[]{:S(2)}) async-start(bf16[8,2,704,256]{3,2,1,0:T(8,128)(2,1)} %copy.643), calls=%async_computation.4 | async-start | bytes 11534336 | tf_op jit(solution)/shard_map/all_to_all | solution.py:228
  252.2 12.6 fusion.185
  304.5 29.7 %attend.1 = (bf16[2048,512]{1,0:T(8,128)(2,1)}, f32[4,1,2048]{2,1,0:T(1,128)}) custom-call(bf16[2048,512]{1,0:T(8,128)(2,1)} %pad_maximum_fusion.9.q_ref, bf16[1024,512]{1,0:T(8,128)(2,1)} %get-tuple-element.405.k_ref, bf16[1024,512]{1,0:T(8,128)(2,1)} %slice.560.v_ref, s32[1,1,2048]{2,1,0:T(1,128)} %bitcast.508, s32[1024,1]{1,0:T(8,128)} %get-tuple-element.435.kb_ref), custom_call_target="tpu_custom_call" | custom-call | flops 2097152 | bytes 4194304 | tf_op jit(solution)/shard_map/attend/pallas_call | solution.py:74
  346.8 12.5 convolution_convert_fusion.18
  363.2 22.5 %collective-permute-done.7 = bf16[256,2048]{1,0:T(8,128)(2,1)S(1)} collective-permute-done((bf16[256,2048]{1,0:T(8,128)(2,1)S(1)}, bf16[256,2048]{1,0:T(8,128)(2,1)S(1)}, u32[]{:S(2)}, u32[]{:S(2)}) %collective-permute-start.7) | collective-permute-done | bytes 1048608 | tf_op jit(solution)/shard_map/ppermute | solution.py:183
  385.8 22.2 %collective-permute-done.8 = bf16[256,2048]{1,0:T(8,128)(2,1)S(1)} collective-permute-done((bf16[256,2048]{1,0:T(8,128)(2,1)S(1)}, bf16[256,2048]{1,0:T(8,128)(2,1)S(1)}, u32[]{:S(2)}, u32[]{:S(2)}) %collective-permute-start.8) | collective-permute-done | bytes 1048608 | tf_op jit(solution)/shard_map/ppermute | solution.py:183
  425.2 77.6 %all-gather.14.cloned.1.call-done = bf16[2048,2048]{1,0:T(8,128)(2,1)} async-done(((bf16[256,2048]{1,0:T(8,128)(2,1)}), bf16[2048,2048]{1,0:T(8,128)(2,1)}) %all-gather.14.cloned.1.call-update) | async-done | bytes 8388624 | tf_op jit(solution)/shard_map/all_gather | solution.py:238
  517.8 10.6 fusion.186
  528.4 56.4 %all-gather.12.cloned.1.call-done = bf16[2048,2048]{1,0:T(8,128)(2,1)} async-done(((bf16[256,2048]{1,0:T(8,128)(2,1)}), bf16[2048,2048]{1,0:T(8,128)(2,1)}) %all-gather.12.cloned.1.call-update) | async-done | bytes 8388624 | tf_op jit(solution)/shard_map/all_gather | solution.py:238
  611.6 12.2 fusion.187
  650.9 12.2 fusion.188
  696.6 13.2 convolution_convert_fusion.9
  722.6 13.0 convolution_convert_fusion.8
  743.6 14.4 convolution_convert_fusion.7
  799.8 13.8 fusion.23
  858.6 13.9 fusion.20
  894.7 41.9 %collective-permute-done.15 = bf16[704,2048]{1,0:T(8,128)(2,1)} collective-permute-done((bf16[704,2048]{1,0:T(8,128)(2,1)}, bf16[704,2048]{1,0:T(8,128)(2,1)}, u32[]{:S(2)}, u32[]{:S(2)}) %collective-permute-start.15) | collective-permute-done | bytes 2883616 | tf_op jit(solution)/shard_map/ppermute | solution.py:183
  979.1 11.9 collective-permute-done.17
  1008.6 12.0 convolution_convert_fusion.1
  1035.2 39.5 %attend_back.1 = (f32[2048,512]{1,0:T(8,128)}, f32[1024,512]{1,0:T(8,128)}, f32[1024,512]{1,0:T(8,128)}) custom-call(bf16[2048,512]{1,0:T(8,128)(2,1)} %pad_maximum_fusion.9.q_ref, bf16[1024,512]{1,0:T(8,128)(2,1)} %get-tuple-element.405.k_ref, bf16[1024,512]{1,0:T(8,128)(2,1)} %slice.560.v_ref, bf16[2048,512]{1,0:T(8,128)(2,1)} %pad_maximum_fusion.10.d_ref, ...), custom_call_target="tpu_custom_call" | custom-call | flops 2097152 | bytes 4194304 | tf_op jit(solution)/shard_map/attend_back/pallas_call | solution.py:129
  1114.2 14.3 add_convert_fusion
  1130.9 13.7 collective-permute-done.22
  1155.8 13.4 convolution_convert_fusion
  1223.3 12.9 collective-permute-done.23
  1237.9 25.4 %collective-permute-done.24 = bf16[256,2176]{1,0:T(8,128)(2,1)S(1)} collective-permute-done((bf16[256,2176]{1,0:T(8,128)(2,1)S(1)}, bf16[256,2176]{1,0:T(8,128)(2,1)S(1)}, u32[]{:S(2)}, u32[]{:S(2)}) %collective-permute-start.24) | collective-permute-done | bytes 1114144 | tf_op jit(solution)/shard_map/ppermute | solution.py:183
  1271.7 14.9 %collective-permute-done.26 = bf16[352,2048]{1,0:T(8,128)(2,1)} collective-permute-done((bf16[352,2048]{1,0:T(8,128)(2,1)S(1)}, bf16[352,2048]{1,0:T(8,128)(2,1)}, u32[]{:S(2)}, u32[]{:S(2)}) %collective-permute-start.26) | collective-permute-done | bytes 1441824 | tf_op jit(solution)/shard_map/ppermute | solution.py:183
  1286.6 14.2 all-to-all-done.6
  (825 shorter events, 734.3 us)
Async XLA Ops:
  17.5 177.5 %all-gather.6.cloned.1.call-start = ((), (), s32[]{:S(2)}) async-start(), calls=%async_computation.15 | async-start | bytes 5308416 | tf_op jit(solution)/shard_map/all_gather | solution.py:238
  38.4 192.4 %all-gather.8.cloned.1.call-start = ((), (), s32[]{:S(2)}) async-start(), calls=%async_computation.16 | async-start | bytes 9437184 | tf_op jit(solution)/shard_map/all_gather | solution.py:238
  69.2 277.7 %all-gather.10.cloned.1.call-start = ((), (), s32[]{:S(2)}) async-start(), calls=%async_computation.17 | async-start | bytes 9437184 | tf_op jit(solution)/shard_map/all_gather | solution.py:238
  136.7 50.5 %collective-permute-start.1 = (bf16[256,2176]{1,0:T(8,128)(2,1)}, bf16[256,2176]{1,0:T(8,128)(2,1)S(1)}, u32[]{:S(2)}, u32[]{:S(2)}) collective-permute-start(bf16[256,2176]{1,0:T(8,128)(2,1)} %pad_maximum_fusion.14), channel_id=1, source_target_pairs={{0,16},{8,24},{16,0},{24,8},{1,17},{9,25},{17,1},{25,9},{2,18},{10... | collective-permute-start | bytes 3342344 | tf_op jit(solution)/shard_map/ppermute | solution.py:183
  139.2 156.5 %collective-permute-start.3 = (bf16[704,2048]{1,0:T(8,128)(2,1)}, bf16[704,2048]{1,0:T(8,128)(2,1)}, u32[]{:S(2)}, u32[]{:S(2)}) collective-permute-start(bf16[704,2048]{1,0:T(8,128)(2,1)} %bitcast.527), channel_id=1, source_target_pairs={{0,8},{8,0},{16,24},{24,16},{1,9},{9,1},{17,25},{25,17},{2,10},{10... | collective-permute-start | bytes 8650760 | tf_op jit(solution)/shard_map/ppermute | solution.py:183
  140.3 155.4 %collective-permute-start.4 = (bf16[704,2048]{1,0:T(8,128)(2,1)}, bf16[704,2048]{1,0:T(8,128)(2,1)}, u32[]{:S(2)}, u32[]{:S(2)}) collective-permute-start(bf16[704,2048]{1,0:T(8,128)(2,1)} %bitcast.528), channel_id=1, source_target_pairs={{0,16},{8,24},{16,0},{24,8},{1,17},{9,25},{17,1},{25,9},{2,18},{10... | collective-permute-start | bytes 8650760 | tf_op jit(solution)/shard_map/ppermute | solution.py:183
  236.5 175.8 %all-to-all-start.4 = ((bf16[8,2,704,256]{3,2,1,0:T(8,128)(2,1)}), bf16[8,2,704,256]{3,2,1,0:T(8,128)(2,1)}, u32[]{:S(2)}, u32[]{:S(2)}) async-start(bf16[8,2,704,256]{3,2,1,0:T(8,128)(2,1)} %copy.643), calls=%async_computation.4 | async-start | bytes 11534336 | tf_op jit(solution)/shard_map/all_to_all | solution.py:228
  252.1 250.7 %all-gather.14.cloned.1.call-start = ((), (), s32[]{:S(2)}) async-start(), calls=%async_computation.19 | async-start | bytes 9437184 | tf_op jit(solution)/shard_map/all_gather | solution.py:238
  420.5 164.3 %all-gather.12.cloned.1.call-start = ((), (), s32[]{:S(2)}) async-start(), calls=%async_computation.18 | async-start | bytes 9437184 | tf_op jit(solution)/shard_map/all_gather | solution.py:238
  421.1 516.8 %reduce-scatter.6.cloned.1.call-start = ((), (), s32[]{:S(2)}) async-start(), calls=%async_computation.20 | async-start | bytes 9437184 | tf_op jit(solution)/shard_map/reduce_scatter | solution.py:241
  423.4 188.2 %collective-permute-start.10 = (bf16[1408,2048]{0,1:T(8,128)(2,1)}, bf16[1408,2048]{0,1:T(8,128)(2,1)}, u32[]{:S(2)}, u32[]{:S(2)}) collective-permute-start(bf16[1408,2048]{0,1:T(8,128)(2,1)} %bitcast.475), channel_id=1, source_target_pairs={{0,8},{8,0},{16,24},{24,16},{1,9},{9,1},{17,25},{25,17},{2,10},{10... | collective-permute-start | bytes 17301512 | tf_op jit(solution)/shard_map/ppermute | solution.py:183
  424.4 226.6 %collective-permute-start.11 = (bf16[1408,2048]{0,1:T(8,128)(2,1)}, bf16[1408,2048]{0,1:T(8,128)(2,1)}, u32[]{:S(2)}, u32[]{:S(2)}) collective-permute-start(bf16[1408,2048]{0,1:T(8,128)(2,1)} %bitcast.476), channel_id=1, source_target_pairs={{0,16},{8,24},{16,0},{24,8},{1,17},{9,25},{17,1},{25,9},{2,18},{10... | collective-permute-start | bytes 17301512 | tf_op jit(solution)/shard_map/ppermute | solution.py:183
  688.8 71.3 %collective-permute-start.13 = (bf16[704,2048]{1,0:T(8,128)(2,1)}, bf16[704,2048]{1,0:T(8,128)(2,1)}, u32[]{:S(2)}, u32[]{:S(2)}) collective-permute-start(bf16[704,2048]{1,0:T(8,128)(2,1)} %copy.654), channel_id=1, source_target_pairs={{0,8},{8,0},{16,24},{24,16},{1,9},{9,1},{17,25},{25,17},{2,10},{10... | collective-permute-start | bytes 8650760 | tf_op jit(solution)/shard_map/ppermute | solution.py:183
  695.2 64.5 %collective-permute-start.12 = (bf16[704,2048]{1,0:T(8,128)(2,1)}, bf16[704,2048]{1,0:T(8,128)(2,1)S(1)}, u32[]{:S(2)}, u32[]{:S(2)}) collective-permute-start(bf16[704,2048]{1,0:T(8,128)(2,1)} %copy.653), channel_id=1, source_target_pairs={{0,16},{8,24},{16,0},{24,8},{1,17},{9,25},{17,1},{25,9},{2,18},{10... | collective-permute-start | bytes 8650760 | tf_op jit(solution)/shard_map/ppermute | solution.py:183
  813.6 317.3 %reduce-scatter.8.cloned.1.call-start = ((), (), s32[]{:S(2)}) async-start(), calls=%async_computation.21 | async-start | bytes 9437184 | tf_op jit(solution)/shard_map/reduce_scatter | solution.py:241
  872.7 63.8 %collective-permute-start.15 = (bf16[704,2048]{1,0:T(8,128)(2,1)}, bf16[704,2048]{1,0:T(8,128)(2,1)}, u32[]{:S(2)}, u32[]{:S(2)}) collective-permute-start(bf16[704,2048]{1,0:T(8,128)(2,1)} %convolution_convert_fusion.26), channel_id=1, source_target_pairs={{0,16},{8,24},{16,0},{24,8},{1,17},{9,25},{17,1},{25,9},{2,18},{10... | collective-permute-start | bytes 8650760 | tf_op jit(solution)/shard_map/ppermute | solution.py:183
  874.3 63.6 %collective-permute-start.14 = (bf16[704,2048]{1,0:T(8,128)(2,1)}, bf16[704,2048]{1,0:T(8,128)(2,1)}, u32[]{:S(2)}, u32[]{:S(2)}) collective-permute-start(bf16[704,2048]{1,0:T(8,128)(2,1)} %convolution_convert_fusion.27), channel_id=1, source_target_pairs={{0,8},{8,0},{16,24},{24,16},{1,9},{9,1},{17,25},{25,17},{2,10},{10... | collective-permute-start | bytes 8650760 | tf_op jit(solution)/shard_map/ppermute | solution.py:183
  879.4 289.8 %reduce-scatter.12.cloned.1.call-start = ((), (), s32[]{:S(2)}) async-start(), calls=%async_computation.23 | async-start | bytes 9437184 | tf_op jit(solution)/shard_map/reduce_scatter | solution.py:241
  1020.7 315.1 %reduce-scatter.10.cloned.1.call-start = ((), (), s32[]{:S(2)}) async-start(), calls=%async_computation.22 | async-start | bytes 4718592 | tf_op jit(solution)/shard_map/reduce_scatter | solution.py:241
  1020.7 68.0 %collective-permute-start.19 = (bf16[704,2048]{1,0:T(8,128)(2,1)}, bf16[704,2048]{1,0:T(8,128)(2,1)}, u32[]{:S(2)}, u32[]{:S(2)}) collective-permute-start(bf16[704,2048]{1,0:T(8,128)(2,1)} %convolution_convert_fusion.23), channel_id=1, source_target_pairs={{0,8},{8,0},{16,24},{24,16},{1,9},{9,1},{17,25},{25,17},{2,10},{10... | collective-permute-start | bytes 8650760 | tf_op jit(solution)/shard_map/ppermute | solution.py:183
  1022.4 66.3 %collective-permute-start.20 = (bf16[704,2048]{1,0:T(8,128)(2,1)}, bf16[704,2048]{1,0:T(8,128)(2,1)}, u32[]{:S(2)}, u32[]{:S(2)}) collective-permute-start(bf16[704,2048]{1,0:T(8,128)(2,1)} %convolution_convert_fusion.20), channel_id=1, source_target_pairs={{0,16},{8,24},{16,0},{24,8},{1,17},{9,25},{17,1},{25,9},{2,18},{10... | collective-permute-start | bytes 8650760 | tf_op jit(solution)/shard_map/ppermute | solution.py:183
  1029.4 115.3 %collective-permute-start.22 = (bf16[704,2048]{1,0:T(8,128)(2,1)}, bf16[704,2048]{1,0:T(8,128)(2,1)}, u32[]{:S(2)}, u32[]{:S(2)}) collective-permute-start(bf16[704,2048]{1,0:T(8,128)(2,1)} %add_convert_fusion.3), channel_id=1, source_target_pairs={{0,8},{8,0},{16,24},{24,16},{1,9},{9,1},{17,25},{25,17},{2,10},{10... | collective-permute-start | bytes 8650760 | tf_op jit(solution)/shard_map/ppermute | solution.py:183
  1034.6 110.1 %collective-permute-start.21 = (bf16[704,2048]{1,0:T(8,128)(2,1)}, bf16[704,2048]{1,0:T(8,128)(2,1)}, u32[]{:S(2)}, u32[]{:S(2)}) collective-permute-start(bf16[704,2048]{1,0:T(8,128)(2,1)} %add_convert_fusion.4), channel_id=1, source_target_pairs={{0,16},{8,24},{16,0},{24,8},{1,17},{9,25},{17,1},{25,9},{2,18},{10... | collective-permute-start | bytes 8650760 | tf_op jit(solution)/shard_map/ppermute | solution.py:183
  1154.2 261.7 %reduce-scatter.14.cloned.1.call-start = ((), (), s32[]{:S(2)}) async-start(), calls=%async_computation.24 | async-start | bytes 9437184 | tf_op jit(solution)/shard_map/reduce_scatter | solution.py:241
  1177.7 89.3 %collective-permute-start.37 = (bf16[352,2048]{1,0:T(8,128)(2,1)}, bf16[352,2048]{1,0:T(8,128)(2,1)}, u32[]{:S(2)}, u32[]{:S(2)}) collective-permute-start(bf16[352,2048]{1,0:T(8,128)(2,1)} %convolution_convert_fusion.31), channel_id=1, source_target_pairs={{0,8},{8,0},{16,24},{24,16},{1,9},{9,1},{17,25},{25,17},{2,10},{10... | collective-permute-start | bytes 4325384 | tf_op jit(solution)/shard_map/ppermute | solution.py:183
  1182.5 89.2 %collective-permute-start.27 = (bf16[352,2048]{1,0:T(8,128)(2,1)}, bf16[352,2048]{1,0:T(8,128)(2,1)}, u32[]{:S(2)}, u32[]{:S(2)}) collective-permute-start(bf16[352,2048]{1,0:T(8,128)(2,1)} %convolution_convert_fusion.34), channel_id=1, source_target_pairs={{0,16},{8,24},{16,0},{24,8},{1,17},{9,25},{17,1},{25,9},{2,18},{10... | collective-permute-start | bytes 4325384 | tf_op jit(solution)/shard_map/ppermute | solution.py:183
  1190.5 110.3 %all-to-all-start.6 = ((bf16[8,704,256]{2,1,0:T(8,128)(2,1)}), bf16[8,704,256]{2,1,0:T(8,128)(2,1)}, u32[]{:S(2)}, u32[]{:S(2)}) async-start(bf16[8,704,256]{2,1,0:T(8,128)(2,1)} %bitcast.384), calls=%async_computation.8 | async-start | bytes 5767168 | tf_op jit(solution)/shard_map/all_to_all | solution.py:228
  1197.9 65.4 %collective-permute-start.24 = (bf16[256,2176]{1,0:T(8,128)(2,1)S(1)}, bf16[256,2176]{1,0:T(8,128)(2,1)S(1)}, u32[]{:S(2)}, u32[]{:S(2)}) collective-permute-start(bf16[256,2176]{1,0:T(8,128)(2,1)S(1)} %get-tuple-element.385), channel_id=1, source_target_pairs={{0,16},{8,24},{16,0},{24,8},{1,17},{9,25},{17,1},{25,9},{2,18},{10... | collective-permute-start | bytes 3342344 | tf_op jit(solution)/shard_map/ppermute | solution.py:183
  1198.6 66.7 %collective-permute-start.25 = (bf16[256,2176]{1,0:T(8,128)(2,1)S(1)}, bf16[256,2176]{1,0:T(8,128)(2,1)S(1)}, u32[]{:S(2)}, u32[]{:S(2)}) collective-permute-start(bf16[256,2176]{1,0:T(8,128)(2,1)S(1)} %get-tuple-element.384), channel_id=1, source_target_pairs={{0,24},{8,16},{16,8},{24,0},{1,25},{9,17},{17,9},{25,1},{2,26},{10... | collective-permute-start | bytes 3342344 | tf_op jit(solution)/shard_map/ppermute | solution.py:183
  1263.4 64.3 %collective-permute-start.39 = (bf16[352,2048]{1,0:T(8,128)(2,1)}, bf16[352,2048]{1,0:T(8,128)(2,1)}, u32[]{:S(2)}, u32[]{:S(2)}) collective-permute-start(bf16[352,2048]{1,0:T(8,128)(2,1)} %convolution_convert_fusion.28), channel_id=1, source_target_pairs={{0,16},{8,24},{16,0},{24,8},{1,17},{9,25},{17,1},{25,9},{2,18},{10... | collective-permute-start | bytes 4325384 | tf_op jit(solution)/shard_map/ppermute | solution.py:183
  1271.7 83.4 %collective-permute-start.38 = (bf16[352,2048]{1,0:T(8,128)(2,1)}, bf16[352,2048]{1,0:T(8,128)(2,1)}, u32[]{:S(2)}, u32[]{:S(2)}) collective-permute-start(bf16[352,2048]{1,0:T(8,128)(2,1)} %add_convert_fusion.6), channel_id=1, source_target_pairs={{0,16},{8,24},{16,0},{24,8},{1,17},{9,25},{17,1},{25,9},{2,18},{10... | collective-permute-start | bytes 4325384 | tf_op jit(solution)/shard_map/ppermute | solution.py:183
  1339.4 70.6 %all-to-all-start.9 = ((bf16[8,704,256]{2,1,0:T(8,128)(2,1)}), bf16[8,704,256]{2,1,0:T(8,128)(2,1)}, u32[]{:S(2)}, u32[]{:S(2)}) async-start(bf16[8,704,256]{2,1,0:T(8,128)(2,1)} %bitcast.410), calls=%async_computation.14 | async-start | bytes 5767168 | tf_op jit(solution)/shard_map/all_to_all | solution.py:228
  (230 other events, 4818.8 us)
Sparse Core Ops, SparseCore 0:
  28.1 51.5 all-gather.5
  81.9 90.8 all-gather.7
  174.4 82.6 all-gather.9
  420.6 82.0 all-gather.13
  504.2 80.5 all-gather.11
  813.7 87.4 reduce-scatter.5
  903.5 87.9 reduce-scatter.7
  1020.8 87.4 reduce-scatter.11
  1154.4 50.1 reduce-scatter.9
  1206.7 125.7 reduce-scatter.13

commit v4 on v3

--- a/solution.py
+++ b/solution.py
@@ -49,103 +49,166 @@
     return jnp.concatenate([cosine, cosine], -1), jnp.concatenate([-sine, sine], -1)
 
 
-def rotate(tensor, cosine, sine):
-    heads = tensor.reshape(tensor.shape[:-1] + (-1, HD))
-    swapped = jnp.concatenate([heads[..., HD // 2:], heads[..., :HD // 2]], -1)
-    return (heads * cosine[:, None, :] + swapped * sine[:, None, :]).reshape(tensor.shape)
-
-
-def attend_kernel(scale, q_ref, k_ref, v_ref, qb_ref, kb_ref, o_ref, l_ref):
-    s = dot_nt(k_ref[...], q_ref[...])
-    s = jnp.where(kb_ref[...] <= qb_ref[0], s * (scale * LOG2E), NEGATIVE)
-    peak = jnp.max(s, axis=0, keepdims=True)
-    p = jnp.exp2(s - peak)
-    total = jnp.sum(p, axis=0, keepdims=True)
-    o = dot_tn(v_ref[...], p.astype(BF))
-    o_ref[...] = (o / total).T.astype(BF)
-    l_ref[0] = peak + jnp.log2(total)
-
-
-def attend(q, k, v, q_blocks, k_blocks):
-    rows, width = q.shape
-    length = k.shape[0]
-    heads = width // HD
+def turn(tile, cosine, sine):
+    return tile * cosine + pltpu.roll(tile, HD // 2, 1) * sine
+
+
+def chosen(ref, route, n_e, width, at):
+    parts = [jnp.where(route == e, ref[:, e * width + at:e * width + at + HD], 0.0) for e in range(n_e)]
+    return functools.reduce(lambda a, b: a + b, parts)
+
+
+def attend_kernel(
+    n_e, scale, q_ref, kv_ref, route_ref, gate_ref, cos_ref, sin_ref, qb_ref, kb_ref,
+    query_ref, key_ref, value_ref, o_ref, l_ref, mixed_ref,
+):
+    width = key_ref.shape[1]
+    tile = q_ref.shape[0]
+    step = pl.program_id(0)
+
+    @pl.when(step == 0)
+    def _():
+        for at in range(0, width, HD):
+            key_ref[:, at:at + HD] = turn(kv_ref[:, at:at + HD], cos_ref[...], sin_ref[...]).astype(BF)
+        value_ref[...] = kv_ref[:, width:].astype(BF)
+
+    here = pl.ds(pl.multiple_of(step * tile, tile), tile)
+    cosine, sine = cos_ref[here, :], sin_ref[here, :]
+    routes = [route_ref[:, j:j + 1] for j in range(TOPK)]
+    gates = [gate_ref[:, j:j + 1] for j in range(TOPK)]
+    allowed = kb_ref[...] <= jnp.concatenate([qb_ref[...]] * TOPK, axis=1)
+    for head in range(width // HD):
+        at = head * HD
+        q = [turn(chosen(q_ref, routes[j], n_e, width, at), cosine, sine).astype(BF) for j in range(TOPK)]
+        for j in range(TOPK):
+            query_ref[j, :, at:at + HD] = q[j]
+        s = dot_nt(key_ref[:, at:at + HD], jnp.concatenate(q, axis=0))
+        s = jnp.where(allowed, s * (scale * LOG2E), NEGATIVE)
+        peak = jnp.max(s, axis=0, keepdims=True)
+        p = jnp.exp2(s - peak)
+        total = jnp.sum(p, axis=0, keepdims=True)
+        o = (dot_tn(value_ref[:, at:at + HD], p.astype(BF)) / total).T.astype(BF)
+        l_ref[0, head:head + 1, :] = peak + jnp.log2(total)
+        o = [o[j * tile:(j + 1) * tile] for j in range(TOPK)]
+        for j in range(TOPK):
+            o_ref[j, :, at:at + HD] = o[j]
+        o = [gates[j] * o[j].astype(F32) for j in range(TOPK)]
+        for e in range(n_e):
+            parts = [jnp.where(routes[j] == e, o[j], 0.0) for j in range(TOPK)]
+            mixed_ref[:, e * width + at:e * width + at + HD] = (parts[0] + parts[1]).astype(BF)
+
+
+def attend(q_raw, kv_raw, routes, gates, cosine, sine, q_blocks, k_blocks):
+    length, wide = q_raw.shape
+    width = kv_raw.shape[1] // 2
+    n_e, heads = wide // width, width // HD
     tile = 256
+    whole = lambda *shape: pl.BlockSpec(shape, lambda i: (0,) * len(shape))
+    tiled = lambda cols: pl.BlockSpec((tile, cols), lambda i: (i, 0))
+    pair = pl.BlockSpec((TOPK, tile, width), lambda i: (0, i, 0))
     return pl.pallas_call(
-        functools.partial(attend_kernel, HD ** -0.5),
-        grid=(heads, rows // tile),
+        functools.partial(attend_kernel, n_e, HD ** -0.5),
+        grid=(length // tile,),
         in_specs=[
-            pl.BlockSpec((tile, HD), lambda h, i: (i, h)),
-            pl.BlockSpec((length, HD), lambda h, i: (0, h)),
-            pl.BlockSpec((length, HD), lambda h, i: (0, h)),
-            pl.BlockSpec((1, 1, tile), lambda h, i: (0, 0, i)),
-            pl.BlockSpec((length, 1), lambda h, i: (0, 0)),
+            tiled(wide), whole(length, 2 * width), tiled(TOPK), tiled(TOPK), whole(length, HD), whole(length, HD),
+            pl.BlockSpec((1, tile), lambda i: (0, i)), whole(length, 1),
         ],
         out_specs=[
-            pl.BlockSpec((tile, HD), lambda h, i: (i, h)),
-            pl.BlockSpec((1, 1, tile), lambda h, i: (h, 0, i)),
+            pair, whole(length, width), whole(length, width), pair,
+            pl.BlockSpec((1, heads, TOPK * tile), lambda i: (i, 0, 0)), tiled(wide),
         ],
         out_shape=[
-            jax.ShapeDtypeStruct((rows, width), BF),
-            jax.ShapeDtypeStruct((heads, 1, rows), F32),
+            jax.ShapeDtypeStruct((TOPK, length, width), BF),
+            jax.ShapeDtypeStruct((length, width), BF),
+            jax.ShapeDtypeStruct((length, width), BF),
+            jax.ShapeDtypeStruct((TOPK, length, width), BF),
+            jax.ShapeDtypeStruct((length // tile, heads, TOPK * tile), F32),
+            jax.ShapeDtypeStruct((length, wide), BF),
         ],
-        cost_estimate=pl.CostEstimate(
-            flops=rows * length, transcendentals=0, bytes_accessed=4 * rows * width
-        ),
+        cost_estimate=pl.CostEstimate(flops=length * length, transcendentals=0, bytes_accessed=8 * length * width),
         name="attend",
-    )(q, k, v, q_blocks.reshape(1, 1, rows), k_blocks.reshape(length, 1))
-
-
-def attend_back_kernel(scale, q_ref, k_ref, v_ref, d_ref, o_ref, l_ref, qb_ref, kb_ref, dq_ref, dk_ref, dv_ref):
-    q, k, d = q_ref[...], k_ref[...], d_ref[...]
-    s = dot_nt(k, q)
-    p = jnp.exp2(s * (scale * LOG2E) - l_ref[0])
-    p = jnp.where(kb_ref[...] <= qb_ref[0], p, 0.0)
-    centre = jnp.sum((d.astype(F32) * o_ref[...].astype(F32)).T, axis=0, keepdims=True)
-    grad_p = dot_nt(v_ref[...], d)
-    grad_s = (p * (grad_p - centre)).astype(BF)
-    dq_ref[...] = (dot_tn(k, grad_s) * scale).T
-    new_k = dot(grad_s, q) * scale
-    new_v = dot(p.astype(BF), d)
-
-    @pl.when(pl.program_id(1) == 0)
+    )(q_raw, kv_raw, routes, gates, cosine, sine, q_blocks, k_blocks)
+
+
+def attend_back_kernel(
+    n_e, scale, g_ref, route_ref, gate_ref, query_ref, key_ref, value_ref, o_ref, l_ref, cos_ref, sin_ref, qb_ref,
+    kb_ref, dq_ref, dkv_ref, note_ref, dk_ref, dv_ref,
+):
+    width = key_ref.shape[1]
+    tile = g_ref.shape[0]
+    step = pl.program_id(0)
+
+    @pl.when(step == 0)
     def _():
-        dk_ref[...] = new_k
-        dv_ref[...] = new_v
-
-    @pl.when(pl.program_id(1) > 0)
+        dk_ref[...] = jnp.zeros_like(dk_ref)
+        dv_ref[...] = jnp.zeros_like(dv_ref)
+
+    here = pl.ds(pl.multiple_of(step * tile, tile), tile)
+    cosine, sine = cos_ref[here, :], sin_ref[here, :]
+    routes = [route_ref[:, j:j + 1] for j in range(TOPK)]
+    gates = [gate_ref[:, j:j + 1] for j in range(TOPK)]
+    allowed = kb_ref[...] <= jnp.concatenate([qb_ref[...]] * TOPK, axis=1)
+    gate_grads = [jnp.zeros((tile, 1), F32) for _ in range(TOPK)]
+    for head in range(width // HD):
+        at = head * HD
+        k, v = key_ref[:, at:at + HD], value_ref[:, at:at + HD]
+        g = [chosen(g_ref, routes[j], n_e, width, at) for j in range(TOPK)]
+        o = [o_ref[j, :, at:at + HD].astype(F32) for j in range(TOPK)]
+        gate_grads = [gate_grads[j] + jnp.sum(g[j] * o[j], axis=1, keepdims=True) for j in range(TOPK)]
+        d = jnp.concatenate([(gates[j] * g[j]).astype(BF) for j in range(TOPK)], axis=0)
+        q = jnp.concatenate([query_ref[j, :, at:at + HD] for j in range(TOPK)], axis=0)
+        centre = jnp.sum((d.astype(F32) * jnp.concatenate(o, axis=0)).T, axis=0, keepdims=True)
+        s = dot_nt(k, q)
+        p = jnp.where(allowed, jnp.exp2(s * (scale * LOG2E) - l_ref[0, head:head + 1, :]), 0.0)
+        grad_s = (p * (dot_nt(v, d) - centre)).astype(BF)
+        dq = (dot_tn(k, grad_s) * scale).T
+        dq = [turn(dq[j * tile:(j + 1) * tile], cosine, -sine) for j in range(TOPK)]
+        for e in range(n_e):
+            parts = [jnp.where(routes[j] == e, dq[j], 0.0) for j in range(TOPK)]
+            dq_ref[:, e * width + at:e * width + at + HD] = (parts[0] + parts[1]).astype(BF)
+        dk_ref[:, at:at + HD] += dot(grad_s, q) * scale
+        dv_ref[:, at:at + HD] += dot(p.astype(BF), d)
+    lane = lax.broadcasted_iota(jnp.int32, (tile, HD), 1)
+    note = jnp.zeros((tile, HD), F32)
+    for j in range(TOPK):
+        high = gate_grads[j].astype(BF).astype(F32)
+        note = jnp.where(lane == j, high, note)
+        note = jnp.where(lane == TOPK + j, gate_grads[j] - high, note)
+    note_ref[...] = note.astype(BF)
+
+    @pl.when(step == pl.num_programs(0) - 1)
     def _():
-        dk_ref[...] += new_k
-        dv_ref[...] += new_v
-
-
-def attend_back(q, k, v, d, o, total, q_blocks, k_blocks):
-    rows, width = q.shape
-    length = k.shape[0]
-    heads = width // HD
+        for at in range(0, width, HD):
+            dkv_ref[:, at:at + HD] = turn(dk_ref[:, at:at + HD], cos_ref[...], -sin_ref[...]).astype(BF)
+        dkv_ref[:, width:] = dv_ref[...].astype(BF)
+
+
+def attend_back(g_raw, routes, gates, queries, keys, values, mixed, log_total, cosine, sine, q_blocks, k_blocks):
+    length, wide = g_raw.shape
+    width = keys.shape[1]
+    n_e, heads = wide // width, width // HD
     tile = 256
-    row_spec = pl.BlockSpec((tile, HD), lambda h, i: (i, h))
-    key_spec = pl.BlockSpec((length, HD), lambda h, i: (0, h))
+    whole = lambda *shape: pl.BlockSpec(shape, lambda i: (0,) * len(shape))
+    tiled = lambda cols: pl.BlockSpec((tile, cols), lambda i: (i, 0))
+    pair = pl.BlockSpec((TOPK, tile, width), lambda i: (0, i, 0))
     return pl.pallas_call(
-        functools.partial(attend_back_kernel, HD ** -0.5),
-        grid=(heads, rows // tile),
+        functools.partial(attend_back_kernel, n_e, HD ** -0.5),
+        grid=(length // tile,),
         in_specs=[
-            row_spec, key_spec, key_spec, row_spec, row_spec,
-            pl.BlockSpec((1, 1, tile), lambda h, i: (h, 0, i)),
-            pl.BlockSpec((1, 1, tile), lambda h, i: (0, 0, i)),
-            pl.BlockSpec((length, 1), lambda h, i: (0, 0)),
+            tiled(wide), tiled(TOPK), tiled(TOPK), pair, whole(length, width), whole(length, width), pair,
+            pl.BlockSpec((1, heads, TOPK * tile), lambda i: (i, 0, 0)), whole(length, HD), whole(length, HD),
+            pl.BlockSpec((1, tile), lambda i: (0, i)), whole(length, 1),
         ],
-        out_specs=[row_spec, key_spec, key_spec],
+        out_specs=[tiled(wide), whole(length, 2 * width), tiled(HD)],
         out_shape=[
-            jax.ShapeDtypeStruct((rows, width), F32),
-            jax.ShapeDtypeStruct((length, width), F32),
-            jax.ShapeDtypeStruct((length, width), F32),
+            jax.ShapeDtypeStruct((length, wide), BF),
+            jax.ShapeDtypeStruct((length, 2 * width), BF),
+            jax.ShapeDtypeStruct((length, HD), BF),
         ],
-        cost_estimate=pl.CostEstimate(
-            flops=rows * length, transcendentals=0, bytes_accessed=4 * rows * width
-        ),
+        scratch_shapes=[pltpu.VMEM((length, width), F32), pltpu.VMEM((length, width), F32)],
+        cost_estimate=pl.CostEstimate(flops=length * length, transcendentals=0, bytes_accessed=8 * length * width),
         name="attend_back",
-    )(q, k, v, d, o, total, q_blocks.reshape(1, 1, rows), k_blocks.reshape(length, 1))
+    )(g_raw, routes, gates, queries, keys, values, mixed, log_total, cosine, sine, q_blocks, k_blocks)
 
 
 def pick(table, routes, ids):
@@ -279,14 +342,8 @@
 
     notes = jnp.concatenate([blocks[0][:, None], attn_routes[0]], axis=1).astype(BF)
     carried = jnp.concatenate([inputs[0], jnp.pad(notes, ((0, 0), (0, 128 - 1 - TOPK)))], axis=1)
-    carried = [carried] + [swap(carried, k) for k in range(1, n_e)]
-    query_w = to_heads(w_query[0])
-    out_w, query_w, carried[1] = lax.optimization_barrier((w_out[0], query_w, carried[1]))
-    carried = jnp.concatenate(carried, axis=0)
-    query_w = gather_shard(query_w)
-    out_rows = out_w.shape[0]
-    turned = shuffle(out_w.T, "shard").reshape(n_s, width // n_s, out_rows).transpose(1, 0, 2)
-    out_wt = gather_shard(to_heads(turned.reshape(width // n_s, n_s * out_rows)))
+    carried = lax.optimization_barrier(spread(carried))
+    query_w = gather_shard(to_heads(w_query[0]))
 
     hidden_units = w_down.shape[1]
     turned = jnp.stack([w_gate[0].T.reshape(n_s, hidden_units, -1), w_up[0].T.reshape(n_s, hidden_units, -1)], axis=1)
@@ -305,16 +362,18 @@
     logits_a = dot(h_attn, router_a.astype(BF))
     gates_a = pair_softmax(pick(logits_a, routes_a, ids))
     key_value = dot(h_attn, key_value_w)
-    keys = rotate(key_value[:, :group], cosine, sine).astype(BF)
-    values = key_value[:, group:].astype(BF)
-    queries = pick(dot(h_attn, query_w), routes_a, ids)
-    queries = jnp.concatenate([rotate(v, cosine, sine).astype(BF) for v in queries], axis=0)
-    row_blocks = jnp.concatenate([seq_blocks, seq_blocks])
-    queries, *down_w = lax.optimization_barrier((queries, *down_w))
+    key_value, out_w = lax.optimization_barrier((key_value, w_out[0]))
+    out_rows = out_w.shape[0]
+    turned = shuffle(out_w.T, "shard").reshape(n_s, width // n_s, out_rows).transpose(1, 0, 2)
+    out_wt = gather_shard(to_heads(turned.reshape(width // n_s, n_s * out_rows)))
+    gate_pair = jnp.concatenate(gates_a, axis=1)
+    row_blocks, key_blocks = seq_blocks.reshape(1, -1), seq_blocks.reshape(-1, 1)
+    query_raw = dot(h_attn, query_w)
+    query_raw, *down_w = lax.optimization_barrier((query_raw, *down_w))
     down_w = fetch_rest(down_w)
-    mixed_rows, log_total = attend(queries, keys, values, row_blocks, seq_blocks)
-    mixed = [v.astype(F32) for v in jnp.split(mixed_rows, TOPK, axis=0)]
-    mixed_all = place([gates_a[j] * mixed[j] for j in range(TOPK)], routes_a, ids).astype(BF)
+    queries, keys, values, mixed, log_total, mixed_all = attend(
+        query_raw, key_value, routes_a, gate_pair, cosine, sine, row_blocks, key_blocks
+    )
     mixed_out, *down_w = lax.optimization_barrier((mixed_all, *down_w))
     middle = own + collect(dot_nt(mixed_out, out_wt).astype(BF)) + bias_a
 
@@ -391,11 +450,11 @@
     halves = deliver_first(grad_gate_up[n_e - 1])
     out_rows_f = []
     for k in range(n_e):
-        hidden = after(hiddens[k], *grad_gate_up[n_e - 1])
+        hidden = after(hiddens[k], *(grad_gate_up[n_e - 1] if k < 2 else halves))
         out_rows_f.append(dot_tn(hidden, down_w[k]).astype(BF).reshape(n_s, capacity, width))
     out_sum = tokens_of(out_rows_f)
     ffn_out = scatter_shard(out_sum)
-    back_f, out_sum, *halves = lax.optimization_barrier((back_f, out_sum, *halves))
+    back_f, out_sum = lax.optimization_barrier((back_f, out_sum))
     back_f = back_f.astype(F32)
     grad_gates_f = jnp.sum(
         shuffle(jnp.stack(grad_gate_f, axis=1).reshape(n_s, TOPK * tokens), "shard"), axis=0
@@ -425,22 +484,15 @@
     seq_grad, grad_gate_up = lax.optimization_barrier((seq_grad, grad_gate_up))
     near = deliver_near(grad_gate_up)
     last = deliver_last(grad_gate_up, halves)
-    grad_mixed = pick(dot(seq_grad, out_wt), routes_a, ids)
-    gate_grads = jnp.concatenate([jnp.sum(grad_mixed[j] * mixed[j], axis=1, keepdims=True) for j in range(TOPK)], axis=1)
-    gate_grads_high = gate_grads.astype(BF)
-    gate_grads_low = (gate_grads - gate_grads_high.astype(F32)).astype(BF)
-    grad_mixed = jnp.concatenate([(gates_a[j] * grad_mixed[j]).astype(BF) for j in range(TOPK)], axis=0)
+    grad_mixed = dot(seq_grad, out_wt)
     grad_out_wt = dot_tn(seq_grad, mixed_all).astype(BF)
     grad_mixed, grad_out_wt = lax.optimization_barrier((grad_mixed, grad_out_wt))
-    grad_q, grad_k, grad_v = attend_back(queries, keys, values, grad_mixed, mixed_rows, log_total, row_blocks, seq_blocks)
-    grad_q, *near = lax.optimization_barrier((grad_q, *near))
-    grad_q = [rotate(v, cosine, -sine) for v in jnp.split(grad_q, TOPK, axis=0)]
-    grad_query_all = place(grad_q, routes_a, ids).astype(BF)
-    grad_key_value = jnp.concatenate([rotate(grad_k, cosine, -sine), grad_v], axis=1).astype(BF)
+    grad_query_all, grad_key_value, gate_notes = attend_back(
+        grad_mixed, routes_a, gate_pair, queries, keys, values, mixed, log_total, cosine, sine, row_blocks, key_blocks
+    )
+    grad_query_all, *near = lax.optimization_barrier((grad_query_all, *near))
     back_a = (dot_nt(grad_query_all, query_w) + dot_nt(grad_key_value, key_value_w)).astype(BF)
-    back_a = jnp.concatenate(
-        [back_a, jnp.pad(jnp.concatenate([gate_grads_high, gate_grads_low], axis=1), ((0, 0), (0, 128 - 2 * TOPK)))], axis=1
-    )
+    back_a = jnp.concatenate([back_a, gate_notes], axis=1)
     value = scatter_shard(grad_out_wt)
     back_a, ffn_out, *last = lax.optimization_barrier((back_a, ffn_out, *last))
     gate_up_total = [v.astype(BF) for v in total(grad_gate_up[0], near, last)]
@@ -457,7 +509,10 @@
         value = shuffle(value.reshape(hidden_units, n_s, width // n_s).transpose(1, 0, 2), "shard")
         return value.reshape(n_s * hidden_units, width // n_s)
 
-    gate_turned = to_rows(gate_up_total[0])
+    grad_out_w = shuffle(value, "shard").reshape(width, out_rows)
+    grad_out_w, gate_total = lax.optimization_barrier((grad_out_w, gate_up_total[0]))
+    grad_out_w = grad_out_w.T.astype(F32)[None]
+    gate_turned = to_rows(gate_total)
     grad_down = []
     for k in range(n_e):
         hidden = after(hiddens[k], back_a)
@@ -468,7 +523,6 @@
     back_a, gate_turned, *near = lax.optimization_barrier((back_a, gate_turned, *near))
     up_total, key_value_grad = lax.optimization_barrier((after(gate_up_total[1], gate_turned), key_value_grad))
     up_turned = to_rows(up_total)
-    grad_out_w = shuffle(after(value, gate_turned), "shard").reshape(width, out_rows).T.astype(F32)[None]
     grad_down_w = jnp.concatenate(total(grad_down[0], near, last), axis=0)[None]
     key_value_grad = trade(key_value_grad.reshape(n_e, small_rows, -1))
     grad_key_w = key_value_grad[:, :, :group].transpose(1, 0, 2).reshape(small_rows, -1).astype(F32)
@@ -478,7 +532,6 @@
     back_a = back_a[:, :width]
     grad_query_w = from_heads(query_grad).astype(F32)[None]
     grad_gate_w = gate_turned.T.astype(F32)[None]
-    grad_up_w = up_turned.T.astype(F32)[None]
 
     h_own = h_attn[:tokens]
     own_routes_a = attn_routes[0]
@@ -494,6 +547,8 @@
         + [v[:, None] for v in (grad_gain_a, grad_gain_f, grad_bias_a, grad_bias_f)],
         axis=1,
     )
+    shared, up_turned = lax.optimization_barrier((shared, up_turned))
+    grad_up_w = up_turned.T.astype(F32)[None]
     shared = shuffle(shared.reshape(n_e * n_s, -1), ("expert", "shard"))
     shared = jnp.sum(shared, axis=0).reshape(small_rows, small_width)
     return (

time: 1460 us -> 1490 us (1.021)
  waiting for transfers between devices: 404 us -> 511 us
  other arithmetic: 187 us -> 139 us
  local copies, waits for them, and re-layouts: 197 us -> 171 us
  blocking collectives: 66 us -> 87.5 us
  starting transfers between devices: 96.1 us -> 77.1 us
    all_to_all x8 -> x7, waiting for transfers between devices: 62.2 us -> 130 us  [shuffle(): return lax.all_to_all(value, axis, split_axis=0, concat_axis=0, tiled=True)]
    ppermute x41, waiting for transfers between devices: 207 us -> 247 us  [swap(): return lax.ppermute(value, 'expert', [(i, i ^ k) for i in range(n_e)])]
    all_to_all x2 -> x3, blocking collectives: 66 us -> 87.5 us  [shuffle(): return lax.all_to_all(value, axis, split_axis=0, concat_axis=0, tiled=True)]
    slice x7 -> x0, local copies, waits for them, and re-layouts: 20.8 us -> none  [the longest x5 19.5 us: rotate(): swapped = jnp.concatenate([heads[..., HD // 2:], heads[..., :HD // 2]], -1)]
    all_to_all x8 -> x7, starting transfers between devices: 46.8 us -> 29.3 us  [shuffle(): return lax.all_to_all(value, axis, split_axis=0, concat_axis=0, tiled=True)]
    convert_element_type x1, other arithmetic: 16.7 us -> 1.36 us  [local(): h_attn = (seq_in * inverse_rms(seq_in) * gain_a).astype(BF)]
    unnamed x429 -> x331, local copies, waits for them, and re-layouts: 54.6 us -> 51.4 us
  transfers between devices with their start and end apart: 59 -> 58, of which waited for: 21 -> 25; matrix products, arithmetic and copies ran while one was open for 46% -> 41% of each run, Pallas kernels for 5% -> 4%
where the time goes in v4:
time: 1490 us; the launch traced here: 1480 us
  waiting for transfers between devices  511 us (34%)
  matrix products  422 us (28%)
  local copies, waits for them, and re-layouts  171 us (11%)
  other arithmetic  139 us (9%)
  blocking collectives  87.5 us (6%)
  starting transfers between devices  77.1 us (5%)
  Pallas kernels  59.4 us (4%)
  between operations  16.8 us (1%)
    ppermute x41, waiting for transfers between devices, swap(): return lax.ppermute(value, 'expert', [(i, i ^ k) for i in range(n_e)])  247 us
    all_gather x5, waiting for transfers between devices, gather_shard(): return lax.all_gather(value, 'shard', axis=0, tiled=True)  134 us
    all_to_all x7, waiting for transfers between devices, shuffle(): return lax.all_to_all(value, axis, split_axis=0, concat_axis=0, tiled=True)  130 us
    dot_general x26, matrix products, dot(): return jnp.dot(a, b, preferred_element_type=F32)  126 us
    dot_general x13, matrix products, dot_tn(): lax.dot_general(a, b, (((0,), (0,)), ((), ())), precision=precision, pref...  112 us
    dot_general x11, matrix products, dot_nt(): lax.dot_general(a, b, (((1,), (1,)), ((), ())), preferred_element_type=F32)  112 us
    all_to_all x3, blocking collectives, shuffle(): return lax.all_to_all(value, axis, split_axis=0, concat_axis=0, tiled=True)  87.5 us
    unnamed x331, local copies, waits for them, and re-layouts  51.4 us
  transfers between devices with their start and end apart: 58, of which 25 were waited for; matrix products, arithmetic and copies ran while one was open for 41% of the time, Pallas kernels for 4%

profile of v4, /device:TPU:0, one launch (start us, length us, event | category | flops | bytes accessed | tf_op | source)
XLA Modules:
  0.0 1484.3 jit_solution(11641581644126277397)
XLA Ops:
  29.2 15.9 %all_to_all.63 = bf16[4,256,512]{2,1,0:T(8,128)(2,1)S(1)} all-to-all(bf16[4,256,512]{2,1,0:T(8,128)(2,1)S(1)} %copy.611), channel_id=1, replica_groups=mesh['expert'=4,'shard'=8] {'expert'}, dimensions={0} | all-to-all | bytes 2097152 | tf_op jit(solution)/shard_map/all_to_all | solution.py:291
  53.5 22.7 %collective-permute-done = bf16[256,2176]{1,0:T(8,128)(2,1)S(1)} collective-permute-done((bf16[256,2176]{1,0:T(8,128)(2,1)}, bf16[256,2176]{1,0:T(8,128)(2,1)S(1)}, u32[]{:S(2)}, u32[]{:S(2)}) %collective-permute-start) | collective-permute-done | bytes 1114144 | tf_op jit(solution)/shard_map/ppermute | solution.py:246
  76.2 21.7 %collective-permute-done.1 = bf16[256,2176]{1,0:T(8,128)(2,1)} collective-permute-done((bf16[256,2176]{1,0:T(8,128)(2,1)}, bf16[256,2176]{1,0:T(8,128)(2,1)}, u32[]{:S(2)}, u32[]{:S(2)}) %collective-permute-start.1) | collective-permute-done | bytes 1114144 | tf_op jit(solution)/shard_map/ppermute | solution.py:246
  121.2 54.1 %all_to_all.64 = bf16[8,256,256]{2,1,0:T(8,128)(2,1)S(1)} all-to-all(bf16[8,256,256]{2,1,0:T(8,128)(2,1)S(1)} %bitcast.423), channel_id=1, replica_groups=mesh['expert'=4,'shard'=8] {'shard'}, dimensions={0} | all-to-all | bytes 2097152 | tf_op jit(solution)/shard_map/all_to_all | solution.py:291
  175.8 17.5 %all_to_all.65 = bf16[4,256,512]{1,2,0:T(8,128)(2,1)} all-to-all(bf16[4,256,512]{1,2,0:T(8,128)(2,1)S(1)} %bitcast.425), channel_id=1, replica_groups=mesh['expert'=4,'shard'=8] {'expert'}, dimensions={0} | all-to-all | bytes 2097152 | tf_op jit(solution)/shard_map/all_to_all | solution.py:291
  224.6 13.2 fusion.138.q_ref
  237.8 46.4 %collective-permute-done.3 = bf16[704,2048]{1,0:T(8,128)(2,1)} collective-permute-done((bf16[704,2048]{1,0:T(8,128)(2,1)}, bf16[704,2048]{1,0:T(8,128)(2,1)}, u32[]{:S(2)}, u32[]{:S(2)}) %collective-permute-start.3) | collective-permute-done | bytes 2883616 | tf_op jit(solution)/shard_map/ppermute | solution.py:246
  299.4 26.8 %attend.1 = (bf16[2,1024,512]{2,1,0:T(8,128)(2,1)}, bf16[1024,512]{1,0:T(8,128)(2,1)}, bf16[1024,512]{1,0:T(8,128)(2,1)}, bf16[2,1024,512]{2,1,0:T(8,128)(2,1)},...) custom-call(f32[1024,2048]{1,0:T(8,128)} %fusion.138.q_ref, f32[1024,1024]{1,0:T(8,128)} %fusion.27.kv_ref, ...), custom_call_target="tpu_custom_call" | custom-call | flops 1048576 | bytes 4194304 | tf_op jit(solution)/shard_map/attend/pallas_call | solution.py:109
  330.1 12.5 convolution_convert_fusion.18
  349.9 44.9 %all-to-all-done.4 = bf16[8,2,704,256]{3,2,1,0:T(8,128)(2,1)} async-done(((bf16[8,2,704,256]{3,2,1,0:T(8,128)(2,1)}), bf16[8,2,704,256]{3,2,1,0:T(8,128)(2,1)}, u32[]{:S(2)}, u32[]{:S(2)}) %all-to-all-start.4) | async-done | bytes 5767200 | tf_op jit(solution)/shard_map/all_to_all | solution.py:291
  414.1 78.3 %all-gather.14.cloned.1.call-done = bf16[2048,2048]{1,0:T(8,128)(2,1)} async-done(((bf16[256,2048]{1,0:T(8,128)(2,1)}), bf16[2048,2048]{1,0:T(8,128)(2,1)}) %all-gather.14.cloned.1.call-update) | async-done | bytes 8388624 | tf_op jit(solution)/shard_map/all_gather | solution.py:301
  508.0 10.6 fusion.139
  518.5 55.9 %all-gather.12.cloned.1.call-done = bf16[2048,2048]{1,0:T(8,128)(2,1)} async-done(((bf16[256,2048]{1,0:T(8,128)(2,1)}), bf16[2048,2048]{1,0:T(8,128)(2,1)}) %all-gather.12.cloned.1.call-update) | async-done | bytes 8388624 | tf_op jit(solution)/shard_map/all_gather | solution.py:301
  601.2 12.2 fusion.140
  640.5 12.2 fusion.141
  686.2 13.2 convolution_convert_fusion.9
  712.2 12.9 convolution_convert_fusion.8
  733.1 14.4 convolution_convert_fusion.7
  789.4 13.8 fusion.22
  833.8 47.5 %collective-permute-done.15 = bf16[704,2048]{1,0:T(8,128)(2,1)S(1)} collective-permute-done((bf16[704,2048]{1,0:T(8,128)(2,1)S(1)}, bf16[704,2048]{1,0:T(8,128)(2,1)S(1)}, u32[]{:S(2)}, u32[]{:S(2)}) %collective-permute-start.15) | collective-permute-done | bytes 2883616 | tf_op jit(solution)/shard_map/ppermute | solution.py:246
  897.4 13.8 fusion.19
  981.0 13.4 collective-permute-done.18
  995.2 11.0 fusion.143.g_ref
  1006.2 11.3 convolution_convert_fusion.1
  1030.3 32.6 %attend_back.1 = (bf16[1024,2048]{1,0:T(8,128)(2,1)}, bf16[1024,1024]{1,0:T(8,128)(2,1)}, bf16[1024,128]{1,0:T(8,128)(2,1)}) custom-call(f32[1024,2048]{1,0:T(8,128)} %fusion.143.g_ref, s32[1024,2]{1,0:T(8,128)} %slice.289.route_ref, f32[1024,2]{1,0:T(8,128)} %pad_maximum_fusion.7.gate_ref, bf16[2,1024,512]{2,1,0:T(8,128)(2,1)} %get-tuple-element.127.query_ref, ...), custom_call_target="tpu_custom_call" | custom-call | flops 1048576 | bytes 4194304 | tf_op jit(solution)/shard_map/attend_back/pallas_call | solution.py:194
  1063.0 10.9 fusion.25
  1084.3 11.2 add_convert_fusion
  1098.1 45.5 %collective-permute-done.22 = bf16[704,2048]{1,0:T(8,128)(2,1)} collective-permute-done((bf16[704,2048]{1,0:T(8,128)(2,1)}, bf16[704,2048]{1,0:T(8,128)(2,1)}, u32[]{:S(2)}, u32[]{:S(2)}) %collective-permute-start.22) | collective-permute-done | bytes 2883616 | tf_op jit(solution)/shard_map/ppermute | solution.py:246
  1158.8 11.6 convolution_convert_fusion
  1228.8 30.2 %all-to-all-done.6 = bf16[8,256,256]{1,2,0:T(8,128)(2,1)} async-done(((bf16[8,256,256]{1,2,0:T(8,128)(2,1)}), bf16[8,256,256]{1,2,0:T(8,128)(2,1)}, u32[]{:S(2)}, u32[]{:S(2)}) %all-to-all-start.6) | async-done | bytes 1048608 | tf_op jit(solution)/shard_map/all_to_all | solution.py:291
  1296.8 23.5 %collective-permute-done.39 = bf16[352,2048]{1,0:T(8,128)(2,1)S(1)} collective-permute-done((bf16[352,2048]{1,0:T(8,128)(2,1)S(1)}, bf16[352,2048]{1,0:T(8,128)(2,1)S(1)}, u32[]{:S(2)}, u32[]{:S(2)}) %collective-permute-start.39) | collective-permute-done | bytes 1441824 | tf_op jit(solution)/shard_map/ppermute | solution.py:246
  1329.5 34.1 %all-to-all-done.7 = bf16[8,704,256]{2,1,0:T(8,128)(2,1)S(1)} async-done(((bf16[8,704,256]{2,1,0:T(8,128)(2,1)}), bf16[8,704,256]{2,1,0:T(8,128)(2,1)S(1)}, u32[]{:S(2)}, u32[]{:S(2)}) %all-to-all-start.7) | async-done | bytes 2883616 | tf_op jit(solution)/shard_map/all_to_all | solution.py:291
  (694 shorter events, 671.9 us)
Async XLA Ops:
  17.5 89.4 %all-gather.6.cloned.1.call-start = ((), (), s32[]{:S(2)}) async-start(), calls=%async_computation.15 | async-start | bytes 5308416 | tf_op jit(solution)/shard_map/all_gather | solution.py:301
  28.0 180.5 %all-gather.8.cloned.1.call-start = ((), (), s32[]{:S(2)}) async-start(), calls=%async_computation.16 | async-start | bytes 9437184 | tf_op jit(solution)/shard_map/all_gather | solution.py:301
  46.4 283.6 %all-gather.10.cloned.1.call-start = ((), (), s32[]{:S(2)}) async-start(), calls=%async_computation.17 | async-start | bytes 9437184 | tf_op jit(solution)/shard_map/all_gather | solution.py:301
  214.1 180.6 %all-to-all-start.4 = ((bf16[8,2,704,256]{3,2,1,0:T(8,128)(2,1)}), bf16[8,2,704,256]{3,2,1,0:T(8,128)(2,1)}, u32[]{:S(2)}, u32[]{:S(2)}) async-start(bf16[8,2,704,256]{3,2,1,0:T(8,128)(2,1)} %copy.623), calls=%async_computation.4 | async-start | bytes 11534336 | tf_op jit(solution)/shard_map/all_to_all | solution.py:291
  218.8 273.6 %all-gather.14.cloned.1.call-start = ((), (), s32[]{:S(2)}) async-start(), calls=%async_computation.19 | async-start | bytes 9437184 | tf_op jit(solution)/shard_map/all_gather | solution.py:301
  219.1 65.1 %collective-permute-start.3 = (bf16[704,2048]{1,0:T(8,128)(2,1)}, bf16[704,2048]{1,0:T(8,128)(2,1)}, u32[]{:S(2)}, u32[]{:S(2)}) collective-permute-start(bf16[704,2048]{1,0:T(8,128)(2,1)} %bitcast.462), channel_id=1, source_target_pairs={{0,8},{8,0},{16,24},{24,16},{1,9},{9,1},{17,25},{25,17},{2,10},{10... | collective-permute-start | bytes 8650760 | tf_op jit(solution)/shard_map/ppermute | solution.py:246
  220.1 64.8 %collective-permute-start.4 = (bf16[704,2048]{1,0:T(8,128)(2,1)}, bf16[704,2048]{1,0:T(8,128)(2,1)}, u32[]{:S(2)}, u32[]{:S(2)}) collective-permute-start(bf16[704,2048]{1,0:T(8,128)(2,1)} %bitcast.463), channel_id=1, source_target_pairs={{0,16},{8,24},{16,0},{24,8},{1,17},{9,25},{17,1},{25,9},{2,18},{10... | collective-permute-start | bytes 8650760 | tf_op jit(solution)/shard_map/ppermute | solution.py:246
  408.8 165.6 %all-gather.12.cloned.1.call-start = ((), (), s32[]{:S(2)}) async-start(), calls=%async_computation.18 | async-start | bytes 9437184 | tf_op jit(solution)/shard_map/all_gather | solution.py:301
  409.4 529.3 %reduce-scatter.6.cloned.1.call-start = ((), (), s32[]{:S(2)}) async-start(), calls=%async_computation.20 | async-start | bytes 9437184 | tf_op jit(solution)/shard_map/reduce_scatter | solution.py:304
  411.2 190.0 %collective-permute-start.10 = (bf16[1408,2048]{0,1:T(8,128)(2,1)}, bf16[1408,2048]{0,1:T(8,128)(2,1)}, u32[]{:S(2)}, u32[]{:S(2)}) collective-permute-start(bf16[1408,2048]{0,1:T(8,128)(2,1)} %bitcast.410), channel_id=1, source_target_pairs={{0,8},{8,0},{16,24},{24,16},{1,9},{9,1},{17,25},{25,17},{2,10},{10... | collective-permute-start | bytes 17301512 | tf_op jit(solution)/shard_map/ppermute | solution.py:246
  412.7 227.8 %collective-permute-start.11 = (bf16[1408,2048]{0,1:T(8,128)(2,1)}, bf16[1408,2048]{0,1:T(8,128)(2,1)}, u32[]{:S(2)}, u32[]{:S(2)}) collective-permute-start(bf16[1408,2048]{0,1:T(8,128)(2,1)} %bitcast.411), channel_id=1, source_target_pairs={{0,16},{8,24},{16,0},{24,8},{1,17},{9,25},{17,1},{25,9},{2,18},{10... | collective-permute-start | bytes 17301512 | tf_op jit(solution)/shard_map/ppermute | solution.py:246
  678.3 71.4 %collective-permute-start.13 = (bf16[704,2048]{1,0:T(8,128)(2,1)}, bf16[704,2048]{1,0:T(8,128)(2,1)}, u32[]{:S(2)}, u32[]{:S(2)}) collective-permute-start(bf16[704,2048]{1,0:T(8,128)(2,1)} %copy.634), channel_id=1, source_target_pairs={{0,8},{8,0},{16,24},{24,16},{1,9},{9,1},{17,25},{25,17},{2,10},{10... | collective-permute-start | bytes 8650760 | tf_op jit(solution)/shard_map/ppermute | solution.py:246
  684.7 64.6 %collective-permute-start.12 = (bf16[704,2048]{1,0:T(8,128)(2,1)}, bf16[704,2048]{1,0:T(8,128)(2,1)S(1)}, u32[]{:S(2)}, u32[]{:S(2)}) collective-permute-start(bf16[704,2048]{1,0:T(8,128)(2,1)} %copy.633), channel_id=1, source_target_pairs={{0,16},{8,24},{16,0},{24,8},{1,17},{9,25},{17,1},{25,9},{2,18},{10... | collective-permute-start | bytes 8650760 | tf_op jit(solution)/shard_map/ppermute | solution.py:246
  803.3 294.8 %reduce-scatter.8.cloned.1.call-start = ((), (), s32[]{:S(2)}) async-start(), calls=%async_computation.21 | async-start | bytes 9437184 | tf_op jit(solution)/shard_map/reduce_scatter | solution.py:304
  817.6 63.6 %collective-permute-start.15 = (bf16[704,2048]{1,0:T(8,128)(2,1)S(1)}, bf16[704,2048]{1,0:T(8,128)(2,1)S(1)}, u32[]{:S(2)}, u32[]{:S(2)}) collective-permute-start(bf16[704,2048]{1,0:T(8,128)(2,1)S(1)} %convolution_convert_fusion.26), channel_id=1, source_target_pairs={{0,16},{8,24},{16,0},{24,8},{1,17},{9,25},{17,1},{25,9},{2,18},{10... | collective-permute-start | bytes 8650760 | tf_op jit(solution)/shard_map/ppermute | solution.py:246
  819.1 63.2 %collective-permute-start.14 = (bf16[704,2048]{1,0:T(8,128)(2,1)S(1)}, bf16[704,2048]{1,0:T(8,128)(2,1)S(1)}, u32[]{:S(2)}, u32[]{:S(2)}) collective-permute-start(bf16[704,2048]{1,0:T(8,128)(2,1)S(1)} %convolution_convert_fusion.27), channel_id=1, source_target_pairs={{0,8},{8,0},{16,24},{24,16},{1,9},{9,1},{17,25},{25,17},{2,10},{10... | collective-permute-start | bytes 8650760 | tf_op jit(solution)/shard_map/ppermute | solution.py:246
  916.2 254.2 %reduce-scatter.10.cloned.1.call-start = ((), (), s32[]{:S(2)}) async-start(), calls=%async_computation.22 | async-start | bytes 9437184 | tf_op jit(solution)/shard_map/reduce_scatter | solution.py:304
  1017.5 346.1 %reduce-scatter.12.cloned.1.call-start = ((), (), s32[]{:S(2)}) async-start(), calls=%async_computation.23 | async-start | bytes 4718592 | tf_op jit(solution)/shard_map/reduce_scatter | solution.py:304
  1017.6 65.7 %collective-permute-start.19 = (bf16[704,2048]{1,0:T(8,128)(2,1)}, bf16[704,2048]{1,0:T(8,128)(2,1)}, u32[]{:S(2)}, u32[]{:S(2)}) collective-permute-start(bf16[704,2048]{1,0:T(8,128)(2,1)} %convolution_convert_fusion.23), channel_id=1, source_target_pairs={{0,8},{8,0},{16,24},{24,16},{1,9},{9,1},{17,25},{25,17},{2,10},{10... | collective-permute-start | bytes 8650760 | tf_op jit(solution)/shard_map/ppermute | solution.py:246
  1018.6 65.7 %collective-permute-start.20 = (bf16[704,2048]{1,0:T(8,128)(2,1)}, bf16[704,2048]{1,0:T(8,128)(2,1)}, u32[]{:S(2)}, u32[]{:S(2)}) collective-permute-start(bf16[704,2048]{1,0:T(8,128)(2,1)} %convolution_convert_fusion.20), channel_id=1, source_target_pairs={{0,16},{8,24},{16,0},{24,8},{1,17},{9,25},{17,1},{25,9},{2,18},{10... | collective-permute-start | bytes 8650760 | tf_op jit(solution)/shard_map/ppermute | solution.py:246
  1026.5 117.1 %collective-permute-start.22 = (bf16[704,2048]{1,0:T(8,128)(2,1)}, bf16[704,2048]{1,0:T(8,128)(2,1)}, u32[]{:S(2)}, u32[]{:S(2)}) collective-permute-start(bf16[704,2048]{1,0:T(8,128)(2,1)} %add_convert_fusion.3), channel_id=1, source_target_pairs={{0,8},{8,0},{16,24},{24,16},{1,9},{9,1},{17,25},{25,17},{2,10},{10... | collective-permute-start | bytes 8650760 | tf_op jit(solution)/shard_map/ppermute | solution.py:246
  1029.3 114.3 %collective-permute-start.21 = (bf16[704,2048]{1,0:T(8,128)(2,1)}, bf16[704,2048]{1,0:T(8,128)(2,1)}, u32[]{:S(2)}, u32[]{:S(2)}) collective-permute-start(bf16[704,2048]{1,0:T(8,128)(2,1)} %add_convert_fusion.4), channel_id=1, source_target_pairs={{0,16},{8,24},{16,0},{24,8},{1,17},{9,25},{17,1},{25,9},{2,18},{10... | collective-permute-start | bytes 8650760 | tf_op jit(solution)/shard_map/ppermute | solution.py:246
  1148.6 305.5 %reduce-scatter.14.cloned.1.call-start = ((), (), s32[]{:S(2)}) async-start(), calls=%async_computation.24 | async-start | bytes 9437184 | tf_op jit(solution)/shard_map/reduce_scatter | solution.py:304
  1157.1 134.7 %collective-permute-start.37 = (bf16[352,2048]{1,0:T(8,128)(2,1)}, bf16[352,2048]{1,0:T(8,128)(2,1)}, u32[]{:S(2)}, u32[]{:S(2)}) collective-permute-start(bf16[352,2048]{1,0:T(8,128)(2,1)} %convolution_convert_fusion.31), channel_id=1, source_target_pairs={{0,8},{8,0},{16,24},{24,16},{1,9},{9,1},{17,25},{25,17},{2,10},{10... | collective-permute-start | bytes 4325384 | tf_op jit(solution)/shard_map/ppermute | solution.py:246
  1187.5 142.0 %collective-permute-start.30 = (bf16[352,2048]{1,0:T(8,128)(2,1)}, bf16[352,2048]{1,0:T(8,128)(2,1)}, u32[]{:S(2)}, u32[]{:S(2)}) collective-permute-start(bf16[352,2048]{1,0:T(8,128)(2,1)} %convolution_convert_fusion.34), channel_id=1, source_target_pairs={{0,16},{8,24},{16,0},{24,8},{1,17},{9,25},{17,1},{25,9},{2,18},{10... | collective-permute-start | bytes 4325384 | tf_op jit(solution)/shard_map/ppermute | solution.py:246
  1197.4 88.1 %collective-permute-start.23 = (bf16[256,2176]{1,0:T(8,128)(2,1)}, bf16[256,2176]{1,0:T(8,128)(2,1)}, u32[]{:S(2)}, u32[]{:S(2)}) collective-permute-start(bf16[256,2176]{1,0:T(8,128)(2,1)} %get-tuple-element.357), channel_id=1, source_target_pairs={{0,8},{8,0},{16,24},{24,16},{1,9},{9,1},{17,25},{25,17},{2,10},{10... | collective-permute-start | bytes 3342344 | tf_op jit(solution)/shard_map/ppermute | solution.py:246
  1200.2 85.5 %collective-permute-start.24 = (bf16[256,2176]{1,0:T(8,128)(2,1)}, bf16[256,2176]{1,0:T(8,128)(2,1)}, u32[]{:S(2)}, u32[]{:S(2)}) collective-permute-start(bf16[256,2176]{1,0:T(8,128)(2,1)} %get-tuple-element.359), channel_id=1, source_target_pairs={{0,16},{8,24},{16,0},{24,8},{1,17},{9,25},{17,1},{25,9},{2,18},{10... | collective-permute-start | bytes 3342344 | tf_op jit(solution)/shard_map/ppermute | solution.py:246
  1204.2 83.2 %collective-permute-start.25 = (bf16[256,2176]{1,0:T(8,128)(2,1)}, bf16[256,2176]{1,0:T(8,128)(2,1)}, u32[]{:S(2)}, u32[]{:S(2)}) collective-permute-start(bf16[256,2176]{1,0:T(8,128)(2,1)} %get-tuple-element.358), channel_id=1, source_target_pairs={{0,24},{8,16},{16,8},{24,0},{1,25},{9,17},{17,9},{25,1},{2,26},{10... | collective-permute-start | bytes 3342344 | tf_op jit(solution)/shard_map/ppermute | solution.py:246
  1263.0 100.6 %all-to-all-start.7 = ((bf16[8,704,256]{2,1,0:T(8,128)(2,1)}), bf16[8,704,256]{2,1,0:T(8,128)(2,1)S(1)}, u32[]{:S(2)}, u32[]{:S(2)}) async-start(bf16[8,704,256]{2,1,0:T(8,128)(2,1)} %bitcast.358), calls=%async_computation.10 | async-start | bytes 5767168 | tf_op jit(solution)/shard_map/all_to_all | solution.py:291
  1296.4 110.4 %collective-permute-start.38 = (bf16[352,2048]{1,0:T(8,128)(2,1)}, bf16[352,2048]{1,0:T(8,128)(2,1)}, u32[]{:S(2)}, u32[]{:S(2)}) collective-permute-start(bf16[352,2048]{1,0:T(8,128)(2,1)} %add_convert_fusion.6), channel_id=1, source_target_pairs={{0,16},{8,24},{16,0},{24,8},{1,17},{9,25},{17,1},{25,9},{2,18},{10... | collective-permute-start | bytes 4325384 | tf_op jit(solution)/shard_map/ppermute | solution.py:246
  1323.5 86.0 %collective-permute-start.40 = (bf16[352,2048]{1,0:T(8,128)(2,1)}, bf16[352,2048]{1,0:T(8,128)(2,1)}, u32[]{:S(2)}, u32[]{:S(2)}) collective-permute-start(bf16[352,2048]{1,0:T(8,128)(2,1)} %add_convert_fusion.5), channel_id=1, source_target_pairs={{0,8},{8,0},{16,24},{24,16},{1,9},{9,1},{17,25},{25,17},{2,10},{10... | collective-permute-start | bytes 4325384 | tf_op jit(solution)/shard_map/ppermute | solution.py:246
  1367.2 70.5 %all-to-all-start.8 = ((bf16[8,704,256]{2,1,0:T(8,128)(2,1)}), bf16[8,704,256]{2,1,0:T(8,128)(2,1)}, u32[]{:S(2)}, u32[]{:S(2)}) async-start(bf16[8,704,256]{2,1,0:T(8,128)(2,1)} %bitcast.333), calls=%async_computation.12 | async-start | bytes 5767168 | tf_op jit(solution)/shard_map/all_to_all | solution.py:291
  (180 other events, 3254.4 us)
Sparse Core Ops, SparseCore 0:
  28.1 51.4 all-gather.5
  81.8 103.6 all-gather.7
  193.4 134.1 all-gather.9
  408.9 83.4 all-gather.13
  493.8 80.5 all-gather.11
  803.4 87.0 reduce-scatter.5
  911.5 87.9 reduce-scatter.7
  1017.6 87.0 reduce-scatter.9
  1148.7 47.4 reduce-scatter.11
  1198.4 132.2 reduce-scatter.13

commit v5 on v4

--- a/solution.py
+++ b/solution.py
@@ -211,6 +211,48 @@
     )(g_raw, routes, gates, queries, keys, values, mixed, log_total, cosine, sine, q_blocks, k_blocks)
 
 
+def expert_kernel(row_ref, cot_ref, gate_ref, wide_ref, down_ref, hidden_ref, grad_ref, back_ref, slot_ref):
+    half = down_ref.shape[0]
+    rows = row_ref[...]
+    gate_pre, up_pre = dot_nt(wide_ref[:half], rows), dot_nt(wide_ref[half:], rows)
+    grad_hidden = dot_nt(down_ref[...], cot_ref[...])
+    sigma = 1.0 / (1.0 + jnp.exp(-gate_pre))
+    silu = gate_pre * sigma
+    hidden = silu * up_pre
+    slot_ref[...] = jnp.sum(grad_hidden * hidden, axis=0, keepdims=True)
+    gate = gate_ref[...]
+    grad_hidden = grad_hidden * gate
+    hidden_ref[...] = (hidden * gate).astype(BF)
+    grad_ref[:half] = (grad_hidden * up_pre * sigma * (1.0 + gate_pre * (1.0 - sigma))).astype(BF)
+    grad_ref[half:] = (grad_hidden * silu).astype(BF)
+    back_ref[...] = dot_tn(grad_ref[...], wide_ref[...]).astype(BF)
+
+
+def expert_pass(rows, cot_rows, gates, wide, down):
+    count, width = rows.shape
+    half = down.shape[0]
+    tile = 256
+    kept = lambda shape: pl.BlockSpec(shape, lambda i: (0, 0), pipeline_mode=pl.Buffered(1))
+    tiled = pl.BlockSpec((tile, width), lambda i: (i, 0))
+    turned = lambda size: pl.BlockSpec((size, tile), lambda i: (0, i))
+    return pl.pallas_call(
+        expert_kernel,
+        grid=(count // tile,),
+        in_specs=[tiled, tiled, turned(1), kept(wide.shape), kept(down.shape)],
+        out_specs=[turned(half), turned(2 * half), tiled, turned(1)],
+        out_shape=[
+            jax.ShapeDtypeStruct((half, count), BF),
+            jax.ShapeDtypeStruct((2 * half, count), BF),
+            jax.ShapeDtypeStruct((count, width), BF),
+            jax.ShapeDtypeStruct((1, count), F32),
+        ],
+        cost_estimate=pl.CostEstimate(
+            flops=10 * count * width * half, transcendentals=count * half, bytes_accessed=6 * count * width + 6 * half * width
+        ),
+        name="expert_pass",
+    )(rows, cot_rows, gates, wide, down)
+
+
 def pick(table, routes, ids):
     parts = jnp.split(table, len(ids), axis=1)
     return [sum(jnp.where(routes[:, j:j + 1] == e, part, 0.0) for e, part in zip(ids, parts)) for j in range(TOPK)]
@@ -342,14 +384,15 @@
 
     notes = jnp.concatenate([blocks[0][:, None], attn_routes[0]], axis=1).astype(BF)
     carried = jnp.concatenate([inputs[0], jnp.pad(notes, ((0, 0), (0, 128 - 1 - TOPK)))], axis=1)
-    carried = lax.optimization_barrier(spread(carried))
+    carried, down_w = lax.optimization_barrier((spread(carried), w_down[0]))
     query_w = gather_shard(to_heads(w_query[0]))
 
     hidden_units = w_down.shape[1]
     turned = jnp.stack([w_gate[0].T.reshape(n_s, hidden_units, -1), w_up[0].T.reshape(n_s, hidden_units, -1)], axis=1)
-    turned = shuffle(after(turned, query_w), "shard").reshape(n_s, 2 * hidden_units, -1)
+    down_w = fetch(down_w)
+    turned, query_w = lax.optimization_barrier((turned, query_w))
+    turned = shuffle(turned, "shard").reshape(n_s, 2 * hidden_units, -1)
     gate_up_own = turned.transpose(1, 0, 2).reshape(2 * hidden_units, width)
-    down_w = fetch(w_down[0])
 
     own = inputs[0].astype(F32)
     cot = cotangent[0]
@@ -365,12 +408,13 @@
     key_value, out_w = lax.optimization_barrier((key_value, w_out[0]))
     out_rows = out_w.shape[0]
     turned = shuffle(out_w.T, "shard").reshape(n_s, width // n_s, out_rows).transpose(1, 0, 2)
-    out_wt = gather_shard(to_heads(turned.reshape(width // n_s, n_s * out_rows)))
+    turned = to_heads(turned.reshape(width // n_s, n_s * out_rows))
+    turned, *down_w = lax.optimization_barrier((turned, *down_w))
+    down_w = fetch_rest(down_w)
+    out_wt = gather_shard(turned)
     gate_pair = jnp.concatenate(gates_a, axis=1)
     row_blocks, key_blocks = seq_blocks.reshape(1, -1), seq_blocks.reshape(-1, 1)
     query_raw = dot(h_attn, query_w)
-    query_raw, *down_w = lax.optimization_barrier((query_raw, *down_w))
-    down_w = fetch_rest(down_w)
     queries, keys, values, mixed, log_total, mixed_all = attend(
         query_raw, key_value, routes_a, gate_pair, cosine, sine, row_blocks, key_blocks
     )
@@ -397,33 +441,27 @@
     selects, hiddens, back_rows_f = [], [], []
     grad_gate_f = [0.0] * TOPK
     grad_pieces = []
+    all_rows = []
     for k in range(n_e):
-        if k == 1:
-            gate_up_w = fetch_rest(gate_up_w, hiddens[0])
         expert = me ^ k
         named = [routes_blocks[:, :, j] == expert for j in range(TOPK)]
         any_named = named[0] | named[1]
         rank = dot(any_named.astype(BF), triangle).astype(jnp.int32) - 1
         hit = (rank[:, None, :] == jnp.arange(capacity, dtype=jnp.int32)[None, :, None]) & any_named[:, None, :]
-        select = hit.astype(BF)
         gate_token = sum(jnp.where(named[j], gates_f[j].reshape(n_s, tokens), 0.0) for j in range(TOPK))
         gate_slot = jnp.sum(jnp.where(hit, gate_token[:, None, :], 0.0), axis=2).reshape(1, -1)
-        rows = rows_of(select, h_blocks)
-        pre = dot_nt(gate_up_w[k], rows)
-        if k == 0:
-            cot_blocks = after(cot_all, pre).reshape(n_s, tokens, width)
-        gate_pre, up_pre = pre[:hidden_units], pre[hidden_units:]
+        all_rows.append((named, hit, gate_slot, rows_of(hit.astype(BF), h_blocks)))
+    cot_all, all_rows, gate_up_w = lax.optimization_barrier((cot_all, all_rows, gate_up_w))
+    cot_blocks = cot_all.reshape(n_s, tokens, width)
+    gate_up_w = fetch_rest(gate_up_w)
+    for k in range(n_e):
+        named, hit, gate_slot, rows = all_rows[k]
+        select = hit.astype(BF)
         cot_rows = rows_of(select, cot_blocks)
-        grad_hidden = dot_nt(down_w[k], cot_rows)
-        sigma = 1.0 / (1.0 + jnp.exp(-gate_pre))
-        silu = gate_pre * sigma
-        hidden = silu * up_pre
-        grad_slot = jnp.sum(grad_hidden * hidden, axis=0).reshape(n_s, capacity)
-        grad_hidden = grad_hidden * gate_slot
-        hidden = (hidden * gate_slot).astype(BF)
-        grad_gate = (grad_hidden * up_pre * sigma * (1.0 + gate_pre * (1.0 - sigma))).astype(BF)
-        grad_pre = jnp.concatenate([grad_gate, (grad_hidden * silu).astype(BF)], axis=0)
-        back = dot_tn(grad_pre, gate_up_w[k]).astype(BF)
+        if k == 2 and n_e == 4:
+            cot_rows, gate_up_w[3] = lax.optimization_barrier((cot_rows, gate_up_w[3]))
+        hidden, grad_pre, back, grad_slot = expert_pass(rows, cot_rows, gate_slot, gate_up_w[k], down_w[k])
+        grad_slot = grad_slot.reshape(n_s, capacity)
         selects.append(select)
         back_rows_f.append(back.reshape(n_s, capacity, width))
         hiddens.append(hidden)
@@ -450,7 +488,7 @@
     halves = deliver_first(grad_gate_up[n_e - 1])
     out_rows_f = []
     for k in range(n_e):
-        hidden = after(hiddens[k], *(grad_gate_up[n_e - 1] if k < 2 else halves))
+        hidden = after(hiddens[k], *(grad_gate_up[n_e - 1] if k < n_e - 1 else halves))
         out_rows_f.append(dot_tn(hidden, down_w[k]).astype(BF).reshape(n_s, capacity, width))
     out_sum = tokens_of(out_rows_f)
     ffn_out = scatter_shard(out_sum)
@@ -491,17 +529,16 @@
         grad_mixed, routes_a, gate_pair, queries, keys, values, mixed, log_total, cosine, sine, row_blocks, key_blocks
     )
     grad_query_all, *near = lax.optimization_barrier((grad_query_all, *near))
+    key_value_grad, query_grad = dot_tn(h_attn, grad_key_value).astype(BF), dot_tn(h_attn, grad_query_all).astype(BF)
+    grad_query_all, key_value_grad, query_grad = lax.optimization_barrier((grad_query_all, key_value_grad, query_grad))
     back_a = (dot_nt(grad_query_all, query_w) + dot_nt(grad_key_value, key_value_w)).astype(BF)
     back_a = jnp.concatenate([back_a, gate_notes], axis=1)
-    value = scatter_shard(grad_out_wt)
     back_a, ffn_out, *last = lax.optimization_barrier((back_a, ffn_out, *last))
     gate_up_total = [v.astype(BF) for v in total(grad_gate_up[0], near, last)]
     outputs = (middle + ffn_out.astype(F32) + bias_f).astype(BF)[None]
-    key_value_grad = after(dot_tn(h_attn, grad_key_value).astype(BF), back_a)
+    value = scatter_shard(grad_out_wt)
     key_value_grad = key_value_grad.reshape(n_e, n_s, small_rows, 2 * group).transpose(1, 0, 2, 3)
     key_value_grad = scatter_shard(key_value_grad.reshape(n_s * n_e * small_rows, 2 * group))
-    query_grad = dot_tn(h_attn, grad_query_all).astype(BF)
-    query_grad, value = lax.optimization_barrier((query_grad, value))
     query_grad = scatter_shard(query_grad)
     value = from_heads(value).reshape(width // n_s, n_s, out_rows).transpose(1, 0, 2)
 
@@ -530,7 +567,7 @@
     gate_grads = back_a[:, width:width + TOPK] + back_a[:, width + TOPK:width + 2 * TOPK]
     grad_gates_a = [gate_grads[:, j:j + 1] for j in range(TOPK)]
     back_a = back_a[:, :width]
-    grad_query_w = from_heads(query_grad).astype(F32)[None]
+    grad_query_w = from_heads(query_grad)
     grad_gate_w = gate_turned.T.astype(F32)[None]
 
     h_own = h_attn[:tokens]
@@ -547,7 +584,8 @@
         + [v[:, None] for v in (grad_gain_a, grad_gain_f, grad_bias_a, grad_bias_f)],
         axis=1,
     )
-    shared, up_turned = lax.optimization_barrier((shared, up_turned))
+    shared, up_turned, grad_query_w = lax.optimization_barrier((shared, up_turned, grad_query_w))
+    grad_query_w = grad_query_w.astype(F32)[None]
     grad_up_w = up_turned.T.astype(F32)[None]
     shared = shuffle(shared.reshape(n_e * n_s, -1), ("expert", "shard"))
     shared = jnp.sum(shared, axis=0).reshape(small_rows, small_width)

time: 1490 us -> 1400 us (0.940)
  Pallas kernels: 59.4 us -> 200 us
  matrix products: 422 us -> 285 us
  waiting for transfers between devices: 511 us -> 477 us
  other arithmetic: 139 us -> 111 us
  blocking collectives: 87.5 us -> 70.4 us
    pallas_call x0 -> x4, Pallas kernels: none -> 140 us  [expert_pass(): pl.pallas_call(expert_kernel, grid=(count // tile,), in_specs=[tiled, til...]
    dot_general x11 -> x3, matrix products: 112 us -> 33.2 us  [dot_nt(): lax.dot_general(a, b, (((1,), (1,)), ((), ())), preferred_element_type=F32)]
    dot_general x13 -> x9, matrix products: 112 us -> 63.5 us  [dot_tn(): lax.dot_general(a, b, (((0,), (0,)), ((), ())), precision=precision, pref...]
    convert_element_type x5 -> x0, other arithmetic: 26.2 us -> none  [the longest x4 26 us: local(): (grad_hidden * up_pre * sigma * (1.0 + gate_pre * (1.0 - sigma))).astype(BF)]
    all_to_all x7 -> x8, waiting for transfers between devices: 130 us -> 104 us  [shuffle(): return lax.all_to_all(value, axis, split_axis=0, concat_axis=0, tiled=True)]
    ppermute x41, waiting for transfers between devices: 247 us -> 228 us  [swap(): return lax.ppermute(value, 'expert', [(i, i ^ k) for i in range(n_e)])]
    all_to_all x3 -> x2, blocking collectives: 87.5 us -> 70.4 us  [shuffle(): return lax.all_to_all(value, axis, split_axis=0, concat_axis=0, tiled=True)]
    unnamed x331 -> x273, local copies, waits for them, and re-layouts: 51.4 us -> 41.6 us
  transfers between devices with their start and end apart: 58 -> 59, of which waited for: 25 -> 26; matrix products, arithmetic and copies ran while one was open for 41% -> 35% of each run, Pallas kernels for 4% -> 9%
where the time goes in v5:
time: 1400 us
  waiting for transfers between devices  477 us (34%)
  matrix products  285 us (20%)
  Pallas kernels  200 us (14%)
  local copies, waits for them, and re-layouts  160 us (11%)
  other arithmetic  111 us (8%)
  starting transfers between devices  81.6 us (6%)
  blocking collectives  70.4 us (5%)
  between operations  16.6 us (1%)
    ppermute x41, waiting for transfers between devices, swap(): return lax.ppermute(value, 'expert', [(i, i ^ k) for i in range(n_e)])  228 us
    all_gather x5, waiting for transfers between devices, gather_shard(): return lax.all_gather(value, 'shard', axis=0, tiled=True)  145 us
    pallas_call x4, Pallas kernels, expert_pass(): pl.pallas_call(expert_kernel, grid=(count // tile,), in_specs=[tiled, til...  140 us
    dot_general x26, matrix products, dot(): return jnp.dot(a, b, preferred_element_type=F32)  117 us
    all_to_all x8, waiting for transfers between devices, shuffle(): return lax.all_to_all(value, axis, split_axis=0, concat_axis=0, tiled=True)  104 us
    all_to_all x2, blocking collectives, shuffle(): return lax.all_to_all(value, axis, split_axis=0, concat_axis=0, tiled=True)  70.4 us
    dot_general x9, matrix products, dot_tn(): lax.dot_general(a, b, (((0,), (0,)), ((), ())), precision=precision, pref...  63.5 us
    ppermute x41, starting transfers between devices, swap(): return lax.ppermute(value, 'expert', [(i, i ^ k) for i in range(n_e)])  47.4 us
  transfers between devices with their start and end apart: 59, of which 26 were waited for; matrix products, arithmetic and copies ran while one was open for 35% of the time, Pallas kernels for 9%

profile of v5, /device:TPU:0, one launch (start us, length us, event | category | flops | bytes accessed | tf_op | source)
XLA Modules:
  0.0 1400.8 jit_solution(6086250134759784389)
XLA Ops:
  17.7 8.6 all-to-all-done
  29.2 16.1 %all_to_all.63 = bf16[4,256,512]{2,1,0:T(8,128)(2,1)S(1)} all-to-all(bf16[4,256,512]{2,1,0:T(8,128)(2,1)S(1)} %copy.594), channel_id=1, replica_groups=mesh['expert'=4,'shard'=8] {'expert'}, dimensions={0} | all-to-all | bytes 2097152 | tf_op jit(solution)/shard_map/all_to_all | solution.py:333
  53.2 23.6 %collective-permute-done.2 = bf16[256,2176]{1,0:T(8,128)(2,1)S(1)} collective-permute-done((bf16[256,2176]{1,0:T(8,128)(2,1)}, bf16[256,2176]{1,0:T(8,128)(2,1)S(1)}, u32[]{:S(2)}, u32[]{:S(2)}) %collective-permute-start.2) | collective-permute-done | bytes 1114144 | tf_op jit(solution)/shard_map/ppermute | solution.py:288
  76.7 20.7 %collective-permute-done.1 = bf16[256,2176]{1,0:T(8,128)(2,1)} collective-permute-done((bf16[256,2176]{1,0:T(8,128)(2,1)}, bf16[256,2176]{1,0:T(8,128)(2,1)}, u32[]{:S(2)}, u32[]{:S(2)}) %collective-permute-start.1) | collective-permute-done | bytes 1114144 | tf_op jit(solution)/shard_map/ppermute | solution.py:288
  121.9 54.3 %all_to_all.64 = bf16[8,256,256]{2,1,0:T(8,128)(2,1)S(1)} all-to-all(bf16[8,256,256]{2,1,0:T(8,128)(2,1)S(1)} %bitcast.352), channel_id=1, replica_groups=mesh['expert'=4,'shard'=8] {'shard'}, dimensions={0} | all-to-all | bytes 2097152 | tf_op jit(solution)/shard_map/all_to_all | solution.py:333
  181.1 13.8 all-to-all-done.3
  239.0 22.2 %collective-permute-done.6 = bf16[352,2048]{1,0:T(8,128)(2,1)S(1)} collective-permute-done((bf16[352,2048]{1,0:T(8,128)(2,1)S(1)}, bf16[352,2048]{1,0:T(8,128)(2,1)S(1)}, u32[]{:S(2)}, u32[]{:S(2)}) %collective-permute-start.6) | collective-permute-done | bytes 1441824 | tf_op jit(solution)/shard_map/ppermute | solution.py:288
  265.7 11.0 fusion.115.q_ref
  276.8 26.6 %attend.1 = (bf16[2,1024,512]{2,1,0:T(8,128)(2,1)}, bf16[1024,512]{1,0:T(8,128)(2,1)}, bf16[1024,512]{1,0:T(8,128)(2,1)}, bf16[2,1024,512]{2,1,0:T(8,128)(2,1)},...) custom-call(f32[1024,2048]{1,0:T(8,128)} %fusion.115.q_ref, f32[1024,1024]{1,0:T(8,128)} %fusion.26.kv_ref, ...), custom_call_target="tpu_custom_call" | custom-call | flops 1048576 | bytes 4194304 | tf_op jit(solution)/shard_map/attend/pallas_call | solution.py:109
  303.3 27.6 %all-gather.10.cloned.1.call-done = bf16[2048,2048]{0,1:T(8,128)(2,1)} async-done(((bf16[256,2048]{0,1:T(8,128)(2,1)}), bf16[2048,2048]{0,1:T(8,128)(2,1)}) %all-gather.10.cloned.1.call-update) | async-done | bytes 8388624 | tf_op jit(solution)/shard_map/all_gather | solution.py:343
  330.9 12.6 convolution_convert_fusion.14
  352.6 45.3 %all-to-all-done.4 = bf16[8,2,704,256]{3,2,1,0:T(8,128)(2,1)} async-done(((bf16[8,2,704,256]{3,2,1,0:T(8,128)(2,1)}), bf16[8,2,704,256]{3,2,1,0:T(8,128)(2,1)}, u32[]{:S(2)}, u32[]{:S(2)}) %all-to-all-start.4) | async-done | bytes 5767200 | tf_op jit(solution)/shard_map/all_to_all | solution.py:333
  415.0 79.9 %all-gather.14.cloned.1.call-done = bf16[2048,2048]{1,0:T(8,128)(2,1)} async-done(((bf16[256,2048]{1,0:T(8,128)(2,1)}), bf16[2048,2048]{1,0:T(8,128)(2,1)}) %all-gather.14.cloned.1.call-update) | async-done | bytes 8388624 | tf_op jit(solution)/shard_map/all_gather | solution.py:343
  539.7 37.2 %all-gather.12.cloned.1.call-done = bf16[2048,2048]{1,0:T(8,128)(2,1)} async-done(((bf16[256,2048]{1,0:T(8,128)(2,1)}), bf16[2048,2048]{1,0:T(8,128)(2,1)}) %all-gather.12.cloned.1.call-update) | async-done | bytes 8388624 | tf_op jit(solution)/shard_map/all_gather | solution.py:343
  606.6 34.8 %expert_pass.5 = (bf16[704,1280]{1,0:T(8,128)(2,1)}, bf16[1408,1280]{1,0:T(8,128)(2,1)}, bf16[1280,2048]{1,0:T(8,128)(2,1)}, f32[1,1280]{1,0:T(1,128)}) custom-call(bf16[1280,2048]{1,0:T(8,128)(2,1)} %bitcast.327, bf16[1280,2048]{1,0:T(8,128)(2,1)} %bitcast.292, f32[1,1280]{1,0:T(1,128)} %reshape.481.gate_ref, ...), custom_call_target="tpu_custom_call" | custom-call | flops 18454937600 | bytes 24379392 | tf_op jit(solution)/shard_map/expert_pass/pallas_call | solution.py:238
  641.3 35.2 %expert_pass.4 = (bf16[704,1280]{1,0:T(8,128)(2,1)}, bf16[1408,1280]{1,0:T(8,128)(2,1)}, bf16[1280,2048]{1,0:T(8,128)(2,1)}, f32[1,1280]{1,0:T(1,128)}) custom-call(bf16[1280,2048]{1,0:T(8,128)(2,1)} %bitcast.332, bf16[1280,2048]{1,0:T(8,128)(2,1)} %bitcast.297, f32[1,1280]{1,0:T(1,128)} %reshape.478.gate_ref, bf16[1408,2048]{1,0:T(8,128)(2,1)} %bitcast.344, ...), custom_call_target="tpu_custom_call" | custom-call | flops 18454937600 | bytes 24379392 | tf_op jit(solution)/shard_map/expert_pass/pallas_call | solution.py:238
  682.7 34.7 %expert_pass.6 = (bf16[704,1280]{1,0:T(8,128)(2,1)}, bf16[1408,1280]{1,0:T(8,128)(2,1)}, bf16[1280,2048]{1,0:T(8,128)(2,1)}, f32[1,1280]{1,0:T(1,128)}) custom-call(bf16[1280,2048]{1,0:T(8,128)(2,1)} %bitcast.322, bf16[1280,2048]{1,0:T(8,128)(2,1)} %bitcast.287, f32[1,1280]{1,0:T(1,128)} %reshape.483.gate_ref, ...), custom_call_target="tpu_custom_call" | custom-call | flops 18454937600 | bytes 24379392 | tf_op jit(solution)/shard_map/expert_pass/pallas_call | solution.py:238
  717.4 34.9 %expert_pass.7 = (bf16[704,1280]{1,0:T(8,128)(2,1)}, bf16[1408,1280]{1,0:T(8,128)(2,1)}, bf16[1280,2048]{1,0:T(8,128)(2,1)}, f32[1,1280]{1,0:T(1,128)}) custom-call(bf16[1280,2048]{1,0:T(8,128)(2,1)} %bitcast.337, bf16[1280,2048]{1,0:T(8,128)(2,1)} %bitcast.300, f32[1,1280]{1,0:T(1,128)} %reshape.485.gate_ref, ...), custom_call_target="tpu_custom_call" | custom-call | flops 18454937600 | bytes 24379392 | tf_op jit(solution)/shard_map/expert_pass/pallas_call | solution.py:238
  752.4 13.8 fusion.22
  801.4 40.5 %collective-permute-done.14 = bf16[704,2048]{1,0:T(8,128)(2,1)S(1)} collective-permute-done((bf16[704,2048]{1,0:T(8,128)(2,1)S(1)}, bf16[704,2048]{1,0:T(8,128)(2,1)S(1)}, u32[]{:S(2)}, u32[]{:S(2)}) %collective-permute-start.14) | collective-permute-done | bytes 2883616 | tf_op jit(solution)/shard_map/ppermute | solution.py:288
  848.2 13.0 fusion.19
  934.3 13.3 collective-permute-done.17
  948.4 11.3 fusion.116.g_ref
  959.6 11.2 convolution_convert_fusion.1
  973.0 33.5 %attend_back.1 = (bf16[1024,2048]{1,0:T(8,128)(2,1)}, bf16[1024,1024]{1,0:T(8,128)(2,1)}, bf16[1024,128]{1,0:T(8,128)(2,1)}) custom-call(f32[1024,2048]{1,0:T(8,128)} %fusion.116.g_ref, s32[1024,2]{1,0:T(8,128)} %slice.255.route_ref, f32[1024,2]{1,0:T(8,128)} %pad_maximum_fusion.8.gate_ref, bf16[2,1024,512]{2,1,0:T(8,128)(2,1)} %get-tuple-element.212.query_ref, ...), custom_call_target="tpu_custom_call" | custom-call | flops 1048576 | bytes 4194304 | tf_op jit(solution)/shard_map/attend_back/pallas_call | solution.py:194
  1006.5 9.6 convolution_convert_fusion.15
  1016.2 19.5 %collective-permute-done.19 = bf16[704,2048]{1,0:T(8,128)(2,1)} collective-permute-done((bf16[704,2048]{1,0:T(8,128)(2,1)}, bf16[704,2048]{1,0:T(8,128)(2,1)}, u32[]{:S(2)}, u32[]{:S(2)}) %collective-permute-start.19) | collective-permute-done | bytes 2883616 | tf_op jit(solution)/shard_map/ppermute | solution.py:288
  1035.8 11.4 convolution_convert_fusion
  1058.7 13.5 fusion.117
  1081.8 35.6 %collective-permute-done.21 = bf16[704,2048]{1,0:T(8,128)(2,1)} collective-permute-done((bf16[704,2048]{1,0:T(8,128)(2,1)S(1)}, bf16[704,2048]{1,0:T(8,128)(2,1)}, u32[]{:S(2)}, u32[]{:S(2)}) %collective-permute-start.21) | collective-permute-done | bytes 2883616 | tf_op jit(solution)/shard_map/ppermute | solution.py:288
  1189.5 26.1 %all-to-all-done.6 = bf16[8,256,256]{1,2,0:T(8,128)(2,1)} async-done(((bf16[8,256,256]{1,2,0:T(8,128)(2,1)}), bf16[8,256,256]{1,2,0:T(8,128)(2,1)}, u32[]{:S(2)}, u32[]{:S(2)}) %all-to-all-start.6) | async-done | bytes 1048608 | tf_op jit(solution)/shard_map/all_to_all | solution.py:333
  1246.4 23.9 %collective-permute-done.37 = bf16[352,2048]{1,0:T(8,128)(2,1)S(1)} collective-permute-done((bf16[352,2048]{1,0:T(8,128)(2,1)S(1)}, bf16[352,2048]{1,0:T(8,128)(2,1)S(1)}, u32[]{:S(2)}, u32[]{:S(2)}) %collective-permute-start.37) | collective-permute-done | bytes 1441824 | tf_op jit(solution)/shard_map/ppermute | solution.py:288
  (632 shorter events, 569.2 us)
Async XLA Ops:
  17.5 90.1 %all-gather.6.cloned.1.call-start = ((), (), s32[]{:S(2)}) async-start(), calls=%async_computation.15 | async-start | bytes 5308416 | tf_op jit(solution)/shard_map/all_gather | solution.py:343
  28.0 183.1 %all-gather.8.cloned.1.call-start = ((), (), s32[]{:S(2)}) async-start(), calls=%async_computation.16 | async-start | bytes 9437184 | tf_op jit(solution)/shard_map/all_gather | solution.py:343
  104.6 76.5 %collective-permute-start.3 = (bf16[704,2048]{1,0:T(8,128)(2,1)}, bf16[704,2048]{1,0:T(8,128)(2,1)}, u32[]{:S(2)}, u32[]{:S(2)}) collective-permute-start(bf16[704,2048]{1,0:T(8,128)(2,1)} %bitcast.3.down_ref), channel_id=1, source_target_pairs={{0,8},{8,0},{16,24},{24,16},{1,9},{9,1},{17,25},{25,17},{2,10},{10... | collective-permute-start | bytes 8650760 | tf_op jit(solution)/shard_map/ppermute | solution.py:288
  106.0 75.1 %collective-permute-start.4 = (bf16[704,2048]{1,0:T(8,128)(2,1)}, bf16[704,2048]{1,0:T(8,128)(2,1)}, u32[]{:S(2)}, u32[]{:S(2)}) collective-permute-start(bf16[704,2048]{1,0:T(8,128)(2,1)} %bitcast.3.down_ref), channel_id=1, source_target_pairs={{0,16},{8,24},{16,0},{24,8},{1,17},{9,25},{17,1},{25,9},{2,18},{10... | collective-permute-start | bytes 8650760 | tf_op jit(solution)/shard_map/ppermute | solution.py:288
  181.0 149.9 %all-gather.10.cloned.1.call-start = ((), (), s32[]{:S(2)}) async-start(), calls=%async_computation.17 | async-start | bytes 9437184 | tf_op jit(solution)/shard_map/all_gather | solution.py:343
  216.7 181.2 %all-to-all-start.4 = ((bf16[8,2,704,256]{3,2,1,0:T(8,128)(2,1)}), bf16[8,2,704,256]{3,2,1,0:T(8,128)(2,1)}, u32[]{:S(2)}, u32[]{:S(2)}) async-start(bf16[8,2,704,256]{3,2,1,0:T(8,128)(2,1)} %copy.602), calls=%async_computation.4 | async-start | bytes 11534336 | tf_op jit(solution)/shard_map/all_to_all | solution.py:333
  221.9 273.0 %all-gather.14.cloned.1.call-start = ((), (), s32[]{:S(2)}) async-start(), calls=%async_computation.19 | async-start | bytes 9437184 | tf_op jit(solution)/shard_map/all_gather | solution.py:343
  347.3 56.6 %collective-permute-start.9 = (bf16[256,2048]{1,0:T(8,128)(2,1)}, bf16[256,2048]{1,0:T(8,128)(2,1)S(1)}, u32[]{:S(2)}, u32[]{:S(2)}) collective-permute-start(bf16[256,2048]{1,0:T(8,128)(2,1)} %get-tuple-element.427), channel_id=1, source_target_pairs={{0,24},{8,16},{16,8},{24,0},{1,25},{9,17},{17,9},{25,1},{2,26},{10... | collective-permute-start | bytes 3145736 | tf_op jit(solution)/shard_map/ppermute | solution.py:288
  409.6 167.2 %all-gather.12.cloned.1.call-start = ((), (), s32[]{:S(2)}) async-start(), calls=%async_computation.18 | async-start | bytes 9437184 | tf_op jit(solution)/shard_map/all_gather | solution.py:343
  410.2 481.6 %reduce-scatter.6.cloned.1.call-start = ((), (), s32[]{:S(2)}) async-start(), calls=%async_computation.20 | async-start | bytes 9437184 | tf_op jit(solution)/shard_map/reduce_scatter | solution.py:346
  412.0 126.5 %collective-permute-start.10 = (bf16[1408,2048]{1,0:T(8,128)(2,1)}, bf16[1408,2048]{1,0:T(8,128)(2,1)}, u32[]{:S(2)}, u32[]{:S(2)}) collective-permute-start(bf16[1408,2048]{1,0:T(8,128)(2,1)} %bitcast.342), channel_id=1, source_target_pairs={{0,8},{8,0},{16,24},{24,16},{1,9},{9,1},{17,25},{25,17},{2,10},{10... | collective-permute-start | bytes 17301512 | tf_op jit(solution)/shard_map/ppermute | solution.py:288
  413.5 126.2 %collective-permute-start.11 = (bf16[1408,2048]{1,0:T(8,128)(2,1)}, bf16[1408,2048]{1,0:T(8,128)(2,1)}, u32[]{:S(2)}, u32[]{:S(2)}) collective-permute-start(bf16[1408,2048]{1,0:T(8,128)(2,1)} %bitcast.343), channel_id=1, source_target_pairs={{0,16},{8,24},{16,0},{24,8},{1,17},{9,25},{17,1},{25,9},{2,18},{10... | collective-permute-start | bytes 17301512 | tf_op jit(solution)/shard_map/ppermute | solution.py:288
  592.0 84.5 %collective-permute-start.13 = (bf16[704,2048]{1,0:T(8,128)(2,1)}, bf16[704,2048]{1,0:T(8,128)(2,1)}, u32[]{:S(2)}, u32[]{:S(2)}) collective-permute-start(bf16[704,2048]{1,0:T(8,128)(2,1)} %slice.271), channel_id=1, source_target_pairs={{0,8},{8,0},{16,24},{24,16},{1,9},{9,1},{17,25},{25,17},{2,10},{10... | collective-permute-start | bytes 8650760 | tf_op jit(solution)/shard_map/ppermute | solution.py:288
  597.2 79.3 %collective-permute-start.12 = (bf16[704,2048]{1,0:T(8,128)(2,1)}, bf16[704,2048]{1,0:T(8,128)(2,1)}, u32[]{:S(2)}, u32[]{:S(2)}) collective-permute-start(bf16[704,2048]{1,0:T(8,128)(2,1)} %slice.270), channel_id=1, source_target_pairs={{0,16},{8,24},{16,0},{24,8},{1,17},{9,25},{17,1},{25,9},{2,18},{10... | collective-permute-start | bytes 8650760 | tf_op jit(solution)/shard_map/ppermute | solution.py:288
  766.2 315.6 %reduce-scatter.8.cloned.1.call-start = ((), (), s32[]{:S(2)}) async-start(), calls=%async_computation.21 | async-start | bytes 9437184 | tf_op jit(solution)/shard_map/reduce_scatter | solution.py:346
  778.2 63.7 %collective-permute-start.14 = (bf16[704,2048]{1,0:T(8,128)(2,1)S(1)}, bf16[704,2048]{1,0:T(8,128)(2,1)S(1)}, u32[]{:S(2)}, u32[]{:S(2)}) collective-permute-start(bf16[704,2048]{1,0:T(8,128)(2,1)S(1)} %convolution_convert_fusion.23), channel_id=1, source_target_pairs={{0,8},{8,0},{16,24},{24,16},{1,9},{9,1},{17,25},{25,17},{2,10},{10... | collective-permute-start | bytes 8650760 | tf_op jit(solution)/shard_map/ppermute | solution.py:288
  778.3 63.8 %collective-permute-start.15 = (bf16[704,2048]{1,0:T(8,128)(2,1)S(1)}, bf16[704,2048]{1,0:T(8,128)(2,1)S(1)}, u32[]{:S(2)}, u32[]{:S(2)}) collective-permute-start(bf16[704,2048]{1,0:T(8,128)(2,1)S(1)} %convolution_convert_fusion.22), channel_id=1, source_target_pairs={{0,16},{8,24},{16,0},{24,8},{1,17},{9,25},{17,1},{25,9},{2,18},{10... | collective-permute-start | bytes 8650760 | tf_op jit(solution)/shard_map/ppermute | solution.py:288
  868.3 267.8 %reduce-scatter.10.cloned.1.call-start = ((), (), s32[]{:S(2)}) async-start(), calls=%async_computation.22 | async-start | bytes 9437184 | tf_op jit(solution)/shard_map/reduce_scatter | solution.py:346
  970.8 302.7 %reduce-scatter.14.cloned.1.call-start = ((), (), s32[]{:S(2)}) async-start(), calls=%async_computation.24 | async-start | bytes 9437184 | tf_op jit(solution)/shard_map/reduce_scatter | solution.py:346
  970.9 64.8 %collective-permute-start.19 = (bf16[704,2048]{1,0:T(8,128)(2,1)}, bf16[704,2048]{1,0:T(8,128)(2,1)}, u32[]{:S(2)}, u32[]{:S(2)}) collective-permute-start(bf16[704,2048]{1,0:T(8,128)(2,1)} %convolution_convert_fusion.19), channel_id=1, source_target_pairs={{0,8},{8,0},{16,24},{24,16},{1,9},{9,1},{17,25},{25,17},{2,10},{10... | collective-permute-start | bytes 8650760 | tf_op jit(solution)/shard_map/ppermute | solution.py:288
  971.6 64.1 %collective-permute-start.20 = (bf16[704,2048]{1,0:T(8,128)(2,1)}, bf16[704,2048]{1,0:T(8,128)(2,1)}, u32[]{:S(2)}, u32[]{:S(2)}) collective-permute-start(bf16[704,2048]{1,0:T(8,128)(2,1)} %convolution_convert_fusion.16), channel_id=1, source_target_pairs={{0,16},{8,24},{16,0},{24,8},{1,17},{9,25},{17,1},{25,9},{2,18},{10... | collective-permute-start | bytes 8650760 | tf_op jit(solution)/shard_map/ppermute | solution.py:288
  1047.2 253.5 %reduce-scatter.12.cloned.1.call-start = ((), (), s32[]{:S(2)}) async-start(), calls=%async_computation.23 | async-start | bytes 4718592 | tf_op jit(solution)/shard_map/reduce_scatter | solution.py:346
  1053.6 63.7 %collective-permute-start.21 = (bf16[704,2048]{1,0:T(8,128)(2,1)S(1)}, bf16[704,2048]{1,0:T(8,128)(2,1)}, u32[]{:S(2)}, u32[]{:S(2)}) collective-permute-start(bf16[704,2048]{1,0:T(8,128)(2,1)S(1)} %add_convert_fusion.4), channel_id=1, source_target_pairs={{0,16},{8,24},{16,0},{24,8},{1,17},{9,25},{17,1},{25,9},{2,18},{10... | collective-permute-start | bytes 8650760 | tf_op jit(solution)/shard_map/ppermute | solution.py:288
  1058.2 63.3 %collective-permute-start.22 = (bf16[704,2048]{1,0:T(8,128)(2,1)}, bf16[704,2048]{1,0:T(8,128)(2,1)}, u32[]{:S(2)}, u32[]{:S(2)}) collective-permute-start(bf16[704,2048]{1,0:T(8,128)(2,1)} %add_convert_fusion.3), channel_id=1, source_target_pairs={{0,8},{8,0},{16,24},{24,16},{1,9},{9,1},{17,25},{25,17},{2,10},{10... | collective-permute-start | bytes 8650760 | tf_op jit(solution)/shard_map/ppermute | solution.py:288
  1125.4 109.8 %collective-permute-start.25 = (bf16[256,2176]{1,0:T(8,128)(2,1)}, bf16[256,2176]{1,0:T(8,128)(2,1)}, u32[]{:S(2)}, u32[]{:S(2)}) collective-permute-start(bf16[256,2176]{1,0:T(8,128)(2,1)} %get-tuple-element.424), channel_id=1, source_target_pairs={{0,24},{8,16},{16,8},{24,0},{1,25},{9,17},{17,9},{25,1},{2,26},{10... | collective-permute-start | bytes 3342344 | tf_op jit(solution)/shard_map/ppermute | solution.py:288
  1149.8 86.7 %collective-permute-start.24 = (bf16[256,2176]{1,0:T(8,128)(2,1)}, bf16[256,2176]{1,0:T(8,128)(2,1)}, u32[]{:S(2)}, u32[]{:S(2)}) collective-permute-start(bf16[256,2176]{1,0:T(8,128)(2,1)} %get-tuple-element.425), channel_id=1, source_target_pairs={{0,16},{8,24},{16,0},{24,8},{1,17},{9,25},{17,1},{25,9},{2,18},{10... | collective-permute-start | bytes 3342344 | tf_op jit(solution)/shard_map/ppermute | solution.py:288
  1158.8 78.9 %collective-permute-start.23 = (bf16[256,2176]{1,0:T(8,128)(2,1)}, bf16[256,2176]{1,0:T(8,128)(2,1)}, u32[]{:S(2)}, u32[]{:S(2)}) collective-permute-start(bf16[256,2176]{1,0:T(8,128)(2,1)} %get-tuple-element.423), channel_id=1, source_target_pairs={{0,8},{8,0},{16,24},{24,16},{1,9},{9,1},{17,25},{25,17},{2,10},{10... | collective-permute-start | bytes 3342344 | tf_op jit(solution)/shard_map/ppermute | solution.py:288
  1160.4 140.3 %collective-permute-start.29 = (bf16[352,2048]{1,0:T(8,128)(2,1)}, bf16[352,2048]{1,0:T(8,128)(2,1)}, u32[]{:S(2)}, u32[]{:S(2)}) collective-permute-start(bf16[352,2048]{1,0:T(8,128)(2,1)} %convolution_convert_fusion.31), channel_id=1, source_target_pairs={{0,8},{8,0},{16,24},{24,16},{1,9},{9,1},{17,25},{25,17},{2,10},{10... | collective-permute-start | bytes 4325384 | tf_op jit(solution)/shard_map/ppermute | solution.py:288
  1165.2 76.6 %collective-permute-start.39 = (bf16[352,2048]{1,0:T(8,128)(2,1)}, bf16[352,2048]{1,0:T(8,128)(2,1)}, u32[]{:S(2)}, u32[]{:S(2)}) collective-permute-start(bf16[352,2048]{1,0:T(8,128)(2,1)} %convolution_convert_fusion.24), channel_id=1, source_target_pairs={{0,16},{8,24},{16,0},{24,8},{1,17},{9,25},{17,1},{25,9},{2,18},{10... | collective-permute-start | bytes 4325384 | tf_op jit(solution)/shard_map/ppermute | solution.py:288
  1219.7 81.0 %all-to-all-start.7 = ((bf16[8,704,256]{2,1,0:T(8,128)(2,1)}), bf16[8,704,256]{2,1,0:T(8,128)(2,1)}, u32[]{:S(2)}, u32[]{:S(2)}) async-start(bf16[8,704,256]{2,1,0:T(8,128)(2,1)} %bitcast.305), calls=%async_computation.10 | async-start | bytes 5767168 | tf_op jit(solution)/shard_map/all_to_all | solution.py:333
  1235.2 65.5 %collective-permute-start.30 = (bf16[352,2048]{1,0:T(8,128)(2,1)}, bf16[352,2048]{1,0:T(8,128)(2,1)}, u32[]{:S(2)}, u32[]{:S(2)}) collective-permute-start(bf16[352,2048]{1,0:T(8,128)(2,1)} %convolution_convert_fusion.30), channel_id=1, source_target_pairs={{0,16},{8,24},{16,0},{24,8},{1,17},{9,25},{17,1},{25,9},{2,18},{10... | collective-permute-start | bytes 4325384 | tf_op jit(solution)/shard_map/ppermute | solution.py:288
  1302.4 70.5 %all-to-all-start.8 = ((bf16[8,704,256]{2,1,0:T(8,128)(2,1)}), bf16[8,704,256]{2,1,0:T(8,128)(2,1)}, u32[]{:S(2)}, u32[]{:S(2)}) async-start(bf16[8,704,256]{2,1,0:T(8,128)(2,1)} %bitcast.265), calls=%async_computation.12 | async-start | bytes 5767168 | tf_op jit(solution)/shard_map/all_to_all | solution.py:333
  (153 other events, 3079.6 us)
Sparse Core Ops, SparseCore 0:
  28.1 51.4 all-gather.5
  81.8 103.6 all-gather.7
  196.0 134.8 all-gather.9
  409.8 85.0 all-gather.13
  496.3 80.5 all-gather.11
  766.3 86.1 reduce-scatter.5
  861.5 87.3 reduce-scatter.7
  971.0 86.7 reduce-scatter.9
  1060.1 87.9 reduce-scatter.13
  1150.8 65.1 reduce-scatter.11

commit v6 on v5

--- a/solution.py
+++ b/solution.py
@@ -211,34 +211,40 @@
     )(g_raw, routes, gates, queries, keys, values, mixed, log_total, cosine, sine, q_blocks, k_blocks)
 
 
-def expert_kernel(row_ref, cot_ref, gate_ref, wide_ref, down_ref, hidden_ref, grad_ref, back_ref, slot_ref):
+def expert_kernel(ready, cot_ref, slot_gate_ref, gate_w_ref, up_w_ref, down_ref, *refs):
     half = down_ref.shape[0]
-    rows = row_ref[...]
-    gate_pre, up_pre = dot_nt(wide_ref[:half], rows), dot_nt(wide_ref[half:], rows)
+    if ready:
+        gate_pre, up_pre = refs[0][...], refs[1][...]
+        hidden_ref, grad_ref, back_ref, slot_ref = refs[2:]
+    else:
+        rows = refs[0][...]
+        gate_pre, up_pre = dot_nt(gate_w_ref[...], rows), dot_nt(up_w_ref[...], rows)
+        hidden_ref, grad_ref, back_ref, slot_ref = refs[1:]
     grad_hidden = dot_nt(down_ref[...], cot_ref[...])
     sigma = 1.0 / (1.0 + jnp.exp(-gate_pre))
     silu = gate_pre * sigma
     hidden = silu * up_pre
     slot_ref[...] = jnp.sum(grad_hidden * hidden, axis=0, keepdims=True)
-    gate = gate_ref[...]
+    gate = slot_gate_ref[...]
     grad_hidden = grad_hidden * gate
     hidden_ref[...] = (hidden * gate).astype(BF)
     grad_ref[:half] = (grad_hidden * up_pre * sigma * (1.0 + gate_pre * (1.0 - sigma))).astype(BF)
     grad_ref[half:] = (grad_hidden * silu).astype(BF)
-    back_ref[...] = dot_tn(grad_ref[...], wide_ref[...]).astype(BF)
-
-
-def expert_pass(rows, cot_rows, gates, wide, down):
-    count, width = rows.shape
+    back_ref[...] = (dot_tn(grad_ref[:half], gate_w_ref[...]) + dot_tn(grad_ref[half:], up_w_ref[...])).astype(BF)
+
+
+def expert_pass(cot_rows, gates, weights, down, sources):
+    count, width = cot_rows.shape
     half = down.shape[0]
     tile = 256
     kept = lambda shape: pl.BlockSpec(shape, lambda i: (0, 0), pipeline_mode=pl.Buffered(1))
     tiled = pl.BlockSpec((tile, width), lambda i: (i, 0))
     turned = lambda size: pl.BlockSpec((size, tile), lambda i: (0, i))
+    ready = len(sources) == 2
     return pl.pallas_call(
-        expert_kernel,
+        functools.partial(expert_kernel, ready),
         grid=(count // tile,),
-        in_specs=[tiled, tiled, turned(1), kept(wide.shape), kept(down.shape)],
+        in_specs=[tiled, turned(1)] + [kept(down.shape)] * 3 + ([turned(half)] * 2 if ready else [tiled]),
         out_specs=[turned(half), turned(2 * half), tiled, turned(1)],
         out_shape=[
             jax.ShapeDtypeStruct((half, count), BF),
@@ -250,7 +256,7 @@
             flops=10 * count * width * half, transcendentals=count * half, bytes_accessed=6 * count * width + 6 * half * width
         ),
         name="expert_pass",
-    )(rows, cot_rows, gates, wide, down)
+    )(cot_rows, gates, *weights, down, *sources)
 
 
 def pick(table, routes, ids):
@@ -392,7 +398,9 @@
     down_w = fetch(down_w)
     turned, query_w = lax.optimization_barrier((turned, query_w))
     turned = shuffle(turned, "shard").reshape(n_s, 2 * hidden_units, -1)
-    gate_up_own = turned.transpose(1, 0, 2).reshape(2 * hidden_units, width)
+    gate_up_own = [
+        turned[:, i * hidden_units:(i + 1) * hidden_units].transpose(1, 0, 2).reshape(hidden_units, width) for i in range(2)
+    ]
 
     own = inputs[0].astype(F32)
     cot = cotangent[0]
@@ -424,7 +432,7 @@
     inv_f = inverse_rms(middle)
     h_ffn = (middle * inv_f * gain_f).astype(BF)
     h_ffn, gate_up_own = lax.optimization_barrier((h_ffn, gate_up_own))
-    gate_up_w = fetch(gate_up_own)
+    gate_w, up_w = fetch(gate_up_own[0]), fetch(gate_up_own[1])
     h_all = gather_shard(h_ffn)
     cot_all = gather_shard(after(cot, h_ffn))
     logits_f = dot(h_all, router_f.astype(BF))
@@ -451,16 +459,20 @@
         gate_token = sum(jnp.where(named[j], gates_f[j].reshape(n_s, tokens), 0.0) for j in range(TOPK))
         gate_slot = jnp.sum(jnp.where(hit, gate_token[:, None, :], 0.0), axis=2).reshape(1, -1)
         all_rows.append((named, hit, gate_slot, rows_of(hit.astype(BF), h_blocks)))
-    cot_all, all_rows, gate_up_w = lax.optimization_barrier((cot_all, all_rows, gate_up_w))
+    ahead = [[dot_nt(gate_w[k], all_rows[k][3]), dot_nt(up_w[k], all_rows[k][3])] for k in range(2)]
+    cot_all, all_rows, gate_w, up_w, ahead = lax.optimization_barrier((cot_all, all_rows, gate_w, up_w, ahead))
     cot_blocks = cot_all.reshape(n_s, tokens, width)
-    gate_up_w = fetch_rest(gate_up_w)
+    if n_e == 4:
+        gate_w, up_w = gate_w + [swap(gate_w[1], 2)], up_w + [swap(up_w[2], 1)]
     for k in range(n_e):
         named, hit, gate_slot, rows = all_rows[k]
         select = hit.astype(BF)
         cot_rows = rows_of(select, cot_blocks)
         if k == 2 and n_e == 4:
-            cot_rows, gate_up_w[3] = lax.optimization_barrier((cot_rows, gate_up_w[3]))
-        hidden, grad_pre, back, grad_slot = expert_pass(rows, cot_rows, gate_slot, gate_up_w[k], down_w[k])
+            cot_rows, gate_w[3], up_w[3] = lax.optimization_barrier((cot_rows, gate_w[3], up_w[3]))
+        hidden, grad_pre, back, grad_slot = expert_pass(
+            cot_rows, gate_slot, (gate_w[k], up_w[k]), down_w[k], ahead[k] if k < len(ahead) else [rows]
+        )
         grad_slot = grad_slot.reshape(n_s, capacity)
         selects.append(select)
         back_rows_f.append(back.reshape(n_s, capacity, width))
@@ -488,7 +500,12 @@
     halves = deliver_first(grad_gate_up[n_e - 1])
     out_rows_f = []
     for k in range(n_e):
-        hidden = after(hiddens[k], *(grad_gate_up[n_e - 1] if k < n_e - 1 else halves))
+        if k < n_e - 1:
+            hidden = after(hiddens[k], *grad_gate_up[n_e - 1])
+        else:
+            for j in reversed(range(n_e - 1)):
+                grad_gate_up[j] = gate_up_grads(j, back_sum)
+            hidden, halves, grad_gate_up = lax.optimization_barrier((hiddens[k], halves, grad_gate_up))
         out_rows_f.append(dot_tn(hidden, down_w[k]).astype(BF).reshape(n_s, capacity, width))
     out_sum = tokens_of(out_rows_f)
     ffn_out = scatter_shard(out_sum)
@@ -516,8 +533,6 @@
     grad_bias_a = jnp.sum(grad_middle, axis=0)
 
     grad_middle_low = grad_middle.astype(BF)
-    for k in range(n_e - 1):
-        grad_gate_up[k] = gate_up_grads(k, back_f)
     seq_grad = spread(grad_middle_low)
     seq_grad, grad_gate_up = lax.optimization_barrier((seq_grad, grad_gate_up))
     near = deliver_near(grad_gate_up)
@@ -528,28 +543,26 @@
     grad_query_all, grad_key_value, gate_notes = attend_back(
         grad_mixed, routes_a, gate_pair, queries, keys, values, mixed, log_total, cosine, sine, row_blocks, key_blocks
     )
-    grad_query_all, *near = lax.optimization_barrier((grad_query_all, *near))
     key_value_grad, query_grad = dot_tn(h_attn, grad_key_value).astype(BF), dot_tn(h_attn, grad_query_all).astype(BF)
-    grad_query_all, key_value_grad, query_grad = lax.optimization_barrier((grad_query_all, key_value_grad, query_grad))
+    grad_query_all, key_value_grad, query_grad, *near = lax.optimization_barrier(
+        (grad_query_all, key_value_grad, query_grad, *near)
+    )
     back_a = (dot_nt(grad_query_all, query_w) + dot_nt(grad_key_value, key_value_w)).astype(BF)
     back_a = jnp.concatenate([back_a, gate_notes], axis=1)
-    back_a, ffn_out, *last = lax.optimization_barrier((back_a, ffn_out, *last))
+    value = scatter_shard(grad_out_wt)
+    back_a, ffn_out, value, *last = lax.optimization_barrier((back_a, ffn_out, value, *last))
     gate_up_total = [v.astype(BF) for v in total(grad_gate_up[0], near, last)]
     outputs = (middle + ffn_out.astype(F32) + bias_f).astype(BF)[None]
-    value = scatter_shard(grad_out_wt)
     key_value_grad = key_value_grad.reshape(n_e, n_s, small_rows, 2 * group).transpose(1, 0, 2, 3)
     key_value_grad = scatter_shard(key_value_grad.reshape(n_s * n_e * small_rows, 2 * group))
     query_grad = scatter_shard(query_grad)
-    value = from_heads(value).reshape(width // n_s, n_s, out_rows).transpose(1, 0, 2)
+    out_part = from_heads(value).reshape(width // n_s, n_s, out_rows).transpose(1, 0, 2)
 
     def to_rows(value):
         value = shuffle(value.reshape(hidden_units, n_s, width // n_s).transpose(1, 0, 2), "shard")
         return value.reshape(n_s * hidden_units, width // n_s)
 
-    grad_out_w = shuffle(value, "shard").reshape(width, out_rows)
-    grad_out_w, gate_total = lax.optimization_barrier((grad_out_w, gate_up_total[0]))
-    grad_out_w = grad_out_w.T.astype(F32)[None]
-    gate_turned = to_rows(gate_total)
+    gate_turned = to_rows(gate_up_total[0])
     grad_down = []
     for k in range(n_e):
         hidden = after(hiddens[k], back_a)
@@ -584,7 +597,8 @@
         + [v[:, None] for v in (grad_gain_a, grad_gain_f, grad_bias_a, grad_bias_f)],
         axis=1,
     )
-    shared, up_turned, grad_query_w = lax.optimization_barrier((shared, up_turned, grad_query_w))
+    shared, up_turned, grad_query_w, value = lax.optimization_barrier((shared, up_turned, grad_query_w, out_part))
+    grad_out_w = shuffle(value, "shard").reshape(width, out_rows).T.astype(F32)[None]
     grad_query_w = grad_query_w.astype(F32)[None]
     grad_up_w = up_turned.T.astype(F32)[None]
     shared = shuffle(shared.reshape(n_e * n_s, -1), ("expert", "shard"))

time: 1400 us -> 1400 us (level)
  waiting for transfers between devices: 477 us -> 445 us
  matrix products: 285 us -> 316 us
    dot_general x3 -> x7, matrix products: 33.2 us -> 64.5 us  [dot_nt(): lax.dot_general(a, b, (((1,), (1,)), ((), ())), preferred_element_type=F32)]
    all_gather x5, waiting for transfers between devices: 145 us -> 122 us  [gather_shard(): return lax.all_gather(value, 'shard', axis=0, tiled=True)]
    ppermute x41 -> x43, starting transfers between devices: 47.4 us -> 49.9 us  [swap(): return lax.ppermute(value, 'expert', [(i, i ^ k) for i in range(n_e)])]
    unnamed x273 -> x282, local copies, waits for them, and re-layouts: 41.6 us -> 43.9 us
    ppermute x41 -> x43, waiting for transfers between devices: 228 us -> 227 us  [swap(): return lax.ppermute(value, 'expert', [(i, i ^ k) for i in range(n_e)])]
  transfers between devices with their start and end apart: 59 -> 61, of which waited for: 26 -> 27; matrix products, arithmetic and copies ran while one was open for 35% -> 37% of each run, Pallas kernels for 9% -> 8%
where the time goes in v6:
time: 1400 us; the launch traced here: 1390 us
  waiting for transfers between devices  445 us (32%)
  matrix products  316 us (23%)
  Pallas kernels  201 us (14%)
  local copies, waits for them, and re-layouts  152 us (11%)
  other arithmetic  105 us (8%)
  starting transfers between devices  84.3 us (6%)
  blocking collectives  70.2 us (5%)
  between operations  16.8 us (1%)
    ppermute x43, waiting for transfers between devices, swap(): return lax.ppermute(value, 'expert', [(i, i ^ k) for i in range(n_e)])  227 us
    pallas_call x4, Pallas kernels, expert_pass(): pl.pallas_call(functools.partial(expert_kernel, ready), grid=(count // ti...  141 us
    all_gather x5, waiting for transfers between devices, gather_shard(): return lax.all_gather(value, 'shard', axis=0, tiled=True)  122 us
    dot_general x26, matrix products, dot(): return jnp.dot(a, b, preferred_element_type=F32)  119 us
    all_to_all x8, waiting for transfers between devices, shuffle(): return lax.all_to_all(value, axis, split_axis=0, concat_axis=0, tiled=True)  95.8 us
    all_to_all x2, blocking collectives, shuffle(): return lax.all_to_all(value, axis, split_axis=0, concat_axis=0, tiled=True)  70.2 us
    dot_general x7, matrix products, dot_nt(): lax.dot_general(a, b, (((1,), (1,)), ((), ())), preferred_element_type=F32)  64.5 us
    dot_general x9, matrix products, dot_tn(): lax.dot_general(a, b, (((0,), (0,)), ((), ())), precision=precision, pref...  63.7 us
  transfers between devices with their start and end apart: 61, of which 27 were waited for; matrix products, arithmetic and copies ran while one was open for 37% of the time, Pallas kernels for 8%

profile of v6, /device:TPU:0, one launch (start us, length us, event | category | flops | bytes accessed | tf_op | source)
XLA Modules:
  0.0 1390.5 jit_solution(12695643505305726609)
XLA Ops:
  29.2 16.1 %all_to_all.63 = bf16[4,256,512]{2,1,0:T(8,128)(2,1)S(1)} all-to-all(bf16[4,256,512]{2,1,0:T(8,128)(2,1)S(1)} %copy.600), channel_id=1, replica_groups=mesh['expert'=4,'shard'=8] {'expert'}, dimensions={0} | all-to-all | bytes 2097152 | tf_op jit(solution)/shard_map/all_to_all | solution.py:339
  53.1 22.7 %collective-permute-done = bf16[256,2176]{1,0:T(8,128)(2,1)S(1)} collective-permute-done((bf16[256,2176]{1,0:T(8,128)(2,1)}, bf16[256,2176]{1,0:T(8,128)(2,1)S(1)}, u32[]{:S(2)}, u32[]{:S(2)}) %collective-permute-start) | collective-permute-done | bytes 1114144 | tf_op jit(solution)/shard_map/ppermute | solution.py:294
  75.8 21.7 %collective-permute-done.1 = bf16[256,2176]{1,0:T(8,128)(2,1)} collective-permute-done((bf16[256,2176]{1,0:T(8,128)(2,1)}, bf16[256,2176]{1,0:T(8,128)(2,1)}, u32[]{:S(2)}, u32[]{:S(2)}) %collective-permute-start.1) | collective-permute-done | bytes 1114144 | tf_op jit(solution)/shard_map/ppermute | solution.py:294
  120.9 54.1 %all_to_all.64 = bf16[8,256,256]{2,1,0:T(8,128)(2,1)S(1)} all-to-all(bf16[8,256,256]{2,1,0:T(8,128)(2,1)S(1)} %bitcast.366), channel_id=1, replica_groups=mesh['expert'=4,'shard'=8] {'shard'}, dimensions={0} | all-to-all | bytes 2097152 | tf_op jit(solution)/shard_map/all_to_all | solution.py:339
  179.9 13.8 all-to-all-done.3
  237.9 22.2 %collective-permute-done.5 = bf16[352,2048]{1,0:T(8,128)(2,1)S(1)} collective-permute-done((bf16[352,2048]{1,0:T(8,128)(2,1)S(1)}, bf16[352,2048]{1,0:T(8,128)(2,1)S(1)}, u32[]{:S(2)}, u32[]{:S(2)}) %collective-permute-start.5) | collective-permute-done | bytes 1441824 | tf_op jit(solution)/shard_map/ppermute | solution.py:294
  264.6 11.1 fusion.116.q_ref
  275.7 26.6 %attend.1 = (bf16[2,1024,512]{2,1,0:T(8,128)(2,1)}, bf16[1024,512]{1,0:T(8,128)(2,1)}, bf16[1024,512]{1,0:T(8,128)(2,1)}, bf16[2,1024,512]{2,1,0:T(8,128)(2,1)},...) custom-call(f32[1024,2048]{1,0:T(8,128)} %fusion.116.q_ref, f32[1024,1024]{1,0:T(8,128)} %fusion.27.kv_ref, ...), custom_call_target="tpu_custom_call" | custom-call | flops 1048576 | bytes 4194304 | tf_op jit(solution)/shard_map/attend/pallas_call | solution.py:109
  302.2 27.3 %all-gather.10.cloned.1.call-done = bf16[2048,2048]{0,1:T(8,128)(2,1)} async-done(((bf16[256,2048]{0,1:T(8,128)(2,1)}), bf16[2048,2048]{0,1:T(8,128)(2,1)}) %all-gather.10.cloned.1.call-update) | async-done | bytes 8388624 | tf_op jit(solution)/shard_map/all_gather | solution.py:349
  329.6 12.6 convolution_convert_fusion.14
  351.3 45.4 %all-to-all-done.4 = bf16[8,2,704,256]{3,2,1,0:T(8,128)(2,1)} async-done(((bf16[8,2,704,256]{3,2,1,0:T(8,128)(2,1)}), bf16[8,2,704,256]{3,2,1,0:T(8,128)(2,1)}, u32[]{:S(2)}, u32[]{:S(2)}) %all-to-all-start.4) | async-done | bytes 5767200 | tf_op jit(solution)/shard_map/all_to_all | solution.py:339
  416.1 77.6 %all-gather.14.cloned.1.call-done = bf16[2048,2048]{1,0:T(8,128)(2,1)} async-done(((bf16[256,2048]{1,0:T(8,128)(2,1)}), bf16[2048,2048]{1,0:T(8,128)(2,1)}) %all-gather.14.cloned.1.call-update) | async-done | bytes 8388624 | tf_op jit(solution)/shard_map/all_gather | solution.py:349
  558.5 17.2 %all-gather.12.cloned.1.call-done = bf16[2048,2048]{1,0:T(8,128)(2,1)} async-done(((bf16[256,2048]{1,0:T(8,128)(2,1)}), bf16[2048,2048]{1,0:T(8,128)(2,1)}) %all-gather.12.cloned.1.call-update) | async-done | bytes 8388624 | tf_op jit(solution)/shard_map/all_gather | solution.py:349
  597.8 27.8 %expert_pass.5 = (bf16[704,1280]{1,0:T(8,128)(2,1)}, bf16[1408,1280]{1,0:T(8,128)(2,1)}, bf16[1280,2048]{1,0:T(8,128)(2,1)}, f32[1,1280]{1,0:T(1,128)}) custom-call(bf16[1280,2048]{1,0:T(8,128)(2,1)} %bitcast.299, f32[1,1280]{1,0:T(1,128)} %reshape.485.slot_gate_ref, bf16[704,2048]{1,0:T(8,128)(2,1)} %collective-permute-done.10.gate_w_ref, ...), custom_call_target="tpu_custom_call" | custom-call | flops 18454937600 | bytes 24379392 | tf_op jit(solution)/shard_map/expert_pass/pallas_call | solution.py:244
  625.6 28.0 %expert_pass.4 = (bf16[704,1280]{1,0:T(8,128)(2,1)}, bf16[1408,1280]{1,0:T(8,128)(2,1)}, bf16[1280,2048]{1,0:T(8,128)(2,1)}, f32[1,1280]{1,0:T(1,128)}) custom-call(bf16[1280,2048]{1,0:T(8,128)(2,1)} %bitcast.311, f32[1,1280]{1,0:T(1,128)} %reshape.482.slot_gate_ref, bf16[704,2048]{1,0:T(8,128)(2,1)} %bitcast.145.gate_w_ref, ...), custom_call_target="tpu_custom_call" | custom-call | flops 18454937600 | bytes 24379392 | tf_op jit(solution)/shard_map/expert_pass/pallas_call | solution.py:244
  657.0 42.6 %expert_pass.6 = (bf16[704,1280]{1,0:T(8,128)(2,1)}, bf16[1408,1280]{1,0:T(8,128)(2,1)}, bf16[1280,2048]{1,0:T(8,128)(2,1)}, f32[1,1280]{1,0:T(1,128)}) custom-call(bf16[1280,2048]{1,0:T(8,128)(2,1)} %bitcast.304, f32[1,1280]{1,0:T(1,128)} %reshape.487.slot_gate_ref, bf16[704,2048]{1,0:T(8,128)(2,1)} %collective-permute-done.11.gate_w_ref, ...), custom_call_target="tpu_custom_call" | custom-call | flops 18454937600 | bytes 24379392 | tf_op jit(solution)/shard_map/expert_pass/pallas_call | solution.py:244
  699.6 43.0 %expert_pass.7 = (bf16[704,1280]{1,0:T(8,128)(2,1)}, bf16[1408,1280]{1,0:T(8,128)(2,1)}, bf16[1280,2048]{1,0:T(8,128)(2,1)}, f32[1,1280]{1,0:T(1,128)}) custom-call(bf16[1280,2048]{1,0:T(8,128)(2,1)} %bitcast.316, f32[1,1280]{1,0:T(1,128)} %reshape.489.slot_gate_ref, bf16[704,2048]{1,0:T(8,128)(2,1)} %collective-permute-done.14.gate_w_ref, ...), custom_call_target="tpu_custom_call" | custom-call | flops 18454937600 | bytes 24379392 | tf_op jit(solution)/shard_map/expert_pass/pallas_call | solution.py:244
  742.6 13.8 fusion.22
  837.9 12.7 fusion.19
  890.8 22.5 %collective-permute-done.18 = bf16[256,2048]{1,0:T(8,128)(2,1)S(1)} collective-permute-done((bf16[256,2048]{1,0:T(8,128)(2,1)S(1)}, bf16[256,2048]{1,0:T(8,128)(2,1)S(1)}, u32[]{:S(2)}, u32[]{:S(2)}) %collective-permute-start.18) | collective-permute-done | bytes 1048608 | tf_op jit(solution)/shard_map/ppermute | solution.py:294
  913.4 22.8 %collective-permute-done.19 = bf16[256,2048]{1,0:T(8,128)(2,1)S(1)} collective-permute-done((bf16[256,2048]{1,0:T(8,128)(2,1)S(1)}, bf16[256,2048]{1,0:T(8,128)(2,1)S(1)}, u32[]{:S(2)}, u32[]{:S(2)}) %collective-permute-start.19) | collective-permute-done | bytes 1048608 | tf_op jit(solution)/shard_map/ppermute | solution.py:294
  936.6 11.1 fusion.121.g_ref
  947.6 11.2 convolution_convert_fusion.1
  961.0 33.2 %attend_back.1 = (bf16[1024,2048]{1,0:T(8,128)(2,1)}, bf16[1024,1024]{1,0:T(8,128)(2,1)}, bf16[1024,128]{1,0:T(8,128)(2,1)}) custom-call(f32[1024,2048]{1,0:T(8,128)} %fusion.121.g_ref, s32[1024,2]{1,0:T(8,128)} %slice.255.route_ref, f32[1024,2]{1,0:T(8,128)} %pad_maximum_fusion.7.gate_ref, bf16[2,1024,512]{2,1,0:T(8,128)(2,1)} %get-tuple-element.243.query_ref, ...), custom_call_target="tpu_custom_call" | custom-call | flops 1048576 | bytes 4194304 | tf_op jit(solution)/shard_map/attend_back/pallas_call | solution.py:194
  994.2 9.7 convolution_convert_fusion.15
  1003.9 11.5 convolution_convert_fusion
  1045.5 13.7 add_convert_fusion
  1061.8 30.8 %collective-permute-done.24 = bf16[704,2048]{1,0:T(8,128)(2,1)} collective-permute-done((bf16[704,2048]{1,0:T(8,128)(2,1)S(1)}, bf16[704,2048]{1,0:T(8,128)(2,1)}, u32[]{:S(2)}, u32[]{:S(2)}) %collective-permute-start.24) | collective-permute-done | bytes 2883616 | tf_op jit(solution)/shard_map/ppermute | solution.py:294
  1151.0 18.2 %collective-permute-done.36 = bf16[256,512]{1,0:T(8,128)(2,1)S(1)} collective-permute-done((bf16[256,512]{1,0:T(8,128)(2,1)S(1)}, bf16[256,512]{1,0:T(8,128)(2,1)S(1)}, u32[]{:S(2)}, u32[]{:S(2)}) %collective-permute-start.36) | collective-permute-done | bytes 262176 | tf_op jit(solution)/shard_map/ppermute | solution.py:294
  1190.2 19.0 %collective-permute-done.39 = bf16[352,2048]{1,0:T(8,128)(2,1)} collective-permute-done((bf16[352,2048]{1,0:T(8,128)(2,1)}, bf16[352,2048]{1,0:T(8,128)(2,1)}, u32[]{:S(2)}, u32[]{:S(2)}) %collective-permute-start.39) | collective-permute-done | bytes 1441824 | tf_op jit(solution)/shard_map/ppermute | solution.py:294
  1223.0 21.4 %collective-permute-done.41 = bf16[352,2048]{1,0:T(8,128)(2,1)} collective-permute-done((bf16[352,2048]{1,0:T(8,128)(2,1)}, bf16[352,2048]{1,0:T(8,128)(2,1)}, u32[]{:S(2)}, u32[]{:S(2)}) %collective-permute-start.41) | collective-permute-done | bytes 1441824 | tf_op jit(solution)/shard_map/ppermute | solution.py:294
  1370.6 10.2 all-to-all-done.9
  (648 shorter events, 602.2 us)
Async XLA Ops:
  17.5 89.1 %all-gather.6.cloned.1.call-start = ((), (), s32[]{:S(2)}) async-start(), calls=%async_computation.15 | async-start | bytes 5308416 | tf_op jit(solution)/shard_map/all_gather | solution.py:349
  28.0 181.8 %all-gather.8.cloned.1.call-start = ((), (), s32[]{:S(2)}) async-start(), calls=%async_computation.16 | async-start | bytes 9437184 | tf_op jit(solution)/shard_map/all_gather | solution.py:349
  103.6 76.3 %collective-permute-start.3 = (bf16[704,2048]{1,0:T(8,128)(2,1)}, bf16[704,2048]{1,0:T(8,128)(2,1)}, u32[]{:S(2)}, u32[]{:S(2)}) collective-permute-start(bf16[704,2048]{1,0:T(8,128)(2,1)} %bitcast.3.down_ref), channel_id=1, source_target_pairs={{0,8},{8,0},{16,24},{24,16},{1,9},{9,1},{17,25},{25,17},{2,10},{10... | collective-permute-start | bytes 8650760 | tf_op jit(solution)/shard_map/ppermute | solution.py:294
  104.4 75.5 %collective-permute-start.4 = (bf16[704,2048]{1,0:T(8,128)(2,1)}, bf16[704,2048]{1,0:T(8,128)(2,1)}, u32[]{:S(2)}, u32[]{:S(2)}) collective-permute-start(bf16[704,2048]{1,0:T(8,128)(2,1)} %bitcast.3.down_ref), channel_id=1, source_target_pairs={{0,16},{8,24},{16,0},{24,8},{1,17},{9,25},{17,1},{25,9},{2,18},{10... | collective-permute-start | bytes 8650760 | tf_op jit(solution)/shard_map/ppermute | solution.py:294
  179.8 149.8 %all-gather.10.cloned.1.call-start = ((), (), s32[]{:S(2)}) async-start(), calls=%async_computation.17 | async-start | bytes 9437184 | tf_op jit(solution)/shard_map/all_gather | solution.py:349
  215.5 181.1 %all-to-all-start.4 = ((bf16[8,2,704,256]{3,2,1,0:T(8,128)(2,1)}), bf16[8,2,704,256]{3,2,1,0:T(8,128)(2,1)}, u32[]{:S(2)}, u32[]{:S(2)}) async-start(bf16[8,2,704,256]{3,2,1,0:T(8,128)(2,1)} %copy.608), calls=%async_computation.4 | async-start | bytes 11534336 | tf_op jit(solution)/shard_map/all_to_all | solution.py:339
  220.7 273.0 %all-gather.14.cloned.1.call-start = ((), (), s32[]{:S(2)}) async-start(), calls=%async_computation.19 | async-start | bytes 9437184 | tf_op jit(solution)/shard_map/all_gather | solution.py:349
  409.6 166.1 %all-gather.12.cloned.1.call-start = ((), (), s32[]{:S(2)}) async-start(), calls=%async_computation.18 | async-start | bytes 9437184 | tf_op jit(solution)/shard_map/all_gather | solution.py:349
  410.2 469.8 %reduce-scatter.6.cloned.1.call-start = ((), (), s32[]{:S(2)}) async-start(), calls=%async_computation.20 | async-start | bytes 9437184 | tf_op jit(solution)/shard_map/reduce_scatter | solution.py:352
  412.0 138.7 %collective-permute-start.10 = (bf16[704,2048]{1,0:T(8,128)(2,1)}, bf16[704,2048]{1,0:T(8,128)(2,1)}, u32[]{:S(2)}, u32[]{:S(2)}) collective-permute-start(bf16[704,2048]{1,0:T(8,128)(2,1)} %bitcast.145.gate_w_ref), channel_id=1, source_target_pairs={{0,8},{8,0},{16,24},{24,16},{1,9},{9,1},{17,25},{25,17},{2,10},{10... | collective-permute-start | bytes 8650760 | tf_op jit(solution)/shard_map/ppermute | solution.py:294
  413.5 145.0 %collective-permute-start.11 = (bf16[704,2048]{1,0:T(8,128)(2,1)}, bf16[704,2048]{1,0:T(8,128)(2,1)}, u32[]{:S(2)}, u32[]{:S(2)}) collective-permute-start(bf16[704,2048]{1,0:T(8,128)(2,1)} %bitcast.145.gate_w_ref), channel_id=1, source_target_pairs={{0,16},{8,24},{16,0},{24,8},{1,17},{9,25},{17,1},{25,9},{2,18},{10... | collective-permute-start | bytes 8650760 | tf_op jit(solution)/shard_map/ppermute | solution.py:294
  414.9 128.1 %collective-permute-start.12 = (bf16[704,2048]{1,0:T(8,128)(2,1)}, bf16[704,2048]{1,0:T(8,128)(2,1)}, u32[]{:S(2)}, u32[]{:S(2)}) collective-permute-start(bf16[704,2048]{1,0:T(8,128)(2,1)} %bitcast.147.up_w_ref), channel_id=1, source_target_pairs={{0,8},{8,0},{16,24},{24,16},{1,9},{9,1},{17,25},{25,17},{2,10},{10... | collective-permute-start | bytes 8650760 | tf_op jit(solution)/shard_map/ppermute | solution.py:294
  415.5 143.0 %collective-permute-start.13 = (bf16[704,2048]{1,0:T(8,128)(2,1)}, bf16[704,2048]{1,0:T(8,128)(2,1)}, u32[]{:S(2)}, u32[]{:S(2)}) collective-permute-start(bf16[704,2048]{1,0:T(8,128)(2,1)} %bitcast.147.up_w_ref), channel_id=1, source_target_pairs={{0,16},{8,24},{16,0},{24,8},{1,17},{9,25},{17,1},{25,9},{2,18},{10... | collective-permute-start | bytes 8650760 | tf_op jit(solution)/shard_map/ppermute | solution.py:294
  590.9 64.9 %collective-permute-start.14 = (bf16[704,2048]{1,0:T(8,128)(2,1)}, bf16[704,2048]{1,0:T(8,128)(2,1)}, u32[]{:S(2)}, u32[]{:S(2)}) collective-permute-start(bf16[704,2048]{1,0:T(8,128)(2,1)} %collective-permute-done.10.gate_w_ref), channel_id=1, source_target_pairs={{0,16},{8,24},{16,0},{24,8},{1,17},{9,25},{17,1},{25,9},{2,18},{10... | collective-permute-start | bytes 8650760 | tf_op jit(solution)/shard_map/ppermute | solution.py:294
  592.4 64.7 %collective-permute-start.15 = (bf16[704,2048]{1,0:T(8,128)(2,1)}, bf16[704,2048]{1,0:T(8,128)(2,1)}, u32[]{:S(2)}, u32[]{:S(2)}) collective-permute-start(bf16[704,2048]{1,0:T(8,128)(2,1)} %collective-permute-done.13.up_w_ref), channel_id=1, source_target_pairs={{0,8},{8,0},{16,24},{24,16},{1,9},{9,1},{17,25},{25,17},{2,10},{10... | collective-permute-start | bytes 8650760 | tf_op jit(solution)/shard_map/ppermute | solution.py:294
  756.4 305.4 %reduce-scatter.8.cloned.1.call-start = ((), (), s32[]{:S(2)}) async-start(), calls=%async_computation.21 | async-start | bytes 9437184 | tf_op jit(solution)/shard_map/reduce_scatter | solution.py:352
  763.6 65.6 %collective-permute-start.17 = (bf16[704,2048]{1,0:T(8,128)(2,1)S(1)}, bf16[704,2048]{1,0:T(8,128)(2,1)S(1)}, u32[]{:S(2)}, u32[]{:S(2)}) collective-permute-start(bf16[704,2048]{1,0:T(8,128)(2,1)S(1)} %convolution_convert_fusion.22), channel_id=1, source_target_pairs={{0,16},{8,24},{16,0},{24,8},{1,17},{9,25},{17,1},{25,9},{2,18},{10... | collective-permute-start | bytes 8650760 | tf_op jit(solution)/shard_map/ppermute | solution.py:294
  768.6 63.3 %collective-permute-start.16 = (bf16[704,2048]{1,0:T(8,128)(2,1)S(1)}, bf16[704,2048]{1,0:T(8,128)(2,1)S(1)}, u32[]{:S(2)}, u32[]{:S(2)}) collective-permute-start(bf16[704,2048]{1,0:T(8,128)(2,1)S(1)} %convolution_convert_fusion.23), channel_id=1, source_target_pairs={{0,8},{8,0},{16,24},{24,16},{1,9},{9,1},{17,25},{25,17},{2,10},{10... | collective-permute-start | bytes 8650760 | tf_op jit(solution)/shard_map/ppermute | solution.py:294
  857.5 240.3 %reduce-scatter.10.cloned.1.call-start = ((), (), s32[]{:S(2)}) async-start(), calls=%async_computation.22 | async-start | bytes 9437184 | tf_op jit(solution)/shard_map/reduce_scatter | solution.py:352
  958.8 255.0 %reduce-scatter.14.cloned.1.call-start = ((), (), s32[]{:S(2)}) async-start(), calls=%async_computation.24 | async-start | bytes 9437184 | tf_op jit(solution)/shard_map/reduce_scatter | solution.py:352
  958.9 63.8 %collective-permute-start.21 = (bf16[704,2048]{1,0:T(8,128)(2,1)}, bf16[704,2048]{1,0:T(8,128)(2,1)}, u32[]{:S(2)}, u32[]{:S(2)}) collective-permute-start(bf16[704,2048]{1,0:T(8,128)(2,1)} %convolution_convert_fusion.19), channel_id=1, source_target_pairs={{0,8},{8,0},{16,24},{24,16},{1,9},{9,1},{17,25},{25,17},{2,10},{10... | collective-permute-start | bytes 8650760 | tf_op jit(solution)/shard_map/ppermute | solution.py:294
  960.1 63.7 %collective-permute-start.22 = (bf16[704,2048]{1,0:T(8,128)(2,1)}, bf16[704,2048]{1,0:T(8,128)(2,1)}, u32[]{:S(2)}, u32[]{:S(2)}) collective-permute-start(bf16[704,2048]{1,0:T(8,128)(2,1)} %convolution_convert_fusion.16), channel_id=1, source_target_pairs={{0,16},{8,24},{16,0},{24,8},{1,17},{9,25},{17,1},{25,9},{2,18},{10... | collective-permute-start | bytes 8650760 | tf_op jit(solution)/shard_map/ppermute | solution.py:294
  1023.9 241.1 %reduce-scatter.12.cloned.1.call-start = ((), (), s32[]{:S(2)}) async-start(), calls=%async_computation.23 | async-start | bytes 4718592 | tf_op jit(solution)/shard_map/reduce_scatter | solution.py:352
  1029.8 62.8 %collective-permute-start.24 = (bf16[704,2048]{1,0:T(8,128)(2,1)S(1)}, bf16[704,2048]{1,0:T(8,128)(2,1)}, u32[]{:S(2)}, u32[]{:S(2)}) collective-permute-start(bf16[704,2048]{1,0:T(8,128)(2,1)S(1)} %add_convert_fusion.3), channel_id=1, source_target_pairs={{0,8},{8,0},{16,24},{24,16},{1,9},{9,1},{17,25},{25,17},{2,10},{10... | collective-permute-start | bytes 8650760 | tf_op jit(solution)/shard_map/ppermute | solution.py:294
  1035.2 62.7 %collective-permute-start.23 = (bf16[704,2048]{1,0:T(8,128)(2,1)}, bf16[704,2048]{1,0:T(8,128)(2,1)}, u32[]{:S(2)}, u32[]{:S(2)}) collective-permute-start(bf16[704,2048]{1,0:T(8,128)(2,1)} %add_convert_fusion.4), channel_id=1, source_target_pairs={{0,16},{8,24},{16,0},{24,8},{1,17},{9,25},{17,1},{25,9},{2,18},{10... | collective-permute-start | bytes 8650760 | tf_op jit(solution)/shard_map/ppermute | solution.py:294
  1108.1 156.9 %all-to-all-start.6 = ((bf16[8,704,256]{2,1,0:T(8,128)(2,1)}), bf16[8,704,256]{2,1,0:T(8,128)(2,1)}, u32[]{:S(2)}, u32[]{:S(2)}) async-start(bf16[8,704,256]{2,1,0:T(8,128)(2,1)} %bitcast.279), calls=%async_computation.9 | async-start | bytes 5767168 | tf_op jit(solution)/shard_map/all_to_all | solution.py:339
  1112.6 70.4 %collective-permute-start.25 = (bf16[256,2176]{1,0:T(8,128)(2,1)}, bf16[256,2176]{1,0:T(8,128)(2,1)}, u32[]{:S(2)}, u32[]{:S(2)}) collective-permute-start(bf16[256,2176]{1,0:T(8,128)(2,1)} %get-tuple-element.457), channel_id=1, source_target_pairs={{0,8},{8,0},{16,24},{24,16},{1,9},{9,1},{17,25},{25,17},{2,10},{10... | collective-permute-start | bytes 3342344 | tf_op jit(solution)/shard_map/ppermute | solution.py:294
  1114.0 70.5 %collective-permute-start.26 = (bf16[256,2176]{1,0:T(8,128)(2,1)}, bf16[256,2176]{1,0:T(8,128)(2,1)}, u32[]{:S(2)}, u32[]{:S(2)}) collective-permute-start(bf16[256,2176]{1,0:T(8,128)(2,1)} %get-tuple-element.459), channel_id=1, source_target_pairs={{0,16},{8,24},{16,0},{24,8},{1,17},{9,25},{17,1},{25,9},{2,18},{10... | collective-permute-start | bytes 3342344 | tf_op jit(solution)/shard_map/ppermute | solution.py:294
  1114.4 71.6 %collective-permute-start.27 = (bf16[256,2176]{1,0:T(8,128)(2,1)S(1)}, bf16[256,2176]{1,0:T(8,128)(2,1)}, u32[]{:S(2)}, u32[]{:S(2)}) collective-permute-start(bf16[256,2176]{1,0:T(8,128)(2,1)S(1)} %copy-done.41), channel_id=1, source_target_pairs={{0,24},{8,16},{16,8},{24,0},{1,25},{9,17},{17,9},{25,1},{2,26},{10... | collective-permute-start | bytes 3342344 | tf_op jit(solution)/shard_map/ppermute | solution.py:294
  1179.4 85.6 %collective-permute-start.29 = (bf16[352,2048]{1,0:T(8,128)(2,1)}, bf16[352,2048]{1,0:T(8,128)(2,1)}, u32[]{:S(2)}, u32[]{:S(2)}) collective-permute-start(bf16[352,2048]{1,0:T(8,128)(2,1)} %convolution_convert_fusion.30), channel_id=1, source_target_pairs={{0,16},{8,24},{16,0},{24,8},{1,17},{9,25},{17,1},{25,9},{2,18},{10... | collective-permute-start | bytes 4325384 | tf_op jit(solution)/shard_map/ppermute | solution.py:294
  1183.1 81.9 %collective-permute-start.28 = (bf16[352,2048]{1,0:T(8,128)(2,1)}, bf16[352,2048]{1,0:T(8,128)(2,1)}, u32[]{:S(2)}, u32[]{:S(2)}) collective-permute-start(bf16[352,2048]{1,0:T(8,128)(2,1)} %convolution_convert_fusion.31), channel_id=1, source_target_pairs={{0,8},{8,0},{16,24},{24,16},{1,9},{9,1},{17,25},{25,17},{2,10},{10... | collective-permute-start | bytes 4325384 | tf_op jit(solution)/shard_map/ppermute | solution.py:294
  1266.8 70.8 %all-to-all-start.7 = ((bf16[8,704,256]{2,1,0:T(8,128)(2,1)}), bf16[8,704,256]{2,1,0:T(8,128)(2,1)}, u32[]{:S(2)}, u32[]{:S(2)}) async-start(bf16[8,704,256]{2,1,0:T(8,128)(2,1)} %bitcast.277), calls=%async_computation.11 | async-start | bytes 5767168 | tf_op jit(solution)/shard_map/all_to_all | solution.py:339
  (159 other events, 3319.6 us)
Sparse Core Ops, SparseCore 0:
  28.1 51.4 all-gather.5
  81.8 103.6 all-gather.7
  194.8 134.7 all-gather.9
  409.7 83.8 all-gather.13
  495.1 80.5 all-gather.11
  756.6 87.0 reduce-scatter.5
  850.9 88.2 reduce-scatter.7
  959.0 86.7 reduce-scatter.9
  1048.0 104.7 reduce-scatter.13
  1155.6 80.4 reduce-scatter.11

commit v7 on v6

--- a/solution.py
+++ b/solution.py
@@ -213,12 +213,25 @@
 
 def expert_kernel(ready, cot_ref, slot_gate_ref, gate_w_ref, up_w_ref, down_ref, *refs):
     half = down_ref.shape[0]
+    *refs, wide_ref, sems = refs
+
+    @pl.when(pl.program_id(0) == 0)
+    def _():
+        copies = [
+            pltpu.make_async_copy(ref, wide_ref.at[pl.ds(i * half, half)], sems.at[i])
+            for i, ref in enumerate((gate_w_ref, up_w_ref))
+        ]
+        for copy in copies:
+            copy.start()
+        for copy in copies:
+            copy.wait()
+
     if ready:
         gate_pre, up_pre = refs[0][...], refs[1][...]
         hidden_ref, grad_ref, back_ref, slot_ref = refs[2:]
     else:
-        rows = refs[0][...]
-        gate_pre, up_pre = dot_nt(gate_w_ref[...], rows), dot_nt(up_w_ref[...], rows)
+        pre = dot_nt(wide_ref[...], refs[0][...])
+        gate_pre, up_pre = pre[:half], pre[half:]
         hidden_ref, grad_ref, back_ref, slot_ref = refs[1:]
     grad_hidden = dot_nt(down_ref[...], cot_ref[...])
     sigma = 1.0 / (1.0 + jnp.exp(-gate_pre))
@@ -230,7 +243,7 @@
     hidden_ref[...] = (hidden * gate).astype(BF)
     grad_ref[:half] = (grad_hidden * up_pre * sigma * (1.0 + gate_pre * (1.0 - sigma))).astype(BF)
     grad_ref[half:] = (grad_hidden * silu).astype(BF)
-    back_ref[...] = (dot_tn(grad_ref[:half], gate_w_ref[...]) + dot_tn(grad_ref[half:], up_w_ref[...])).astype(BF)
+    back_ref[...] = dot_tn(grad_ref[...], wide_ref[...]).astype(BF)
 
 
 def expert_pass(cot_rows, gates, weights, down, sources):
@@ -244,7 +257,8 @@
     return pl.pallas_call(
         functools.partial(expert_kernel, ready),
         grid=(count // tile,),
-        in_specs=[tiled, turned(1)] + [kept(down.shape)] * 3 + ([turned(half)] * 2 if ready else [tiled]),
+        in_specs=[tiled, turned(1)] + [pl.BlockSpec(memory_space=pl.ANY)] * 2 + [kept(down.shape)]
+        + ([turned(half)] * 2 if ready else [tiled]),
         out_specs=[turned(half), turned(2 * half), tiled, turned(1)],
         out_shape=[
             jax.ShapeDtypeStruct((half, count), BF),
@@ -252,6 +266,7 @@
             jax.ShapeDtypeStruct((count, width), BF),
             jax.ShapeDtypeStruct((1, count), F32),
         ],
+        scratch_shapes=[pltpu.VMEM((2 * half, width), BF), pltpu.SemaphoreType.DMA((2,))],
         cost_estimate=pl.CostEstimate(
             flops=10 * count * width * half, transcendentals=count * half, bytes_accessed=6 * count * width + 6 * half * width
         ),
@@ -498,6 +513,7 @@
     grad_gate_up = [None] * n_e
     grad_gate_up[n_e - 1] = gate_up_grads(n_e - 1, back_sum)
     halves = deliver_first(grad_gate_up[n_e - 1])
+    gate_grads_f = shuffle(jnp.stack(grad_gate_f, axis=1).reshape(n_s, TOPK * tokens), "shard")
     out_rows_f = []
     for k in range(n_e):
         if k < n_e - 1:
@@ -505,16 +521,15 @@
         else:
             for j in reversed(range(n_e - 1)):
                 grad_gate_up[j] = gate_up_grads(j, back_sum)
-            hidden, halves, grad_gate_up = lax.optimization_barrier((hiddens[k], halves, grad_gate_up))
+            hidden, halves, grad_gate_up, gate_grads_f = lax.optimization_barrier(
+                (hiddens[k], halves, grad_gate_up, gate_grads_f)
+            )
         out_rows_f.append(dot_tn(hidden, down_w[k]).astype(BF).reshape(n_s, capacity, width))
     out_sum = tokens_of(out_rows_f)
     ffn_out = scatter_shard(out_sum)
     back_f, out_sum = lax.optimization_barrier((back_f, out_sum))
     back_f = back_f.astype(F32)
-    grad_gates_f = jnp.sum(
-        shuffle(jnp.stack(grad_gate_f, axis=1).reshape(n_s, TOPK * tokens), "shard"), axis=0
-    ).reshape(TOPK, tokens, 1)
-
+    grad_gates_f = jnp.sum(gate_grads_f, axis=0).reshape(TOPK, tokens, 1)
 
     grad_out = cot.astype(F32)
     own_routes_f = ffn_routes[0]
@@ -550,7 +565,9 @@
     back_a = (dot_nt(grad_query_all, query_w) + dot_nt(grad_key_value, key_value_w)).astype(BF)
     back_a = jnp.concatenate([back_a, gate_notes], axis=1)
     value = scatter_shard(grad_out_wt)
-    back_a, ffn_out, value, *last = lax.optimization_barrier((back_a, ffn_out, value, *last))
+    back_a, ffn_out, value, key_value_grad, *last = lax.optimization_barrier(
+        (back_a, ffn_out, value, key_value_grad, *last)
+    )
     gate_up_total = [v.astype(BF) for v in total(grad_gate_up[0], near, last)]
     outputs = (middle + ffn_out.astype(F32) + bias_f).astype(BF)[None]
     key_value_grad = key_value_grad.reshape(n_e, n_s, small_rows, 2 * group).transpose(1, 0, 2, 3)
@@ -570,13 +587,9 @@
     halves = deliver_first(grad_down[n_e - 1])
     back_a = collect(back_a)
     near, last = deliver_near(grad_down), deliver_last(grad_down, halves)
-    back_a, gate_turned, *near = lax.optimization_barrier((back_a, gate_turned, *near))
-    up_total, key_value_grad = lax.optimization_barrier((after(gate_up_total[1], gate_turned), key_value_grad))
+    back_a, gate_turned, up_total = lax.optimization_barrier((back_a, gate_turned, gate_up_total[1]))
     up_turned = to_rows(up_total)
-    grad_down_w = jnp.concatenate(total(grad_down[0], near, last), axis=0)[None]
     key_value_grad = trade(key_value_grad.reshape(n_e, small_rows, -1))
-    grad_key_w = key_value_grad[:, :, :group].transpose(1, 0, 2).reshape(small_rows, -1).astype(F32)
-    grad_value_w = key_value_grad[:, :, group:].transpose(1, 0, 2).reshape(small_rows, -1).astype(F32)
     gate_grads = back_a[:, width:width + TOPK] + back_a[:, width + TOPK:width + 2 * TOPK]
     grad_gates_a = [gate_grads[:, j:j + 1] for j in range(TOPK)]
     back_a = back_a[:, :width]
@@ -597,7 +610,12 @@
         + [v[:, None] for v in (grad_gain_a, grad_gain_f, grad_bias_a, grad_bias_f)],
         axis=1,
     )
-    shared, up_turned, grad_query_w, value = lax.optimization_barrier((shared, up_turned, grad_query_w, out_part))
+    shared, up_turned, grad_query_w, value, key_value_grad, near, last = lax.optimization_barrier(
+        (shared, up_turned, grad_query_w, out_part, key_value_grad, near, last)
+    )
+    grad_down_w = jnp.concatenate(total(grad_down[0], near, last), axis=0)[None]
+    grad_key_w = key_value_grad[:, :, :group].transpose(1, 0, 2).reshape(small_rows, -1).astype(F32)
+    grad_value_w = key_value_grad[:, :, group:].transpose(1, 0, 2).reshape(small_rows, -1).astype(F32)
     grad_out_w = shuffle(value, "shard").reshape(width, out_rows).T.astype(F32)[None]
     grad_query_w = grad_query_w.astype(F32)[None]
     grad_up_w = up_turned.T.astype(F32)[None]

time: 1400 us -> 1420 us (1.014)
  waiting for transfers between devices: 445 us -> 465 us
  matrix products: 316 us -> 334 us
    ppermute x43, waiting for transfers between devices: 227 us -> 255 us  [swap(): return lax.ppermute(value, 'expert', [(i, i ^ k) for i in range(n_e)])]
    unnamed x282 -> x257, local copies, waits for them, and re-layouts: 43.9 us -> 47.3 us
  transfers between devices with their start and end apart: 61 -> 61, of which waited for: 27 -> 28; matrix products, arithmetic and copies ran while one was open for 37% -> 36% of each run, Pallas kernels for 8% -> 8%
where the time goes in v7:
time: 1420 us; the launch traced here: 1410 us
  waiting for transfers between devices  465 us (33%)
  matrix products  334 us (24%)
  Pallas kernels  191 us (13%)
  local copies, waits for them, and re-layouts  143 us (10%)
  other arithmetic  104 us (7%)
  starting transfers between devices  87.2 us (6%)
  blocking collectives  70.2 us (5%)
  between operations  16.5 us (1%)
    ppermute x43, waiting for transfers between devices, swap(): return lax.ppermute(value, 'expert', [(i, i ^ k) for i in range(n_e)])  255 us
    pallas_call x4, Pallas kernels, expert_pass(): pl.pallas_call(functools.partial(expert_kernel, ready), grid=(count // ti...  132 us
    dot_general x26, matrix products, dot(): return jnp.dot(a, b, preferred_element_type=F32)  131 us
    all_gather x5, waiting for transfers between devices, gather_shard(): return lax.all_gather(value, 'shard', axis=0, tiled=True)  123 us
    all_to_all x8, waiting for transfers between devices, shuffle(): return lax.all_to_all(value, axis, split_axis=0, concat_axis=0, tiled=True)  86.3 us
    all_to_all x2, blocking collectives, shuffle(): return lax.all_to_all(value, axis, split_axis=0, concat_axis=0, tiled=True)  70.2 us
    dot_general x9, matrix products, dot_tn(): lax.dot_general(a, b, (((0,), (0,)), ((), ())), precision=precision, pref...  70.1 us
    dot_general x7, matrix products, dot_nt(): lax.dot_general(a, b, (((1,), (1,)), ((), ())), preferred_element_type=F32)  62.3 us
  transfers between devices with their start and end apart: 61, of which 28 were waited for; matrix products, arithmetic and copies ran while one was open for 36% of the time, Pallas kernels for 8%

profile of v7, /device:TPU:0, one launch (start us, length us, event | category | flops | bytes accessed | tf_op | source)
XLA Modules:
  0.0 1410.3 jit_solution(12780934803832632448)
XLA Ops:
  29.2 16.1 %all_to_all.66 = bf16[4,256,512]{2,1,0:T(8,128)(2,1)S(1)} all-to-all(bf16[4,256,512]{2,1,0:T(8,128)(2,1)S(1)} %copy.600), channel_id=1, replica_groups=mesh['expert'=4,'shard'=8] {'expert'}, dimensions={0} | all-to-all | bytes 2097152 | tf_op jit(solution)/shard_map/all_to_all | solution.py:354
  53.1 22.7 %collective-permute-done = bf16[256,2176]{1,0:T(8,128)(2,1)S(1)} collective-permute-done((bf16[256,2176]{1,0:T(8,128)(2,1)}, bf16[256,2176]{1,0:T(8,128)(2,1)S(1)}, u32[]{:S(2)}, u32[]{:S(2)}) %collective-permute-start) | collective-permute-done | bytes 1114144 | tf_op jit(solution)/shard_map/ppermute | solution.py:309
  75.8 21.7 %collective-permute-done.1 = bf16[256,2176]{1,0:T(8,128)(2,1)} collective-permute-done((bf16[256,2176]{1,0:T(8,128)(2,1)}, bf16[256,2176]{1,0:T(8,128)(2,1)}, u32[]{:S(2)}, u32[]{:S(2)}) %collective-permute-start.1) | collective-permute-done | bytes 1114144 | tf_op jit(solution)/shard_map/ppermute | solution.py:309
  120.9 54.1 %all_to_all.67 = bf16[8,256,256]{2,1,0:T(8,128)(2,1)S(1)} all-to-all(bf16[8,256,256]{2,1,0:T(8,128)(2,1)S(1)} %bitcast.363), channel_id=1, replica_groups=mesh['expert'=4,'shard'=8] {'shard'}, dimensions={0} | all-to-all | bytes 2097152 | tf_op jit(solution)/shard_map/all_to_all | solution.py:354
  179.9 13.8 all-to-all-done.3
  237.7 22.1 %collective-permute-done.5 = bf16[352,2048]{1,0:T(8,128)(2,1)S(1)} collective-permute-done((bf16[352,2048]{1,0:T(8,128)(2,1)S(1)}, bf16[352,2048]{1,0:T(8,128)(2,1)S(1)}, u32[]{:S(2)}, u32[]{:S(2)}) %collective-permute-start.5) | collective-permute-done | bytes 1441824 | tf_op jit(solution)/shard_map/ppermute | solution.py:309
  264.3 11.0 fusion.113.q_ref
  275.4 26.6 %attend.1 = (bf16[2,1024,512]{2,1,0:T(8,128)(2,1)}, bf16[1024,512]{1,0:T(8,128)(2,1)}, bf16[1024,512]{1,0:T(8,128)(2,1)}, bf16[2,1024,512]{2,1,0:T(8,128)(2,1)},...) custom-call(f32[1024,2048]{1,0:T(8,128)} %fusion.113.q_ref, f32[1024,1024]{1,0:T(8,128)} %fusion.27.kv_ref, ...), custom_call_target="tpu_custom_call" | custom-call | flops 1048576 | bytes 4194304 | tf_op jit(solution)/shard_map/attend/pallas_call | solution.py:109
  302.0 28.0 %all-gather.10.cloned.1.call-done = bf16[2048,2048]{0,1:T(8,128)(2,1)} async-done(((bf16[256,2048]{0,1:T(8,128)(2,1)}), bf16[2048,2048]{0,1:T(8,128)(2,1)}) %all-gather.10.cloned.1.call-update) | async-done | bytes 8388624 | tf_op jit(solution)/shard_map/all_gather | solution.py:364
  330.0 12.9 convolution_convert_fusion.14
  351.8 44.8 %all-to-all-done.4 = bf16[8,2,704,256]{3,2,1,0:T(8,128)(2,1)} async-done(((bf16[8,2,704,256]{3,2,1,0:T(8,128)(2,1)}), bf16[8,2,704,256]{3,2,1,0:T(8,128)(2,1)}, u32[]{:S(2)}, u32[]{:S(2)}) %all-to-all-start.4) | async-done | bytes 5767200 | tf_op jit(solution)/shard_map/all_to_all | solution.py:354
  415.9 78.3 %all-gather.14.cloned.1.call-done = bf16[2048,2048]{1,0:T(8,128)(2,1)} async-done(((bf16[256,2048]{1,0:T(8,128)(2,1)}), bf16[2048,2048]{1,0:T(8,128)(2,1)}) %all-gather.14.cloned.1.call-update) | async-done | bytes 8388624 | tf_op jit(solution)/shard_map/all_gather | solution.py:364
  559.5 16.8 %all-gather.12.cloned.1.call-done = bf16[2048,2048]{1,0:T(8,128)(2,1)} async-done(((bf16[256,2048]{1,0:T(8,128)(2,1)}), bf16[2048,2048]{1,0:T(8,128)(2,1)}) %all-gather.12.cloned.1.call-update) | async-done | bytes 8388624 | tf_op jit(solution)/shard_map/all_gather | solution.py:364
  598.6 28.7 %expert_pass.5 = (bf16[704,1280]{1,0:T(8,128)(2,1)}, bf16[1408,1280]{1,0:T(8,128)(2,1)}, bf16[1280,2048]{1,0:T(8,128)(2,1)}, f32[1,1280]{1,0:T(1,128)}) custom-call(bf16[1280,2048]{1,0:T(8,128)(2,1)} %bitcast.307, f32[1,1280]{1,0:T(1,128)} %reshape.485.slot_gate_ref, bf16[704,2048]{1,0:T(8,128)(2,1)} %collective-permute-done.10.gate_w_ref, ...), custom_call_target="tpu_custom_call" | custom-call | flops 18454937600 | bytes 24379392 | tf_op jit(solution)/shard_map/expert_pass/pallas_call | solution.py:257
  627.3 29.0 %expert_pass.4 = (bf16[704,1280]{1,0:T(8,128)(2,1)}, bf16[1408,1280]{1,0:T(8,128)(2,1)}, bf16[1280,2048]{1,0:T(8,128)(2,1)}, f32[1,1280]{1,0:T(1,128)}) custom-call(bf16[1280,2048]{1,0:T(8,128)(2,1)} %bitcast.317, f32[1,1280]{1,0:T(1,128)} %reshape.482.slot_gate_ref, bf16[704,2048]{1,0:T(8,128)(2,1)} %bitcast.146.gate_w_ref, ...), custom_call_target="tpu_custom_call" | custom-call | flops 18454937600 | bytes 24379392 | tf_op jit(solution)/shard_map/expert_pass/pallas_call | solution.py:257
  657.7 36.9 %expert_pass.6 = (bf16[704,1280]{1,0:T(8,128)(2,1)}, bf16[1408,1280]{1,0:T(8,128)(2,1)}, bf16[1280,2048]{1,0:T(8,128)(2,1)}, f32[1,1280]{1,0:T(1,128)}) custom-call(bf16[1280,2048]{1,0:T(8,128)(2,1)} %bitcast.302, f32[1,1280]{1,0:T(1,128)} %reshape.487.slot_gate_ref, bf16[704,2048]{1,0:T(8,128)(2,1)} %collective-permute-done.11.gate_w_ref, ...), custom_call_target="tpu_custom_call" | custom-call | flops 18454937600 | bytes 24379392 | tf_op jit(solution)/shard_map/expert_pass/pallas_call | solution.py:257
  694.6 36.8 %expert_pass.7 = (bf16[704,1280]{1,0:T(8,128)(2,1)}, bf16[1408,1280]{1,0:T(8,128)(2,1)}, bf16[1280,2048]{1,0:T(8,128)(2,1)}, f32[1,1280]{1,0:T(1,128)}) custom-call(bf16[1280,2048]{1,0:T(8,128)(2,1)} %bitcast.312, f32[1,1280]{1,0:T(1,128)} %reshape.489.slot_gate_ref, bf16[704,2048]{1,0:T(8,128)(2,1)} %collective-permute-done.14.gate_w_ref, ...), custom_call_target="tpu_custom_call" | custom-call | flops 18454937600 | bytes 24379392 | tf_op jit(solution)/shard_map/expert_pass/pallas_call | solution.py:257
  731.5 14.0 fusion.22
  841.0 12.7 fusion.19
  883.9 22.5 %collective-permute-done.18 = bf16[256,2048]{1,0:T(8,128)(2,1)S(1)} collective-permute-done((bf16[256,2048]{1,0:T(8,128)(2,1)S(1)}, bf16[256,2048]{1,0:T(8,128)(2,1)S(1)}, u32[]{:S(2)}, u32[]{:S(2)}) %collective-permute-start.18) | collective-permute-done | bytes 1048608 | tf_op jit(solution)/shard_map/ppermute | solution.py:309
  906.4 21.6 %collective-permute-done.19 = bf16[256,2048]{1,0:T(8,128)(2,1)S(1)} collective-permute-done((bf16[256,2048]{1,0:T(8,128)(2,1)S(1)}, bf16[256,2048]{1,0:T(8,128)(2,1)S(1)}, u32[]{:S(2)}, u32[]{:S(2)}) %collective-permute-start.19) | collective-permute-done | bytes 1048608 | tf_op jit(solution)/shard_map/ppermute | solution.py:309
  930.0 11.0 fusion.118.g_ref
  941.0 11.2 convolution_convert_fusion.1
  954.7 32.8 %attend_back.1 = (bf16[1024,2048]{1,0:T(8,128)(2,1)}, bf16[1024,1024]{1,0:T(8,128)(2,1)}, bf16[1024,128]{1,0:T(8,128)(2,1)}) custom-call(f32[1024,2048]{1,0:T(8,128)} %fusion.118.g_ref, s32[1024,2]{1,0:T(8,128)} %slice.255.route_ref, f32[1024,2]{1,0:T(8,128)} %pad_maximum_fusion.7.gate_ref, bf16[2,1024,512]{2,1,0:T(8,128)(2,1)} %get-tuple-element.247.query_ref, ...), custom_call_target="tpu_custom_call" | custom-call | flops 1048576 | bytes 4194304 | tf_op jit(solution)/shard_map/attend_back/pallas_call | solution.py:194
  997.2 11.4 convolution_convert_fusion
  1035.9 11.2 add_convert_fusion
  1049.8 35.6 %collective-permute-done.24 = bf16[704,2048]{1,0:T(8,128)(2,1)} collective-permute-done((bf16[704,2048]{1,0:T(8,128)(2,1)S(1)}, bf16[704,2048]{1,0:T(8,128)(2,1)}, u32[]{:S(2)}, u32[]{:S(2)}) %collective-permute-start.24) | collective-permute-done | bytes 2883616 | tf_op jit(solution)/shard_map/ppermute | solution.py:309
  1177.3 12.0 collective-permute-done.25
  1190.4 26.0 %collective-permute-done.26 = bf16[256,2176]{1,0:T(8,128)(2,1)} collective-permute-done((bf16[256,2176]{1,0:T(8,128)(2,1)}, bf16[256,2176]{1,0:T(8,128)(2,1)}, u32[]{:S(2)}, u32[]{:S(2)}) %collective-permute-start.26) | collective-permute-done | bytes 1114144 | tf_op jit(solution)/shard_map/ppermute | solution.py:309
  1222.1 25.2 %collective-permute-done.41 = bf16[352,2048]{1,0:T(8,128)(2,1)} collective-permute-done((bf16[352,2048]{1,0:T(8,128)(2,1)}, bf16[352,2048]{1,0:T(8,128)(2,1)}, u32[]{:S(2)}, u32[]{:S(2)}) %collective-permute-start.41) | collective-permute-done | bytes 1441824 | tf_op jit(solution)/shard_map/ppermute | solution.py:309
  1306.0 12.8 collective-permute-done.34
  1383.4 16.5 %all-to-all-done.9 = bf16[8,256,256]{1,2,0:T(8,128)(2,1)} async-done(((bf16[8,256,256]{1,2,0:T(8,128)(2,1)}), bf16[8,256,256]{1,2,0:T(8,128)(2,1)}, u32[]{:S(2)}, u32[]{:S(2)}) %all-to-all-start.9) | async-done | bytes 1048608 | tf_op jit(solution)/shard_map/all_to_all | solution.py:354
  (621 shorter events, 616.8 us)
Async XLA Ops:
  17.5 89.0 %all-gather.6.cloned.1.call-start = ((), (), s32[]{:S(2)}) async-start(), calls=%async_computation.15 | async-start | bytes 5308416 | tf_op jit(solution)/shard_map/all_gather | solution.py:364
  28.0 181.8 %all-gather.8.cloned.1.call-start = ((), (), s32[]{:S(2)}) async-start(), calls=%async_computation.16 | async-start | bytes 9437184 | tf_op jit(solution)/shard_map/all_gather | solution.py:364
  103.5 76.3 %collective-permute-start.3 = (bf16[704,2048]{1,0:T(8,128)(2,1)}, bf16[704,2048]{1,0:T(8,128)(2,1)}, u32[]{:S(2)}, u32[]{:S(2)}) collective-permute-start(bf16[704,2048]{1,0:T(8,128)(2,1)} %bitcast.3.down_ref), channel_id=1, source_target_pairs={{0,8},{8,0},{16,24},{24,16},{1,9},{9,1},{17,25},{25,17},{2,10},{10... | collective-permute-start | bytes 8650760 | tf_op jit(solution)/shard_map/ppermute | solution.py:309
  104.4 75.5 %collective-permute-start.4 = (bf16[704,2048]{1,0:T(8,128)(2,1)}, bf16[704,2048]{1,0:T(8,128)(2,1)}, u32[]{:S(2)}, u32[]{:S(2)}) collective-permute-start(bf16[704,2048]{1,0:T(8,128)(2,1)} %bitcast.3.down_ref), channel_id=1, source_target_pairs={{0,16},{8,24},{16,0},{24,8},{1,17},{9,25},{17,1},{25,9},{2,18},{10... | collective-permute-start | bytes 8650760 | tf_op jit(solution)/shard_map/ppermute | solution.py:309
  179.8 150.2 %all-gather.10.cloned.1.call-start = ((), (), s32[]{:S(2)}) async-start(), calls=%async_computation.17 | async-start | bytes 9437184 | tf_op jit(solution)/shard_map/all_gather | solution.py:364
  215.5 181.1 %all-to-all-start.4 = ((bf16[8,2,704,256]{3,2,1,0:T(8,128)(2,1)}), bf16[8,2,704,256]{3,2,1,0:T(8,128)(2,1)}, u32[]{:S(2)}, u32[]{:S(2)}) async-start(bf16[8,2,704,256]{3,2,1,0:T(8,128)(2,1)} %copy.608), calls=%async_computation.4 | async-start | bytes 11534336 | tf_op jit(solution)/shard_map/all_to_all | solution.py:354
  220.4 273.8 %all-gather.14.cloned.1.call-start = ((), (), s32[]{:S(2)}) async-start(), calls=%async_computation.19 | async-start | bytes 9437184 | tf_op jit(solution)/shard_map/all_gather | solution.py:364
  409.5 166.8 %all-gather.12.cloned.1.call-start = ((), (), s32[]{:S(2)}) async-start(), calls=%async_computation.18 | async-start | bytes 9437184 | tf_op jit(solution)/shard_map/all_gather | solution.py:364
  410.1 463.0 %reduce-scatter.6.cloned.1.call-start = ((), (), s32[]{:S(2)}) async-start(), calls=%async_computation.20 | async-start | bytes 9437184 | tf_op jit(solution)/shard_map/reduce_scatter | solution.py:367
  411.9 139.6 %collective-permute-start.10 = (bf16[704,2048]{1,0:T(8,128)(2,1)}, bf16[704,2048]{1,0:T(8,128)(2,1)}, u32[]{:S(2)}, u32[]{:S(2)}) collective-permute-start(bf16[704,2048]{1,0:T(8,128)(2,1)} %bitcast.146.gate_w_ref), channel_id=1, source_target_pairs={{0,8},{8,0},{16,24},{24,16},{1,9},{9,1},{17,25},{25,17},{2,10},{10... | collective-permute-start | bytes 8650760 | tf_op jit(solution)/shard_map/ppermute | solution.py:309
  413.3 146.2 %collective-permute-start.11 = (bf16[704,2048]{1,0:T(8,128)(2,1)}, bf16[704,2048]{1,0:T(8,128)(2,1)}, u32[]{:S(2)}, u32[]{:S(2)}) collective-permute-start(bf16[704,2048]{1,0:T(8,128)(2,1)} %bitcast.146.gate_w_ref), channel_id=1, source_target_pairs={{0,16},{8,24},{16,0},{24,8},{1,17},{9,25},{17,1},{25,9},{2,18},{10... | collective-permute-start | bytes 8650760 | tf_op jit(solution)/shard_map/ppermute | solution.py:309
  414.8 128.8 %collective-permute-start.12 = (bf16[704,2048]{1,0:T(8,128)(2,1)}, bf16[704,2048]{1,0:T(8,128)(2,1)}, u32[]{:S(2)}, u32[]{:S(2)}) collective-permute-start(bf16[704,2048]{1,0:T(8,128)(2,1)} %bitcast.148.up_w_ref), channel_id=1, source_target_pairs={{0,8},{8,0},{16,24},{24,16},{1,9},{9,1},{17,25},{25,17},{2,10},{10... | collective-permute-start | bytes 8650760 | tf_op jit(solution)/shard_map/ppermute | solution.py:309
  415.4 144.2 %collective-permute-start.13 = (bf16[704,2048]{1,0:T(8,128)(2,1)}, bf16[704,2048]{1,0:T(8,128)(2,1)}, u32[]{:S(2)}, u32[]{:S(2)}) collective-permute-start(bf16[704,2048]{1,0:T(8,128)(2,1)} %bitcast.148.up_w_ref), channel_id=1, source_target_pairs={{0,16},{8,24},{16,0},{24,8},{1,17},{9,25},{17,1},{25,9},{2,18},{10... | collective-permute-start | bytes 8650760 | tf_op jit(solution)/shard_map/ppermute | solution.py:309
  591.6 64.9 %collective-permute-start.14 = (bf16[704,2048]{1,0:T(8,128)(2,1)}, bf16[704,2048]{1,0:T(8,128)(2,1)}, u32[]{:S(2)}, u32[]{:S(2)}) collective-permute-start(bf16[704,2048]{1,0:T(8,128)(2,1)} %collective-permute-done.10.gate_w_ref), channel_id=1, source_target_pairs={{0,16},{8,24},{16,0},{24,8},{1,17},{9,25},{17,1},{25,9},{2,18},{10... | collective-permute-start | bytes 8650760 | tf_op jit(solution)/shard_map/ppermute | solution.py:309
  593.0 64.7 %collective-permute-start.15 = (bf16[704,2048]{1,0:T(8,128)(2,1)}, bf16[704,2048]{1,0:T(8,128)(2,1)}, u32[]{:S(2)}, u32[]{:S(2)}) collective-permute-start(bf16[704,2048]{1,0:T(8,128)(2,1)} %collective-permute-done.13.up_w_ref), channel_id=1, source_target_pairs={{0,8},{8,0},{16,24},{24,16},{1,9},{9,1},{17,25},{25,17},{2,10},{10... | collective-permute-start | bytes 8650760 | tf_op jit(solution)/shard_map/ppermute | solution.py:309
  756.6 75.1 %collective-permute-start.17 = (bf16[704,2048]{1,0:T(8,128)(2,1)}, bf16[704,2048]{1,0:T(8,128)(2,1)}, u32[]{:S(2)}, u32[]{:S(2)}) collective-permute-start(bf16[704,2048]{1,0:T(8,128)(2,1)} %convolution_convert_fusion.22), channel_id=1, source_target_pairs={{0,16},{8,24},{16,0},{24,8},{1,17},{9,25},{17,1},{25,9},{2,18},{10... | collective-permute-start | bytes 8650760 | tf_op jit(solution)/shard_map/ppermute | solution.py:309
  761.8 69.9 %collective-permute-start.16 = (bf16[704,2048]{1,0:T(8,128)(2,1)}, bf16[704,2048]{1,0:T(8,128)(2,1)}, u32[]{:S(2)}, u32[]{:S(2)}) collective-permute-start(bf16[704,2048]{1,0:T(8,128)(2,1)} %convolution_convert_fusion.23), channel_id=1, source_target_pairs={{0,8},{8,0},{16,24},{24,16},{1,9},{9,1},{17,25},{25,17},{2,10},{10... | collective-permute-start | bytes 8650760 | tf_op jit(solution)/shard_map/ppermute | solution.py:309
  807.1 242.7 %reduce-scatter.8.cloned.1.call-start = ((), (), s32[]{:S(2)}) async-start(), calls=%async_computation.21 | async-start | bytes 9437184 | tf_op jit(solution)/shard_map/reduce_scatter | solution.py:367
  853.8 237.8 %reduce-scatter.10.cloned.1.call-start = ((), (), s32[]{:S(2)}) async-start(), calls=%async_computation.22 | async-start | bytes 9437184 | tf_op jit(solution)/shard_map/reduce_scatter | solution.py:367
  952.2 299.6 %reduce-scatter.12.cloned.1.call-start = ((), (), s32[]{:S(2)}) async-start(), calls=%async_computation.23 | async-start | bytes 9437184 | tf_op jit(solution)/shard_map/reduce_scatter | solution.py:367
  952.3 64.4 %collective-permute-start.21 = (bf16[704,2048]{1,0:T(8,128)(2,1)}, bf16[704,2048]{1,0:T(8,128)(2,1)}, u32[]{:S(2)}, u32[]{:S(2)}) collective-permute-start(bf16[704,2048]{1,0:T(8,128)(2,1)} %convolution_convert_fusion.19), channel_id=1, source_target_pairs={{0,8},{8,0},{16,24},{24,16},{1,9},{9,1},{17,25},{25,17},{2,10},{10... | collective-permute-start | bytes 8650760 | tf_op jit(solution)/shard_map/ppermute | solution.py:309
  953.0 63.9 %collective-permute-start.22 = (bf16[704,2048]{1,0:T(8,128)(2,1)}, bf16[704,2048]{1,0:T(8,128)(2,1)}, u32[]{:S(2)}, u32[]{:S(2)}) collective-permute-start(bf16[704,2048]{1,0:T(8,128)(2,1)} %convolution_convert_fusion.16), channel_id=1, source_target_pairs={{0,16},{8,24},{16,0},{24,8},{1,17},{9,25},{17,1},{25,9},{2,18},{10... | collective-permute-start | bytes 8650760 | tf_op jit(solution)/shard_map/ppermute | solution.py:309
  1022.3 63.1 %collective-permute-start.24 = (bf16[704,2048]{1,0:T(8,128)(2,1)S(1)}, bf16[704,2048]{1,0:T(8,128)(2,1)}, u32[]{:S(2)}, u32[]{:S(2)}) collective-permute-start(bf16[704,2048]{1,0:T(8,128)(2,1)S(1)} %add_convert_fusion.3), channel_id=1, source_target_pairs={{0,8},{8,0},{16,24},{24,16},{1,9},{9,1},{17,25},{25,17},{2,10},{10... | collective-permute-start | bytes 8650760 | tf_op jit(solution)/shard_map/ppermute | solution.py:309
  1028.7 62.9 %collective-permute-start.23 = (bf16[704,2048]{1,0:T(8,128)(2,1)}, bf16[704,2048]{1,0:T(8,128)(2,1)}, u32[]{:S(2)}, u32[]{:S(2)}) collective-permute-start(bf16[704,2048]{1,0:T(8,128)(2,1)} %add_convert_fusion.4), channel_id=1, source_target_pairs={{0,16},{8,24},{16,0},{24,8},{1,17},{9,25},{17,1},{25,9},{2,18},{10... | collective-permute-start | bytes 8650760 | tf_op jit(solution)/shard_map/ppermute | solution.py:309
  1103.4 159.8 %all-to-all-start.6 = ((bf16[8,704,256]{2,1,0:T(8,128)(2,1)}), bf16[8,704,256]{2,1,0:T(8,128)(2,1)}, u32[]{:S(2)}, u32[]{:S(2)}) async-start(bf16[8,704,256]{2,1,0:T(8,128)(2,1)} %bitcast.281), calls=%async_computation.9 | async-start | bytes 5767168 | tf_op jit(solution)/shard_map/all_to_all | solution.py:354
  1107.9 195.6 %reduce-scatter.14.cloned.1.call-start = ((), (), s32[]{:S(2)}) async-start(), calls=%async_computation.24 | async-start | bytes 4718592 | tf_op jit(solution)/shard_map/reduce_scatter | solution.py:367
  1168.7 78.6 %collective-permute-start.41 = (bf16[352,2048]{1,0:T(8,128)(2,1)}, bf16[352,2048]{1,0:T(8,128)(2,1)}, u32[]{:S(2)}, u32[]{:S(2)}) collective-permute-start(bf16[352,2048]{1,0:T(8,128)(2,1)} %convolution_convert_fusion.26), channel_id=1, source_target_pairs={{0,16},{8,24},{16,0},{24,8},{1,17},{9,25},{17,1},{25,9},{2,18},{10... | collective-permute-start | bytes 4325384 | tf_op jit(solution)/shard_map/ppermute | solution.py:309
  1172.6 97.8 %collective-permute-start.39 = (bf16[352,2048]{1,0:T(8,128)(2,1)}, bf16[352,2048]{1,0:T(8,128)(2,1)}, u32[]{:S(2)}, u32[]{:S(2)}) collective-permute-start(bf16[352,2048]{1,0:T(8,128)(2,1)} %convolution_convert_fusion.28), channel_id=1, source_target_pairs={{0,8},{8,0},{16,24},{24,16},{1,9},{9,1},{17,25},{25,17},{2,10},{10... | collective-permute-start | bytes 4325384 | tf_op jit(solution)/shard_map/ppermute | solution.py:309
  1189.3 152.6 %collective-permute-start.38 = (bf16[352,2048]{1,0:T(8,128)(2,1)}, bf16[352,2048]{1,0:T(8,128)(2,1)}, u32[]{:S(2)}, u32[]{:S(2)}) collective-permute-start(bf16[352,2048]{1,0:T(8,128)(2,1)} %convolution_convert_fusion.30), channel_id=1, source_target_pairs={{0,16},{8,24},{16,0},{24,8},{1,17},{9,25},{17,1},{25,9},{2,18},{10... | collective-permute-start | bytes 4325384 | tf_op jit(solution)/shard_map/ppermute | solution.py:309
  1216.4 125.5 %collective-permute-start.37 = (bf16[352,2048]{1,0:T(8,128)(2,1)}, bf16[352,2048]{1,0:T(8,128)(2,1)}, u32[]{:S(2)}, u32[]{:S(2)}) collective-permute-start(bf16[352,2048]{1,0:T(8,128)(2,1)} %convolution_convert_fusion.31), channel_id=1, source_target_pairs={{0,8},{8,0},{16,24},{24,16},{1,9},{9,1},{17,25},{25,17},{2,10},{10... | collective-permute-start | bytes 4325384 | tf_op jit(solution)/shard_map/ppermute | solution.py:309
  1264.9 77.1 %all-to-all-start.7 = ((bf16[8,704,256]{2,1,0:T(8,128)(2,1)}), bf16[8,704,256]{2,1,0:T(8,128)(2,1)}, u32[]{:S(2)}, u32[]{:S(2)}) async-start(bf16[8,704,256]{2,1,0:T(8,128)(2,1)} %bitcast.279), calls=%async_computation.10 | async-start | bytes 5767168 | tf_op jit(solution)/shard_map/all_to_all | solution.py:354
  1280.7 61.3 %collective-permute-start.42 = (bf16[352,2048]{1,0:T(8,128)(2,1)}, bf16[352,2048]{1,0:T(8,128)(2,1)}, u32[]{:S(2)}, u32[]{:S(2)}) collective-permute-start(bf16[352,2048]{1,0:T(8,128)(2,1)} %add_convert_fusion.5), channel_id=1, source_target_pairs={{0,8},{8,0},{16,24},{24,16},{1,9},{9,1},{17,25},{25,17},{2,10},{10... | collective-permute-start | bytes 4325384 | tf_op jit(solution)/shard_map/ppermute | solution.py:309
  (146 other events, 2686.6 us)
Sparse Core Ops, SparseCore 0:
  28.1 51.4 all-gather.5
  81.8 103.6 all-gather.7
  194.8 135.1 all-gather.9
  409.6 84.5 all-gather.13
  495.7 80.5 all-gather.11
  745.6 87.3 reduce-scatter.5
  853.9 90.3 reduce-scatter.7
  952.4 89.8 reduce-scatter.9
  1044.6 106.0 reduce-scatter.11
  1152.8 80.4 reduce-scatter.13

commit v8 on v7

--- a/solution.py
+++ b/solution.py
@@ -516,30 +516,27 @@
     gate_grads_f = shuffle(jnp.stack(grad_gate_f, axis=1).reshape(n_s, TOPK * tokens), "shard")
     out_rows_f = []
     for k in range(n_e):
-        if k < n_e - 1:
-            hidden = after(hiddens[k], *grad_gate_up[n_e - 1])
-        else:
-            for j in reversed(range(n_e - 1)):
-                grad_gate_up[j] = gate_up_grads(j, back_sum)
-            hidden, halves, grad_gate_up, gate_grads_f = lax.optimization_barrier(
-                (hiddens[k], halves, grad_gate_up, gate_grads_f)
-            )
+        hidden = after(hiddens[k], *grad_gate_up[n_e - 1])
         out_rows_f.append(dot_tn(hidden, down_w[k]).astype(BF).reshape(n_s, capacity, width))
+    for j in range(1, n_e - 1):
+        grad_gate_up[j] = gate_up_grads(j, back_sum)
+
+    def logit_grads(gates, grads, routes):
+        centre = sum(gates[j] * grads[j] for j in range(TOPK))
+        return place([gates[j] * (grads[j] - centre) for j in range(TOPK)], routes, ids)
+
+    own_routes_f = ffn_routes[0]
+    own_gates_f = pair_softmax(pick(dot(h_ffn, router_f.astype(BF)), own_routes_f, ids))
+    grad_gates_f = jnp.sum(gate_grads_f, axis=0).reshape(TOPK, tokens, 1)
+    grad_logits_f = logit_grads(own_gates_f, grad_gates_f, own_routes_f)
+    out_rows_f, halves, grad_gate_up[1:], grad_logits_f = lax.optimization_barrier(
+        (out_rows_f, halves, grad_gate_up[1:], grad_logits_f)
+    )
     out_sum = tokens_of(out_rows_f)
     ffn_out = scatter_shard(out_sum)
     back_f, out_sum = lax.optimization_barrier((back_f, out_sum))
     back_f = back_f.astype(F32)
-    grad_gates_f = jnp.sum(gate_grads_f, axis=0).reshape(TOPK, tokens, 1)
-
     grad_out = cot.astype(F32)
-    own_routes_f = ffn_routes[0]
-    own_gates_f = pair_softmax(pick(dot(h_ffn, router_f.astype(BF)), own_routes_f, ids))
-
-    def logit_grads(gates, grads, routes):
-        centre = sum(gates[j] * grads[j] for j in range(TOPK))
-        return place([gates[j] * (grads[j] - centre) for j in range(TOPK)], routes, ids)
-
-    grad_logits_f = logit_grads(own_gates_f, grad_gates_f, own_routes_f)
     grad_router_f = dot_tn(h_ffn.astype(F32), grad_logits_f, PRECISE)
     grad_h_ffn = back_f + jnp.dot(grad_logits_f, router_f.T, precision=PRECISE)
     grad_norm, grad_gain_f = norm_back(grad_h_ffn, middle, inv_f, gain_f)
@@ -548,6 +545,7 @@
     grad_bias_a = jnp.sum(grad_middle, axis=0)
 
     grad_middle_low = grad_middle.astype(BF)
+    grad_gate_up[0] = gate_up_grads(0, back_f)
     seq_grad = spread(grad_middle_low)
     seq_grad, grad_gate_up = lax.optimization_barrier((seq_grad, grad_gate_up))
     near = deliver_near(grad_gate_up)
@@ -565,9 +563,7 @@
     back_a = (dot_nt(grad_query_all, query_w) + dot_nt(grad_key_value, key_value_w)).astype(BF)
     back_a = jnp.concatenate([back_a, gate_notes], axis=1)
     value = scatter_shard(grad_out_wt)
-    back_a, ffn_out, value, key_value_grad, *last = lax.optimization_barrier(
-        (back_a, ffn_out, value, key_value_grad, *last)
-    )
+    back_a, ffn_out, value, *last = lax.optimization_barrier((back_a, ffn_out, value, *last))
     gate_up_total = [v.astype(BF) for v in total(grad_gate_up[0], near, last)]
     outputs = (middle + ffn_out.astype(F32) + bias_f).astype(BF)[None]
     key_value_grad = key_value_grad.reshape(n_e, n_s, small_rows, 2 * group).transpose(1, 0, 2, 3)
@@ -587,9 +583,13 @@
     halves = deliver_first(grad_down[n_e - 1])
     back_a = collect(back_a)
     near, last = deliver_near(grad_down), deliver_last(grad_down, halves)
-    back_a, gate_turned, up_total = lax.optimization_barrier((back_a, gate_turned, gate_up_total[1]))
+    back_a, gate_turned, *near = lax.optimization_barrier((back_a, gate_turned, *near))
+    up_total, key_value_grad = lax.optimization_barrier((after(gate_up_total[1], gate_turned), key_value_grad))
     up_turned = to_rows(up_total)
+    grad_down_w = jnp.concatenate(total(grad_down[0], near, last), axis=0)[None]
     key_value_grad = trade(key_value_grad.reshape(n_e, small_rows, -1))
+    grad_key_w = key_value_grad[:, :, :group].transpose(1, 0, 2).reshape(small_rows, -1).astype(F32)
+    grad_value_w = key_value_grad[:, :, group:].transpose(1, 0, 2).reshape(small_rows, -1).astype(F32)
     gate_grads = back_a[:, width:width + TOPK] + back_a[:, width + TOPK:width + 2 * TOPK]
     grad_gates_a = [gate_grads[:, j:j + 1] for j in range(TOPK)]
     back_a = back_a[:, :width]
@@ -610,12 +610,7 @@
         + [v[:, None] for v in (grad_gain_a, grad_gain_f, grad_bias_a, grad_bias_f)],
         axis=1,
     )
-    shared, up_turned, grad_query_w, value, key_value_grad, near, last = lax.optimization_barrier(
-        (shared, up_turned, grad_query_w, out_part, key_value_grad, near, last)
-    )
-    grad_down_w = jnp.concatenate(total(grad_down[0], near, last), axis=0)[None]
-    grad_key_w = key_value_grad[:, :, :group].transpose(1, 0, 2).reshape(small_rows, -1).astype(F32)
-    grad_value_w = key_value_grad[:, :, group:].transpose(1, 0, 2).reshape(small_rows, -1).astype(F32)
+    shared, up_turned, grad_query_w, value = lax.optimization_barrier((shared, up_turned, grad_query_w, out_part))
     grad_out_w = shuffle(value, "shard").reshape(width, out_rows).T.astype(F32)[None]
     grad_query_w = grad_query_w.astype(F32)[None]
     grad_up_w = up_turned.T.astype(F32)[None]

time: 1420 us -> 1360 us (0.958)
  waiting for transfers between devices: 465 us -> 435 us
  matrix products: 334 us -> 317 us
    ppermute x43, waiting for transfers between devices: 255 us -> 220 us  [swap(): return lax.ppermute(value, 'expert', [(i, i ^ k) for i in range(n_e)])]
    dot_general x26, matrix products: 131 us -> 117 us  [dot(): return jnp.dot(a, b, preferred_element_type=F32)]
    unnamed x257 -> x280, local copies, waits for them, and re-layouts: 47.3 us -> 45.3 us
  transfers between devices with their start and end apart: 61 -> 61, of which waited for: 28 -> 27; matrix products, arithmetic and copies ran while one was open for 36% -> 37% of each run, Pallas kernels for 8% -> 9%
where the time goes in v8:
time: 1360 us
  waiting for transfers between devices  435 us (32%)
  matrix products  317 us (23%)
  Pallas kernels  191 us (14%)
  local copies, waits for them, and re-layouts  146 us (11%)
  other arithmetic  101 us (7%)
  starting transfers between devices  83.1 us (6%)
  blocking collectives  70.2 us (5%)
  between operations  16.8 us (1%)
    ppermute x43, waiting for transfers between devices, swap(): return lax.ppermute(value, 'expert', [(i, i ^ k) for i in range(n_e)])  220 us
    pallas_call x4, Pallas kernels, expert_pass(): pl.pallas_call(functools.partial(expert_kernel, ready), grid=(count // ti...  131 us
    all_gather x5, waiting for transfers between devices, gather_shard(): return lax.all_gather(value, 'shard', axis=0, tiled=True)  123 us
    dot_general x26, matrix products, dot(): return jnp.dot(a, b, preferred_element_type=F32)  117 us
    all_to_all x8, waiting for transfers between devices, shuffle(): return lax.all_to_all(value, axis, split_axis=0, concat_axis=0, tiled=True)  91.7 us
    all_to_all x2, blocking collectives, shuffle(): return lax.all_to_all(value, axis, split_axis=0, concat_axis=0, tiled=True)  70.2 us
    dot_general x9, matrix products, dot_tn(): lax.dot_general(a, b, (((0,), (0,)), ((), ())), precision=precision, pref...  65.2 us
    dot_general x7, matrix products, dot_nt(): lax.dot_general(a, b, (((1,), (1,)), ((), ())), preferred_element_type=F32)  64.7 us
  transfers between devices with their start and end apart: 61, of which 27 were waited for; matrix products, arithmetic and copies ran while one was open for 37% of the time, Pallas kernels for 9%

profile of v8, /device:TPU:0, one launch (start us, length us, event | category | flops | bytes accessed | tf_op | source)
XLA Modules:
  0.0 1359.3 jit_solution(3063164338797774363)
XLA Ops:
  29.2 16.1 %all_to_all.63 = bf16[4,256,512]{2,1,0:T(8,128)(2,1)S(1)} all-to-all(bf16[4,256,512]{2,1,0:T(8,128)(2,1)S(1)} %copy.600), channel_id=1, replica_groups=mesh['expert'=4,'shard'=8] {'expert'}, dimensions={0} | all-to-all | bytes 2097152 | tf_op jit(solution)/shard_map/all_to_all | solution.py:354
  53.1 22.7 %collective-permute-done = bf16[256,2176]{1,0:T(8,128)(2,1)S(1)} collective-permute-done((bf16[256,2176]{1,0:T(8,128)(2,1)}, bf16[256,2176]{1,0:T(8,128)(2,1)S(1)}, u32[]{:S(2)}, u32[]{:S(2)}) %collective-permute-start) | collective-permute-done | bytes 1114144 | tf_op jit(solution)/shard_map/ppermute | solution.py:309
  75.8 21.7 %collective-permute-done.1 = bf16[256,2176]{1,0:T(8,128)(2,1)} collective-permute-done((bf16[256,2176]{1,0:T(8,128)(2,1)}, bf16[256,2176]{1,0:T(8,128)(2,1)}, u32[]{:S(2)}, u32[]{:S(2)}) %collective-permute-start.1) | collective-permute-done | bytes 1114144 | tf_op jit(solution)/shard_map/ppermute | solution.py:309
  120.9 54.1 %all_to_all.64 = bf16[8,256,256]{2,1,0:T(8,128)(2,1)S(1)} all-to-all(bf16[8,256,256]{2,1,0:T(8,128)(2,1)S(1)} %bitcast.368), channel_id=1, replica_groups=mesh['expert'=4,'shard'=8] {'shard'}, dimensions={0} | all-to-all | bytes 2097152 | tf_op jit(solution)/shard_map/all_to_all | solution.py:354
  179.9 13.8 %all-to-all-done.3 = bf16[4,256,512]{1,2,0:T(8,128)(2,1)S(1)} async-done(((bf16[4,256,512]{1,2,0:T(8,128)(2,1)}), bf16[4,256,512]{1,2,0:T(8,128)(2,1)S(1)}, u32[]{:S(2)}, u32[]{:S(2)}) %all-to-all-start.3) | async-done | bytes 1048608 | tf_op jit(solution)/shard_map/all_to_all | solution.py:354
  237.7 22.2 %collective-permute-done.5 = bf16[352,2048]{1,0:T(8,128)(2,1)S(1)} collective-permute-done((bf16[352,2048]{1,0:T(8,128)(2,1)S(1)}, bf16[352,2048]{1,0:T(8,128)(2,1)S(1)}, u32[]{:S(2)}, u32[]{:S(2)}) %collective-permute-start.5) | collective-permute-done | bytes 1441824 | tf_op jit(solution)/shard_map/ppermute | solution.py:309
  264.4 11.0 fusion.113.q_ref
  275.5 26.6 %attend.1 = (bf16[2,1024,512]{2,1,0:T(8,128)(2,1)}, bf16[1024,512]{1,0:T(8,128)(2,1)}, bf16[1024,512]{1,0:T(8,128)(2,1)}, bf16[2,1024,512]{2,1,0:T(8,128)(2,1)},...) custom-call(f32[1024,2048]{1,0:T(8,128)} %fusion.113.q_ref, f32[1024,1024]{1,0:T(8,128)} %fusion.27.kv_ref, ...), custom_call_target="tpu_custom_call" | custom-call | flops 1048576 | bytes 4194304 | tf_op jit(solution)/shard_map/attend/pallas_call | solution.py:109
  302.1 27.6 %all-gather.10.cloned.1.call-done = bf16[2048,2048]{0,1:T(8,128)(2,1)} async-done(((bf16[256,2048]{0,1:T(8,128)(2,1)}), bf16[2048,2048]{0,1:T(8,128)(2,1)}) %all-gather.10.cloned.1.call-update) | async-done | bytes 8388624 | tf_op jit(solution)/shard_map/all_gather | solution.py:364
  329.7 12.6 convolution_convert_fusion.14
  351.3 45.3 %all-to-all-done.4 = bf16[8,2,704,256]{3,2,1,0:T(8,128)(2,1)} async-done(((bf16[8,2,704,256]{3,2,1,0:T(8,128)(2,1)}), bf16[8,2,704,256]{3,2,1,0:T(8,128)(2,1)}, u32[]{:S(2)}, u32[]{:S(2)}) %all-to-all-start.4) | async-done | bytes 5767200 | tf_op jit(solution)/shard_map/all_to_all | solution.py:354
  416.0 77.8 %all-gather.14.cloned.1.call-done = bf16[2048,2048]{1,0:T(8,128)(2,1)} async-done(((bf16[256,2048]{1,0:T(8,128)(2,1)}), bf16[2048,2048]{1,0:T(8,128)(2,1)}) %all-gather.14.cloned.1.call-update) | async-done | bytes 8388624 | tf_op jit(solution)/shard_map/all_gather | solution.py:364
  558.7 17.1 %all-gather.12.cloned.1.call-done = bf16[2048,2048]{1,0:T(8,128)(2,1)} async-done(((bf16[256,2048]{1,0:T(8,128)(2,1)}), bf16[2048,2048]{1,0:T(8,128)(2,1)}) %all-gather.12.cloned.1.call-update) | async-done | bytes 8388624 | tf_op jit(solution)/shard_map/all_gather | solution.py:364
  598.0 28.7 %expert_pass.5 = (bf16[704,1280]{1,0:T(8,128)(2,1)}, bf16[1408,1280]{1,0:T(8,128)(2,1)}, bf16[1280,2048]{1,0:T(8,128)(2,1)}, f32[1,1280]{1,0:T(1,128)}) custom-call(bf16[1280,2048]{1,0:T(8,128)(2,1)} %bitcast.301, f32[1,1280]{1,0:T(1,128)} %reshape.485.slot_gate_ref, bf16[704,2048]{1,0:T(8,128)(2,1)} %collective-permute-done.10.gate_w_ref, ...), custom_call_target="tpu_custom_call" | custom-call | flops 18454937600 | bytes 24379392 | tf_op jit(solution)/shard_map/expert_pass/pallas_call | solution.py:257
  626.7 29.0 %expert_pass.4 = (bf16[704,1280]{1,0:T(8,128)(2,1)}, bf16[1408,1280]{1,0:T(8,128)(2,1)}, bf16[1280,2048]{1,0:T(8,128)(2,1)}, f32[1,1280]{1,0:T(1,128)}) custom-call(bf16[1280,2048]{1,0:T(8,128)(2,1)} %bitcast.313, f32[1,1280]{1,0:T(1,128)} %reshape.482.slot_gate_ref, bf16[704,2048]{1,0:T(8,128)(2,1)} %bitcast.145.gate_w_ref, ...), custom_call_target="tpu_custom_call" | custom-call | flops 18454937600 | bytes 24379392 | tf_op jit(solution)/shard_map/expert_pass/pallas_call | solution.py:257
  657.2 36.9 %expert_pass.6 = (bf16[704,1280]{1,0:T(8,128)(2,1)}, bf16[1408,1280]{1,0:T(8,128)(2,1)}, bf16[1280,2048]{1,0:T(8,128)(2,1)}, f32[1,1280]{1,0:T(1,128)}) custom-call(bf16[1280,2048]{1,0:T(8,128)(2,1)} %bitcast.306, f32[1,1280]{1,0:T(1,128)} %reshape.487.slot_gate_ref, bf16[704,2048]{1,0:T(8,128)(2,1)} %collective-permute-done.11.gate_w_ref, ...), custom_call_target="tpu_custom_call" | custom-call | flops 18454937600 | bytes 24379392 | tf_op jit(solution)/shard_map/expert_pass/pallas_call | solution.py:257
  694.1 36.8 %expert_pass.7 = (bf16[704,1280]{1,0:T(8,128)(2,1)}, bf16[1408,1280]{1,0:T(8,128)(2,1)}, bf16[1280,2048]{1,0:T(8,128)(2,1)}, f32[1,1280]{1,0:T(1,128)}) custom-call(bf16[1280,2048]{1,0:T(8,128)(2,1)} %bitcast.318, f32[1,1280]{1,0:T(1,128)} %reshape.489.slot_gate_ref, bf16[704,2048]{1,0:T(8,128)(2,1)} %collective-permute-done.14.gate_w_ref, ...), custom_call_target="tpu_custom_call" | custom-call | flops 18454937600 | bytes 24379392 | tf_op jit(solution)/shard_map/expert_pass/pallas_call | solution.py:257
  731.0 14.2 %fusion.22 = bf16[8,256,2048]{2,1,0:T(8,128)(2,1)} fusion(bf16[8,160,2048]{2,1,0:T(8,128)(2,1)} %bitcast.409, bf16[8,160,2048]{2,1,0:T(8,128)(2,1)} %bitcast.408, bf16[8,160,2048]{2,1,0:T(8,128)(2,1)} %bitcast.406, bf16[8,160,2048]{2,1,0:T(8,128)(2,1)} %bitcast.407, pred[8,160,256]{1,2,0:T(32,128)(4,1)S(1)} %fusion.42, ...), kind=kOutput, calls=%fused_computation.37 | convolution fusion | flops 5460721664 | bytes 30670848 | tf_op jit(solution)/shard_map/dot_general | solution.py:501
  835.7 13.8 %fusion.19 = bf16[8,256,2048]{2,1,0:T(8,128)(2,1)} fusion(bf16[8,160,2048]{2,1,0:T(8,128)(2,1)} %bitcast.402, bf16[8,160,2048]{2,1,0:T(8,128)(2,1)} %bitcast.403, bf16[8,160,2048]{2,1,0:T(8,128)(2,1)} %bitcast.404, bf16[8,160,2048]{2,1,0:T(8,128)(2,1)} %bitcast.405, pred[8,160,256]{1,2,0:T(32,128)(4,1)S(1)} %fusion.42, ...), kind=kOutput, calls=%fused_computation.36 | convolution fusion | flops 5460721664 | bytes 30670848 | tf_op jit(solution)/shard_map/dot_general | solution.py:501
  872.8 11.6 collective-permute-done.18
  884.5 21.9 %collective-permute-done.19 = bf16[256,2048]{1,0:T(8,128)(2,1)S(1)} collective-permute-done((bf16[256,2048]{1,0:T(8,128)(2,1)S(1)}, bf16[256,2048]{1,0:T(8,128)(2,1)S(1)}, u32[]{:S(2)}, u32[]{:S(2)}) %collective-permute-start.19) | collective-permute-done | bytes 1048608 | tf_op jit(solution)/shard_map/ppermute | solution.py:309
  906.8 11.0 fusion.118.g_ref
  917.8 11.2 convolution_convert_fusion.1
  931.3 32.5 %attend_back.1 = (bf16[1024,2048]{1,0:T(8,128)(2,1)}, bf16[1024,1024]{1,0:T(8,128)(2,1)}, bf16[1024,128]{1,0:T(8,128)(2,1)}) custom-call(f32[1024,2048]{1,0:T(8,128)} %fusion.118.g_ref, s32[1024,2]{1,0:T(8,128)} %slice.255.route_ref, f32[1024,2]{1,0:T(8,128)} %pad_maximum_fusion.7.gate_ref, bf16[2,1024,512]{2,1,0:T(8,128)(2,1)} %get-tuple-element.249.query_ref, ...), custom_call_target="tpu_custom_call" | custom-call | flops 1048576 | bytes 4194304 | tf_op jit(solution)/shard_map/attend_back/pallas_call | solution.py:194
  963.8 9.7 convolution_convert_fusion.15
  973.5 11.4 convolution_convert_fusion
  1014.8 13.8 %add_convert_fusion = bf16[1024,2048]{1,0:T(8,128)(2,1)S(1)} fusion(f32[1024,2048]{1,0:T(8,128)} %fusion.25, bf16[1024,2048]{1,0:T(8,128)(2,1)} %get-tuple-element.258, bf16[2048,2048]{0,1:T(8,128)(2,1)} %all-gather.8.cloned.1.call-done), kind=kOutput, calls=%fused_computation.21 | convolution fusion | flops 8594128896 | bytes 25165824 | tf_op jit(solution)/shard_map/dot_general | solution.py:31
  1031.2 30.0 %collective-permute-done.24 = bf16[704,2048]{1,0:T(8,128)(2,1)} collective-permute-done((bf16[704,2048]{1,0:T(8,128)(2,1)S(1)}, bf16[704,2048]{1,0:T(8,128)(2,1)}, u32[]{:S(2)}, u32[]{:S(2)}) %collective-permute-start.24) | collective-permute-done | bytes 2883616 | tf_op jit(solution)/shard_map/ppermute | solution.py:309
  1119.4 18.6 %collective-permute-done.36 = bf16[256,512]{1,0:T(8,128)(2,1)S(1)} collective-permute-done((bf16[256,512]{1,0:T(8,128)(2,1)S(1)}, bf16[256,512]{1,0:T(8,128)(2,1)S(1)}, u32[]{:S(2)}, u32[]{:S(2)}) %collective-permute-start.36) | collective-permute-done | bytes 262176 | tf_op jit(solution)/shard_map/ppermute | solution.py:309
  1158.8 19.1 %collective-permute-done.39 = bf16[352,2048]{1,0:T(8,128)(2,1)} collective-permute-done((bf16[352,2048]{1,0:T(8,128)(2,1)}, bf16[352,2048]{1,0:T(8,128)(2,1)}, u32[]{:S(2)}, u32[]{:S(2)}) %collective-permute-start.39) | collective-permute-done | bytes 1441824 | tf_op jit(solution)/shard_map/ppermute | solution.py:309
  1191.6 21.6 %collective-permute-done.41 = bf16[352,2048]{1,0:T(8,128)(2,1)} collective-permute-done((bf16[352,2048]{1,0:T(8,128)(2,1)}, bf16[352,2048]{1,0:T(8,128)(2,1)}, u32[]{:S(2)}, u32[]{:S(2)}) %collective-permute-start.41) | collective-permute-done | bytes 1441824 | tf_op jit(solution)/shard_map/ppermute | solution.py:309
  1339.5 10.2 all-to-all-done.9
  (647 shorter events, 591.8 us)
Async XLA Ops:
  17.5 89.1 %all-gather.6.cloned.1.call-start = ((), (), s32[]{:S(2)}) async-start(), calls=%async_computation.15 | async-start | bytes 5308416 | tf_op jit(solution)/shard_map/all_gather | solution.py:364
  28.0 181.8 %all-gather.8.cloned.1.call-start = ((), (), s32[]{:S(2)}) async-start(), calls=%async_computation.16 | async-start | bytes 9437184 | tf_op jit(solution)/shard_map/all_gather | solution.py:364
  103.6 76.3 %collective-permute-start.3 = (bf16[704,2048]{1,0:T(8,128)(2,1)}, bf16[704,2048]{1,0:T(8,128)(2,1)}, u32[]{:S(2)}, u32[]{:S(2)}) collective-permute-start(bf16[704,2048]{1,0:T(8,128)(2,1)} %bitcast.3.down_ref), channel_id=1, source_target_pairs={{0,8},{8,0},{16,24},{24,16},{1,9},{9,1},{17,25},{25,17},{2,10},{10... | collective-permute-start | bytes 8650760 | tf_op jit(solution)/shard_map/ppermute | solution.py:309
  104.4 75.5 %collective-permute-start.4 = (bf16[704,2048]{1,0:T(8,128)(2,1)}, bf16[704,2048]{1,0:T(8,128)(2,1)}, u32[]{:S(2)}, u32[]{:S(2)}) collective-permute-start(bf16[704,2048]{1,0:T(8,128)(2,1)} %bitcast.3.down_ref), channel_id=1, source_target_pairs={{0,16},{8,24},{16,0},{24,8},{1,17},{9,25},{17,1},{25,9},{2,18},{10... | collective-permute-start | bytes 8650760 | tf_op jit(solution)/shard_map/ppermute | solution.py:309
  179.8 149.9 %all-gather.10.cloned.1.call-start = ((), (), s32[]{:S(2)}) async-start(), calls=%async_computation.17 | async-start | bytes 9437184 | tf_op jit(solution)/shard_map/all_gather | solution.py:364
  215.5 181.2 %all-to-all-start.4 = ((bf16[8,2,704,256]{3,2,1,0:T(8,128)(2,1)}), bf16[8,2,704,256]{3,2,1,0:T(8,128)(2,1)}, u32[]{:S(2)}, u32[]{:S(2)}) async-start(bf16[8,2,704,256]{3,2,1,0:T(8,128)(2,1)} %copy.608), calls=%async_computation.4 | async-start | bytes 11534336 | tf_op jit(solution)/shard_map/all_to_all | solution.py:354
  220.6 273.2 %all-gather.14.cloned.1.call-start = ((), (), s32[]{:S(2)}) async-start(), calls=%async_computation.19 | async-start | bytes 9437184 | tf_op jit(solution)/shard_map/all_gather | solution.py:364
  409.5 166.3 %all-gather.12.cloned.1.call-start = ((), (), s32[]{:S(2)}) async-start(), calls=%async_computation.18 | async-start | bytes 9437184 | tf_op jit(solution)/shard_map/all_gather | solution.py:364
  410.1 439.5 %reduce-scatter.6.cloned.1.call-start = ((), (), s32[]{:S(2)}) async-start(), calls=%async_computation.20 | async-start | bytes 9437184 | tf_op jit(solution)/shard_map/reduce_scatter | solution.py:367
  411.9 138.9 %collective-permute-start.10 = (bf16[704,2048]{1,0:T(8,128)(2,1)}, bf16[704,2048]{1,0:T(8,128)(2,1)}, u32[]{:S(2)}, u32[]{:S(2)}) collective-permute-start(bf16[704,2048]{1,0:T(8,128)(2,1)} %bitcast.145.gate_w_ref), channel_id=1, source_target_pairs={{0,8},{8,0},{16,24},{24,16},{1,9},{9,1},{17,25},{25,17},{2,10},{10... | collective-permute-start | bytes 8650760 | tf_op jit(solution)/shard_map/ppermute | solution.py:309
  413.4 145.3 %collective-permute-start.11 = (bf16[704,2048]{1,0:T(8,128)(2,1)}, bf16[704,2048]{1,0:T(8,128)(2,1)}, u32[]{:S(2)}, u32[]{:S(2)}) collective-permute-start(bf16[704,2048]{1,0:T(8,128)(2,1)} %bitcast.145.gate_w_ref), channel_id=1, source_target_pairs={{0,16},{8,24},{16,0},{24,8},{1,17},{9,25},{17,1},{25,9},{2,18},{10... | collective-permute-start | bytes 8650760 | tf_op jit(solution)/shard_map/ppermute | solution.py:309
  414.9 128.1 %collective-permute-start.12 = (bf16[704,2048]{1,0:T(8,128)(2,1)}, bf16[704,2048]{1,0:T(8,128)(2,1)}, u32[]{:S(2)}, u32[]{:S(2)}) collective-permute-start(bf16[704,2048]{1,0:T(8,128)(2,1)} %bitcast.147.up_w_ref), channel_id=1, source_target_pairs={{0,8},{8,0},{16,24},{24,16},{1,9},{9,1},{17,25},{25,17},{2,10},{10... | collective-permute-start | bytes 8650760 | tf_op jit(solution)/shard_map/ppermute | solution.py:309
  415.4 143.3 %collective-permute-start.13 = (bf16[704,2048]{1,0:T(8,128)(2,1)}, bf16[704,2048]{1,0:T(8,128)(2,1)}, u32[]{:S(2)}, u32[]{:S(2)}) collective-permute-start(bf16[704,2048]{1,0:T(8,128)(2,1)} %bitcast.147.up_w_ref), channel_id=1, source_target_pairs={{0,16},{8,24},{16,0},{24,8},{1,17},{9,25},{17,1},{25,9},{2,18},{10... | collective-permute-start | bytes 8650760 | tf_op jit(solution)/shard_map/ppermute | solution.py:309
  591.1 64.9 %collective-permute-start.14 = (bf16[704,2048]{1,0:T(8,128)(2,1)}, bf16[704,2048]{1,0:T(8,128)(2,1)}, u32[]{:S(2)}, u32[]{:S(2)}) collective-permute-start(bf16[704,2048]{1,0:T(8,128)(2,1)} %collective-permute-done.10.gate_w_ref), channel_id=1, source_target_pairs={{0,16},{8,24},{16,0},{24,8},{1,17},{9,25},{17,1},{25,9},{2,18},{10... | collective-permute-start | bytes 8650760 | tf_op jit(solution)/shard_map/ppermute | solution.py:309
  592.6 64.7 %collective-permute-start.15 = (bf16[704,2048]{1,0:T(8,128)(2,1)}, bf16[704,2048]{1,0:T(8,128)(2,1)}, u32[]{:S(2)}, u32[]{:S(2)}) collective-permute-start(bf16[704,2048]{1,0:T(8,128)(2,1)} %collective-permute-done.13.up_w_ref), channel_id=1, source_target_pairs={{0,8},{8,0},{16,24},{24,16},{1,9},{9,1},{17,25},{25,17},{2,10},{10... | collective-permute-start | bytes 8650760 | tf_op jit(solution)/shard_map/ppermute | solution.py:309
  752.9 70.4 %all-to-all-start.5 = ((f32[8,1,512]{2,1,0:T(1,128)}), f32[8,1,512]{2,1,0:T(1,128)S(1)}, u32[]{:S(2)}, u32[]{:S(2)}) async-start(f32[8,1,512]{2,1,0:T(1,128)} %copy.627), calls=%async_computation.6 | async-start | bytes 32768 | tf_op jit(solution)/shard_map/all_to_all | solution.py:354
  756.3 274.9 %reduce-scatter.8.cloned.1.call-start = ((), (), s32[]{:S(2)}) async-start(), calls=%async_computation.21 | async-start | bytes 9437184 | tf_op jit(solution)/shard_map/reduce_scatter | solution.py:367
  765.0 65.1 %collective-permute-start.17 = (bf16[704,2048]{1,0:T(8,128)(2,1)}, bf16[704,2048]{1,0:T(8,128)(2,1)}, u32[]{:S(2)}, u32[]{:S(2)}) collective-permute-start(bf16[704,2048]{1,0:T(8,128)(2,1)} %convolution_convert_fusion.22), channel_id=1, source_target_pairs={{0,16},{8,24},{16,0},{24,8},{1,17},{9,25},{17,1},{25,9},{2,18},{10... | collective-permute-start | bytes 8650760 | tf_op jit(solution)/shard_map/ppermute | solution.py:309
  770.9 64.8 %collective-permute-start.16 = (bf16[704,2048]{1,0:T(8,128)(2,1)}, bf16[704,2048]{1,0:T(8,128)(2,1)}, u32[]{:S(2)}, u32[]{:S(2)}) collective-permute-start(bf16[704,2048]{1,0:T(8,128)(2,1)} %convolution_convert_fusion.23), channel_id=1, source_target_pairs={{0,8},{8,0},{16,24},{24,16},{1,9},{9,1},{17,25},{25,17},{2,10},{10... | collective-permute-start | bytes 8650760 | tf_op jit(solution)/shard_map/ppermute | solution.py:309
  849.6 217.0 %reduce-scatter.10.cloned.1.call-start = ((), (), s32[]{:S(2)}) async-start(), calls=%async_computation.22 | async-start | bytes 9437184 | tf_op jit(solution)/shard_map/reduce_scatter | solution.py:367
  929.0 253.4 %reduce-scatter.14.cloned.1.call-start = ((), (), s32[]{:S(2)}) async-start(), calls=%async_computation.24 | async-start | bytes 9437184 | tf_op jit(solution)/shard_map/reduce_scatter | solution.py:367
  929.1 63.1 %collective-permute-start.21 = (bf16[704,2048]{1,0:T(8,128)(2,1)}, bf16[704,2048]{1,0:T(8,128)(2,1)}, u32[]{:S(2)}, u32[]{:S(2)}) collective-permute-start(bf16[704,2048]{1,0:T(8,128)(2,1)} %convolution_convert_fusion.21), channel_id=1, source_target_pairs={{0,8},{8,0},{16,24},{24,16},{1,9},{9,1},{17,25},{25,17},{2,10},{10... | collective-permute-start | bytes 8650760 | tf_op jit(solution)/shard_map/ppermute | solution.py:309
  930.4 62.9 %collective-permute-start.22 = (bf16[704,2048]{1,0:T(8,128)(2,1)}, bf16[704,2048]{1,0:T(8,128)(2,1)}, u32[]{:S(2)}, u32[]{:S(2)}) collective-permute-start(bf16[704,2048]{1,0:T(8,128)(2,1)} %convolution_convert_fusion.18), channel_id=1, source_target_pairs={{0,16},{8,24},{16,0},{24,8},{1,17},{9,25},{17,1},{25,9},{2,18},{10... | collective-permute-start | bytes 8650760 | tf_op jit(solution)/shard_map/ppermute | solution.py:309
  993.3 240.4 %reduce-scatter.12.cloned.1.call-start = ((), (), s32[]{:S(2)}) async-start(), calls=%async_computation.23 | async-start | bytes 4718592 | tf_op jit(solution)/shard_map/reduce_scatter | solution.py:367
  1004.7 61.9 %collective-permute-start.23 = (bf16[704,2048]{1,0:T(8,128)(2,1)}, bf16[704,2048]{1,0:T(8,128)(2,1)}, u32[]{:S(2)}, u32[]{:S(2)}) collective-permute-start(bf16[704,2048]{1,0:T(8,128)(2,1)} %add_convert_fusion.4), channel_id=1, source_target_pairs={{0,16},{8,24},{16,0},{24,8},{1,17},{9,25},{17,1},{25,9},{2,18},{10... | collective-permute-start | bytes 8650760 | tf_op jit(solution)/shard_map/ppermute | solution.py:309
  1076.8 156.9 %all-to-all-start.6 = ((bf16[8,704,256]{2,1,0:T(8,128)(2,1)}), bf16[8,704,256]{2,1,0:T(8,128)(2,1)}, u32[]{:S(2)}, u32[]{:S(2)}) async-start(bf16[8,704,256]{2,1,0:T(8,128)(2,1)} %bitcast.281), calls=%async_computation.9 | async-start | bytes 5767168 | tf_op jit(solution)/shard_map/all_to_all | solution.py:354
  1081.4 70.3 %collective-permute-start.25 = (bf16[256,2176]{1,0:T(8,128)(2,1)}, bf16[256,2176]{1,0:T(8,128)(2,1)}, u32[]{:S(2)}, u32[]{:S(2)}) collective-permute-start(bf16[256,2176]{1,0:T(8,128)(2,1)} %get-tuple-element.463), channel_id=1, source_target_pairs={{0,8},{8,0},{16,24},{24,16},{1,9},{9,1},{17,25},{25,17},{2,10},{10... | collective-permute-start | bytes 3342344 | tf_op jit(solution)/shard_map/ppermute | solution.py:309
  1082.6 70.3 %collective-permute-start.26 = (bf16[256,2176]{1,0:T(8,128)(2,1)}, bf16[256,2176]{1,0:T(8,128)(2,1)}, u32[]{:S(2)}, u32[]{:S(2)}) collective-permute-start(bf16[256,2176]{1,0:T(8,128)(2,1)} %get-tuple-element.465), channel_id=1, source_target_pairs={{0,16},{8,24},{16,0},{24,8},{1,17},{9,25},{17,1},{25,9},{2,18},{10... | collective-permute-start | bytes 3342344 | tf_op jit(solution)/shard_map/ppermute | solution.py:309
  1082.9 71.8 %collective-permute-start.27 = (bf16[256,2176]{1,0:T(8,128)(2,1)S(1)}, bf16[256,2176]{1,0:T(8,128)(2,1)}, u32[]{:S(2)}, u32[]{:S(2)}) collective-permute-start(bf16[256,2176]{1,0:T(8,128)(2,1)S(1)} %copy-done.40), channel_id=1, source_target_pairs={{0,24},{8,16},{16,8},{24,0},{1,25},{9,17},{17,9},{25,1},{2,26},{10... | collective-permute-start | bytes 3342344 | tf_op jit(solution)/shard_map/ppermute | solution.py:309
  1148.2 85.6 %collective-permute-start.29 = (bf16[352,2048]{1,0:T(8,128)(2,1)}, bf16[352,2048]{1,0:T(8,128)(2,1)}, u32[]{:S(2)}, u32[]{:S(2)}) collective-permute-start(bf16[352,2048]{1,0:T(8,128)(2,1)} %convolution_convert_fusion.30), channel_id=1, source_target_pairs={{0,16},{8,24},{16,0},{24,8},{1,17},{9,25},{17,1},{25,9},{2,18},{10... | collective-permute-start | bytes 4325384 | tf_op jit(solution)/shard_map/ppermute | solution.py:309
  1151.7 82.0 %collective-permute-start.28 = (bf16[352,2048]{1,0:T(8,128)(2,1)}, bf16[352,2048]{1,0:T(8,128)(2,1)}, u32[]{:S(2)}, u32[]{:S(2)}) collective-permute-start(bf16[352,2048]{1,0:T(8,128)(2,1)} %convolution_convert_fusion.31), channel_id=1, source_target_pairs={{0,8},{8,0},{16,24},{24,16},{1,9},{9,1},{17,25},{25,17},{2,10},{10... | collective-permute-start | bytes 4325384 | tf_op jit(solution)/shard_map/ppermute | solution.py:309
  1235.6 70.8 %all-to-all-start.7 = ((bf16[8,704,256]{2,1,0:T(8,128)(2,1)}), bf16[8,704,256]{2,1,0:T(8,128)(2,1)}, u32[]{:S(2)}, u32[]{:S(2)}) async-start(bf16[8,704,256]{2,1,0:T(8,128)(2,1)} %bitcast.279), calls=%async_computation.11 | async-start | bytes 5767168 | tf_op jit(solution)/shard_map/all_to_all | solution.py:354
  (158 other events, 3120.7 us)
Sparse Core Ops, SparseCore 0:
  28.1 51.4 all-gather.5
  81.8 103.6 all-gather.7
  194.8 134.8 all-gather.9
  409.6 84.0 all-gather.13
  495.2 80.5 all-gather.11
  745.4 87.3 reduce-scatter.5
  849.7 90.5 reduce-scatter.7
  942.5 87.9 reduce-scatter.9
  1032.9 118.0 reduce-scatter.13
  1153.7 79.3 reduce-scatter.11
